TPU v7x, 512 devices: a whole 4x4x16 slice. The times are simulated.
512 devices in a mesh: tok: 64 (over y_lo, z, core), row: 8 (over y_hi, x).
Axes of the slice: x: 4, y: 4 (y_hi: 2, y_lo: 2; y = y_hi * 2 + y_lo), z: 16, core: 2. Of those that a mesh axis runs over, the one named last changes fastest.
Arguments:
- calib: bfloat16 [8192, 4096], P('row', 'tok'), may hold values from -8 to 8
- base_weight: bfloat16 [8192, 4096], P('tok', 'row'), may hold values from -6 to 6
- keep_blocks: int32 [64, 16], replicated, may hold values from 0 to 31, all different within a row
Outputs:
- refined: bfloat16 [8192, 4096], P('tok', 'row')
Inputs may be any that keep to these rules, and one draw needn't show every extreme that they name: `keep_blocks`: each row lists 16 different block columns, and every block column is listed in some row.
All inputs are finite; a program needn't handle non-finite values.
Results may differ from a plain program's by a relative error of at most 0.0085.
Values may be sent and summed in bfloat16 or wider, within the bound.
No kernel may reach another device: no remote copies, remote signals or barrier semaphores. Data moves between devices by JAX's collectives and lax.ppermute only.
A program may use at most 64 MiB of HBM per device.

v0:
```python
import jax
import jax.numpy as jnp
from jax import lax
from jax.sharding import PartitionSpec as P

BLOCK = 128


def block_table(keep_blocks, ncols):
    labels = jnp.arange(ncols, dtype=jnp.int32)
    hits = (keep_blocks[:, :, None] == labels[None, None, :]).astype(jnp.float32)
    return jnp.sum(hits, axis=1)


def selector(first, count, nblocks):
    ids = (first + jnp.arange(count, dtype=jnp.int32)) // BLOCK
    return (ids[:, None] == jnp.arange(nblocks, dtype=jnp.int32)[None, :]).astype(jnp.float32)


def residual_product(diff, gram_cols):
    return jnp.dot(
        lax.all_gather(diff, "row", axis=1, tiled=True),
        gram_cols,
        preferred_element_type=jnp.float32,
    )


def on_device(calib, base_weight, keep_blocks):
    tok_pos = lax.axis_index("tok")
    row_pos = lax.axis_index("row")
    rows = base_weight.shape[0]
    cols = base_weight.shape[1]
    width = cols * lax.axis_size("row")
    tokens = calib.shape[0] * lax.axis_size("row")
    block_map = block_table(keep_blocks, width // BLOCK)
    row_sel = selector(tok_pos * rows, rows, block_map.shape[0])
    col_sel = selector(row_pos * cols, cols, block_map.shape[1])
    row_map = jnp.dot(row_sel, block_map)
    keep_local = jnp.dot(row_map, col_sel.T)
    base_float = base_weight.astype(jnp.float32)
    weight = (keep_local * base_float).astype(jnp.bfloat16)
    partial_value = lax.dot_general(
        calib,
        lax.all_gather(calib, "tok", axis=1, tiled=True),
        (((0,), (0,)), ((), ())),
        preferred_element_type=jnp.float32,
    )
    summed = lax.psum_scatter(partial_value, "row", scatter_dimension=1, tiled=True)
    gram_block = (summed / tokens).astype(jnp.bfloat16)
    gram_cols = lax.all_gather(gram_block, "tok", axis=0, tiled=True)
    diff = (weight.astype(jnp.float32) - base_float).astype(jnp.bfloat16)
    grad = residual_product(diff, gram_cols)
    weight = (weight.astype(jnp.float32) - 0.25 * keep_local * grad).astype(jnp.bfloat16)
    diff = (weight.astype(jnp.float32) - base_float).astype(jnp.bfloat16)
    grad = residual_product(diff, gram_cols)
    weight = (weight.astype(jnp.float32) - 0.25 * keep_local * grad).astype(jnp.bfloat16)
    return weight


def solution(mesh):
    return jax.shard_map(
        on_device,
        mesh=mesh,
        in_specs=(P("row", "tok"), P("tok", "row"), P()),
        out_specs=P("tok", "row"),
        check_vma=False,
    )
```

profile of v0, /device:TPU:1, one launch (start us, length us, event | category | flops | bytes accessed | tf_op | source)
XLA Modules:
  0.0 499.3 jit_solution(11192664810128790291)
XLA Ops:
  6.5 0.0 all-gather.7.cloned.1.call-start
  6.5 0.7 all-gather.7.cloned.1.call-update
  7.3 0.0 copy-start.1
  7.3 0.0 copy-start
  7.3 0.0 reduce-scatter.2.cloned.1.call-start
  7.3 136.8 %all-gather.7.cloned.1.call-done = bf16[1024,4096]{0,1:T(8,128)(2,1)} async-done(((bf16[1024,64]{0,1:T(8,128)(2,1)}), bf16[1024,4096]{0,1:T(8,128)(2,1)}) %all-gather.7.cloned.1.call-update) | async-done | bytes 8388624 | tf_op jit(solution)/shard_map/all_gather | solution.py:44
  144.1 7.2 %fusion.17 = f32[64,4096]{1,0:T(8,128)} fusion(bf16[1024,64]{0,1:T(8,128)(2,1)} %param.3, bf16[1024,4096]{0,1:T(8,128)(2,1)} %all-gather.7.cloned.1.call-done), kind=kOutput, calls=%fused_computation.35 | convolution fusion | flops 536870912 | bytes 9568256 | tf_op jit(solution)/shard_map/dot_general | solution.py:42
  151.3 0.0 reduce-scatter.2.cloned.1.call-update
  151.3 0.0 all-gather.5.cloned.1.call-start
  151.4 0.0 copy-done.1
  151.5 0.0 copy-done
  151.5 1.0 fusion.9
  152.5 0.0 all-gather.5.cloned.1.call-update
  152.5 0.0 all-gather.9.cloned.1.call-start
  152.6 80.1 %reduce-scatter.2.cloned.1.call-done = f32[64,512]{1,0:T(8,128)} async-done(((f32[64,4096]{1,0:T(8,128)}), f32[64,512]{1,0:T(8,128)}) %reduce-scatter.2.cloned.1.call-update) | async-done | bytes 131088 | tf_op jit(solution)/shard_map/reduce_scatter | solution.py:48
  232.6 1.5 multiply_convert_fusion
  234.2 0.0 all-gather.9.cloned.1.call-update
  234.2 0.0 all-gather.11.cloned.1.call-start
  234.2 65.2 %all-gather.5.cloned.1.call-done = bf16[128,4096]{1,0:T(8,128)(2,1)} async-done(((bf16[128,512]{1,0:T(8,128)(2,1)}), bf16[128,4096]{1,0:T(8,128)(2,1)}) %all-gather.5.cloned.1.call-update) | async-done | bytes 1048592 | tf_op jit(solution)/shard_map/all_gather | solution.py:22
  299.5 127.4 %all-gather.9.cloned.1.call-done = bf16[4096,512]{1,0:T(8,128)(2,1)} async-done(((bf16[64,512]{1,0:T(8,128)(2,1)}), bf16[4096,512]{1,0:T(8,128)(2,1)}) %all-gather.9.cloned.1.call-update) | async-done | bytes 4194320 | tf_op jit(solution)/shard_map/all_gather | solution.py:50
  426.9 3.9 fusion.10
  430.8 0.0 all-gather.11.cloned.1.call-update
  430.8 58.0 %all-gather.11.cloned.1.call-done = bf16[128,4096]{1,0:T(8,128)(2,1)} async-done(((bf16[128,512]{1,0:T(8,128)(2,1)}), bf16[128,4096]{1,0:T(8,128)(2,1)}) %all-gather.11.cloned.1.call-update) | async-done | bytes 1048592 | tf_op jit(solution)/shard_map/all_gather | solution.py:22
  488.9 3.9 fusion.4
  (3 shorter events, 0.1 us)
Async XLA Ops:
  6.5 137.6 %all-gather.7.cloned.1.call-start = ((), (), s32[]{:S(2)}) async-start(), calls=%async_computation.2 | async-start | bytes 8519680 | tf_op jit(solution)/shard_map/all_gather | solution.py:44
  7.3 144.2 %copy-start.1 = (s32[64,16]{0,1:T(8,128)S(1)}, s32[64,16]{0,1:T(8,128)}, u32[]{:S(2)}) copy-start(s32[64,16]{0,1:T(8,128)} %param.5) | copy-start | bytes 12292
  7.3 144.2 %copy-start = (bf16[128,512]{1,0:T(8,128)(2,1)S(1)}, bf16[128,512]{1,0:T(8,128)(2,1)}, u32[]{:S(2)}) copy-start(bf16[128,512]{1,0:T(8,128)(2,1)} %param.4) | copy-start | bytes 393220
  7.3 225.4 %reduce-scatter.2.cloned.1.call-start = ((), (), s32[]{:S(2)}) async-start(), calls=%async_computation.3 | async-start | bytes 1179648 | tf_op jit(solution)/shard_map/reduce_scatter | solution.py:48
  151.3 148.2 %all-gather.5.cloned.1.call-start = ((), (), s32[]{:S(2)}) async-start(), calls=%async_computation.1 | async-start | bytes 1179648 | tf_op jit(solution)/shard_map/all_gather | solution.py:22
  152.5 274.4 %all-gather.9.cloned.1.call-start = ((), (), s32[]{:S(2)}) async-start(), calls=%async_computation.4 | async-start | bytes 4259840 | tf_op jit(solution)/shard_map/all_gather | solution.py:50
  234.2 254.7 %all-gather.11.cloned.1.call-start = ((), (), s32[]{:S(2)}) async-start(), calls=%async_computation.5 | async-start | bytes 1179648 | tf_op jit(solution)/shard_map/all_gather | solution.py:22
Sparse Core Ops, SparseCore 0:
  9.5 134.5 all-gather.6
  151.4 81.1 reduce-scatter.1
  236.1 63.2 all-gather.4
  301.7 125.1 all-gather.8
  430.9 57.8 all-gather.10
where the time goes:
time: 500 us; the launch traced here: 499 us
  waiting for transfers between devices  468 us (94%)
  matrix products  16 us (3%)
  between operations  13.2 us (3%)
    all_gather x1, waiting for transfers between devices, on_device(): lax.all_gather(calib, 'tok', axis=1, tiled=True)  137 us
    all_gather x1, waiting for transfers between devices, on_device(): gram_cols = lax.all_gather(gram_block, 'tok', axis=0, tiled=True)  127 us
    all_gather x2, waiting for transfers between devices, residual_product(): lax.all_gather(diff, 'row', axis=1, tiled=True)  123 us
    reduce_scatter x1, waiting for transfers between devices, on_device(): lax.psum_scatter(partial_value, 'row', scatter_dimension=1, tiled=True)  80.1 us
  transfers between devices with their start and end apart: 5, of which 5 were waited for; matrix products, arithmetic and copies ran while one was open for 1% of the time, Pallas kernels for 0%

commit v1 on v0

v1 whole, which is shorter than its diff:
```python
import functools

import jax
import jax.numpy as jnp
from jax import lax
from jax.experimental import pallas as pl
from jax.experimental.pallas import tpu as pltpu
from jax.sharding import Mesh, PartitionSpec as P

BLOCK = 128
RATE = 0.25
NT = (((1,), (1,)), ((), ()))
AXES = ("ylo", "zh", "zl", "core", "yhi", "x")
SIZES = (2, 4, 4, 2, 2, 4)
TOK = ("ylo", "zh", "zl", "core")
ROW = ("yhi", "x")
SWAP = ((0, 1), (1, 0))


def vmem():
    return pl.BlockSpec(memory_space=pltpu.VMEM)


def smem():
    return pl.BlockSpec(memory_space=pltpu.SMEM)


def partial_gram_kernel(where, rows, own, other, out):
    ylo = where[0]
    half = out.shape[3]
    for j, cols in enumerate((own, other)):
        term = lax.dot_general(cols[...], rows[...], NT, preferred_element_type=jnp.float32)
        term = term.astype(jnp.bfloat16)
        first = (ylo ^ j) * 4
        for c in range(2):
            piece = term[:, c * half : (c + 1) * half]
            out[c, pl.ds(first, 4)] = piece.reshape(4, BLOCK, half)


def partial_gram(where, rows, own, other):
    k = rows.shape[0]
    return pl.pallas_call(
        partial_gram_kernel,
        out_shape=jax.ShapeDtypeStruct((2, 8, BLOCK, k // 2), jnp.bfloat16),
        in_specs=[smem(), vmem(), vmem(), vmem()],
        out_specs=vmem(),
        name="partial_gram",
        cost_estimate=pl.CostEstimate(
            flops=4 * k * k * rows.shape[1], bytes_accessed=5 * rows.size, transcendentals=0
        ),
    )(where, rows, own, other)


def step_kernel(last, where, flags, diffs, g00, g10, g01, g11, weight, base, *outs):
    ylo, core = where[0], where[1]
    half = g00.shape[2]
    total = jnp.zeros(weight.shape, jnp.float32)
    for dy, dc, gram in ((0, 0, g00), (0, 1, g01), (1, 0, g10), (1, 1, g11)):
        lanes = pl.ds(pl.multiple_of((core ^ dc) * half, half), half)
        for h in range(4):
            total += lax.dot_general(
                diffs[(ylo ^ dy) * 4 + h, :, lanes], gram[h], NT,
                preferred_element_type=jnp.float32,
            )
    block = lax.broadcasted_iota(jnp.int32, weight.shape, 1) // BLOCK
    keep = jnp.zeros(weight.shape, jnp.float32)
    for b in range(weight.shape[1] // BLOCK):
        keep = jnp.where(block == b, flags[b].astype(jnp.float32), keep)
    new = (weight[...].astype(jnp.float32) - RATE * keep * total).astype(jnp.bfloat16)
    outs[0][...] = new
    if not last:
        diff = (new.astype(jnp.float32) - base[...].astype(jnp.float32)).astype(jnp.bfloat16)
        for i in range(outs[1].shape[0]):
            outs[1][i] = diff


def step(last, where, flags, diffs, grams, weight, base):
    shape = jax.ShapeDtypeStruct(weight.shape, weight.dtype)
    outs = (shape,) if last else (shape, jax.ShapeDtypeStruct(diffs.shape, diffs.dtype))
    return pl.pallas_call(
        functools.partial(step_kernel, last),
        out_shape=outs,
        in_specs=[smem(), smem()] + [vmem()] * 7,
        out_specs=tuple(vmem() for _ in outs),
        name="last_step" if last else "first_step",
        compiler_params=pltpu.CompilerParams(vmem_limit_bytes=32 << 20),
        cost_estimate=pl.CostEstimate(
            flops=2 * diffs.size * weight.shape[1], bytes_accessed=12 * diffs.size // 2,
            transcendentals=0,
        ),
    )(where, flags, diffs, *grams, weight, base)


def spread(x, axes, n):
    return lax.all_to_all(jnp.broadcast_to(x[None], (n,) + x.shape), axes, 0, 0, tiled=True)


def on_device(calib, base_weight, keep_blocks):
    ylo, core = lax.axis_index("ylo"), lax.axis_index("core")
    tok_pos, row_pos = lax.axis_index(TOK), lax.axis_index(ROW)
    rows, cols = base_weight.shape
    tokens = calib.shape[0] * 8
    where = jnp.stack([ylo, core]).astype(jnp.int32)
    kept = lax.dynamic_slice(keep_blocks, (tok_pos, 0), (1, keep_blocks.shape[1]))
    nblocks = cols // BLOCK
    mine = row_pos * nblocks + jnp.arange(nblocks, dtype=jnp.int32)
    flags = jnp.any(kept[0][:, None] == mine[None, :], axis=0).astype(jnp.int32)
    keep = jnp.repeat(flags.astype(jnp.float32), BLOCK)[None, :]
    base_float = base_weight.astype(jnp.float32)
    weight = (keep * base_float).astype(jnp.bfloat16)
    diff = (weight.astype(jnp.float32) - base_float).astype(jnp.bfloat16)
    diff, calib = lax.optimization_barrier((diff, calib))
    diffs = lax.all_gather(diff, ROW, axis=0)

    feats = lax.all_to_all(calib.T, "core", 1, 0, tiled=True)
    own = lax.all_gather(feats, "zh", axis=0, tiled=True)
    other = lax.ppermute(own, "ylo", SWAP)
    mates = lax.all_gather(feats, "zl", axis=0, tiled=True)
    term = partial_gram(where, mates, own, other)
    half = term.shape[3]
    terms = lax.all_to_all(term.reshape(16, BLOCK, half), ("core",) + ROW, 0, 0, tiled=True)
    gram = (jnp.sum(terms.astype(jnp.float32), axis=0) / tokens).astype(jnp.bfloat16)

    g00 = spread(gram, ("zh", "zl"), 16).reshape(4, 4 * BLOCK, half)
    g10 = lax.ppermute(g00, "ylo", SWAP)
    g01 = lax.ppermute(g00, "core", SWAP)
    g11 = lax.ppermute(g10, "core", SWAP)
    grams = (g00, g10, g01, g11)

    weight, sent = step(False, where, flags, diffs, grams, weight, base_weight)
    diffs = lax.all_to_all(sent, ROW, 0, 0, tiled=True)
    return step(True, where, flags, diffs, grams, weight, base_weight)[0]


def solution(mesh):
    split = Mesh(mesh.devices.reshape(SIZES), AXES)
    return jax.shard_map(
        on_device,
        mesh=split,
        in_specs=(P(ROW, TOK), P(TOK, ROW), P()),
        out_specs=P(TOK, ROW),
        check_vma=False,
    )
```

time: 500 us -> 247 us (0.49)
  waiting for transfers between devices: 468 us -> 40.9 us
  blocking collectives: 0 us -> 149 us
  starting transfers between devices: 0.17 us -> 25.7 us
  matrix products: 16 us -> 0 us
  Pallas kernels: 0 us -> 9.17 us
    all_gather x4 -> x1, waiting for transfers between devices: 387 us -> 32.6 us  [on_device(): diffs = lax.all_gather(diff, ROW, axis=0)]
    all_to_all x0 -> x4, blocking collectives: none -> 109 us  [the longest x1 52.5 us: spread(): lax.all_to_all(jnp.broadcast_to(x[None], (n,) + x.shape), axes, 0, 0, til...]
    reduce_scatter x1 -> x0, waiting for transfers between devices: 80.1 us -> none  [on_device(): lax.psum_scatter(partial_value, 'row', scatter_dimension=1, tiled=True)]
    all_gather x0 -> x2, blocking collectives: none -> 40.3 us  [the longest x1 26 us: on_device(): own = lax.all_gather(feats, 'zh', axis=0, tiled=True)]
    ppermute x0 -> x4, starting transfers between devices: none -> 25.7 us  [the longest x1 11.4 us: on_device(): g11 = lax.ppermute(g10, 'core', SWAP)]
    dot_general x4 -> x0, matrix products: 16 us -> none  [the longest x2 7.8 us: residual_product(): jnp.dot(lax.all_gather(diff, 'row', axis=1, tiled=True), gram_cols, prefe...]
    pallas_call x0 -> x3, Pallas kernels: none -> 9.17 us  [the longest x2 6.1 us: step(): pl.pallas_call(functools.partial(step_kernel, last), out_shape=outs, in_s...]
    ppermute x0 -> x4, waiting for transfers between devices: none -> 8.21 us  [the longest x1 8.2 us: on_device(): g10 = lax.ppermute(g00, 'ylo', SWAP)]
  transfers between devices with their start and end apart: 5 -> 5, of which waited for: 5 -> 2; matrix products, arithmetic and copies ran while one was open for 1% -> 0% of each run, Pallas kernels for 0% -> 0%
where the time goes in v1:
time: 247 us; the launch traced here: 245 us
  blocking collectives  149 us (60%)
  waiting for transfers between devices  40.9 us (17%)
  starting transfers between devices  25.7 us (10%)
  between operations  13.5 us (5%)
  Pallas kernels  9.17 us (4%)
  local copies, waits for them, and re-layouts  3.98 us (2%)
  other arithmetic  2.61 us (1%)
    all_to_all x1, blocking collectives, spread(): lax.all_to_all(jnp.broadcast_to(x[None], (n,) + x.shape), axes, 0, 0, til...  52.5 us
    all_gather x1, waiting for transfers between devices, on_device(): diffs = lax.all_gather(diff, ROW, axis=0)  32.6 us
    all_to_all x1, blocking collectives, on_device(): lax.all_to_all(term.reshape(16, BLOCK, half), ('core',) + ROW, 0, 0, tile...  28.8 us
    all_gather x1, blocking collectives, on_device(): own = lax.all_gather(feats, 'zh', axis=0, tiled=True)  26 us
    all_to_all x1, blocking collectives, on_device(): diffs = lax.all_to_all(sent, ROW, 0, 0, tiled=True)  16.9 us
    all_gather x1, blocking collectives, on_device(): mates = lax.all_gather(feats, 'zl', axis=0, tiled=True)  14.3 us
    ppermute x1, starting transfers between devices, on_device(): g11 = lax.ppermute(g10, 'core', SWAP)  11.4 us
    all_to_all x1, blocking collectives, on_device(): feats = lax.all_to_all(calib.T, 'core', 1, 0, tiled=True)  10.4 us
  transfers between devices with their start and end apart: 5, of which 2 were waited for; matrix products, arithmetic and copies ran while one was open for 0% of the time, Pallas kernels for 0%

profile of v1, /device:TPU:1, one launch (start us, length us, event | category | flops | bytes accessed | tf_op | source)
XLA Modules:
  0.0 244.7 jit_solution(7436657838886575711)
XLA Ops:
  6.5 0.7 copy-done
  7.2 0.2 dynamic-slice_reduce_fusion
  7.4 0.2 compare_reduce_fusion
  7.7 1.6 fusion
  9.3 0.9 copy.9
  10.2 10.4 %all_to_all.34 = bf16[64,2,512]{2,0,1:T(8,128)(2,1)S(1)} all-to-all(bf16[64,2,512]{2,0,1:T(8,128)(2,1)S(1)} %bitcast.23), channel_id=1, replica_groups=mesh['ylo'=2,'zh'=4,'zl'=4,'core'=2,'yhi'=2,'x'=4] {'core'}, dimensions={1} | all-to-all | bytes 262144 | tf_op jit(solution)/shard_map/all_to_all | solution.py:115
  20.6 26.0 %all_gather.15.own = bf16[512,512]{1,0:T(8,128)(2,1)S(1)} all-gather(bf16[128,512]{1,0:T(8,128)(2,1)S(1)} %bitcast.21), channel_id=1, replica_groups=mesh['ylo'=2,'zh'=4,'zl'=4,'core'=2,'yhi'=2,'x'=4] {'zh'}, dimensions={0}, use_global_device_ids=true | all-gather | bytes 655360 | tf_op jit(solution)/shard_map/all_gather | solution.py:116
  46.6 3.2 %collective-permute-start = (bf16[512,512]{1,0:T(8,128)(2,1)S(1)}, bf16[512,512]{1,0:T(8,128)(2,1)S(1)}, u32[]{:S(2)}, u32[]{:S(2)}) collective-permute-start(bf16[512,512]{1,0:T(8,128)(2,1)S(1)} %all_gather.15.own), channel_id=1, source_target_pairs={{0,256},{256,0},{1,257},{257,1},{2,258},{258,2},{3,259},{259,3},{4... | collective-permute-start | bytes 1572872 | tf_op jit(solution)/shard_map/ppermute | solution.py:117
  49.8 0.7 pad_add_fusion.where
  50.5 14.3 %all_gather.14.rows = bf16[512,512]{1,0:T(8,128)(2,1)} all-gather(bf16[128,512]{1,0:T(8,128)(2,1)S(1)} %bitcast.22), channel_id=1, replica_groups=mesh['ylo'=2,'zh'=4,'zl'=4,'core'=2,'yhi'=2,'x'=4] {'zl'}, dimensions={0}, use_global_device_ids=true | all-gather | bytes 655360 | tf_op jit(solution)/shard_map/all_gather | solution.py:118
  64.8 0.8 copy-done.5
  65.5 3.1 %partial_gram.1 = bf16[2,8,128,256]{3,2,1,0:T(8,128)(2,1)} custom-call(s32[2]{0:T(128)} %pad_add_fusion.where, bf16[512,512]{1,0:T(8,128)(2,1)} %all_gather.14.rows, bf16[512,512]{1,0:T(8,128)(2,1)} %copy-done.4, bf16[512,512]{1,0:T(8,128)(2,1)} %copy-done.5), custom_call_target="tpu_custom_call" | custom-call | flops 536870912 | bytes 1310720 | tf_op jit(solution)/shard_map/partial_gram/pallas_call | solution.py:42
  68.6 28.8 %all_to_all.35 = bf16[16,128,256]{2,1,0:T(8,128)(2,1)S(1)} all-to-all(bf16[16,128,256]{2,1,0:T(8,128)(2,1)} %bitcast.20), channel_id=1, replica_groups=mesh['ylo'=2,'zh'=4,'zl'=4,'core'=2,'yhi'=2,'x'=4] {'core','yhi','x'}, dimensions={0} | all-to-all | bytes 2097152 | tf_op jit(solution)/shard_map/all_to_all | solution.py:121
  97.4 0.1 convert_reduce_fusion
  97.7 52.5 %all_to_all.36 = bf16[16,128,256]{2,1,0:T(8,128)(2,1)S(1)} all-to-all(bf16[16,128,256]{2,1,0:T(8,128)(2,1)S(1)} %broadcast_in_dim.5), channel_id=1, replica_groups=mesh['ylo'=2,'zh'=4,'zl'=4,'core'=2,'yhi'=2,'x'=4] {'zh','zl'}, dimensions={0} | all-to-all | bytes 2097152 | tf_op jit(solution)/shard_map/all_to_all | solution.py:95
  150.2 1.9 collective-permute-start.1
  152.2 9.2 %collective-permute-start.2 = (bf16[4,512,256]{2,1,0:T(8,128)(2,1)S(1)}, bf16[4,512,256]{2,1,0:T(8,128)(2,1)S(1)}, u32[]{:S(2)}, u32[]{:S(2)}) collective-permute-start(bf16[4,512,256]{2,1,0:T(8,128)(2,1)S(1)} %bitcast.16), channel_id=1, source_target_pairs={{0,8},{8,0},{1,9},{9,1},{2,10},{10,2},{3,11},{11,3},{4,12},{12,4},... | collective-permute-start | bytes 3145736 | tf_op jit(solution)/shard_map/ppermute | solution.py:126
  161.4 8.2 %collective-permute-done.1.g10 = bf16[4,512,256]{2,1,0:T(8,128)(2,1)S(1)} collective-permute-done((bf16[4,512,256]{2,1,0:T(8,128)(2,1)S(1)}, bf16[4,512,256]{2,1,0:T(8,128)(2,1)S(1)}, u32[]{:S(2)}, u32[]{:S(2)}) %collective-permute-start.1) | collective-permute-done | bytes 1048608 | tf_op jit(solution)/shard_map/ppermute | solution.py:125
  169.6 11.4 %collective-permute-start.3 = (bf16[4,512,256]{2,1,0:T(8,128)(2,1)S(1)}, bf16[4,512,256]{2,1,0:T(8,128)(2,1)}, u32[]{:S(2)}, u32[]{:S(2)}) collective-permute-start(bf16[4,512,256]{2,1,0:T(8,128)(2,1)S(1)} %collective-permute-done.1.g10), channel_id=1, source_target_pairs={{0,8},{8,0},{1,9},{9,1},{2,10},{10,2},{3,11},{11,3},{4,12},{12,4},... | collective-permute-start | bytes 3145736 | tf_op jit(solution)/shard_map/ppermute | solution.py:127
  181.0 32.6 %all-gather.3.cloned.1.call-done = bf16[1024,512]{1,0:T(8,128)(2,1)} async-done(((bf16[128,512]{1,0:T(8,128)(2,1)}), bf16[1024,512]{1,0:T(8,128)(2,1)}) %all-gather.3.cloned.1.call-update) | async-done | bytes 1048592 | tf_op jit(solution)/shard_map/all_gather | solution.py:113
  213.6 1.2 copy-done.2
  214.9 2.7 %first_step.1 = (bf16[128,512]{1,0:T(8,128)(2,1)S(1)}, bf16[8,128,512]{2,1,0:T(8,128)(2,1)S(1)}) custom-call(s32[2]{0:T(128)S(1)} %copy-done.3, s32[4]{0:T(128)S(1)} %get-tuple-element.16.flags, bf16[8,128,512]{2,1,0:T(8,128)(2,1)S(1)} %bitcast.19, bf16[4,512,256]{2,1,0:T(8,128)(2,1)S(1)} %bitcast.17, bf16[4,512,256]{2,1,0:T(8,128)(2,1)S(1)} %collective-permute-done.1.g10, ...), custom_call_target="tpu_custom_call" | custom-call | flops 536870912 | bytes 3145728 | tf_op jit(solution)/shard_map/first_step/pallas_call | solution.py:80
  217.6 16.9 %all_to_all.37.diffs = bf16[8,128,512]{2,1,0:T(8,128)(2,1)S(1)} all-to-all(bf16[8,128,512]{2,1,0:T(8,128)(2,1)S(1)} %get-tuple-element.11), channel_id=1, replica_groups=mesh['ylo'=2,'zh'=4,'zl'=4,'core'=2,'yhi'=2,'x'=4] {'yhi','x'}, dimensions={0} | all-to-all | bytes 2097152 | tf_op jit(solution)/shard_map/all_to_all | solution.py:131
  234.5 3.4 %last_step.1 = bf16[128,512]{1,0:T(8,128)(2,1)} custom-call(s32[2]{0:T(128)S(1)} %copy-done.3, s32[4]{0:T(128)S(1)} %get-tuple-element.16.flags, bf16[8,128,512]{2,1,0:T(8,128)(2,1)S(1)} %all_to_all.37.diffs, bf16[4,512,256]{2,1,0:T(8,128)(2,1)S(1)} %bitcast.18, bf16[4,512,256]{2,1,0:T(8,128)(2,1)S(1)} %collective-permute-done.1.g10, ...), custom_call_target="tpu_custom_call" | custom-call | flops 536870912 | bytes 3145728 | tf_op jit(solution)/shard_map/last_step/pallas_call | solution.py:80
  (19 shorter events, 0.2 us)
Async XLA Ops:
  6.5 0.7 copy-start
  6.5 207.1 %all-gather.3.cloned.1.call-start = ((), (), s32[]{:S(2)}) async-start(), calls=%async_computation.4 | async-start | bytes 1179648 | tf_op jit(solution)/shard_map/all_gather | solution.py:113
  46.6 18.1 %copy-start.4 = (bf16[512,512]{1,0:T(8,128)(2,1)}, bf16[512,512]{1,0:T(8,128)(2,1)S(1)}, u32[]{:S(2)}) copy-start(bf16[512,512]{1,0:T(8,128)(2,1)S(1)} %all_gather.15.own) | copy-start | bytes 1572868
  46.6 18.1 %collective-permute-start = (bf16[512,512]{1,0:T(8,128)(2,1)S(1)}, bf16[512,512]{1,0:T(8,128)(2,1)S(1)}, u32[]{:S(2)}, u32[]{:S(2)}) collective-permute-start(bf16[512,512]{1,0:T(8,128)(2,1)S(1)} %all_gather.15.own), channel_id=1, source_target_pairs={{0,256},{256,0},{1,257},{257,1},{2,258},{258,2},{3,259},{259,3},{4... | collective-permute-start | bytes 1572872 | tf_op jit(solution)/shard_map/ppermute | solution.py:117
  64.7 0.8 copy-start.5
  97.7 115.9 %copy-start.1 = (bf16[128,512]{1,0:T(8,128)(2,1)S(1)}, bf16[128,512]{1,0:T(8,128)(2,1)}, u32[]{:S(2)}) copy-start(bf16[128,512]{1,0:T(8,128)(2,1)} %base.3) | copy-start | bytes 393220
  97.7 115.9 %copy-start.3 = (s32[2]{0:T(128)S(1)}, s32[2]{0:T(128)}, u32[]{:S(2)}) copy-start(s32[2]{0:T(128)} %pad_add_fusion.where) | copy-start | bytes 28
  150.2 19.4 %collective-permute-start.1 = (bf16[4,512,256]{2,1,0:T(8,128)(2,1)S(1)}, bf16[4,512,256]{2,1,0:T(8,128)(2,1)S(1)}, u32[]{:S(2)}, u32[]{:S(2)}) collective-permute-start(bf16[4,512,256]{2,1,0:T(8,128)(2,1)S(1)} %bitcast.15), channel_id=1, source_target_pairs={{0,256},{256,0},{1,257},{257,1},{2,258},{258,2},{3,259},{259,3},{4... | collective-permute-start | bytes 3145736 | tf_op jit(solution)/shard_map/ppermute | solution.py:125
  152.2 61.5 %collective-permute-start.2 = (bf16[4,512,256]{2,1,0:T(8,128)(2,1)S(1)}, bf16[4,512,256]{2,1,0:T(8,128)(2,1)S(1)}, u32[]{:S(2)}, u32[]{:S(2)}) collective-permute-start(bf16[4,512,256]{2,1,0:T(8,128)(2,1)S(1)} %bitcast.16), channel_id=1, source_target_pairs={{0,8},{8,0},{1,9},{9,1},{2,10},{10,2},{3,11},{11,3},{4,12},{12,4},... | collective-permute-start | bytes 3145736 | tf_op jit(solution)/shard_map/ppermute | solution.py:126
  169.6 44.0 %collective-permute-start.3 = (bf16[4,512,256]{2,1,0:T(8,128)(2,1)S(1)}, bf16[4,512,256]{2,1,0:T(8,128)(2,1)}, u32[]{:S(2)}, u32[]{:S(2)}) collective-permute-start(bf16[4,512,256]{2,1,0:T(8,128)(2,1)S(1)} %collective-permute-done.1.g10), channel_id=1, source_target_pairs={{0,8},{8,0},{1,9},{9,1},{2,10},{10,2},{3,11},{11,3},{4,12},{12,4},... | collective-permute-start | bytes 3145736 | tf_op jit(solution)/shard_map/ppermute | solution.py:127
  213.6 1.2 copy-start.2
Sparse Core Ops, SparseCore 0:
  152.3 61.2 all-gather.2

commit v2 on v1

--- a/solution.py
+++ b/solution.py
@@ -15,6 +15,11 @@
 TOK = ("ylo", "zh", "zl", "core")
 ROW = ("yhi", "x")
 SWAP = ((0, 1), (1, 0))
+CLASSES = (0, 1, 3, 2)
+
+
+def from_z(*steps):
+    return [((z + s) % 16 * 2 + c, z * 2 + c) for z in range(16) for c, s in enumerate(steps)]
 
 
 def vmem():
@@ -51,22 +56,28 @@
     )(where, rows, own, other)
 
 
-def step_kernel(last, where, flags, diffs, g00, g10, g01, g11, weight, base, *outs):
-    ylo, core = where[0], where[1]
-    half = g00.shape[2]
-    total = jnp.zeros(weight.shape, jnp.float32)
-    for dy, dc, gram in ((0, 0, g00), (0, 1, g01), (1, 0, g10), (1, 1, g11)):
-        lanes = pl.ds(pl.multiple_of((core ^ dc) * half, half), half)
-        for h in range(4):
-            total += lax.dot_general(
-                diffs[(ylo ^ dy) * 4 + h, :, lanes], gram[h], NT,
-                preferred_element_type=jnp.float32,
-            )
+def step_kernel(last, where, flags, diffs, *refs):
+    grams, (weight, base), outs, total = refs[:16], refs[16:18], refs[18:-1], refs[-1]
+    ylo, zl, core = where[0], where[1], where[2]
+    half = grams[0].shape[2]
+    for j, shift in enumerate(CLASSES):
+        part = jnp.zeros((weight.shape[0], BLOCK), jnp.float32)
+        for dy in range(2):
+            for dc in range(2):
+                gram = grams[(dy * 2 + dc) * 4 + j]
+                lanes = pl.ds(pl.multiple_of((core ^ dc) * half, half), half)
+                for h in range(4):
+                    part += lax.dot_general(
+                        diffs[(ylo ^ dy) * 4 + h, :, lanes], gram[h], NT,
+                        preferred_element_type=jnp.float32,
+                    )
+        place = lax.rem(zl + shift, 4) * BLOCK
+        total[:, pl.ds(pl.multiple_of(place, BLOCK), BLOCK)] = part
     block = lax.broadcasted_iota(jnp.int32, weight.shape, 1) // BLOCK
     keep = jnp.zeros(weight.shape, jnp.float32)
     for b in range(weight.shape[1] // BLOCK):
         keep = jnp.where(block == b, flags[b].astype(jnp.float32), keep)
-    new = (weight[...].astype(jnp.float32) - RATE * keep * total).astype(jnp.bfloat16)
+    new = (weight[...].astype(jnp.float32) - RATE * keep * total[...]).astype(jnp.bfloat16)
     outs[0][...] = new
     if not last:
         diff = (new.astype(jnp.float32) - base[...].astype(jnp.float32)).astype(jnp.bfloat16)
@@ -80,8 +91,9 @@
     return pl.pallas_call(
         functools.partial(step_kernel, last),
         out_shape=outs,
-        in_specs=[smem(), smem()] + [vmem()] * 7,
+        in_specs=[smem(), smem()] + [vmem()] * (len(grams) + 3),
         out_specs=tuple(vmem() for _ in outs),
+        scratch_shapes=[pltpu.VMEM(weight.shape, jnp.float32)],
         name="last_step" if last else "first_step",
         compiler_params=pltpu.CompilerParams(vmem_limit_bytes=32 << 20),
         cost_estimate=pl.CostEstimate(
@@ -91,20 +103,15 @@
     )(where, flags, diffs, *grams, weight, base)
 
 
-def spread(x, axes, n):
-    return lax.all_to_all(jnp.broadcast_to(x[None], (n,) + x.shape), axes, 0, 0, tiled=True)
-
-
 def on_device(calib, base_weight, keep_blocks):
-    ylo, core = lax.axis_index("ylo"), lax.axis_index("core")
     tok_pos, row_pos = lax.axis_index(TOK), lax.axis_index(ROW)
     rows, cols = base_weight.shape
     tokens = calib.shape[0] * 8
-    where = jnp.stack([ylo, core]).astype(jnp.int32)
+    where = jnp.stack([lax.axis_index(a) for a in ("ylo", "zl", "core")]).astype(jnp.int32)
     kept = lax.dynamic_slice(keep_blocks, (tok_pos, 0), (1, keep_blocks.shape[1]))
     nblocks = cols // BLOCK
-    mine = row_pos * nblocks + jnp.arange(nblocks, dtype=jnp.int32)
-    flags = jnp.any(kept[0][:, None] == mine[None, :], axis=0).astype(jnp.int32)
+    labels = row_pos * nblocks + jnp.arange(nblocks, dtype=jnp.int32)
+    flags = jnp.any(kept[0][:, None] == labels[None, :], axis=0).astype(jnp.int32)
     keep = jnp.repeat(flags.astype(jnp.float32), BLOCK)[None, :]
     base_float = base_weight.astype(jnp.float32)
     weight = (keep * base_float).astype(jnp.bfloat16)
@@ -118,14 +125,17 @@
     mates = lax.all_gather(feats, "zl", axis=0, tiled=True)
     term = partial_gram(where, mates, own, other)
     half = term.shape[3]
+    diffs, term = lax.optimization_barrier((diffs, term))
     terms = lax.all_to_all(term.reshape(16, BLOCK, half), ("core",) + ROW, 0, 0, tiled=True)
     gram = (jnp.sum(terms.astype(jnp.float32), axis=0) / tokens).astype(jnp.bfloat16)
 
-    g00 = spread(gram, ("zh", "zl"), 16).reshape(4, 4 * BLOCK, half)
-    g10 = lax.ppermute(g00, "ylo", SWAP)
-    g01 = lax.ppermute(g00, "core", SWAP)
-    g11 = lax.ppermute(g10, "core", SWAP)
-    grams = (g00, g10, g01, g11)
+    line = ("zh", "zl", "core")
+    mine = lax.all_gather(gram, "zh", axis=0)
+    near = [mine] + [lax.ppermute(mine, line, from_z(*s)) for s in ((1, 1), (-1, -1), (2, -2))]
+    far = [lax.ppermute(g, "ylo", SWAP) for g in near]
+    near_mate = [lax.ppermute(g, "core", SWAP) for g in near]
+    far_mate = [lax.ppermute(g, "core", SWAP) for g in far]
+    grams = near + near_mate + far + far_mate
 
     weight, sent = step(False, where, flags, diffs, grams, weight, base_weight)
     diffs = lax.all_to_all(sent, ROW, 0, 0, tiled=True)

time: 247 us -> 200 us (0.81)
  blocking collectives: 149 us -> 116 us
  waiting for transfers between devices: 40.9 us -> 12.7 us
  starting transfers between devices: 25.7 us -> 44.6 us
    all_to_all x1 -> x0, blocking collectives: 52.5 us -> none  [spread(): lax.all_to_all(jnp.broadcast_to(x[None], (n,) + x.shape), axes, 0, 0, til...]
    all_gather x1, waiting for transfers between devices: 32.6 us -> 9.13 us  [on_device(): diffs = lax.all_gather(diff, ROW, axis=0)]
    all_gather x0 -> x1, blocking collectives: none -> 22.2 us  [on_device(): mine = lax.all_gather(gram, 'zh', axis=0)]
    ppermute x3 -> x15, starting transfers between devices: 22.5 us -> 41.4 us  [the longest x3 12 us: on_device(): lax.ppermute(mine, line, from_z(*s))]
    all_to_all x1, blocking collectives: 28.8 us -> 23.1 us  [on_device(): lax.all_to_all(term.reshape(16, BLOCK, half), ('core',) + ROW, 0, 0, tile...]
    ppermute x3 -> x15, waiting for transfers between devices: 8.21 us -> 3.53 us  [the longest x4 2.41 us: on_device(): far = [lax.ppermute(g, 'ylo', SWAP) for g in near]]
    all_to_all x1, blocking collectives: 16.9 us -> 19.8 us  [on_device(): diffs = lax.all_to_all(sent, ROW, 0, 0, tiled=True)]
  transfers between devices with their start and end apart: 5 -> 17, of which waited for: 2 -> 3; matrix products, arithmetic and copies ran while one was open for 0% -> 1% of each run, Pallas kernels for 0% -> 2%
where the time goes in v2:
time: 200 us; the launch traced here: 199 us
  blocking collectives  116 us (58%)
  starting transfers between devices  44.6 us (22%)
  between operations  13.7 us (7%)
  waiting for transfers between devices  12.7 us (6%)
  Pallas kernels  7.49 us (4%)
  local copies, waits for them, and re-layouts  2.66 us (1%)
  other arithmetic  2.54 us (1%)
    all_gather x1, blocking collectives, on_device(): own = lax.all_gather(feats, 'zh', axis=0, tiled=True)  26 us
    all_to_all x1, blocking collectives, on_device(): lax.all_to_all(term.reshape(16, BLOCK, half), ('core',) + ROW, 0, 0, tile...  23.1 us
    all_gather x1, blocking collectives, on_device(): mine = lax.all_gather(gram, 'zh', axis=0)  22.2 us
    all_to_all x1, blocking collectives, on_device(): diffs = lax.all_to_all(sent, ROW, 0, 0, tiled=True)  19.8 us
    all_gather x1, blocking collectives, on_device(): mates = lax.all_gather(feats, 'zl', axis=0, tiled=True)  14.3 us
    ppermute x3, starting transfers between devices, on_device(): lax.ppermute(mine, line, from_z(*s))  12 us
    ppermute x4, starting transfers between devices, on_device(): far = [lax.ppermute(g, 'ylo', SWAP) for g in near]  10.4 us
    all_to_all x1, blocking collectives, on_device(): feats = lax.all_to_all(calib.T, 'core', 1, 0, tiled=True)  10.4 us
  transfers between devices with their start and end apart: 17, of which 3 were waited for; matrix products, arithmetic and copies ran while one was open for 1% of the time, Pallas kernels for 2%

profile of v2, /device:TPU:1, one launch (start us, length us, event | category | flops | bytes accessed | tf_op | source)
XLA Modules:
  0.0 199.4 jit_solution(189871623462115642)
XLA Ops:
  10.2 10.4 %all_to_all.29 = bf16[64,2,512]{2,0,1:T(8,128)(2,1)S(1)} all-to-all(bf16[64,2,512]{2,0,1:T(8,128)(2,1)S(1)} %bitcast.27), channel_id=1, replica_groups=mesh['ylo'=2,'zh'=4,'zl'=4,'core'=2,'yhi'=2,'x'=4] {'core'}, dimensions={1} | all-to-all | bytes 262144 | tf_op jit(solution)/shard_map/all_to_all | solution.py:122
  20.6 26.0 %all_gather.19.own = bf16[512,512]{1,0:T(8,128)(2,1)S(1)} all-gather(bf16[128,512]{1,0:T(8,128)(2,1)S(1)} %bitcast.25), channel_id=1, replica_groups=mesh['ylo'=2,'zh'=4,'zl'=4,'core'=2,'yhi'=2,'x'=4] {'zh'}, dimensions={0}, use_global_device_ids=true | all-gather | bytes 655360 | tf_op jit(solution)/shard_map/all_gather | solution.py:123
  46.6 3.2 %collective-permute-start = (bf16[512,512]{1,0:T(8,128)(2,1)S(1)}, bf16[512,512]{1,0:T(8,128)(2,1)S(1)}, u32[]{:S(2)}, u32[]{:S(2)}) collective-permute-start(bf16[512,512]{1,0:T(8,128)(2,1)S(1)} %all_gather.19.own), channel_id=1, source_target_pairs={{0,256},{256,0},{1,257},{257,1},{2,258},{258,2},{3,259},{259,3},{4... | collective-permute-start | bytes 1572872 | tf_op jit(solution)/shard_map/ppermute | solution.py:124
  50.4 14.3 %all_gather.18.rows = bf16[512,512]{1,0:T(8,128)(2,1)} all-gather(bf16[128,512]{1,0:T(8,128)(2,1)S(1)} %bitcast.26), channel_id=1, replica_groups=mesh['ylo'=2,'zh'=4,'zl'=4,'core'=2,'yhi'=2,'x'=4] {'zl'}, dimensions={0}, use_global_device_ids=true | all-gather | bytes 655360 | tf_op jit(solution)/shard_map/all_gather | solution.py:125
  65.5 3.1 %partial_gram.1 = bf16[2,8,128,256]{3,2,1,0:T(8,128)(2,1)} custom-call(s32[3]{0:T(128)} %pad_add_fusion.where, bf16[512,512]{1,0:T(8,128)(2,1)} %all_gather.18.rows, bf16[512,512]{1,0:T(8,128)(2,1)} %copy-done.4, bf16[512,512]{1,0:T(8,128)(2,1)} %copy-done.5), custom_call_target="tpu_custom_call" | custom-call | flops 536870912 | bytes 1310720 | tf_op jit(solution)/shard_map/partial_gram/pallas_call | solution.py:47
  68.6 9.1 %all-gather.4.cloned.1.call-done = bf16[1024,512]{1,0:T(8,128)(2,1)} async-done(((bf16[128,512]{1,0:T(8,128)(2,1)}), bf16[1024,512]{1,0:T(8,128)(2,1)}) %all-gather.4.cloned.1.call-update) | async-done | bytes 1048592 | tf_op jit(solution)/shard_map/all_gather | solution.py:120
  77.7 23.1 %all_to_all.30 = bf16[16,128,256]{2,1,0:T(8,128)(2,1)S(1)} all-to-all(bf16[16,128,256]{2,1,0:T(8,128)(2,1)} %bitcast.24), channel_id=1, replica_groups=mesh['ylo'=2,'zh'=4,'zl'=4,'core'=2,'yhi'=2,'x'=4] {'core','yhi','x'}, dimensions={0} | all-to-all | bytes 2097152 | tf_op jit(solution)/shard_map/all_to_all | solution.py:129
  101.0 22.2 %all-gather.1 = bf16[512,256]{1,0:T(8,128)(2,1)S(1)} all-gather(bf16[128,256]{1,0:T(8,128)(2,1)S(1)} %multiply_convert_fusion), channel_id=3, replica_groups=mesh['ylo'=2,'zh'=4,'zl'=4,'core'=2,'yhi'=2,'x'=4] {'zh'}, dimensions={0}, use_global_device_ids=true | all-gather | bytes 327680 | tf_op jit(solution)/shard_map/all_gather | solution.py:133
  123.2 3.0 %collective-permute-start.8 = (bf16[4,128,256]{2,1,0:T(8,128)(2,1)S(1)}, bf16[4,128,256]{2,1,0:T(8,128)(2,1)S(1)}, u32[]{:S(2)}, u32[]{:S(2)}) collective-permute-start(bf16[4,128,256]{2,1,0:T(8,128)(2,1)S(1)} %bitcast.16), channel_id=1, source_target_pairs={{0,256},{256,0},{1,257},{257,1},{2,258},{258,2},{3,259},{259,3},{4... | collective-permute-start | bytes 786440 | tf_op jit(solution)/shard_map/ppermute | solution.py:135
  126.2 5.5 %collective-permute-start.3 = (bf16[4,128,256]{2,1,0:T(8,128)(2,1)S(1)}, bf16[4,128,256]{2,1,0:T(8,128)(2,1)S(1)}, u32[]{:S(2)}, u32[]{:S(2)}) collective-permute-start(bf16[4,128,256]{2,1,0:T(8,128)(2,1)S(1)} %bitcast.17), channel_id=1, source_target_pairs={{32,0},{232,8},{48,16},{248,24},{64,32},{8,40},{80,48},{24,56},{96... | collective-permute-start | bytes 786440 | tf_op jit(solution)/shard_map/ppermute | solution.py:134
  131.7 2.7 %collective-permute-start.4 = (bf16[4,128,256]{2,1,0:T(8,128)(2,1)S(1)}, bf16[4,128,256]{2,1,0:T(8,128)(2,1)S(1)}, u32[]{:S(2)}, u32[]{:S(2)}) collective-permute-start(bf16[4,128,256]{2,1,0:T(8,128)(2,1)S(1)} %bitcast.18), channel_id=1, source_target_pairs={{0,8},{8,0},{1,9},{9,1},{2,10},{10,2},{3,11},{11,3},{4,12},{12,4},... | collective-permute-start | bytes 786440 | tf_op jit(solution)/shard_map/ppermute | solution.py:136
  134.4 3.2 %collective-permute-start.2 = (bf16[4,128,256]{2,1,0:T(8,128)(2,1)S(1)}, bf16[4,128,256]{2,1,0:T(8,128)(2,1)S(1)}, u32[]{:S(2)}, u32[]{:S(2)}) collective-permute-start(bf16[4,128,256]{2,1,0:T(8,128)(2,1)S(1)} %bitcast.19), channel_id=1, source_target_pairs={{240,0},{248,8},{0,16},{8,24},{16,32},{24,40},{32,48},{40,56},{48,... | collective-permute-start | bytes 786440 | tf_op jit(solution)/shard_map/ppermute | solution.py:134
  137.6 3.3 %collective-permute-start.1 = (bf16[4,128,256]{2,1,0:T(8,128)(2,1)S(1)}, bf16[4,128,256]{2,1,0:T(8,128)(2,1)S(1)}, u32[]{:S(2)}, u32[]{:S(2)}) collective-permute-start(bf16[4,128,256]{2,1,0:T(8,128)(2,1)S(1)} %bitcast.20), channel_id=1, source_target_pairs={{16,0},{24,8},{32,16},{40,24},{48,32},{56,40},{64,48},{72,56},{80,... | collective-permute-start | bytes 786440 | tf_op jit(solution)/shard_map/ppermute | solution.py:134
  140.9 2.5 %collective-permute-start.12 = (bf16[4,128,256]{2,1,0:T(8,128)(2,1)S(1)}, bf16[4,128,256]{2,1,0:T(8,128)(2,1)S(1)}, u32[]{:S(2)}, u32[]{:S(2)}) collective-permute-start(bf16[4,128,256]{2,1,0:T(8,128)(2,1)S(1)} %collective-permute-done.8.refs_8_), channel_id=1, source_target_pairs={{0,8},{8,0},{1,9},{9,1},{2,10},{10,2},{3,11},{11,3},{4,12},{12,4},... | collective-permute-start | bytes 786440 | tf_op jit(solution)/shard_map/ppermute | solution.py:137
  143.4 2.1 %collective-permute-start.11 = (bf16[4,128,256]{2,1,0:T(8,128)(2,1)S(1)}, bf16[4,128,256]{2,1,0:T(8,128)(2,1)S(1)}, u32[]{:S(2)}, u32[]{:S(2)}) collective-permute-start(bf16[4,128,256]{2,1,0:T(8,128)(2,1)S(1)} %collective-permute-done.3.refs_3_), channel_id=1, source_target_pairs={{0,256},{256,0},{1,257},{257,1},{2,258},{258,2},{3,259},{259,3},{4... | collective-permute-start | bytes 786440 | tf_op jit(solution)/shard_map/ppermute | solution.py:135
  145.5 2.2 %collective-permute-start.7 = (bf16[4,128,256]{2,1,0:T(8,128)(2,1)S(1)}, bf16[4,128,256]{2,1,0:T(8,128)(2,1)S(1)}, u32[]{:S(2)}, u32[]{:S(2)}) collective-permute-start(bf16[4,128,256]{2,1,0:T(8,128)(2,1)S(1)} %collective-permute-done.3.refs_3_), channel_id=1, source_target_pairs={{0,8},{8,0},{1,9},{9,1},{2,10},{10,2},{3,11},{11,3},{4,12},{12,4},... | collective-permute-start | bytes 786440 | tf_op jit(solution)/shard_map/ppermute | solution.py:136
  147.7 3.2 %collective-permute-start.10 = (bf16[4,128,256]{2,1,0:T(8,128)(2,1)S(1)}, bf16[4,128,256]{2,1,0:T(8,128)(2,1)S(1)}, u32[]{:S(2)}, u32[]{:S(2)}) collective-permute-start(bf16[4,128,256]{2,1,0:T(8,128)(2,1)S(1)} %collective-permute-done.2.refs_2_), channel_id=1, source_target_pairs={{0,256},{256,0},{1,257},{257,1},{2,258},{258,2},{3,259},{259,3},{4... | collective-permute-start | bytes 786440 | tf_op jit(solution)/shard_map/ppermute | solution.py:135
  150.9 2.1 %collective-permute-start.9 = (bf16[4,128,256]{2,1,0:T(8,128)(2,1)S(1)}, bf16[4,128,256]{2,1,0:T(8,128)(2,1)S(1)}, u32[]{:S(2)}, u32[]{:S(2)}) collective-permute-start(bf16[4,128,256]{2,1,0:T(8,128)(2,1)S(1)} %collective-permute-done.1.refs_1_), channel_id=1, source_target_pairs={{0,256},{256,0},{1,257},{257,1},{2,258},{258,2},{3,259},{259,3},{4... | collective-permute-start | bytes 786440 | tf_op jit(solution)/shard_map/ppermute | solution.py:135
  153.1 2.7 %collective-permute-start.6 = (bf16[4,128,256]{2,1,0:T(8,128)(2,1)S(1)}, bf16[4,128,256]{2,1,0:T(8,128)(2,1)S(1)}, u32[]{:S(2)}, u32[]{:S(2)}) collective-permute-start(bf16[4,128,256]{2,1,0:T(8,128)(2,1)S(1)} %collective-permute-done.2.refs_2_), channel_id=1, source_target_pairs={{0,8},{8,0},{1,9},{9,1},{2,10},{10,2},{3,11},{11,3},{4,12},{12,4},... | collective-permute-start | bytes 786440 | tf_op jit(solution)/shard_map/ppermute | solution.py:136
  157.7 2.4 %collective-permute-start.15 = (bf16[4,128,256]{2,1,0:T(8,128)(2,1)S(1)}, bf16[4,128,256]{2,1,0:T(8,128)(2,1)S(1)}, u32[]{:S(2)}, u32[]{:S(2)}) collective-permute-start(bf16[4,128,256]{2,1,0:T(8,128)(2,1)S(1)} %collective-permute-done.11.refs_11_), channel_id=1, source_target_pairs={{0,8},{8,0},{1,9},{9,1},{2,10},{10,2},{3,11},{11,3},{4,12},{12,4},... | collective-permute-start | bytes 786440 | tf_op jit(solution)/shard_map/ppermute | solution.py:137
  162.1 2.4 %collective-permute-done.9.refs_9_ = bf16[4,128,256]{2,1,0:T(8,128)(2,1)S(1)} collective-permute-done((bf16[4,128,256]{2,1,0:T(8,128)(2,1)S(1)}, bf16[4,128,256]{2,1,0:T(8,128)(2,1)S(1)}, u32[]{:S(2)}, u32[]{:S(2)}) %collective-permute-start.9) | collective-permute-done | bytes 262176 | tf_op jit(solution)/shard_map/ppermute | solution.py:135
  164.5 2.7 %collective-permute-start.13 = (bf16[4,128,256]{2,1,0:T(8,128)(2,1)S(1)}, bf16[4,128,256]{2,1,0:T(8,128)(2,1)S(1)}, u32[]{:S(2)}, u32[]{:S(2)}) collective-permute-start(bf16[4,128,256]{2,1,0:T(8,128)(2,1)S(1)} %collective-permute-done.9.refs_9_), channel_id=1, source_target_pairs={{0,8},{8,0},{1,9},{9,1},{2,10},{10,2},{3,11},{11,3},{4,12},{12,4},... | collective-permute-start | bytes 786440 | tf_op jit(solution)/shard_map/ppermute | solution.py:137
  170.2 19.8 %all_to_all.31.diffs = bf16[8,128,512]{2,1,0:T(8,128)(2,1)S(1)} all-to-all(bf16[8,128,512]{2,1,0:T(8,128)(2,1)S(1)} %get-tuple-element.15), channel_id=1, replica_groups=mesh['ylo'=2,'zh'=4,'zl'=4,'core'=2,'yhi'=2,'x'=4] {'yhi','x'}, dimensions={0} | all-to-all | bytes 2097152 | tf_op jit(solution)/shard_map/all_to_all | solution.py:141
  190.0 2.5 %last_step.1 = bf16[128,512]{1,0:T(8,128)(2,1)} custom-call(s32[3]{0:T(128)S(1)} %copy-done.3, s32[4]{0:T(128)S(1)} %get-tuple-element.20.flags, bf16[8,128,512]{2,1,0:T(8,128)(2,1)S(1)} %all_to_all.31.diffs, bf16[4,128,256]{2,1,0:T(8,128)(2,1)S(1)} %bitcast.22, bf16[4,128,256]{2,1,0:T(8,128)(2,1)S(1)} %collective-permute-done.1.refs_1_, ...), custom_call_target="tpu_custom_call" | custom-call | flops 536870912 | bytes 3145728 | tf_op jit(solution)/shard_map/last_step/pallas_call | solution.py:91
  (42 shorter events, 12.1 us)
Async XLA Ops:
  6.5 0.7 copy-start
  6.5 71.2 %all-gather.4.cloned.1.call-start = ((), (), s32[]{:S(2)}) async-start(), calls=%async_computation.3 | async-start | bytes 1179648 | tf_op jit(solution)/shard_map/all_gather | solution.py:120
  46.6 18.1 %copy-start.4 = (bf16[512,512]{1,0:T(8,128)(2,1)}, bf16[512,512]{1,0:T(8,128)(2,1)S(1)}, u32[]{:S(2)}) copy-start(bf16[512,512]{1,0:T(8,128)(2,1)S(1)} %all_gather.19.own) | copy-start | bytes 1572868
  46.6 18.1 %collective-permute-start = (bf16[512,512]{1,0:T(8,128)(2,1)S(1)}, bf16[512,512]{1,0:T(8,128)(2,1)S(1)}, u32[]{:S(2)}, u32[]{:S(2)}) collective-permute-start(bf16[512,512]{1,0:T(8,128)(2,1)S(1)} %all_gather.19.own), channel_id=1, source_target_pairs={{0,256},{256,0},{1,257},{257,1},{2,258},{258,2},{3,259},{259,3},{4... | collective-permute-start | bytes 1572872 | tf_op jit(solution)/shard_map/ppermute | solution.py:124
  64.7 0.8 copy-start.5
  100.8 67.5 %copy-start.1 = (bf16[128,512]{1,0:T(8,128)(2,1)S(1)}, bf16[128,512]{1,0:T(8,128)(2,1)}, u32[]{:S(2)}) copy-start(bf16[128,512]{1,0:T(8,128)(2,1)} %refs_17_.3) | copy-start | bytes 393220
  100.8 67.5 %copy-start.2 = (bf16[1024,512]{1,0:T(8,128)(2,1)S(1)}, bf16[1024,512]{1,0:T(8,128)(2,1)}, u32[]{:S(2)}) copy-start(bf16[1024,512]{1,0:T(8,128)(2,1)} %all-gather.4.cloned.1.call-done) | copy-start | bytes 3145732
  100.8 67.5 %copy-start.3 = (s32[3]{0:T(128)S(1)}, s32[3]{0:T(128)}, u32[]{:S(2)}) copy-start(s32[3]{0:T(128)} %pad_add_fusion.where) | copy-start | bytes 40
  123.2 17.7 %collective-permute-start.8 = (bf16[4,128,256]{2,1,0:T(8,128)(2,1)S(1)}, bf16[4,128,256]{2,1,0:T(8,128)(2,1)S(1)}, u32[]{:S(2)}, u32[]{:S(2)}) collective-permute-start(bf16[4,128,256]{2,1,0:T(8,128)(2,1)S(1)} %bitcast.16), channel_id=1, source_target_pairs={{0,256},{256,0},{1,257},{257,1},{2,258},{258,2},{3,259},{259,3},{4... | collective-permute-start | bytes 786440 | tf_op jit(solution)/shard_map/ppermute | solution.py:135
  126.2 17.2 %collective-permute-start.3 = (bf16[4,128,256]{2,1,0:T(8,128)(2,1)S(1)}, bf16[4,128,256]{2,1,0:T(8,128)(2,1)S(1)}, u32[]{:S(2)}, u32[]{:S(2)}) collective-permute-start(bf16[4,128,256]{2,1,0:T(8,128)(2,1)S(1)} %bitcast.17), channel_id=1, source_target_pairs={{32,0},{232,8},{48,16},{248,24},{64,32},{8,40},{80,48},{24,56},{96... | collective-permute-start | bytes 786440 | tf_op jit(solution)/shard_map/ppermute | solution.py:134
  131.7 13.9 %collective-permute-start.4 = (bf16[4,128,256]{2,1,0:T(8,128)(2,1)S(1)}, bf16[4,128,256]{2,1,0:T(8,128)(2,1)S(1)}, u32[]{:S(2)}, u32[]{:S(2)}) collective-permute-start(bf16[4,128,256]{2,1,0:T(8,128)(2,1)S(1)} %bitcast.18), channel_id=1, source_target_pairs={{0,8},{8,0},{1,9},{9,1},{2,10},{10,2},{3,11},{11,3},{4,12},{12,4},... | collective-permute-start | bytes 786440 | tf_op jit(solution)/shard_map/ppermute | solution.py:136
  134.4 13.3 %collective-permute-start.2 = (bf16[4,128,256]{2,1,0:T(8,128)(2,1)S(1)}, bf16[4,128,256]{2,1,0:T(8,128)(2,1)S(1)}, u32[]{:S(2)}, u32[]{:S(2)}) collective-permute-start(bf16[4,128,256]{2,1,0:T(8,128)(2,1)S(1)} %bitcast.19), channel_id=1, source_target_pairs={{240,0},{248,8},{0,16},{8,24},{16,32},{24,40},{32,48},{40,56},{48,... | collective-permute-start | bytes 786440 | tf_op jit(solution)/shard_map/ppermute | solution.py:134
  137.6 13.3 %collective-permute-start.1 = (bf16[4,128,256]{2,1,0:T(8,128)(2,1)S(1)}, bf16[4,128,256]{2,1,0:T(8,128)(2,1)S(1)}, u32[]{:S(2)}, u32[]{:S(2)}) collective-permute-start(bf16[4,128,256]{2,1,0:T(8,128)(2,1)S(1)} %bitcast.20), channel_id=1, source_target_pairs={{16,0},{24,8},{32,16},{40,24},{48,32},{56,40},{64,48},{72,56},{80,... | collective-permute-start | bytes 786440 | tf_op jit(solution)/shard_map/ppermute | solution.py:134
  140.9 12.2 %collective-permute-start.12 = (bf16[4,128,256]{2,1,0:T(8,128)(2,1)S(1)}, bf16[4,128,256]{2,1,0:T(8,128)(2,1)S(1)}, u32[]{:S(2)}, u32[]{:S(2)}) collective-permute-start(bf16[4,128,256]{2,1,0:T(8,128)(2,1)S(1)} %collective-permute-done.8.refs_8_), channel_id=1, source_target_pairs={{0,8},{8,0},{1,9},{9,1},{2,10},{10,2},{3,11},{11,3},{4,12},{12,4},... | collective-permute-start | bytes 786440 | tf_op jit(solution)/shard_map/ppermute | solution.py:137
  143.4 12.4 %collective-permute-start.11 = (bf16[4,128,256]{2,1,0:T(8,128)(2,1)S(1)}, bf16[4,128,256]{2,1,0:T(8,128)(2,1)S(1)}, u32[]{:S(2)}, u32[]{:S(2)}) collective-permute-start(bf16[4,128,256]{2,1,0:T(8,128)(2,1)S(1)} %collective-permute-done.3.refs_3_), channel_id=1, source_target_pairs={{0,256},{256,0},{1,257},{257,1},{2,258},{258,2},{3,259},{259,3},{4... | collective-permute-start | bytes 786440 | tf_op jit(solution)/shard_map/ppermute | solution.py:135
  145.5 12.2 %collective-permute-start.7 = (bf16[4,128,256]{2,1,0:T(8,128)(2,1)S(1)}, bf16[4,128,256]{2,1,0:T(8,128)(2,1)S(1)}, u32[]{:S(2)}, u32[]{:S(2)}) collective-permute-start(bf16[4,128,256]{2,1,0:T(8,128)(2,1)S(1)} %collective-permute-done.3.refs_3_), channel_id=1, source_target_pairs={{0,8},{8,0},{1,9},{9,1},{2,10},{10,2},{3,11},{11,3},{4,12},{12,4},... | collective-permute-start | bytes 786440 | tf_op jit(solution)/shard_map/ppermute | solution.py:136
  147.7 12.4 %collective-permute-start.10 = (bf16[4,128,256]{2,1,0:T(8,128)(2,1)S(1)}, bf16[4,128,256]{2,1,0:T(8,128)(2,1)S(1)}, u32[]{:S(2)}, u32[]{:S(2)}) collective-permute-start(bf16[4,128,256]{2,1,0:T(8,128)(2,1)S(1)} %collective-permute-done.2.refs_2_), channel_id=1, source_target_pairs={{0,256},{256,0},{1,257},{257,1},{2,258},{258,2},{3,259},{259,3},{4... | collective-permute-start | bytes 786440 | tf_op jit(solution)/shard_map/ppermute | solution.py:135
  150.9 13.5 %collective-permute-start.9 = (bf16[4,128,256]{2,1,0:T(8,128)(2,1)S(1)}, bf16[4,128,256]{2,1,0:T(8,128)(2,1)S(1)}, u32[]{:S(2)}, u32[]{:S(2)}) collective-permute-start(bf16[4,128,256]{2,1,0:T(8,128)(2,1)S(1)} %collective-permute-done.1.refs_1_), channel_id=1, source_target_pairs={{0,256},{256,0},{1,257},{257,1},{2,258},{258,2},{3,259},{259,3},{4... | collective-permute-start | bytes 786440 | tf_op jit(solution)/shard_map/ppermute | solution.py:135
  153.1 14.1 %collective-permute-start.6 = (bf16[4,128,256]{2,1,0:T(8,128)(2,1)S(1)}, bf16[4,128,256]{2,1,0:T(8,128)(2,1)S(1)}, u32[]{:S(2)}, u32[]{:S(2)}) collective-permute-start(bf16[4,128,256]{2,1,0:T(8,128)(2,1)S(1)} %collective-permute-done.2.refs_2_), channel_id=1, source_target_pairs={{0,8},{8,0},{1,9},{9,1},{2,10},{10,2},{3,11},{11,3},{4,12},{12,4},... | collective-permute-start | bytes 786440 | tf_op jit(solution)/shard_map/ppermute | solution.py:136
  155.8 11.4 %collective-permute-start.5 = (bf16[4,128,256]{2,1,0:T(8,128)(2,1)S(1)}, bf16[4,128,256]{2,1,0:T(8,128)(2,1)S(1)}, u32[]{:S(2)}, u32[]{:S(2)}) collective-permute-start(bf16[4,128,256]{2,1,0:T(8,128)(2,1)S(1)} %collective-permute-done.1.refs_1_), channel_id=1, source_target_pairs={{0,8},{8,0},{1,9},{9,1},{2,10},{10,2},{3,11},{11,3},{4,12},{12,4},... | collective-permute-start | bytes 786440 | tf_op jit(solution)/shard_map/ppermute | solution.py:136
  157.7 9.5 %collective-permute-start.15 = (bf16[4,128,256]{2,1,0:T(8,128)(2,1)S(1)}, bf16[4,128,256]{2,1,0:T(8,128)(2,1)S(1)}, u32[]{:S(2)}, u32[]{:S(2)}) collective-permute-start(bf16[4,128,256]{2,1,0:T(8,128)(2,1)S(1)} %collective-permute-done.11.refs_11_), channel_id=1, source_target_pairs={{0,8},{8,0},{1,9},{9,1},{2,10},{10,2},{3,11},{11,3},{4,12},{12,4},... | collective-permute-start | bytes 786440 | tf_op jit(solution)/shard_map/ppermute | solution.py:137
  160.1 7.1 %collective-permute-start.14 = (bf16[4,128,256]{2,1,0:T(8,128)(2,1)S(1)}, bf16[4,128,256]{2,1,0:T(8,128)(2,1)S(1)}, u32[]{:S(2)}, u32[]{:S(2)}) collective-permute-start(bf16[4,128,256]{2,1,0:T(8,128)(2,1)S(1)} %collective-permute-done.10.refs_10_), channel_id=1, source_target_pairs={{0,8},{8,0},{1,9},{9,1},{2,10},{10,2},{3,11},{11,3},{4,12},{12,4},... | collective-permute-start | bytes 786440 | tf_op jit(solution)/shard_map/ppermute | solution.py:137
  164.5 3.8 %collective-permute-start.13 = (bf16[4,128,256]{2,1,0:T(8,128)(2,1)S(1)}, bf16[4,128,256]{2,1,0:T(8,128)(2,1)S(1)}, u32[]{:S(2)}, u32[]{:S(2)}) collective-permute-start(bf16[4,128,256]{2,1,0:T(8,128)(2,1)S(1)} %collective-permute-done.9.refs_9_), channel_id=1, source_target_pairs={{0,8},{8,0},{1,9},{9,1},{2,10},{10,2},{3,11},{11,3},{4,12},{12,4},... | collective-permute-start | bytes 786440 | tf_op jit(solution)/shard_map/ppermute | solution.py:137
Sparse Core Ops, SparseCore 0:
  10.6 67.1 all-gather.3

commit v3 on v2

--- a/solution.py
+++ b/solution.py
@@ -50,6 +50,7 @@
         in_specs=[smem(), vmem(), vmem(), vmem()],
         out_specs=vmem(),
         name="partial_gram",
+        compiler_params=pltpu.CompilerParams(vmem_limit_bytes=8 << 20),
         cost_estimate=pl.CostEstimate(
             flops=4 * k * k * rows.shape[1], bytes_accessed=5 * rows.size, transcendentals=0
         ),
@@ -57,7 +58,9 @@
 
 
 def step_kernel(last, where, flags, diffs, *refs):
-    grams, (weight, base), outs, total = refs[:16], refs[16:18], refs[18:-1], refs[-1]
+    near, near_mate, far, far_mate = refs[:4], refs[4], refs[5:9], refs[9:13]
+    grams = (*near, *(near_mate.at[j] for j in range(4)), *far, *far_mate)
+    (weight, base), outs, total = refs[13:15], refs[15:-1], refs[-1]
     ylo, zl, core = where[0], where[1], where[2]
     half = grams[0].shape[2]
     for j, shift in enumerate(CLASSES):
@@ -95,12 +98,32 @@
         out_specs=tuple(vmem() for _ in outs),
         scratch_shapes=[pltpu.VMEM(weight.shape, jnp.float32)],
         name="last_step" if last else "first_step",
-        compiler_params=pltpu.CompilerParams(vmem_limit_bytes=32 << 20),
+        compiler_params=pltpu.CompilerParams(vmem_limit_bytes=16 << 20),
         cost_estimate=pl.CostEstimate(
             flops=2 * diffs.size * weight.shape[1], bytes_accessed=12 * diffs.size // 2,
             transcendentals=0,
         ),
     )(where, flags, diffs, *grams, weight, base)
+
+
+def pack_kernel(*refs):
+    for i, ref in enumerate(refs[:-1]):
+        refs[-1][i] = ref[...]
+
+
+def pack(parts):
+    part = parts[0]
+    return pl.pallas_call(
+        pack_kernel,
+        out_shape=jax.ShapeDtypeStruct((len(parts),) + part.shape, part.dtype),
+        in_specs=[vmem()] * len(parts),
+        out_specs=vmem(),
+        name="pack",
+        compiler_params=pltpu.CompilerParams(vmem_limit_bytes=4 << 20),
+        cost_estimate=pl.CostEstimate(
+            flops=0, bytes_accessed=4 * len(parts) * part.size, transcendentals=0
+        ),
+    )(*parts)
 
 
 def on_device(calib, base_weight, keep_blocks):
@@ -125,17 +148,21 @@
     mates = lax.all_gather(feats, "zl", axis=0, tiled=True)
     term = partial_gram(where, mates, own, other)
     half = term.shape[3]
-    diffs, term = lax.optimization_barrier((diffs, term))
     terms = lax.all_to_all(term.reshape(16, BLOCK, half), ("core",) + ROW, 0, 0, tiled=True)
+    diffs, terms = lax.optimization_barrier((diffs, terms))
     gram = (jnp.sum(terms.astype(jnp.float32), axis=0) / tokens).astype(jnp.bfloat16)
 
     line = ("zh", "zl", "core")
-    mine = lax.all_gather(gram, "zh", axis=0)
-    near = [mine] + [lax.ppermute(mine, line, from_z(*s)) for s in ((1, 1), (-1, -1), (2, -2))]
-    far = [lax.ppermute(g, "ylo", SWAP) for g in near]
-    near_mate = [lax.ppermute(g, "core", SWAP) for g in near]
+    mine = lax.all_to_all(jnp.broadcast_to(gram[None], (4,) + gram.shape), "zh", 0, 0, tiled=True)
+    up, down, two = from_z(1, 1), from_z(-1, -1), from_z(2, -2)
+    far = lax.ppermute(mine, "ylo", SWAP)
+    near = [mine] + [lax.ppermute(mine, line, s) for s in (up, down, two)]
+    far = [far] + [lax.ppermute(g, "ylo", SWAP) for g in near[1:3]] + [lax.ppermute(far, line, two)]
     far_mate = [lax.ppermute(g, "core", SWAP) for g in far]
-    grams = near + near_mate + far + far_mate
+    ahead = [far[2], far_mate[0], far_mate[1], far_mate[3]]
+    far[2], far_mate[0], far_mate[1], far_mate[3], *held = lax.optimization_barrier((*ahead, *near))
+    near_mate = lax.ppermute(pack(held), "core", SWAP)
+    grams = near + [near_mate] + far + far_mate
 
     weight, sent = step(False, where, flags, diffs, grams, weight, base_weight)
     diffs = lax.all_to_all(sent, ROW, 0, 0, tiled=True)

time: 200 us -> 189 us (0.945)
  waiting for transfers between devices: 12.7 us -> 5.52 us
  starting transfers between devices: 44.6 us -> 39 us
  blocking collectives: 116 us -> 121 us
    all_to_all x0 -> x1, blocking collectives: none -> 22.9 us  [on_device(): lax.all_to_all(jnp.broadcast_to(gram[None], (4,) + gram.shape), 'zh', 0,...]
    all_gather x1 -> x0, blocking collectives: 22.2 us -> none  [on_device(): mine = lax.all_gather(gram, 'zh', axis=0)]
    all_gather x1, waiting for transfers between devices: 9.13 us -> 0.01 us  [on_device(): diffs = lax.all_gather(diff, ROW, axis=0)]
    ppermute x11 -> x8, starting transfers between devices: 31.9 us -> 24.3 us  [the longest x3 11.9 us: on_device(): near = [mine] + [lax.ppermute(mine, line, s) for s in (up, down, two)]]
    all_to_all x1, blocking collectives: 23.1 us -> 28 us  [on_device(): lax.all_to_all(term.reshape(16, BLOCK, half), ('core',) + ROW, 0, 0, tile...]
    ppermute x4, starting transfers between devices: 9.5 us -> 11.5 us  [on_device(): far_mate = [lax.ppermute(g, 'core', SWAP) for g in far]]
  transfers between devices with their start and end apart: 17 -> 14, of which waited for: 3 -> 3; matrix products, arithmetic and copies ran while one was open for 1% -> 1% of each run, Pallas kernels for 2% -> 1%
where the time goes in v3:
time: 189 us; the launch traced here: 188 us
  blocking collectives  121 us (64%)
  starting transfers between devices  39 us (21%)
  between operations  13.6 us (7%)
  Pallas kernels  5.76 us (3%)
  waiting for transfers between devices  5.52 us (3%)
  other arithmetic  2.03 us (1%)
    all_to_all x1, blocking collectives, on_device(): lax.all_to_all(term.reshape(16, BLOCK, half), ('core',) + ROW, 0, 0, tile...  28 us
    all_gather x1, blocking collectives, on_device(): own = lax.all_gather(feats, 'zh', axis=0, tiled=True)  26 us
    all_to_all x1, blocking collectives, on_device(): lax.all_to_all(jnp.broadcast_to(gram[None], (4,) + gram.shape), 'zh', 0,...  22.9 us
    all_to_all x1, blocking collectives, on_device(): diffs = lax.all_to_all(sent, ROW, 0, 0, tiled=True)  19.4 us
    all_gather x1, blocking collectives, on_device(): mates = lax.all_gather(feats, 'zl', axis=0, tiled=True)  13.9 us
    ppermute x3, starting transfers between devices, on_device(): near = [mine] + [lax.ppermute(mine, line, s) for s in (up, down, two)]  11.9 us
    ppermute x4, starting transfers between devices, on_device(): far_mate = [lax.ppermute(g, 'core', SWAP) for g in far]  11.5 us
    all_to_all x1, blocking collectives, on_device(): feats = lax.all_to_all(calib.T, 'core', 1, 0, tiled=True)  10.4 us
  transfers between devices with their start and end apart: 14, of which 3 were waited for; matrix products, arithmetic and copies ran while one was open for 1% of the time, Pallas kernels for 1%

profile of v3, /device:TPU:1, one launch (start us, length us, event | category | flops | bytes accessed | tf_op | source)
XLA Modules:
  0.0 188.4 jit_solution(7696698199031812686)
XLA Ops:
  7.7 1.6 fusion
  10.2 10.4 %all_to_all.34 = bf16[64,2,512]{2,0,1:T(8,128)(2,1)S(1)} all-to-all(bf16[64,2,512]{2,0,1:T(8,128)(2,1)S(1)} %bitcast.19), channel_id=1, replica_groups=mesh['ylo'=2,'zh'=4,'zl'=4,'core'=2,'yhi'=2,'x'=4] {'core'}, dimensions={1} | all-to-all | bytes 262144 | tf_op jit(solution)/shard_map/all_to_all | solution.py:145
  20.6 26.0 %all_gather.15.own = bf16[512,512]{1,0:T(8,128)(2,1)S(1)} all-gather(bf16[128,512]{1,0:T(8,128)(2,1)S(1)} %bitcast.17), channel_id=1, replica_groups=mesh['ylo'=2,'zh'=4,'zl'=4,'core'=2,'yhi'=2,'x'=4] {'zh'}, dimensions={0}, use_global_device_ids=true | all-gather | bytes 655360 | tf_op jit(solution)/shard_map/all_gather | solution.py:146
  46.6 3.2 %collective-permute-start = (bf16[512,512]{1,0:T(8,128)(2,1)S(1)}, bf16[512,512]{1,0:T(8,128)(2,1)S(1)}, u32[]{:S(2)}, u32[]{:S(2)}) collective-permute-start(bf16[512,512]{1,0:T(8,128)(2,1)S(1)} %all_gather.15.own), channel_id=1, source_target_pairs={{0,256},{256,0},{1,257},{257,1},{2,258},{258,2},{3,259},{259,3},{4... | collective-permute-start | bytes 1572872 | tf_op jit(solution)/shard_map/ppermute | solution.py:147
  49.9 13.9 %all_gather.14.rows = bf16[512,512]{1,0:T(8,128)(2,1)S(1)} all-gather(bf16[128,512]{1,0:T(8,128)(2,1)S(1)} %bitcast.18), channel_id=1, replica_groups=mesh['ylo'=2,'zh'=4,'zl'=4,'core'=2,'yhi'=2,'x'=4] {'zl'}, dimensions={0}, use_global_device_ids=true | all-gather | bytes 655360 | tf_op jit(solution)/shard_map/all_gather | solution.py:148
  65.1 28.0 %all_to_all.35 = bf16[16,128,256]{2,1,0:T(8,128)(2,1)S(1)} all-to-all(bf16[16,128,256]{2,1,0:T(8,128)(2,1)S(1)} %bitcast.15), channel_id=1, replica_groups=mesh['ylo'=2,'zh'=4,'zl'=4,'core'=2,'yhi'=2,'x'=4] {'core','yhi','x'}, dimensions={0} | all-to-all | bytes 2097152 | tf_op jit(solution)/shard_map/all_to_all | solution.py:151
  93.3 22.9 %all_to_all.36.refs_0_ = bf16[4,128,256]{2,1,0:T(8,128)(2,1)S(1)} all-to-all(bf16[4,128,256]{2,1,0:T(8,128)(2,1)S(1)} %broadcast_in_dim.5), channel_id=1, replica_groups=mesh['ylo'=2,'zh'=4,'zl'=4,'core'=2,'yhi'=2,'x'=4] {'zh'}, dimensions={0} | all-to-all | bytes 524288 | tf_op jit(solution)/shard_map/all_to_all | solution.py:156
  116.2 2.8 %collective-permute-start.5 = (bf16[4,128,256]{2,1,0:T(8,128)(2,1)S(1)}, bf16[4,128,256]{2,1,0:T(8,128)(2,1)S(1)}, u32[]{:S(2)}, u32[]{:S(2)}) collective-permute-start(bf16[4,128,256]{2,1,0:T(8,128)(2,1)S(1)} %all_to_all.36.refs_0_), channel_id=1, source_target_pairs={{0,256},{256,0},{1,257},{257,1},{2,258},{258,2},{3,259},{259,3},{4... | collective-permute-start | bytes 786440 | tf_op jit(solution)/shard_map/ppermute | solution.py:158
  119.0 5.0 %collective-permute-start.1 = (bf16[4,128,256]{2,1,0:T(8,128)(2,1)S(1)}, bf16[4,128,256]{2,1,0:T(8,128)(2,1)S(1)}, u32[]{:S(2)}, u32[]{:S(2)}) collective-permute-start(bf16[4,128,256]{2,1,0:T(8,128)(2,1)S(1)} %all_to_all.36.refs_0_), channel_id=1, source_target_pairs={{16,0},{24,8},{32,16},{40,24},{48,32},{56,40},{64,48},{72,56},{80,... | collective-permute-start | bytes 786440 | tf_op jit(solution)/shard_map/ppermute | solution.py:159
  124.0 4.7 %collective-permute-start.2 = (bf16[4,128,256]{2,1,0:T(8,128)(2,1)S(1)}, bf16[4,128,256]{2,1,0:T(8,128)(2,1)S(1)}, u32[]{:S(2)}, u32[]{:S(2)}) collective-permute-start(bf16[4,128,256]{2,1,0:T(8,128)(2,1)S(1)} %all_to_all.36.refs_0_), channel_id=1, source_target_pairs={{240,0},{248,8},{0,16},{8,24},{16,32},{24,40},{32,48},{40,56},{48,... | collective-permute-start | bytes 786440 | tf_op jit(solution)/shard_map/ppermute | solution.py:159
  128.8 3.1 %collective-permute-start.9 = (bf16[4,128,256]{2,1,0:T(8,128)(2,1)S(1)}, bf16[4,128,256]{2,1,0:T(8,128)(2,1)S(1)}, u32[]{:S(2)}, u32[]{:S(2)}) collective-permute-start(bf16[4,128,256]{2,1,0:T(8,128)(2,1)S(1)} %collective-permute-done.5.refs_5_), channel_id=1, source_target_pairs={{32,0},{232,8},{48,16},{248,24},{64,32},{8,40},{80,48},{24,56},{96... | collective-permute-start | bytes 786440 | tf_op jit(solution)/shard_map/ppermute | solution.py:160
  132.4 1.9 %collective-permute-start.7 = (bf16[4,128,256]{2,1,0:T(8,128)(2,1)S(1)}, bf16[4,128,256]{2,1,0:T(8,128)(2,1)S(1)}, u32[]{:S(2)}, u32[]{:S(2)}) collective-permute-start(bf16[4,128,256]{2,1,0:T(8,128)(2,1)S(1)} %collective-permute-done.1.refs_1_), channel_id=1, source_target_pairs={{0,256},{256,0},{1,257},{257,1},{2,258},{258,2},{3,259},{259,3},{4... | collective-permute-start | bytes 786440 | tf_op jit(solution)/shard_map/ppermute | solution.py:160
  134.3 2.1 %collective-permute-start.3 = (bf16[4,128,256]{2,1,0:T(8,128)(2,1)S(1)}, bf16[4,128,256]{2,1,0:T(8,128)(2,1)S(1)}, u32[]{:S(2)}, u32[]{:S(2)}) collective-permute-start(bf16[4,128,256]{2,1,0:T(8,128)(2,1)S(1)} %all_to_all.36.refs_0_), channel_id=1, source_target_pairs={{32,0},{232,8},{48,16},{248,24},{64,32},{8,40},{80,48},{24,56},{96... | collective-permute-start | bytes 786440 | tf_op jit(solution)/shard_map/ppermute | solution.py:159
  136.4 5.3 %collective-permute-start.6 = (bf16[4,128,256]{2,1,0:T(8,128)(2,1)S(1)}, bf16[4,128,256]{2,1,0:T(8,128)(2,1)S(1)}, u32[]{:S(2)}, u32[]{:S(2)}) collective-permute-start(bf16[4,128,256]{2,1,0:T(8,128)(2,1)S(1)} %collective-permute-done.5.refs_5_), channel_id=1, source_target_pairs={{0,8},{8,0},{1,9},{9,1},{2,10},{10,2},{3,11},{11,3},{4,12},{12,4},... | collective-permute-start | bytes 786440 | tf_op jit(solution)/shard_map/ppermute | solution.py:161
  141.7 1.9 %collective-permute-start.4 = (bf16[4,128,256]{2,1,0:T(8,128)(2,1)S(1)}, bf16[4,128,256]{2,1,0:T(8,128)(2,1)S(1)}, u32[]{:S(2)}, u32[]{:S(2)}) collective-permute-start(bf16[4,128,256]{2,1,0:T(8,128)(2,1)S(1)} %collective-permute-done.2.refs_2_), channel_id=1, source_target_pairs={{0,256},{256,0},{1,257},{257,1},{2,258},{258,2},{3,259},{259,3},{4... | collective-permute-start | bytes 786440 | tf_op jit(solution)/shard_map/ppermute | solution.py:160
  143.6 2.2 %collective-permute-start.10 = (bf16[4,128,256]{2,1,0:T(8,128)(2,1)S(1)}, bf16[4,128,256]{2,1,0:T(8,128)(2,1)S(1)}, u32[]{:S(2)}, u32[]{:S(2)}) collective-permute-start(bf16[4,128,256]{2,1,0:T(8,128)(2,1)S(1)} %collective-permute-done.9.refs_8_), channel_id=1, source_target_pairs={{0,8},{8,0},{1,9},{9,1},{2,10},{10,2},{3,11},{11,3},{4,12},{12,4},... | collective-permute-start | bytes 786440 | tf_op jit(solution)/shard_map/ppermute | solution.py:161
  145.9 2.1 %collective-permute-start.8 = (bf16[4,128,256]{2,1,0:T(8,128)(2,1)S(1)}, bf16[4,128,256]{2,1,0:T(8,128)(2,1)S(1)}, u32[]{:S(2)}, u32[]{:S(2)}) collective-permute-start(bf16[4,128,256]{2,1,0:T(8,128)(2,1)S(1)} %collective-permute-done.7.refs_6_), channel_id=1, source_target_pairs={{0,8},{8,0},{1,9},{9,1},{2,10},{10,2},{3,11},{11,3},{4,12},{12,4},... | collective-permute-start | bytes 786440 | tf_op jit(solution)/shard_map/ppermute | solution.py:161
  148.0 3.5 %collective-permute-done.4.refs_7_ = bf16[4,128,256]{2,1,0:T(8,128)(2,1)S(1)} collective-permute-done((bf16[4,128,256]{2,1,0:T(8,128)(2,1)S(1)}, bf16[4,128,256]{2,1,0:T(8,128)(2,1)S(1)}, u32[]{:S(2)}, u32[]{:S(2)}) %collective-permute-start.4) | collective-permute-done | bytes 262176 | tf_op jit(solution)/shard_map/ppermute | solution.py:160
  151.6 2.7 %collective-permute-start.11 = (bf16[4,4,128,256]{3,2,1,0:T(8,128)(2,1)S(1)}, bf16[4,4,128,256]{3,2,1,0:T(8,128)(2,1)S(1)}, u32[]{:S(2)}, u32[]{:S(2)}) collective-permute-start(bf16[4,4,128,256]{3,2,1,0:T(8,128)(2,1)S(1)} %pack.1), channel_id=1, source_target_pairs={{0,8},{8,0},{1,9},{9,1},{2,10},{10,2},{3,11},{11,3},{4,12},{12,4},... | collective-permute-start | bytes 3145736 | tf_op jit(solution)/shard_map/ppermute | solution.py:164
  154.3 1.9 %collective-permute-start.12 = (bf16[4,128,256]{2,1,0:T(8,128)(2,1)S(1)}, bf16[4,128,256]{2,1,0:T(8,128)(2,1)S(1)}, u32[]{:S(2)}, u32[]{:S(2)}) collective-permute-start(bf16[4,128,256]{2,1,0:T(8,128)(2,1)S(1)} %collective-permute-done.4.refs_7_), channel_id=1, source_target_pairs={{0,8},{8,0},{1,9},{9,1},{2,10},{10,2},{3,11},{11,3},{4,12},{12,4},... | collective-permute-start | bytes 786440 | tf_op jit(solution)/shard_map/ppermute | solution.py:161
  156.2 1.5 collective-permute-done.12.refs_11_
  157.8 1.9 %first_step.1 = (bf16[128,512]{1,0:T(8,128)(2,1)S(1)}, bf16[8,128,512]{2,1,0:T(8,128)(2,1)S(1)}) custom-call(s32[3]{0:T(128)S(1)} %pad_add_fusion.where, s32[4]{0:T(128)S(1)} %get-tuple-element.36.flags, bf16[8,128,512]{2,1,0:T(8,128)(2,1)S(1)} %bitcast.16, bf16[4,128,256]{2,1,0:T(8,128)(2,1)S(1)} %all_to_all.36.refs_0_, ...), custom_call_target="tpu_custom_call" | custom-call | flops 536870912 | bytes 3145728 | tf_op jit(solution)/shard_map/first_step/pallas_call | solution.py:94
  159.7 19.4 %all_to_all.37.diffs = bf16[8,128,512]{2,1,0:T(8,128)(2,1)S(1)} all-to-all(bf16[8,128,512]{2,1,0:T(8,128)(2,1)S(1)} %get-tuple-element.31), channel_id=1, replica_groups=mesh['ylo'=2,'zh'=4,'zl'=4,'core'=2,'yhi'=2,'x'=4] {'yhi','x'}, dimensions={0} | all-to-all | bytes 2097152 | tf_op jit(solution)/shard_map/all_to_all | solution.py:168
  179.0 2.5 %last_step.1 = bf16[128,512]{1,0:T(8,128)(2,1)} custom-call(s32[3]{0:T(128)S(1)} %pad_add_fusion.where, s32[4]{0:T(128)S(1)} %get-tuple-element.36.flags, bf16[8,128,512]{2,1,0:T(8,128)(2,1)S(1)} %all_to_all.37.diffs, bf16[4,128,256]{2,1,0:T(8,128)(2,1)S(1)} %all_to_all.36.refs_0_, bf16[4,128,256]{2,1,0:T(8,128)(2,1)S(1)} %collective-permute-done.1.refs_1_, ...), custom_call_target="tpu_custom_call" | custom-call | flops 536870912 | bytes 3145728 | tf_op jit(solution)/shard_map/last_step/pallas_call | solution.py:94
  (32 shorter events, 4.2 us)
Async XLA Ops:
  6.5 0.7 copy-start
  6.5 86.6 %all-gather.3.cloned.1.call-start = ((), (), s32[]{:S(2)}) async-start(), calls=%async_computation.4 | async-start | bytes 1179648 | tf_op jit(solution)/shard_map/all_gather | solution.py:143
  46.6 17.2 %collective-permute-start = (bf16[512,512]{1,0:T(8,128)(2,1)S(1)}, bf16[512,512]{1,0:T(8,128)(2,1)S(1)}, u32[]{:S(2)}, u32[]{:S(2)}) collective-permute-start(bf16[512,512]{1,0:T(8,128)(2,1)S(1)} %all_gather.15.own), channel_id=1, source_target_pairs={{0,256},{256,0},{1,257},{257,1},{2,258},{258,2},{3,259},{259,3},{4... | collective-permute-start | bytes 1572872 | tf_op jit(solution)/shard_map/ppermute | solution.py:147
  116.2 41.5 %copy-start.1 = (bf16[128,512]{1,0:T(8,128)(2,1)S(1)}, bf16[128,512]{1,0:T(8,128)(2,1)}, u32[]{:S(2)}) copy-start(bf16[128,512]{1,0:T(8,128)(2,1)} %refs_14_.3) | copy-start | bytes 393220
  116.2 41.5 %copy-start.2 = (bf16[1024,512]{1,0:T(8,128)(2,1)S(1)}, bf16[1024,512]{1,0:T(8,128)(2,1)}, u32[]{:S(2)}) copy-start(bf16[1024,512]{1,0:T(8,128)(2,1)} %all-gather.3.cloned.1.call-done) | copy-start | bytes 3145732
  116.2 12.6 %collective-permute-start.5 = (bf16[4,128,256]{2,1,0:T(8,128)(2,1)S(1)}, bf16[4,128,256]{2,1,0:T(8,128)(2,1)S(1)}, u32[]{:S(2)}, u32[]{:S(2)}) collective-permute-start(bf16[4,128,256]{2,1,0:T(8,128)(2,1)S(1)} %all_to_all.36.refs_0_), channel_id=1, source_target_pairs={{0,256},{256,0},{1,257},{257,1},{2,258},{258,2},{3,259},{259,3},{4... | collective-permute-start | bytes 786440 | tf_op jit(solution)/shard_map/ppermute | solution.py:158
  119.0 13.4 %collective-permute-start.1 = (bf16[4,128,256]{2,1,0:T(8,128)(2,1)S(1)}, bf16[4,128,256]{2,1,0:T(8,128)(2,1)S(1)}, u32[]{:S(2)}, u32[]{:S(2)}) collective-permute-start(bf16[4,128,256]{2,1,0:T(8,128)(2,1)S(1)} %all_to_all.36.refs_0_), channel_id=1, source_target_pairs={{16,0},{24,8},{32,16},{40,24},{48,32},{56,40},{64,48},{72,56},{80,... | collective-permute-start | bytes 786440 | tf_op jit(solution)/shard_map/ppermute | solution.py:159
  124.0 17.7 %collective-permute-start.2 = (bf16[4,128,256]{2,1,0:T(8,128)(2,1)S(1)}, bf16[4,128,256]{2,1,0:T(8,128)(2,1)S(1)}, u32[]{:S(2)}, u32[]{:S(2)}) collective-permute-start(bf16[4,128,256]{2,1,0:T(8,128)(2,1)S(1)} %all_to_all.36.refs_0_), channel_id=1, source_target_pairs={{240,0},{248,8},{0,16},{8,24},{16,32},{24,40},{32,48},{40,56},{48,... | collective-permute-start | bytes 786440 | tf_op jit(solution)/shard_map/ppermute | solution.py:159
  128.8 14.8 %collective-permute-start.9 = (bf16[4,128,256]{2,1,0:T(8,128)(2,1)S(1)}, bf16[4,128,256]{2,1,0:T(8,128)(2,1)S(1)}, u32[]{:S(2)}, u32[]{:S(2)}) collective-permute-start(bf16[4,128,256]{2,1,0:T(8,128)(2,1)S(1)} %collective-permute-done.5.refs_5_), channel_id=1, source_target_pairs={{32,0},{232,8},{48,16},{248,24},{64,32},{8,40},{80,48},{24,56},{96... | collective-permute-start | bytes 786440 | tf_op jit(solution)/shard_map/ppermute | solution.py:160
  132.4 13.5 %collective-permute-start.7 = (bf16[4,128,256]{2,1,0:T(8,128)(2,1)S(1)}, bf16[4,128,256]{2,1,0:T(8,128)(2,1)S(1)}, u32[]{:S(2)}, u32[]{:S(2)}) collective-permute-start(bf16[4,128,256]{2,1,0:T(8,128)(2,1)S(1)} %collective-permute-done.1.refs_1_), channel_id=1, source_target_pairs={{0,256},{256,0},{1,257},{257,1},{2,258},{258,2},{3,259},{259,3},{4... | collective-permute-start | bytes 786440 | tf_op jit(solution)/shard_map/ppermute | solution.py:160
  134.3 13.7 %collective-permute-start.3 = (bf16[4,128,256]{2,1,0:T(8,128)(2,1)S(1)}, bf16[4,128,256]{2,1,0:T(8,128)(2,1)S(1)}, u32[]{:S(2)}, u32[]{:S(2)}) collective-permute-start(bf16[4,128,256]{2,1,0:T(8,128)(2,1)S(1)} %all_to_all.36.refs_0_), channel_id=1, source_target_pairs={{32,0},{232,8},{48,16},{248,24},{64,32},{8,40},{80,48},{24,56},{96... | collective-permute-start | bytes 786440 | tf_op jit(solution)/shard_map/ppermute | solution.py:159
  136.4 11.6 %collective-permute-start.6 = (bf16[4,128,256]{2,1,0:T(8,128)(2,1)S(1)}, bf16[4,128,256]{2,1,0:T(8,128)(2,1)S(1)}, u32[]{:S(2)}, u32[]{:S(2)}) collective-permute-start(bf16[4,128,256]{2,1,0:T(8,128)(2,1)S(1)} %collective-permute-done.5.refs_5_), channel_id=1, source_target_pairs={{0,8},{8,0},{1,9},{9,1},{2,10},{10,2},{3,11},{11,3},{4,12},{12,4},... | collective-permute-start | bytes 786440 | tf_op jit(solution)/shard_map/ppermute | solution.py:161
  141.7 9.8 %collective-permute-start.4 = (bf16[4,128,256]{2,1,0:T(8,128)(2,1)S(1)}, bf16[4,128,256]{2,1,0:T(8,128)(2,1)S(1)}, u32[]{:S(2)}, u32[]{:S(2)}) collective-permute-start(bf16[4,128,256]{2,1,0:T(8,128)(2,1)S(1)} %collective-permute-done.2.refs_2_), channel_id=1, source_target_pairs={{0,256},{256,0},{1,257},{257,1},{2,258},{258,2},{3,259},{259,3},{4... | collective-permute-start | bytes 786440 | tf_op jit(solution)/shard_map/ppermute | solution.py:160
  143.6 7.9 %collective-permute-start.10 = (bf16[4,128,256]{2,1,0:T(8,128)(2,1)S(1)}, bf16[4,128,256]{2,1,0:T(8,128)(2,1)S(1)}, u32[]{:S(2)}, u32[]{:S(2)}) collective-permute-start(bf16[4,128,256]{2,1,0:T(8,128)(2,1)S(1)} %collective-permute-done.9.refs_8_), channel_id=1, source_target_pairs={{0,8},{8,0},{1,9},{9,1},{2,10},{10,2},{3,11},{11,3},{4,12},{12,4},... | collective-permute-start | bytes 786440 | tf_op jit(solution)/shard_map/ppermute | solution.py:161
  145.9 5.7 %collective-permute-start.8 = (bf16[4,128,256]{2,1,0:T(8,128)(2,1)S(1)}, bf16[4,128,256]{2,1,0:T(8,128)(2,1)S(1)}, u32[]{:S(2)}, u32[]{:S(2)}) collective-permute-start(bf16[4,128,256]{2,1,0:T(8,128)(2,1)S(1)} %collective-permute-done.7.refs_6_), channel_id=1, source_target_pairs={{0,8},{8,0},{1,9},{9,1},{2,10},{10,2},{3,11},{11,3},{4,12},{12,4},... | collective-permute-start | bytes 786440 | tf_op jit(solution)/shard_map/ppermute | solution.py:161
  151.6 6.1 %collective-permute-start.11 = (bf16[4,4,128,256]{3,2,1,0:T(8,128)(2,1)S(1)}, bf16[4,4,128,256]{3,2,1,0:T(8,128)(2,1)S(1)}, u32[]{:S(2)}, u32[]{:S(2)}) collective-permute-start(bf16[4,4,128,256]{3,2,1,0:T(8,128)(2,1)S(1)} %pack.1), channel_id=1, source_target_pairs={{0,8},{8,0},{1,9},{9,1},{2,10},{10,2},{3,11},{11,3},{4,12},{12,4},... | collective-permute-start | bytes 3145736 | tf_op jit(solution)/shard_map/ppermute | solution.py:164
  154.3 3.4 %collective-permute-start.12 = (bf16[4,128,256]{2,1,0:T(8,128)(2,1)S(1)}, bf16[4,128,256]{2,1,0:T(8,128)(2,1)S(1)}, u32[]{:S(2)}, u32[]{:S(2)}) collective-permute-start(bf16[4,128,256]{2,1,0:T(8,128)(2,1)S(1)} %collective-permute-done.4.refs_7_), channel_id=1, source_target_pairs={{0,8},{8,0},{1,9},{9,1},{2,10},{10,2},{3,11},{11,3},{4,12},{12,4},... | collective-permute-start | bytes 786440 | tf_op jit(solution)/shard_map/ppermute | solution.py:161
Sparse Core Ops, SparseCore 0:
  10.6 67.1 all-gather.2

commit v4 on v3

v4 whole, which is shorter than its diff:
```python
import functools

import jax
import jax.numpy as jnp
from jax import lax
from jax.experimental import pallas as pl
from jax.experimental.pallas import tpu as pltpu
from jax.sharding import Mesh, PartitionSpec as P

BLOCK = 128
RATE = 0.25
NT = (((1,), (1,)), ((), ()))
AXES = ("ylo", "zh", "zl", "core", "yhi", "x")
SIZES = (2, 4, 4, 2, 2, 4)
TOK = ("ylo", "zh", "zl", "core")
ROW = ("yhi", "x")
SWAP = ((0, 1), (1, 0))
CLASSES = (0, 1, 3, 2)


def from_z(*steps):
    return [((z + s) % 16 * 2 + c, z * 2 + c) for z in range(16) for c, s in enumerate(steps)]


def vmem():
    return pl.BlockSpec(memory_space=pltpu.VMEM)


def smem():
    return pl.BlockSpec(memory_space=pltpu.SMEM)


def by_core(x):
    chunk = BLOCK // 2
    order = [2 * i + c for c in range(2) for i in range(x.shape[1] // BLOCK)]
    return jnp.concatenate([x[:, i * chunk : (i + 1) * chunk] for i in order], axis=1)


def start_kernel(kept, base, weight, diff, keep_out):
    tok = lax.axis_index(TOK)
    first = lax.axis_index(ROW) * (base.shape[1] // BLOCK)
    block = lax.broadcasted_iota(jnp.int32, base.shape, 1) // BLOCK
    keep = jnp.zeros(base.shape, jnp.float32)
    for b in range(base.shape[1] // BLOCK):
        listed = jnp.int32(0)
        for j in range(kept.shape[0]):
            listed = jnp.where(kept[j, tok] == first + b, 1, listed)
        keep = jnp.where(block == b, listed.astype(jnp.float32), keep)
    base_float = base[...].astype(jnp.float32)
    new = (keep * base_float).astype(jnp.bfloat16)
    weight[...] = new
    keep_out[...] = keep
    diff[...] = by_core((new.astype(jnp.float32) - base_float).astype(jnp.bfloat16))


def start(keep_blocks, base):
    bf16 = jax.ShapeDtypeStruct(base.shape, base.dtype)
    return pl.pallas_call(
        start_kernel,
        out_shape=(bf16, bf16, jax.ShapeDtypeStruct(base.shape, jnp.float32)),
        in_specs=[smem(), vmem()],
        out_specs=(vmem(),) * 3,
        name="start",
        compiler_params=pltpu.CompilerParams(vmem_limit_bytes=4 << 20),
    )(keep_blocks.T, base)


def partial_gram_kernel(rows, s00, s10, s01, s11, out):
    ylo, core = lax.axis_index("ylo"), lax.axis_index("core")
    chunk = BLOCK // 2
    for dy, dc, cols in ((0, 0, s00), (1, 0, s10), (0, 1, s01), (1, 1, s11)):
        term = lax.dot_general(cols[...], rows[...], NT, preferred_element_type=jnp.float32)
        term = term.astype(jnp.bfloat16).reshape(4, chunk, rows.shape[0])
        half = pl.ds(pl.multiple_of((core ^ dc) * chunk, chunk), chunk)
        out[pl.ds((ylo ^ dy) * 4, 4), half, :] = term


def partial_gram(rows, *cols):
    k = rows.shape[0]
    return pl.pallas_call(
        partial_gram_kernel,
        out_shape=jax.ShapeDtypeStruct((8, BLOCK, k), jnp.bfloat16),
        in_specs=[vmem()] * 5,
        out_specs=vmem(),
        name="partial_gram",
        compiler_params=pltpu.CompilerParams(vmem_limit_bytes=8 << 20),
        cost_estimate=pl.CostEstimate(
            flops=8 * k * k * rows.shape[1], bytes_accessed=12 * rows.size, transcendentals=0
        ),
    )(rows, *cols)


def step_kernel(last, diffs, *refs):
    near, near_mate, far, far_mate = refs[:4], refs[4], refs[5:9], refs[9]
    (weight, base, keep), outs, total = refs[10:13], refs[13:-1], refs[-1]
    ylo, zl, core = (lax.axis_index(a) for a in ("ylo", "zl", "core"))
    half = near[0].shape[2]
    for j, shift in enumerate(CLASSES):
        part = jnp.zeros((weight.shape[0], BLOCK), jnp.float32)
        for dy, dc, gram in (
            (0, 0, near[j]), (0, 1, near_mate.at[j]), (1, 0, far[j]), (1, 1, far_mate.at[j])
        ):
            lanes = pl.ds(pl.multiple_of((core ^ dc) * half, half), half)
            for h in range(4):
                part += lax.dot_general(
                    diffs[(ylo ^ dy) * 4 + h, :, lanes], gram[h], NT,
                    preferred_element_type=jnp.float32,
                )
        place = lax.rem(zl + shift, 4) * BLOCK
        total[:, pl.ds(pl.multiple_of(place, BLOCK), BLOCK)] = part
    old = weight[...].astype(jnp.float32)
    new = (old - RATE * keep[...] * total[...]).astype(jnp.bfloat16)
    outs[0][...] = new
    if not last:
        diff = (new.astype(jnp.float32) - base[...].astype(jnp.float32)).astype(jnp.bfloat16)
        diff = by_core(diff)
        for i in range(outs[1].shape[0]):
            outs[1][i] = diff


def step(last, diffs, grams, weight, base, keep):
    shape = jax.ShapeDtypeStruct(weight.shape, weight.dtype)
    outs = (shape,) if last else (shape, jax.ShapeDtypeStruct(diffs.shape, diffs.dtype))
    return pl.pallas_call(
        functools.partial(step_kernel, last),
        out_shape=outs,
        in_specs=[vmem()] * (len(grams) + 4),
        out_specs=tuple(vmem() for _ in outs),
        scratch_shapes=[pltpu.VMEM(weight.shape, jnp.float32)],
        name="last_step" if last else "first_step",
        compiler_params=pltpu.CompilerParams(vmem_limit_bytes=16 << 20),
        cost_estimate=pl.CostEstimate(
            flops=2 * diffs.size * weight.shape[1], bytes_accessed=12 * diffs.size // 2,
            transcendentals=0,
        ),
    )(diffs, *grams, weight, base, keep)


def pack_kernel(*refs):
    for i, ref in enumerate(refs[:-1]):
        refs[-1][i] = ref[...]


def pack(parts):
    part = parts[0]
    return pl.pallas_call(
        pack_kernel,
        out_shape=jax.ShapeDtypeStruct((len(parts),) + part.shape, part.dtype),
        in_specs=[vmem()] * len(parts),
        out_specs=vmem(),
        name="pack",
        compiler_params=pltpu.CompilerParams(vmem_limit_bytes=4 << 20),
        cost_estimate=pl.CostEstimate(
            flops=0, bytes_accessed=4 * len(parts) * part.size, transcendentals=0
        ),
    )(*parts)


def on_device(calib, base_weight, keep_blocks):
    tokens = calib.shape[0] * 8
    weight, diff, keep = start(keep_blocks, base_weight)
    diff, calib = lax.optimization_barrier((diff, calib))
    diffs = lax.all_gather(diff, ROW, axis=0)

    feats = calib.T
    own = lax.all_gather(feats, "zh", axis=0, tiled=True)
    other = lax.ppermute(own, "ylo", SWAP)
    own_mate = lax.ppermute(own, "core", SWAP)
    rows = lax.all_gather(feats, "zl", axis=0, tiled=True)
    rows, other = lax.optimization_barrier((rows, other))
    other_mate = lax.ppermute(other, "core", SWAP)
    term = partial_gram(rows, own, other, own_mate, other_mate)
    terms = lax.all_to_all(term, ROW, 0, 0, tiled=True)
    diffs, terms = lax.optimization_barrier((diffs, terms))
    gram = (jnp.sum(terms.astype(jnp.float32), axis=0) / tokens).astype(jnp.bfloat16)

    line = ("zh", "zl", "core")
    mine = lax.all_to_all(jnp.broadcast_to(gram[None], (4,) + gram.shape), "zh", 0, 0, tiled=True)
    up, down, two = from_z(1, 1), from_z(-1, -1), from_z(2, -2)
    far = lax.ppermute(mine, "ylo", SWAP)
    near = [mine] + [lax.ppermute(mine, line, s) for s in (up, down, two)]
    far = [far] + [lax.ppermute(g, "ylo", SWAP) for g in near[1:3]] + [lax.ppermute(far, line, two)]
    far[1], far[3], *held = lax.optimization_barrier((far[1], far[3], *near))
    near_mate = lax.ppermute(pack(held), "core", SWAP)
    far[2], near_mate = lax.optimization_barrier((far[2], near_mate))
    far_mate = lax.ppermute(pack(far), "core", SWAP)
    grams = near + [near_mate] + far + [far_mate]

    weight, sent = step(False, diffs, grams, weight, base_weight, keep)
    diffs = lax.all_to_all(sent, ROW, 0, 0, tiled=True)
    return step(True, diffs, grams, weight, base_weight, keep)[0]


def solution(mesh):
    split = Mesh(mesh.devices.reshape(SIZES), AXES)
    return jax.shard_map(
        on_device,
        mesh=split,
        in_specs=(P(ROW, TOK), P(TOK, ROW), P()),
        out_specs=P(TOK, ROW),
        check_vma=False,
    )
```

time: 189 us -> 190 us (level)
  blocking collectives: 121 us -> 105 us
  waiting for transfers between devices: 5.52 us -> 20.1 us
  starting transfers between devices: 39 us -> 42.8 us
  other arithmetic: 2.03 us -> 0.08 us
    all_to_all x2 -> x1, blocking collectives: 38.3 us -> 17.1 us  [on_device(): terms = lax.all_to_all(term, ROW, 0, 0, tiled=True)]
    ppermute x3, waiting for transfers between devices: 0.48 us -> 8.44 us  [on_device(): near = [mine] + [lax.ppermute(mine, line, s) for s in (up, down, two)]]
    all_gather x1, blocking collectives: 26 us -> 31.2 us  [on_device(): own = lax.all_gather(feats, 'zh', axis=0, tiled=True)]
    ppermute x3, starting transfers between devices: 11.9 us -> 15.6 us  [on_device(): near = [mine] + [lax.ppermute(mine, line, s) for s in (up, down, two)]]
    ppermute x2, waiting for transfers between devices: 3.5 us -> 6.07 us  [on_device(): lax.ppermute(g, 'ylo', SWAP)]
    ppermute x2, starting transfers between devices: 3.84 us -> 6.32 us  [on_device(): lax.ppermute(g, 'ylo', SWAP)]
    ppermute x4 -> x3, waiting for transfers between devices: 1.51 us -> 3.77 us  [the longest x1 2.26 us: on_device(): far_mate = lax.ppermute(pack(far), 'core', SWAP)]
    all_to_all x1, blocking collectives: 22.9 us -> 20.7 us  [on_device(): lax.all_to_all(jnp.broadcast_to(gram[None], (4,) + gram.shape), 'zh', 0,...]
  transfers between devices with their start and end apart: 14 -> 13, of which waited for: 3 -> 6; matrix products, arithmetic and copies ran while one was open for 1% -> 0% of each run, Pallas kernels for 1% -> 0%
where the time goes in v4:
time: 190 us; the launch traced here: 189 us
  blocking collectives  105 us (55%)
  starting transfers between devices  42.8 us (23%)
  waiting for transfers between devices  20.1 us (11%)
  between operations  13.6 us (7%)
  Pallas kernels  5.78 us (3%)
    all_gather x1, blocking collectives, on_device(): own = lax.all_gather(feats, 'zh', axis=0, tiled=True)  31.2 us
    all_to_all x1, blocking collectives, on_device(): lax.all_to_all(jnp.broadcast_to(gram[None], (4,) + gram.shape), 'zh', 0,...  20.7 us
    all_to_all x1, blocking collectives, on_device(): diffs = lax.all_to_all(sent, ROW, 0, 0, tiled=True)  20.6 us
    all_to_all x1, blocking collectives, on_device(): terms = lax.all_to_all(term, ROW, 0, 0, tiled=True)  17.1 us
    ppermute x3, starting transfers between devices, on_device(): near = [mine] + [lax.ppermute(mine, line, s) for s in (up, down, two)]  15.6 us
    all_gather x1, blocking collectives, on_device(): rows = lax.all_gather(feats, 'zl', axis=0, tiled=True)  15.2 us
    ppermute x3, waiting for transfers between devices, on_device(): near = [mine] + [lax.ppermute(mine, line, s) for s in (up, down, two)]  8.44 us
    ppermute x2, starting transfers between devices, on_device(): lax.ppermute(g, 'ylo', SWAP)  6.32 us
  transfers between devices with their start and end apart: 13, of which 6 were waited for; matrix products, arithmetic and copies ran while one was open for 0% of the time, Pallas kernels for 0%

profile of v4, /device:TPU:1, one launch (start us, length us, event | category | flops | bytes accessed | tf_op | source)
XLA Modules:
  0.0 188.7 jit_solution(10810834420945040424)
XLA Ops:
  8.1 1.5 start.1
  9.7 31.2 %all_gather.15.s00 = bf16[256,1024]{1,0:T(8,128)(2,1)S(1)} all-gather(bf16[64,1024]{1,0:T(8,128)(2,1)S(1)} %bitcast.5), channel_id=1, replica_groups=mesh['ylo'=2,'zh'=4,'zl'=4,'core'=2,'yhi'=2,'x'=4] {'zh'}, dimensions={0}, use_global_device_ids=true | all-gather | bytes 655360 | tf_op jit(solution)/shard_map/all_gather | solution.py:166
  40.9 3.2 %collective-permute-start = (bf16[256,1024]{1,0:T(8,128)(2,1)S(1)}, bf16[256,1024]{1,0:T(8,128)(2,1)S(1)}, u32[]{:S(2)}, u32[]{:S(2)}) collective-permute-start(bf16[256,1024]{1,0:T(8,128)(2,1)S(1)} %all_gather.15.s00), channel_id=1, source_target_pairs={{0,256},{256,0},{1,257},{257,1},{2,258},{258,2},{3,259},{259,3},{4... | collective-permute-start | bytes 1572872 | tf_op jit(solution)/shard_map/ppermute | solution.py:167
  44.1 5.3 %collective-permute-start.1 = (bf16[256,1024]{1,0:T(8,128)(2,1)S(1)}, bf16[256,1024]{1,0:T(8,128)(2,1)S(1)}, u32[]{:S(2)}, u32[]{:S(2)}) collective-permute-start(bf16[256,1024]{1,0:T(8,128)(2,1)S(1)} %all_gather.15.s00), channel_id=1, source_target_pairs={{0,8},{8,0},{1,9},{9,1},{2,10},{10,2},{3,11},{11,3},{4,12},{12,4},... | collective-permute-start | bytes 1572872 | tf_op jit(solution)/shard_map/ppermute | solution.py:168
  49.4 15.2 %all_gather.14.rows = bf16[256,1024]{1,0:T(8,128)(2,1)S(1)} all-gather(bf16[64,1024]{1,0:T(8,128)(2,1)S(1)} %bitcast.6), channel_id=1, replica_groups=mesh['ylo'=2,'zh'=4,'zl'=4,'core'=2,'yhi'=2,'x'=4] {'zl'}, dimensions={0}, use_global_device_ids=true | all-gather | bytes 655360 | tf_op jit(solution)/shard_map/all_gather | solution.py:169
  64.6 3.2 %collective-permute-start.2 = (bf16[256,1024]{1,0:T(8,128)(2,1)S(1)}, bf16[256,1024]{1,0:T(8,128)(2,1)S(1)}, u32[]{:S(2)}, u32[]{:S(2)}) collective-permute-start(bf16[256,1024]{1,0:T(8,128)(2,1)S(1)} %collective-permute-done.s10), channel_id=1, source_target_pairs={{0,8},{8,0},{1,9},{9,1},{2,10},{10,2},{3,11},{11,3},{4,12},{12,4},... | collective-permute-start | bytes 1572872 | tf_op jit(solution)/shard_map/ppermute | solution.py:171
  67.8 1.5 collective-permute-done.2.s11
  70.1 17.1 %all_to_all.15 = bf16[8,128,256]{2,1,0:T(8,128)(2,1)S(1)} all-to-all(bf16[8,128,256]{2,1,0:T(8,128)(2,1)S(1)} %partial_gram.1), channel_id=1, replica_groups=mesh['ylo'=2,'zh'=4,'zl'=4,'core'=2,'yhi'=2,'x'=4] {'yhi','x'}, dimensions={0} | all-to-all | bytes 1048576 | tf_op jit(solution)/shard_map/all_to_all | solution.py:173
  87.3 20.7 %all_to_all.16.refs_0_ = bf16[4,128,256]{2,1,0:T(8,128)(2,1)S(1)} all-to-all(bf16[4,128,256]{2,1,0:T(8,128)(2,1)S(1)} %broadcast_in_dim.2), channel_id=1, replica_groups=mesh['ylo'=2,'zh'=4,'zl'=4,'core'=2,'yhi'=2,'x'=4] {'zh'}, dimensions={0} | all-to-all | bytes 524288 | tf_op jit(solution)/shard_map/all_to_all | solution.py:178
  108.0 1.9 %collective-permute-start.8 = (bf16[4,128,256]{2,1,0:T(8,128)(2,1)S(1)}, bf16[4,128,256]{2,1,0:T(8,128)(2,1)S(1)}, u32[]{:S(2)}, u32[]{:S(2)}) collective-permute-start(bf16[4,128,256]{2,1,0:T(8,128)(2,1)S(1)} %all_to_all.16.refs_0_), channel_id=1, source_target_pairs={{0,256},{256,0},{1,257},{257,1},{2,258},{258,2},{3,259},{259,3},{4... | collective-permute-start | bytes 786440 | tf_op jit(solution)/shard_map/ppermute | solution.py:180
  109.9 9.0 %collective-permute-start.3 = (bf16[4,128,256]{2,1,0:T(8,128)(2,1)S(1)}, bf16[4,128,256]{2,1,0:T(8,128)(2,1)S(1)}, u32[]{:S(2)}, u32[]{:S(2)}) collective-permute-start(bf16[4,128,256]{2,1,0:T(8,128)(2,1)S(1)} %all_to_all.16.refs_0_), channel_id=1, source_target_pairs={{16,0},{24,8},{32,16},{40,24},{48,32},{56,40},{64,48},{72,56},{80,... | collective-permute-start | bytes 786440 | tf_op jit(solution)/shard_map/ppermute | solution.py:181
  118.9 4.7 %collective-permute-start.5 = (bf16[4,128,256]{2,1,0:T(8,128)(2,1)S(1)}, bf16[4,128,256]{2,1,0:T(8,128)(2,1)S(1)}, u32[]{:S(2)}, u32[]{:S(2)}) collective-permute-start(bf16[4,128,256]{2,1,0:T(8,128)(2,1)S(1)} %all_to_all.16.refs_0_), channel_id=1, source_target_pairs={{32,0},{232,8},{48,16},{248,24},{64,32},{8,40},{80,48},{24,56},{96... | collective-permute-start | bytes 786440 | tf_op jit(solution)/shard_map/ppermute | solution.py:181
  123.6 1.9 %collective-permute-start.4 = (bf16[4,128,256]{2,1,0:T(8,128)(2,1)S(1)}, bf16[4,128,256]{2,1,0:T(8,128)(2,1)S(1)}, u32[]{:S(2)}, u32[]{:S(2)}) collective-permute-start(bf16[4,128,256]{2,1,0:T(8,128)(2,1)S(1)} %all_to_all.16.refs_0_), channel_id=1, source_target_pairs={{240,0},{248,8},{0,16},{8,24},{16,32},{24,40},{32,48},{40,56},{48,... | collective-permute-start | bytes 786440 | tf_op jit(solution)/shard_map/ppermute | solution.py:181
  125.6 2.1 %collective-permute-start.9 = (bf16[4,128,256]{2,1,0:T(8,128)(2,1)S(1)}, bf16[4,128,256]{2,1,0:T(8,128)(2,1)S(1)}, u32[]{:S(2)}, u32[]{:S(2)}) collective-permute-start(bf16[4,128,256]{2,1,0:T(8,128)(2,1)S(1)} %collective-permute-done.8.refs_0_.refs_5_), channel_id=1, source_target_pairs={{32,0},{232,8},{48,16},{248,24},{64,32},{8,40},{80,48},{24,56},{96... | collective-permute-start | bytes 786440 | tf_op jit(solution)/shard_map/ppermute | solution.py:182
  127.7 2.8 %collective-permute-start.7 = (bf16[4,128,256]{2,1,0:T(8,128)(2,1)S(1)}, bf16[4,128,256]{2,1,0:T(8,128)(2,1)S(1)}, u32[]{:S(2)}, u32[]{:S(2)}) collective-permute-start(bf16[4,128,256]{2,1,0:T(8,128)(2,1)S(1)} %collective-permute-done.3.refs_1_), channel_id=1, source_target_pairs={{0,256},{256,0},{1,257},{257,1},{2,258},{258,2},{3,259},{259,3},{4... | collective-permute-start | bytes 786440 | tf_op jit(solution)/shard_map/ppermute | solution.py:182
  131.1 7.8 %collective-permute-done.4.refs_2_ = bf16[4,128,256]{2,1,0:T(8,128)(2,1)S(1)} collective-permute-done((bf16[4,128,256]{2,1,0:T(8,128)(2,1)S(1)}, bf16[4,128,256]{2,1,0:T(8,128)(2,1)S(1)}, u32[]{:S(2)}, u32[]{:S(2)}) %collective-permute-start.4) | collective-permute-done | bytes 262176 | tf_op jit(solution)/shard_map/ppermute | solution.py:181
  138.9 1.8 collective-permute-done.9.refs_3_.refs_8_
  140.8 2.1 %collective-permute-start.10 = (bf16[4,4,128,256]{3,2,1,0:T(8,128)(2,1)S(1)}, bf16[4,4,128,256]{3,2,1,0:T(8,128)(2,1)S(1)}, u32[]{:S(2)}, u32[]{:S(2)}) collective-permute-start(bf16[4,4,128,256]{3,2,1,0:T(8,128)(2,1)S(1)} %pack.2), channel_id=1, source_target_pairs={{0,8},{8,0},{1,9},{9,1},{2,10},{10,2},{3,11},{11,3},{4,12},{12,4},... | collective-permute-start | bytes 3145736 | tf_op jit(solution)/shard_map/ppermute | solution.py:184
  142.9 3.5 %collective-permute-start.6 = (bf16[4,128,256]{2,1,0:T(8,128)(2,1)S(1)}, bf16[4,128,256]{2,1,0:T(8,128)(2,1)S(1)}, u32[]{:S(2)}, u32[]{:S(2)}) collective-permute-start(bf16[4,128,256]{2,1,0:T(8,128)(2,1)S(1)} %collective-permute-done.4.refs_2_), channel_id=1, source_target_pairs={{0,256},{256,0},{1,257},{257,1},{2,258},{258,2},{3,259},{259,3},{4... | collective-permute-start | bytes 786440 | tf_op jit(solution)/shard_map/ppermute | solution.py:182
  146.4 6.1 %collective-permute-done.6.refs_2_.refs_7_ = bf16[4,128,256]{2,1,0:T(8,128)(2,1)S(1)} collective-permute-done((bf16[4,128,256]{2,1,0:T(8,128)(2,1)S(1)}, bf16[4,128,256]{2,1,0:T(8,128)(2,1)S(1)}, u32[]{:S(2)}, u32[]{:S(2)}) %collective-permute-start.6) | collective-permute-done | bytes 262176 | tf_op jit(solution)/shard_map/ppermute | solution.py:182
  152.5 3.1 %collective-permute-start.11 = (bf16[4,4,128,256]{3,2,1,0:T(8,128)(2,1)S(1)}, bf16[4,4,128,256]{3,2,1,0:T(8,128)(2,1)S(1)}, u32[]{:S(2)}, u32[]{:S(2)}) collective-permute-start(bf16[4,4,128,256]{3,2,1,0:T(8,128)(2,1)S(1)} %pack.3), channel_id=1, source_target_pairs={{0,8},{8,0},{1,9},{9,1},{2,10},{10,2},{3,11},{11,3},{4,12},{12,4},... | collective-permute-start | bytes 3145736 | tf_op jit(solution)/shard_map/ppermute | solution.py:186
  155.6 2.3 %collective-permute-done.11.refs_9_ = bf16[4,4,128,256]{3,2,1,0:T(8,128)(2,1)S(1)} collective-permute-done((bf16[4,4,128,256]{3,2,1,0:T(8,128)(2,1)S(1)}, bf16[4,4,128,256]{3,2,1,0:T(8,128)(2,1)S(1)}, u32[]{:S(2)}, u32[]{:S(2)}) %collective-permute-start.11) | collective-permute-done | bytes 1048608 | tf_op jit(solution)/shard_map/ppermute | solution.py:186
  159.3 20.6 %all_to_all.17.diffs = bf16[8,128,512]{2,1,0:T(8,128)(2,1)S(1)} all-to-all(bf16[8,128,512]{2,1,0:T(8,128)(2,1)S(1)} %get-tuple-element.41), channel_id=1, replica_groups=mesh['ylo'=2,'zh'=4,'zl'=4,'core'=2,'yhi'=2,'x'=4] {'yhi','x'}, dimensions={0} | all-to-all | bytes 2097152 | tf_op jit(solution)/shard_map/all_to_all | solution.py:190
  179.9 2.0 %last_step.1 = bf16[128,512]{1,0:T(8,128)(2,1)} custom-call(bf16[8,128,512]{2,1,0:T(8,128)(2,1)S(1)} %all_to_all.17.diffs, bf16[4,128,256]{2,1,0:T(8,128)(2,1)S(1)} %all_to_all.16.refs_0_, bf16[4,128,256]{2,1,0:T(8,128)(2,1)S(1)} %collective-permute-done.3.refs_1_, bf16[4,128,256]{2,1,0:T(8,128)(2,1)S(1)} %collective-permute-done.4.refs_2_, ...), custom_call_target="tpu_custom_call" | custom-call | flops 536870912 | bytes 3145728 | tf_op jit(solution)/shard_map/last_step/pallas_call | solution.py:124
  (27 shorter events, 4.7 us)
Async XLA Ops:
  6.5 80.6 %all-gather.3.cloned.1.call-start = ((), (), s32[]{:S(2)}) async-start(), calls=%async_computation.3 | async-start | bytes 1179648 | tf_op jit(solution)/shard_map/all_gather | solution.py:163
  6.5 0.9 copy-start
  7.4 0.7 copy-start.3
  8.1 1.5 copy-start.4
  40.9 23.7 %collective-permute-start = (bf16[256,1024]{1,0:T(8,128)(2,1)S(1)}, bf16[256,1024]{1,0:T(8,128)(2,1)S(1)}, u32[]{:S(2)}, u32[]{:S(2)}) collective-permute-start(bf16[256,1024]{1,0:T(8,128)(2,1)S(1)} %all_gather.15.s00), channel_id=1, source_target_pairs={{0,256},{256,0},{1,257},{257,1},{2,258},{258,2},{3,259},{259,3},{4... | collective-permute-start | bytes 1572872 | tf_op jit(solution)/shard_map/ppermute | solution.py:167
  44.1 23.7 %collective-permute-start.1 = (bf16[256,1024]{1,0:T(8,128)(2,1)S(1)}, bf16[256,1024]{1,0:T(8,128)(2,1)S(1)}, u32[]{:S(2)}, u32[]{:S(2)}) collective-permute-start(bf16[256,1024]{1,0:T(8,128)(2,1)S(1)} %all_gather.15.s00), channel_id=1, source_target_pairs={{0,8},{8,0},{1,9},{9,1},{2,10},{10,2},{3,11},{11,3},{4,12},{12,4},... | collective-permute-start | bytes 1572872 | tf_op jit(solution)/shard_map/ppermute | solution.py:168
  64.6 4.7 %collective-permute-start.2 = (bf16[256,1024]{1,0:T(8,128)(2,1)S(1)}, bf16[256,1024]{1,0:T(8,128)(2,1)S(1)}, u32[]{:S(2)}, u32[]{:S(2)}) collective-permute-start(bf16[256,1024]{1,0:T(8,128)(2,1)S(1)} %collective-permute-done.s10), channel_id=1, source_target_pairs={{0,8},{8,0},{1,9},{9,1},{2,10},{10,2},{3,11},{11,3},{4,12},{12,4},... | collective-permute-start | bytes 1572872 | tf_op jit(solution)/shard_map/ppermute | solution.py:171
  108.0 17.6 %collective-permute-start.8 = (bf16[4,128,256]{2,1,0:T(8,128)(2,1)S(1)}, bf16[4,128,256]{2,1,0:T(8,128)(2,1)S(1)}, u32[]{:S(2)}, u32[]{:S(2)}) collective-permute-start(bf16[4,128,256]{2,1,0:T(8,128)(2,1)S(1)} %all_to_all.16.refs_0_), channel_id=1, source_target_pairs={{0,256},{256,0},{1,257},{257,1},{2,258},{258,2},{3,259},{259,3},{4... | collective-permute-start | bytes 786440 | tf_op jit(solution)/shard_map/ppermute | solution.py:180
  109.9 17.8 %collective-permute-start.3 = (bf16[4,128,256]{2,1,0:T(8,128)(2,1)S(1)}, bf16[4,128,256]{2,1,0:T(8,128)(2,1)S(1)}, u32[]{:S(2)}, u32[]{:S(2)}) collective-permute-start(bf16[4,128,256]{2,1,0:T(8,128)(2,1)S(1)} %all_to_all.16.refs_0_), channel_id=1, source_target_pairs={{16,0},{24,8},{32,16},{40,24},{48,32},{56,40},{64,48},{72,56},{80,... | collective-permute-start | bytes 786440 | tf_op jit(solution)/shard_map/ppermute | solution.py:181
  118.9 12.2 %collective-permute-start.5 = (bf16[4,128,256]{2,1,0:T(8,128)(2,1)S(1)}, bf16[4,128,256]{2,1,0:T(8,128)(2,1)S(1)}, u32[]{:S(2)}, u32[]{:S(2)}) collective-permute-start(bf16[4,128,256]{2,1,0:T(8,128)(2,1)S(1)} %all_to_all.16.refs_0_), channel_id=1, source_target_pairs={{32,0},{232,8},{48,16},{248,24},{64,32},{8,40},{80,48},{24,56},{96... | collective-permute-start | bytes 786440 | tf_op jit(solution)/shard_map/ppermute | solution.py:181
  123.6 15.3 %collective-permute-start.4 = (bf16[4,128,256]{2,1,0:T(8,128)(2,1)S(1)}, bf16[4,128,256]{2,1,0:T(8,128)(2,1)S(1)}, u32[]{:S(2)}, u32[]{:S(2)}) collective-permute-start(bf16[4,128,256]{2,1,0:T(8,128)(2,1)S(1)} %all_to_all.16.refs_0_), channel_id=1, source_target_pairs={{240,0},{248,8},{0,16},{8,24},{16,32},{24,40},{32,48},{40,56},{48,... | collective-permute-start | bytes 786440 | tf_op jit(solution)/shard_map/ppermute | solution.py:181
  125.6 15.1 %collective-permute-start.9 = (bf16[4,128,256]{2,1,0:T(8,128)(2,1)S(1)}, bf16[4,128,256]{2,1,0:T(8,128)(2,1)S(1)}, u32[]{:S(2)}, u32[]{:S(2)}) collective-permute-start(bf16[4,128,256]{2,1,0:T(8,128)(2,1)S(1)} %collective-permute-done.8.refs_0_.refs_5_), channel_id=1, source_target_pairs={{32,0},{232,8},{48,16},{248,24},{64,32},{8,40},{80,48},{24,56},{96... | collective-permute-start | bytes 786440 | tf_op jit(solution)/shard_map/ppermute | solution.py:182
  127.7 13.0 %collective-permute-start.7 = (bf16[4,128,256]{2,1,0:T(8,128)(2,1)S(1)}, bf16[4,128,256]{2,1,0:T(8,128)(2,1)S(1)}, u32[]{:S(2)}, u32[]{:S(2)}) collective-permute-start(bf16[4,128,256]{2,1,0:T(8,128)(2,1)S(1)} %collective-permute-done.3.refs_1_), channel_id=1, source_target_pairs={{0,256},{256,0},{1,257},{257,1},{2,258},{258,2},{3,259},{259,3},{4... | collective-permute-start | bytes 786440 | tf_op jit(solution)/shard_map/ppermute | solution.py:182
  140.8 17.1 %copy-start.1 = (bf16[128,512]{1,0:T(8,128)(2,1)S(1)}, bf16[128,512]{1,0:T(8,128)(2,1)}, u32[]{:S(2)}) copy-start(bf16[128,512]{1,0:T(8,128)(2,1)} %refs_11_.3) | copy-start | bytes 393220
  140.8 17.1 %copy-start.2 = (bf16[1024,512]{1,0:T(8,128)(2,1)S(1)}, bf16[1024,512]{1,0:T(8,128)(2,1)}, u32[]{:S(2)}) copy-start(bf16[1024,512]{1,0:T(8,128)(2,1)} %all-gather.3.cloned.1.call-done) | copy-start | bytes 3145732
  140.8 11.7 %collective-permute-start.10 = (bf16[4,4,128,256]{3,2,1,0:T(8,128)(2,1)S(1)}, bf16[4,4,128,256]{3,2,1,0:T(8,128)(2,1)S(1)}, u32[]{:S(2)}, u32[]{:S(2)}) collective-permute-start(bf16[4,4,128,256]{3,2,1,0:T(8,128)(2,1)S(1)} %pack.2), channel_id=1, source_target_pairs={{0,8},{8,0},{1,9},{9,1},{2,10},{10,2},{3,11},{11,3},{4,12},{12,4},... | collective-permute-start | bytes 3145736 | tf_op jit(solution)/shard_map/ppermute | solution.py:184
  142.9 9.6 %collective-permute-start.6 = (bf16[4,128,256]{2,1,0:T(8,128)(2,1)S(1)}, bf16[4,128,256]{2,1,0:T(8,128)(2,1)S(1)}, u32[]{:S(2)}, u32[]{:S(2)}) collective-permute-start(bf16[4,128,256]{2,1,0:T(8,128)(2,1)S(1)} %collective-permute-done.4.refs_2_), channel_id=1, source_target_pairs={{0,256},{256,0},{1,257},{257,1},{2,258},{258,2},{3,259},{259,3},{4... | collective-permute-start | bytes 786440 | tf_op jit(solution)/shard_map/ppermute | solution.py:182
  152.5 5.4 %collective-permute-start.11 = (bf16[4,4,128,256]{3,2,1,0:T(8,128)(2,1)S(1)}, bf16[4,4,128,256]{3,2,1,0:T(8,128)(2,1)S(1)}, u32[]{:S(2)}, u32[]{:S(2)}) collective-permute-start(bf16[4,4,128,256]{3,2,1,0:T(8,128)(2,1)S(1)} %pack.3), channel_id=1, source_target_pairs={{0,8},{8,0},{1,9},{9,1},{2,10},{10,2},{3,11},{11,3},{4,12},{12,4},... | collective-permute-start | bytes 3145736 | tf_op jit(solution)/shard_map/ppermute | solution.py:186
Sparse Core Ops, SparseCore 0:
  10.6 67.1 all-gather.2

commit v5 on v4

--- a/solution.py
+++ b/solution.py
@@ -91,21 +91,20 @@
 
 
 def step_kernel(last, diffs, *refs):
-    near, near_mate, far, far_mate = refs[:4], refs[4], refs[5:9], refs[9]
-    (weight, base, keep), outs, total = refs[10:13], refs[13:-1], refs[-1]
-    ylo, zl, core = (lax.axis_index(a) for a in ("ylo", "zl", "core"))
-    half = near[0].shape[2]
+    grams, (weight, base, keep), outs, total = refs[:4], refs[4:7], refs[7:-1], refs[-1]
+    zl, core = lax.axis_index("zl"), lax.axis_index("core")
+    half = grams[0].shape[3]
     for j, shift in enumerate(CLASSES):
         part = jnp.zeros((weight.shape[0], BLOCK), jnp.float32)
-        for dy, dc, gram in (
-            (0, 0, near[j]), (0, 1, near_mate.at[j]), (1, 0, far[j]), (1, 1, far_mate.at[j])
-        ):
-            lanes = pl.ds(pl.multiple_of((core ^ dc) * half, half), half)
+        for c in range(2):
+            gram = grams[2 * c + 1].at[j - 1] if j else grams[2 * c]
+            lanes = pl.ds(pl.multiple_of((core ^ c) * half, half), half)
             for h in range(4):
-                part += lax.dot_general(
-                    diffs[(ylo ^ dy) * 4 + h, :, lanes], gram[h], NT,
-                    preferred_element_type=jnp.float32,
-                )
+                for y in range(2):
+                    part += lax.dot_general(
+                        diffs[y * 4 + h, :, lanes], gram[h, y], NT,
+                        preferred_element_type=jnp.float32,
+                    )
         place = lax.rem(zl + shift, 4) * BLOCK
         total[:, pl.ds(pl.multiple_of(place, BLOCK), BLOCK)] = part
     old = weight[...].astype(jnp.float32)
@@ -136,24 +135,26 @@
     )(diffs, *grams, weight, base, keep)
 
 
-def pack_kernel(*refs):
-    for i, ref in enumerate(refs[:-1]):
-        refs[-1][i] = ref[...]
-
-
-def pack(parts):
-    part = parts[0]
+def pack_kernel(up, down, two, two_far, out):
+    ylo = lax.axis_index("ylo")
+    out[0] = up[...]
+    out[1] = down[...]
+    out[2, :, ylo] = two[...]
+    out[2, :, 1 - ylo] = two_far[...]
+
+
+def pack(up, *others):
     return pl.pallas_call(
         pack_kernel,
-        out_shape=jax.ShapeDtypeStruct((len(parts),) + part.shape, part.dtype),
-        in_specs=[vmem()] * len(parts),
+        out_shape=jax.ShapeDtypeStruct((3,) + up.shape, up.dtype),
+        in_specs=[vmem()] * 4,
         out_specs=vmem(),
         name="pack",
         compiler_params=pltpu.CompilerParams(vmem_limit_bytes=4 << 20),
         cost_estimate=pl.CostEstimate(
-            flops=0, bytes_accessed=4 * len(parts) * part.size, transcendentals=0
+            flops=0, bytes_accessed=12 * up.size, transcendentals=0
         ),
-    )(*parts)
+    )(up, *others)
 
 
 def on_device(calib, base_weight, keep_blocks):
@@ -175,16 +176,16 @@
     gram = (jnp.sum(terms.astype(jnp.float32), axis=0) / tokens).astype(jnp.bfloat16)
 
     line = ("zh", "zl", "core")
-    mine = lax.all_to_all(jnp.broadcast_to(gram[None], (4,) + gram.shape), "zh", 0, 0, tiled=True)
-    up, down, two = from_z(1, 1), from_z(-1, -1), from_z(2, -2)
-    far = lax.ppermute(mine, "ylo", SWAP)
-    near = [mine] + [lax.ppermute(mine, line, s) for s in (up, down, two)]
-    far = [far] + [lax.ppermute(g, "ylo", SWAP) for g in near[1:3]] + [lax.ppermute(far, line, two)]
-    far[1], far[3], *held = lax.optimization_barrier((far[1], far[3], *near))
-    near_mate = lax.ppermute(pack(held), "core", SWAP)
-    far[2], near_mate = lax.optimization_barrier((far[2], near_mate))
-    far_mate = lax.ppermute(pack(far), "core", SWAP)
-    grams = near + [near_mate] + far + [far_mate]
+    mine = lax.all_gather(lax.all_gather(gram, "ylo", axis=0), "zh", axis=0)
+    half = lax.dynamic_index_in_dim(mine, lax.axis_index("ylo"), 1, keepdims=False)
+    two = lax.ppermute(half, line, from_z(2, -2))
+    up, down = (lax.ppermute(mine, line, from_z(s, s)) for s in (1, -1))
+    mine_mate = lax.ppermute(mine, "core", SWAP)
+    two_far = lax.ppermute(two, "ylo", SWAP)
+    mine_mate, up = lax.optimization_barrier((mine_mate, up))
+    packed = pack(up, down, two, two_far)
+    packed_mate = lax.ppermute(packed, "core", SWAP)
+    grams = (mine, packed, mine_mate, packed_mate)
 
     weight, sent = step(False, diffs, grams, weight, base_weight, keep)
     diffs = lax.all_to_all(sent, ROW, 0, 0, tiled=True)

time: 190 us -> 185 us (0.974)
  waiting for transfers between devices: 20.1 us -> 30.2 us
  blocking collectives: 105 us -> 95.4 us
  starting transfers between devices: 42.8 us -> 37.3 us
    all_to_all x2 -> x0, blocking collectives: 37.8 us -> none  [the longest x1 20.7 us: on_device(): lax.all_to_all(jnp.broadcast_to(gram[None], (4,) + gram.shape), 'zh', 0,...]
    all_gather x0 -> x2, blocking collectives: none -> 27.5 us  [on_device(): mine = lax.all_gather(lax.all_gather(gram, 'ylo', axis=0), 'zh', axis=0)]
    ppermute x9 -> x6, starting transfers between devices: 31.1 us -> 19.3 us  [the longest x1 6.38 us: on_device(): mine_mate = lax.ppermute(mine, 'core', SWAP)]
    all_to_all x0 -> x1, waiting for transfers between devices: none -> 11.7 us  [on_device(): terms = lax.all_to_all(term, ROW, 0, 0, tiled=True)]
    all_to_all x0 -> x1, starting transfers between devices: none -> 6.35 us  [on_device(): terms = lax.all_to_all(term, ROW, 0, 0, tiled=True)]
    ppermute x9 -> x6, waiting for transfers between devices: 18.6 us -> 16.9 us  [the longest x1 7.03 us: on_device(): two_far = lax.ppermute(two, 'ylo', SWAP)]
  transfers between devices with their start and end apart: 13 -> 11, of which waited for: 6 -> 6; matrix products, arithmetic and copies ran while one was open for 0% -> 0% of each run, Pallas kernels for 0% -> 1%
where the time goes in v5:
time: 185 us
  blocking collectives  95.4 us (52%)
  starting transfers between devices  37.3 us (20%)
  waiting for transfers between devices  30.2 us (16%)
  between operations  13.5 us (7%)
  Pallas kernels  6.57 us (4%)
    all_gather x1, blocking collectives, on_device(): own = lax.all_gather(feats, 'zh', axis=0, tiled=True)  31.4 us
    all_gather x2, blocking collectives, on_device(): mine = lax.all_gather(lax.all_gather(gram, 'ylo', axis=0), 'zh', axis=0)  27.5 us
    all_to_all x1, blocking collectives, on_device(): diffs = lax.all_to_all(sent, ROW, 0, 0, tiled=True)  21 us
    all_gather x1, blocking collectives, on_device(): rows = lax.all_gather(feats, 'zl', axis=0, tiled=True)  15.4 us
    all_to_all x1, waiting for transfers between devices, on_device(): terms = lax.all_to_all(term, ROW, 0, 0, tiled=True)  11.7 us
    ppermute x1, waiting for transfers between devices, on_device(): two_far = lax.ppermute(two, 'ylo', SWAP)  7.03 us
    ppermute x1, starting transfers between devices, on_device(): mine_mate = lax.ppermute(mine, 'core', SWAP)  6.38 us
    all_to_all x1, starting transfers between devices, on_device(): terms = lax.all_to_all(term, ROW, 0, 0, tiled=True)  6.35 us
  transfers between devices with their start and end apart: 11, of which 6 were waited for; matrix products, arithmetic and copies ran while one was open for 0% of the time, Pallas kernels for 1%

profile of v5, /device:TPU:1, one launch (start us, length us, event | category | flops | bytes accessed | tf_op | source)
XLA Modules:
  0.0 184.7 jit_solution(2658246412087543110)
XLA Ops:
  8.1 1.5 start.1
  9.7 31.4 %all_gather.25.s00 = bf16[256,1024]{1,0:T(8,128)(2,1)S(1)} all-gather(bf16[64,1024]{1,0:T(8,128)(2,1)} %bitcast.15), channel_id=1, replica_groups=mesh['ylo'=2,'zh'=4,'zl'=4,'core'=2,'yhi'=2,'x'=4] {'zh'}, dimensions={0}, use_global_device_ids=true | all-gather | bytes 655360 | tf_op jit(solution)/shard_map/all_gather | solution.py:167
  41.1 3.2 %collective-permute-start = (bf16[256,1024]{1,0:T(8,128)(2,1)S(1)}, bf16[256,1024]{1,0:T(8,128)(2,1)S(1)}, u32[]{:S(2)}, u32[]{:S(2)}) collective-permute-start(bf16[256,1024]{1,0:T(8,128)(2,1)S(1)} %all_gather.25.s00), channel_id=1, source_target_pairs={{0,256},{256,0},{1,257},{257,1},{2,258},{258,2},{3,259},{259,3},{4... | collective-permute-start | bytes 1572872 | tf_op jit(solution)/shard_map/ppermute | solution.py:168
  44.3 5.3 %collective-permute-start.1 = (bf16[256,1024]{1,0:T(8,128)(2,1)S(1)}, bf16[256,1024]{1,0:T(8,128)(2,1)S(1)}, u32[]{:S(2)}, u32[]{:S(2)}) collective-permute-start(bf16[256,1024]{1,0:T(8,128)(2,1)S(1)} %all_gather.25.s00), channel_id=1, source_target_pairs={{0,8},{8,0},{1,9},{9,1},{2,10},{10,2},{3,11},{11,3},{4,12},{12,4},... | collective-permute-start | bytes 1572872 | tf_op jit(solution)/shard_map/ppermute | solution.py:169
  49.6 15.4 %all_gather.24.rows = bf16[256,1024]{1,0:T(8,128)(2,1)S(1)} all-gather(bf16[64,1024]{1,0:T(8,128)(2,1)} %bitcast.16), channel_id=1, replica_groups=mesh['ylo'=2,'zh'=4,'zl'=4,'core'=2,'yhi'=2,'x'=4] {'zl'}, dimensions={0}, use_global_device_ids=true | all-gather | bytes 655360 | tf_op jit(solution)/shard_map/all_gather | solution.py:170
  65.0 3.2 %collective-permute-start.2 = (bf16[256,1024]{1,0:T(8,128)(2,1)S(1)}, bf16[256,1024]{1,0:T(8,128)(2,1)S(1)}, u32[]{:S(2)}, u32[]{:S(2)}) collective-permute-start(bf16[256,1024]{1,0:T(8,128)(2,1)S(1)} %collective-permute-done.s10), channel_id=1, source_target_pairs={{0,8},{8,0},{1,9},{9,1},{2,10},{10,2},{3,11},{11,3},{4,12},{12,4},... | collective-permute-start | bytes 1572872 | tf_op jit(solution)/shard_map/ppermute | solution.py:172
  68.2 1.5 collective-permute-done.2.s11
  69.7 1.6 partial_gram.1
  71.3 6.3 %all-to-all-start = ((bf16[8,128,256]{2,1,0:T(8,128)(2,1)}), bf16[8,128,256]{2,1,0:T(8,128)(2,1)S(1)}, u32[]{:S(2)}, u32[]{:S(2)}) async-start(bf16[8,128,256]{2,1,0:T(8,128)(2,1)} %partial_gram.1), calls=%async_computation | async-start | bytes 1048576 | tf_op jit(solution)/shard_map/all_to_all | solution.py:174
  77.6 11.7 %all-to-all-done = bf16[8,128,256]{2,1,0:T(8,128)(2,1)S(1)} async-done(((bf16[8,128,256]{2,1,0:T(8,128)(2,1)}), bf16[8,128,256]{2,1,0:T(8,128)(2,1)S(1)}, u32[]{:S(2)}, u32[]{:S(2)}) %all-to-all-start) | async-done | bytes 524320 | tf_op jit(solution)/shard_map/all_to_all | solution.py:174
  89.5 3.8 %all-gather.1 = bf16[256,256]{1,0:T(8,128)(2,1)S(1)} all-gather(bf16[128,256]{1,0:T(8,128)(2,1)S(1)} %multiply_convert_fusion), channel_id=3, replica_groups=mesh['ylo'=2,'zh'=4,'zl'=4,'core'=2,'yhi'=2,'x'=4] {'ylo'}, dimensions={0}, use_global_device_ids=true | all-gather | bytes 196608 | tf_op jit(solution)/shard_map/all_gather | solution.py:179
  93.3 23.8 %all-gather.2 = bf16[8,128,256]{2,1,0:T(8,128)(2,1)S(1)} all-gather(bf16[2,128,256]{2,1,0:T(8,128)(2,1)S(1)} %bitcast.17), channel_id=4, replica_groups=mesh['ylo'=2,'zh'=4,'zl'=4,'core'=2,'yhi'=2,'x'=4] {'zh'}, dimensions={0}, use_global_device_ids=true | all-gather | bytes 655360 | tf_op jit(solution)/shard_map/all_gather | solution.py:179
  117.0 2.9 %collective-permute-start.4 = (bf16[4,2,128,256]{3,2,1,0:T(8,128)(2,1)S(1)}, bf16[4,2,128,256]{3,2,1,0:T(8,128)(2,1)S(1)}, u32[]{:S(2)}, u32[]{:S(2)}) collective-permute-start(bf16[4,2,128,256]{3,2,1,0:T(8,128)(2,1)S(1)} %bitcast.7), channel_id=1, source_target_pairs={{16,0},{24,8},{32,16},{40,24},{48,32},{56,40},{64,48},{72,56},{80,... | collective-permute-start | bytes 1572872 | tf_op jit(solution)/shard_map/ppermute | solution.py:182
  120.0 6.4 %collective-permute-start.3 = (bf16[4,2,128,256]{3,2,1,0:T(8,128)(2,1)S(1)}, bf16[4,2,128,256]{3,2,1,0:T(8,128)(2,1)S(1)}, u32[]{:S(2)}, u32[]{:S(2)}) collective-permute-start(bf16[4,2,128,256]{3,2,1,0:T(8,128)(2,1)S(1)} %bitcast.8), channel_id=1, source_target_pairs={{0,8},{8,0},{1,9},{9,1},{2,10},{10,2},{3,11},{11,3},{4,12},{12,4},... | collective-permute-start | bytes 1572872 | tf_op jit(solution)/shard_map/ppermute | solution.py:183
  126.4 2.1 %collective-permute-start.6 = (bf16[4,128,256]{2,1,0:T(8,128)(2,1)S(1)}, bf16[4,128,256]{2,1,0:T(8,128)(2,1)S(1)}, u32[]{:S(2)}, u32[]{:S(2)}) collective-permute-start(bf16[4,128,256]{2,1,0:T(8,128)(2,1)S(1)} %dynamic-slice_bitcast_fusion), channel_id=1, source_target_pairs={{32,0},{232,8},{48,16},{248,24},{64,32},{8,40},{80,48},{24,56},{96... | collective-permute-start | bytes 786440 | tf_op jit(solution)/shard_map/ppermute | solution.py:181
  128.5 3.2 %collective-permute-start.5 = (bf16[4,2,128,256]{3,2,1,0:T(8,128)(2,1)S(1)}, bf16[4,2,128,256]{3,2,1,0:T(8,128)(2,1)S(1)}, u32[]{:S(2)}, u32[]{:S(2)}) collective-permute-start(bf16[4,2,128,256]{3,2,1,0:T(8,128)(2,1)S(1)} %bitcast.10), channel_id=1, source_target_pairs={{240,0},{248,8},{0,16},{8,24},{16,32},{24,40},{32,48},{40,56},{48,... | collective-permute-start | bytes 1572872 | tf_op jit(solution)/shard_map/ppermute | solution.py:182
  131.8 6.0 %collective-permute-done.6.two = bf16[4,128,256]{2,1,0:T(8,128)(2,1)S(1)} collective-permute-done((bf16[4,128,256]{2,1,0:T(8,128)(2,1)S(1)}, bf16[4,128,256]{2,1,0:T(8,128)(2,1)S(1)}, u32[]{:S(2)}, u32[]{:S(2)}) %collective-permute-start.6) | collective-permute-done | bytes 262176 | tf_op jit(solution)/shard_map/ppermute | solution.py:181
  137.8 1.9 %collective-permute-start.7 = (bf16[4,128,256]{2,1,0:T(8,128)(2,1)S(1)}, bf16[4,128,256]{2,1,0:T(8,128)(2,1)S(1)}, u32[]{:S(2)}, u32[]{:S(2)}) collective-permute-start(bf16[4,128,256]{2,1,0:T(8,128)(2,1)S(1)} %collective-permute-done.6.two), channel_id=1, source_target_pairs={{0,256},{256,0},{1,257},{257,1},{2,258},{258,2},{3,259},{259,3},{4... | collective-permute-start | bytes 786440 | tf_op jit(solution)/shard_map/ppermute | solution.py:184
  139.7 7.0 %collective-permute-done.7.two_far = bf16[4,128,256]{2,1,0:T(8,128)(2,1)S(1)} collective-permute-done((bf16[4,128,256]{2,1,0:T(8,128)(2,1)S(1)}, bf16[4,128,256]{2,1,0:T(8,128)(2,1)S(1)}, u32[]{:S(2)}, u32[]{:S(2)}) %collective-permute-start.7) | collective-permute-done | bytes 262176 | tf_op jit(solution)/shard_map/ppermute | solution.py:184
  147.8 2.7 %collective-permute-start.8 = (bf16[3,4,2,128,256]{4,3,2,1,0:T(8,128)(2,1)S(1)}, bf16[3,4,2,128,256]{4,3,2,1,0:T(8,128)(2,1)S(1)}, u32[]{:S(2)}, u32[]{:S(2)}) collective-permute-start(bf16[3,4,2,128,256]{4,3,2,1,0:T(8,128)(2,1)S(1)} %pack.1.refs_1_), channel_id=1, source_target_pairs={{0,8},{8,0},{1,9},{9,1},{2,10},{10,2},{3,11},{11,3},{4,12},{12,4},... | collective-permute-start | bytes 4718600 | tf_op jit(solution)/shard_map/ppermute | solution.py:187
  150.4 3.0 %collective-permute-done.8.refs_3_ = bf16[3,4,2,128,256]{4,3,2,1,0:T(8,128)(2,1)S(1)} collective-permute-done((bf16[3,4,2,128,256]{4,3,2,1,0:T(8,128)(2,1)S(1)}, bf16[3,4,2,128,256]{4,3,2,1,0:T(8,128)(2,1)S(1)}, u32[]{:S(2)}, u32[]{:S(2)}) %collective-permute-start.8) | collective-permute-done | bytes 1572896 | tf_op jit(solution)/shard_map/ppermute | solution.py:187
  153.4 1.4 first_step.1
  154.8 21.0 %all_to_all.10.diffs = bf16[8,128,512]{2,1,0:T(8,128)(2,1)S(1)} all-to-all(bf16[8,128,512]{2,1,0:T(8,128)(2,1)S(1)} %get-tuple-element.29), channel_id=1, replica_groups=mesh['ylo'=2,'zh'=4,'zl'=4,'core'=2,'yhi'=2,'x'=4] {'yhi','x'}, dimensions={0} | all-to-all | bytes 2097152 | tf_op jit(solution)/shard_map/all_to_all | solution.py:191
  175.9 2.0 %last_step.1 = bf16[128,512]{1,0:T(8,128)(2,1)} custom-call(bf16[8,128,512]{2,1,0:T(8,128)(2,1)S(1)} %all_to_all.10.diffs, bf16[4,2,128,256]{3,2,1,0:T(8,128)(2,1)S(1)} %bitcast.12, bf16[3,4,2,128,256]{4,3,2,1,0:T(8,128)(2,1)S(1)} %pack.1.refs_1_, bf16[4,2,128,256]{3,2,1,0:T(8,128)(2,1)S(1)} %collective-permute-done.3.refs_2_, ...), custom_call_target="tpu_custom_call" | custom-call | flops 536870912 | bytes 3145728 | tf_op jit(solution)/shard_map/last_step/pallas_call | solution.py:123
  (20 shorter events, 2.8 us)
Async XLA Ops:
  6.5 82.8 %all-gather.5.cloned.1.call-start = ((), (), s32[]{:S(2)}) async-start(), calls=%async_computation.2 | async-start | bytes 1179648 | tf_op jit(solution)/shard_map/all_gather | solution.py:164
  6.5 0.9 copy-start
  7.4 0.7 copy-start.3
  41.1 23.9 %collective-permute-start = (bf16[256,1024]{1,0:T(8,128)(2,1)S(1)}, bf16[256,1024]{1,0:T(8,128)(2,1)S(1)}, u32[]{:S(2)}, u32[]{:S(2)}) collective-permute-start(bf16[256,1024]{1,0:T(8,128)(2,1)S(1)} %all_gather.25.s00), channel_id=1, source_target_pairs={{0,256},{256,0},{1,257},{257,1},{2,258},{258,2},{3,259},{259,3},{4... | collective-permute-start | bytes 1572872 | tf_op jit(solution)/shard_map/ppermute | solution.py:168
  44.3 23.9 %collective-permute-start.1 = (bf16[256,1024]{1,0:T(8,128)(2,1)S(1)}, bf16[256,1024]{1,0:T(8,128)(2,1)S(1)}, u32[]{:S(2)}, u32[]{:S(2)}) collective-permute-start(bf16[256,1024]{1,0:T(8,128)(2,1)S(1)} %all_gather.25.s00), channel_id=1, source_target_pairs={{0,8},{8,0},{1,9},{9,1},{2,10},{10,2},{3,11},{11,3},{4,12},{12,4},... | collective-permute-start | bytes 1572872 | tf_op jit(solution)/shard_map/ppermute | solution.py:169
  65.0 4.7 %collective-permute-start.2 = (bf16[256,1024]{1,0:T(8,128)(2,1)S(1)}, bf16[256,1024]{1,0:T(8,128)(2,1)S(1)}, u32[]{:S(2)}, u32[]{:S(2)}) collective-permute-start(bf16[256,1024]{1,0:T(8,128)(2,1)S(1)} %collective-permute-done.s10), channel_id=1, source_target_pairs={{0,8},{8,0},{1,9},{9,1},{2,10},{10,2},{3,11},{11,3},{4,12},{12,4},... | collective-permute-start | bytes 1572872 | tf_op jit(solution)/shard_map/ppermute | solution.py:172
  71.3 18.1 %all-to-all-start = ((bf16[8,128,256]{2,1,0:T(8,128)(2,1)}), bf16[8,128,256]{2,1,0:T(8,128)(2,1)S(1)}, u32[]{:S(2)}, u32[]{:S(2)}) async-start(bf16[8,128,256]{2,1,0:T(8,128)(2,1)} %partial_gram.1), calls=%async_computation | async-start | bytes 1048576 | tf_op jit(solution)/shard_map/all_to_all | solution.py:174
  117.0 22.7 %collective-permute-start.4 = (bf16[4,2,128,256]{3,2,1,0:T(8,128)(2,1)S(1)}, bf16[4,2,128,256]{3,2,1,0:T(8,128)(2,1)S(1)}, u32[]{:S(2)}, u32[]{:S(2)}) collective-permute-start(bf16[4,2,128,256]{3,2,1,0:T(8,128)(2,1)S(1)} %bitcast.7), channel_id=1, source_target_pairs={{16,0},{24,8},{32,16},{40,24},{48,32},{56,40},{64,48},{72,56},{80,... | collective-permute-start | bytes 1572872 | tf_op jit(solution)/shard_map/ppermute | solution.py:182
  120.0 19.8 %collective-permute-start.3 = (bf16[4,2,128,256]{3,2,1,0:T(8,128)(2,1)S(1)}, bf16[4,2,128,256]{3,2,1,0:T(8,128)(2,1)S(1)}, u32[]{:S(2)}, u32[]{:S(2)}) collective-permute-start(bf16[4,2,128,256]{3,2,1,0:T(8,128)(2,1)S(1)} %bitcast.8), channel_id=1, source_target_pairs={{0,8},{8,0},{1,9},{9,1},{2,10},{10,2},{3,11},{11,3},{4,12},{12,4},... | collective-permute-start | bytes 1572872 | tf_op jit(solution)/shard_map/ppermute | solution.py:183
  126.4 27.1 %copy-start.1 = (bf16[128,512]{1,0:T(8,128)(2,1)S(1)}, bf16[128,512]{1,0:T(8,128)(2,1)}, u32[]{:S(2)}) copy-start(bf16[128,512]{1,0:T(8,128)(2,1)} %refs_5_.3) | copy-start | bytes 393220
  126.4 27.0 %copy-start.2 = (bf16[1024,512]{1,0:T(8,128)(2,1)S(1)}, bf16[1024,512]{1,0:T(8,128)(2,1)}, u32[]{:S(2)}) copy-start(bf16[1024,512]{1,0:T(8,128)(2,1)} %all-gather.5.cloned.1.call-done) | copy-start | bytes 3145732
  126.4 11.4 %collective-permute-start.6 = (bf16[4,128,256]{2,1,0:T(8,128)(2,1)S(1)}, bf16[4,128,256]{2,1,0:T(8,128)(2,1)S(1)}, u32[]{:S(2)}, u32[]{:S(2)}) collective-permute-start(bf16[4,128,256]{2,1,0:T(8,128)(2,1)S(1)} %dynamic-slice_bitcast_fusion), channel_id=1, source_target_pairs={{32,0},{232,8},{48,16},{248,24},{64,32},{8,40},{80,48},{24,56},{96... | collective-permute-start | bytes 786440 | tf_op jit(solution)/shard_map/ppermute | solution.py:181
  128.5 19.1 %collective-permute-start.5 = (bf16[4,2,128,256]{3,2,1,0:T(8,128)(2,1)S(1)}, bf16[4,2,128,256]{3,2,1,0:T(8,128)(2,1)S(1)}, u32[]{:S(2)}, u32[]{:S(2)}) collective-permute-start(bf16[4,2,128,256]{3,2,1,0:T(8,128)(2,1)S(1)} %bitcast.10), channel_id=1, source_target_pairs={{240,0},{248,8},{0,16},{8,24},{16,32},{24,40},{32,48},{40,56},{48,... | collective-permute-start | bytes 1572872 | tf_op jit(solution)/shard_map/ppermute | solution.py:182
  137.8 9.0 %collective-permute-start.7 = (bf16[4,128,256]{2,1,0:T(8,128)(2,1)S(1)}, bf16[4,128,256]{2,1,0:T(8,128)(2,1)S(1)}, u32[]{:S(2)}, u32[]{:S(2)}) collective-permute-start(bf16[4,128,256]{2,1,0:T(8,128)(2,1)S(1)} %collective-permute-done.6.two), channel_id=1, source_target_pairs={{0,256},{256,0},{1,257},{257,1},{2,258},{258,2},{3,259},{259,3},{4... | collective-permute-start | bytes 786440 | tf_op jit(solution)/shard_map/ppermute | solution.py:184
  147.8 5.7 %collective-permute-start.8 = (bf16[3,4,2,128,256]{4,3,2,1,0:T(8,128)(2,1)S(1)}, bf16[3,4,2,128,256]{4,3,2,1,0:T(8,128)(2,1)S(1)}, u32[]{:S(2)}, u32[]{:S(2)}) collective-permute-start(bf16[3,4,2,128,256]{4,3,2,1,0:T(8,128)(2,1)S(1)} %pack.1.refs_1_), channel_id=1, source_target_pairs={{0,8},{8,0},{1,9},{9,1},{2,10},{10,2},{3,11},{11,3},{4,12},{12,4},... | collective-permute-start | bytes 4718600 | tf_op jit(solution)/shard_map/ppermute | solution.py:187
Sparse Core Ops, SparseCore 0:
  10.6 67.1 all-gather.4

commit v6 on v5

--- a/solution.py
+++ b/solution.py
@@ -65,9 +65,12 @@
     )(keep_blocks.T, base)
 
 
-def partial_gram_kernel(rows, s00, s10, s01, s11, out):
-    ylo, core = lax.axis_index("ylo"), lax.axis_index("core")
+def partial_gram_kernel(r0, r1, r2, r3, s00, s10, s01, s11, out, rows):
+    ylo, zl, core = (lax.axis_index(a) for a in ("ylo", "zl", "core"))
     chunk = BLOCK // 2
+    for d, part in enumerate((r0, r1, r2, r3)):
+        place = lax.rem(zl + d, 4) * chunk
+        rows[pl.ds(pl.multiple_of(place, chunk), chunk), :] = part[...]
     for dy, dc, cols in ((0, 0, s00), (1, 0, s10), (0, 1, s01), (1, 1, s11)):
         term = lax.dot_general(cols[...], rows[...], NT, preferred_element_type=jnp.float32)
         term = term.astype(jnp.bfloat16).reshape(4, chunk, rows.shape[0])
@@ -76,18 +79,19 @@
 
 
 def partial_gram(rows, *cols):
-    k = rows.shape[0]
+    k, depth = cols[0].shape
     return pl.pallas_call(
         partial_gram_kernel,
         out_shape=jax.ShapeDtypeStruct((8, BLOCK, k), jnp.bfloat16),
-        in_specs=[vmem()] * 5,
+        in_specs=[vmem()] * 8,
         out_specs=vmem(),
+        scratch_shapes=[pltpu.VMEM((k, depth), jnp.bfloat16)],
         name="partial_gram",
         compiler_params=pltpu.CompilerParams(vmem_limit_bytes=8 << 20),
         cost_estimate=pl.CostEstimate(
-            flops=8 * k * k * rows.shape[1], bytes_accessed=12 * rows.size, transcendentals=0
+            flops=8 * k * k * depth, bytes_accessed=12 * k * depth, transcendentals=0
         ),
-    )(rows, *cols)
+    )(*rows, *cols)
 
 
 def step_kernel(last, diffs, *refs):
@@ -167,8 +171,9 @@
     own = lax.all_gather(feats, "zh", axis=0, tiled=True)
     other = lax.ppermute(own, "ylo", SWAP)
     own_mate = lax.ppermute(own, "core", SWAP)
-    rows = lax.all_gather(feats, "zl", axis=0, tiled=True)
-    rows, other = lax.optimization_barrier((rows, other))
+    near = lax.optimization_barrier((feats, own))[0]
+    rows = [feats] + [lax.ppermute(near, "zl", [((i + d) % 4, i) for i in range(4)]) for d in (1, 2, 3)]
+    other, *rows[1:] = lax.optimization_barrier((other, *rows[1:]))
     other_mate = lax.ppermute(other, "core", SWAP)
     term = partial_gram(rows, own, other, own_mate, other_mate)
     terms = lax.all_to_all(term, ROW, 0, 0, tiled=True)
@@ -182,7 +187,7 @@
     up, down = (lax.ppermute(mine, line, from_z(s, s)) for s in (1, -1))
     mine_mate = lax.ppermute(mine, "core", SWAP)
     two_far = lax.ppermute(two, "ylo", SWAP)
-    mine_mate, up = lax.optimization_barrier((mine_mate, up))
+    mine_mate, two_far = lax.optimization_barrier((mine_mate, two_far))
     packed = pack(up, down, two, two_far)
     packed_mate = lax.ppermute(packed, "core", SWAP)
     grams = (mine, packed, mine_mate, packed_mate)

time: 185 us -> 180 us (0.973)
  blocking collectives: 95.4 us -> 75.6 us
  starting transfers between devices: 37.3 us -> 53.8 us
  waiting for transfers between devices: 30.2 us -> 26.7 us
    all_gather x1 -> x0, blocking collectives: 15.4 us -> none  [on_device(): rows = lax.all_gather(feats, 'zl', axis=0, tiled=True)]
    ppermute x0 -> x3, starting transfers between devices: none -> 9.29 us  [on_device(): lax.ppermute(near, 'zl', [((i + d) % 4, i) for i in range(4)])]
    ppermute x1, waiting for transfers between devices: 5.98 us -> 0.01 us  [on_device(): two = lax.ppermute(half, line, from_z(2, -2))]
    ppermute x2, waiting for transfers between devices: 0.9 us -> 4.95 us  [on_device(): up, down = (lax.ppermute(mine, line, from_z(s, s)) for s in (1, -1))]
    ppermute x1, starting transfers between devices: 6.38 us -> 9.69 us  [on_device(): mine_mate = lax.ppermute(mine, 'core', SWAP)]
    all_gather x2, blocking collectives: 27.5 us -> 24.9 us  [on_device(): mine = lax.all_gather(lax.all_gather(gram, 'ylo', axis=0), 'zh', axis=0)]
    ppermute x1, starting transfers between devices: 5.29 us -> 7.17 us  [on_device(): own_mate = lax.ppermute(own, 'core', SWAP)]
  transfers between devices with their start and end apart: 11 -> 14, of which waited for: 6 -> 6; matrix products, arithmetic and copies ran while one was open for 0% -> 0% of each run, Pallas kernels for 1% -> 1%
where the time goes in v6:
time: 180 us; the launch traced here: 179 us
  blocking collectives  75.6 us (42%)
  starting transfers between devices  53.8 us (30%)
  waiting for transfers between devices  26.7 us (15%)
  between operations  13.6 us (8%)
  Pallas kernels  6.59 us (4%)
  local copies, waits for them, and re-layouts  2.53 us (1%)
    all_gather x1, blocking collectives, on_device(): own = lax.all_gather(feats, 'zh', axis=0, tiled=True)  31.4 us
    all_gather x2, blocking collectives, on_device(): mine = lax.all_gather(lax.all_gather(gram, 'ylo', axis=0), 'zh', axis=0)  24.9 us
    all_to_all x1, blocking collectives, on_device(): diffs = lax.all_to_all(sent, ROW, 0, 0, tiled=True)  19.3 us
    all_to_all x1, waiting for transfers between devices, on_device(): terms = lax.all_to_all(term, ROW, 0, 0, tiled=True)  11.7 us
    ppermute x1, starting transfers between devices, on_device(): mine_mate = lax.ppermute(mine, 'core', SWAP)  9.69 us
    ppermute x3, starting transfers between devices, on_device(): lax.ppermute(near, 'zl', [((i + d) % 4, i) for i in range(4)])  9.29 us
    ppermute x1, starting transfers between devices, on_device(): own_mate = lax.ppermute(own, 'core', SWAP)  7.17 us
    ppermute x2, starting transfers between devices, on_device(): up, down = (lax.ppermute(mine, line, from_z(s, s)) for s in (1, -1))  6.49 us
  transfers between devices with their start and end apart: 14, of which 6 were waited for; matrix products, arithmetic and copies ran while one was open for 0% of the time, Pallas kernels for 1%

profile of v6, /device:TPU:1, one launch (start us, length us, event | category | flops | bytes accessed | tf_op | source)
XLA Modules:
  0.0 178.8 jit_solution(18116797433933017315)
XLA Ops:
  9.7 31.4 %all_gather.21.s00 = bf16[256,1024]{1,0:T(8,128)(2,1)S(1)} all-gather(bf16[64,1024]{1,0:T(8,128)(2,1)} %bitcast.14), channel_id=1, replica_groups=mesh['ylo'=2,'zh'=4,'zl'=4,'core'=2,'yhi'=2,'x'=4] {'zh'}, dimensions={0}, use_global_device_ids=true | all-gather | bytes 655360 | tf_op jit(solution)/shard_map/all_gather | solution.py:171
  41.1 3.2 %collective-permute-start = (bf16[256,1024]{1,0:T(8,128)(2,1)S(1)}, bf16[256,1024]{1,0:T(8,128)(2,1)S(1)}, u32[]{:S(2)}, u32[]{:S(2)}) collective-permute-start(bf16[256,1024]{1,0:T(8,128)(2,1)S(1)} %all_gather.21.s00), channel_id=1, source_target_pairs={{0,256},{256,0},{1,257},{257,1},{2,258},{258,2},{3,259},{259,3},{4... | collective-permute-start | bytes 1572872 | tf_op jit(solution)/shard_map/ppermute | solution.py:172
  44.3 2.5 %collective-permute-start.3 = (bf16[64,1024]{1,0:T(8,128)(2,1)}, bf16[64,1024]{1,0:T(8,128)(2,1)S(1)}, u32[]{:S(2)}, u32[]{:S(2)}) collective-permute-start(bf16[64,1024]{1,0:T(8,128)(2,1)} %bitcast.15), channel_id=1, source_target_pairs={{48,0},{0,16},{16,32},{32,48},{49,1},{1,17},{17,33},{33,49},{50,2}... | collective-permute-start | bytes 393224 | tf_op jit(solution)/shard_map/ppermute | solution.py:175
  46.8 2.6 %collective-permute-start.2 = (bf16[64,1024]{1,0:T(8,128)(2,1)}, bf16[64,1024]{1,0:T(8,128)(2,1)S(1)}, u32[]{:S(2)}, u32[]{:S(2)}) collective-permute-start(bf16[64,1024]{1,0:T(8,128)(2,1)} %bitcast.16), channel_id=1, source_target_pairs={{32,0},{48,16},{0,32},{16,48},{33,1},{49,17},{1,33},{17,49},{34,2}... | collective-permute-start | bytes 393224 | tf_op jit(solution)/shard_map/ppermute | solution.py:175
  49.4 4.2 %collective-permute-start.1 = (bf16[64,1024]{1,0:T(8,128)(2,1)}, bf16[64,1024]{1,0:T(8,128)(2,1)S(1)}, u32[]{:S(2)}, u32[]{:S(2)}) collective-permute-start(bf16[64,1024]{1,0:T(8,128)(2,1)} %bitcast.17), channel_id=1, source_target_pairs={{16,0},{32,16},{48,32},{0,48},{17,1},{33,17},{49,33},{1,49},{18,2}... | collective-permute-start | bytes 393224 | tf_op jit(solution)/shard_map/ppermute | solution.py:175
  53.6 7.2 %collective-permute-start.4 = (bf16[256,1024]{1,0:T(8,128)(2,1)S(1)}, bf16[256,1024]{1,0:T(8,128)(2,1)S(1)}, u32[]{:S(2)}, u32[]{:S(2)}) collective-permute-start(bf16[256,1024]{1,0:T(8,128)(2,1)S(1)} %all_gather.21.s00), channel_id=1, source_target_pairs={{0,8},{8,0},{1,9},{9,1},{2,10},{10,2},{3,11},{11,3},{4,12},{12,4},... | collective-permute-start | bytes 1572872 | tf_op jit(solution)/shard_map/ppermute | solution.py:173
  60.8 3.8 %collective-permute-start.5 = (bf16[256,1024]{1,0:T(8,128)(2,1)S(1)}, bf16[256,1024]{1,0:T(8,128)(2,1)S(1)}, u32[]{:S(2)}, u32[]{:S(2)}) collective-permute-start(bf16[256,1024]{1,0:T(8,128)(2,1)S(1)} %collective-permute-done.s10), channel_id=1, source_target_pairs={{0,8},{8,0},{1,9},{9,1},{2,10},{10,2},{3,11},{11,3},{4,12},{12,4},... | collective-permute-start | bytes 1572872 | tf_op jit(solution)/shard_map/ppermute | solution.py:177
  67.1 1.6 partial_gram.1
  68.7 6.4 %all-to-all-start = ((bf16[8,128,256]{2,1,0:T(8,128)(2,1)}), bf16[8,128,256]{2,1,0:T(8,128)(2,1)S(1)}, u32[]{:S(2)}, u32[]{:S(2)}) async-start(bf16[8,128,256]{2,1,0:T(8,128)(2,1)} %partial_gram.1), calls=%async_computation | async-start | bytes 1048576 | tf_op jit(solution)/shard_map/all_to_all | solution.py:179
  75.0 11.7 %all-to-all-done = bf16[8,128,256]{2,1,0:T(8,128)(2,1)S(1)} async-done(((bf16[8,128,256]{2,1,0:T(8,128)(2,1)}), bf16[8,128,256]{2,1,0:T(8,128)(2,1)S(1)}, u32[]{:S(2)}, u32[]{:S(2)}) %all-to-all-start) | async-done | bytes 524320 | tf_op jit(solution)/shard_map/all_to_all | solution.py:179
  86.9 3.8 %all-gather.1 = bf16[256,256]{1,0:T(8,128)(2,1)S(1)} all-gather(bf16[128,256]{1,0:T(8,128)(2,1)S(1)} %multiply_convert_fusion), channel_id=3, replica_groups=mesh['ylo'=2,'zh'=4,'zl'=4,'core'=2,'yhi'=2,'x'=4] {'ylo'}, dimensions={0}, use_global_device_ids=true | all-gather | bytes 196608 | tf_op jit(solution)/shard_map/all_gather | solution.py:184
  90.7 21.1 %all-gather.2 = bf16[8,128,256]{2,1,0:T(8,128)(2,1)S(1)} all-gather(bf16[2,128,256]{2,1,0:T(8,128)(2,1)S(1)} %bitcast.20), channel_id=4, replica_groups=mesh['ylo'=2,'zh'=4,'zl'=4,'core'=2,'yhi'=2,'x'=4] {'zh'}, dimensions={0}, use_global_device_ids=true | all-gather | bytes 655360 | tf_op jit(solution)/shard_map/all_gather | solution.py:184
  111.8 2.1 %collective-permute-start.8 = (bf16[4,128,256]{2,1,0:T(8,128)(2,1)S(1)}, bf16[4,128,256]{2,1,0:T(8,128)(2,1)S(1)}, u32[]{:S(2)}, u32[]{:S(2)}) collective-permute-start(bf16[4,128,256]{2,1,0:T(8,128)(2,1)S(1)} %dynamic-slice_bitcast_fusion), channel_id=1, source_target_pairs={{32,0},{232,8},{48,16},{248,24},{64,32},{8,40},{80,48},{24,56},{96... | collective-permute-start | bytes 786440 | tf_op jit(solution)/shard_map/ppermute | solution.py:186
  113.9 9.7 %collective-permute-start.9 = (bf16[4,2,128,256]{3,2,1,0:T(8,128)(2,1)S(1)}, bf16[4,2,128,256]{3,2,1,0:T(8,128)(2,1)S(1)}, u32[]{:S(2)}, u32[]{:S(2)}) collective-permute-start(bf16[4,2,128,256]{3,2,1,0:T(8,128)(2,1)S(1)} %bitcast.8), channel_id=1, source_target_pairs={{0,8},{8,0},{1,9},{9,1},{2,10},{10,2},{3,11},{11,3},{4,12},{12,4},... | collective-permute-start | bytes 1572872 | tf_op jit(solution)/shard_map/ppermute | solution.py:188
  123.6 4.5 %collective-permute-start.7 = (bf16[4,2,128,256]{3,2,1,0:T(8,128)(2,1)S(1)}, bf16[4,2,128,256]{3,2,1,0:T(8,128)(2,1)S(1)}, u32[]{:S(2)}, u32[]{:S(2)}) collective-permute-start(bf16[4,2,128,256]{3,2,1,0:T(8,128)(2,1)S(1)} %bitcast.9), channel_id=1, source_target_pairs={{240,0},{248,8},{0,16},{8,24},{16,32},{24,40},{32,48},{40,56},{48,... | collective-permute-start | bytes 1572872 | tf_op jit(solution)/shard_map/ppermute | solution.py:187
  128.1 2.0 %collective-permute-start.6 = (bf16[4,2,128,256]{3,2,1,0:T(8,128)(2,1)S(1)}, bf16[4,2,128,256]{3,2,1,0:T(8,128)(2,1)S(1)}, u32[]{:S(2)}, u32[]{:S(2)}) collective-permute-start(bf16[4,2,128,256]{3,2,1,0:T(8,128)(2,1)S(1)} %bitcast.10), channel_id=1, source_target_pairs={{16,0},{24,8},{32,16},{40,24},{48,32},{56,40},{64,48},{72,56},{80,... | collective-permute-start | bytes 1572872 | tf_op jit(solution)/shard_map/ppermute | solution.py:187
  130.1 2.7 %collective-permute-start.10 = (bf16[4,128,256]{2,1,0:T(8,128)(2,1)S(1)}, bf16[4,128,256]{2,1,0:T(8,128)(2,1)S(1)}, u32[]{:S(2)}, u32[]{:S(2)}) collective-permute-start(bf16[4,128,256]{2,1,0:T(8,128)(2,1)S(1)} %collective-permute-done.8.two), channel_id=1, source_target_pairs={{0,256},{256,0},{1,257},{257,1},{2,258},{258,2},{3,259},{259,3},{4... | collective-permute-start | bytes 786440 | tf_op jit(solution)/shard_map/ppermute | solution.py:189
  132.8 5.4 %collective-permute-done.10.two_far = bf16[4,128,256]{2,1,0:T(8,128)(2,1)S(1)} collective-permute-done((bf16[4,128,256]{2,1,0:T(8,128)(2,1)S(1)}, bf16[4,128,256]{2,1,0:T(8,128)(2,1)S(1)}, u32[]{:S(2)}, u32[]{:S(2)}) %collective-permute-start.10) | collective-permute-done | bytes 262176 | tf_op jit(solution)/shard_map/ppermute | solution.py:189
  138.2 2.0 %collective-permute-done.7.down = bf16[4,2,128,256]{3,2,1,0:T(8,128)(2,1)S(1)} collective-permute-done((bf16[4,2,128,256]{3,2,1,0:T(8,128)(2,1)S(1)}, bf16[4,2,128,256]{3,2,1,0:T(8,128)(2,1)S(1)}, u32[]{:S(2)}, u32[]{:S(2)}) %collective-permute-start.7) | collective-permute-done | bytes 524320 | tf_op jit(solution)/shard_map/ppermute | solution.py:187
  140.2 3.0 %collective-permute-done.6.up = bf16[4,2,128,256]{3,2,1,0:T(8,128)(2,1)S(1)} collective-permute-done((bf16[4,2,128,256]{3,2,1,0:T(8,128)(2,1)S(1)}, bf16[4,2,128,256]{3,2,1,0:T(8,128)(2,1)S(1)}, u32[]{:S(2)}, u32[]{:S(2)}) %collective-permute-start.6) | collective-permute-done | bytes 524320 | tf_op jit(solution)/shard_map/ppermute | solution.py:187
  143.3 3.0 %collective-permute-start.11 = (bf16[3,4,2,128,256]{4,3,2,1,0:T(8,128)(2,1)S(1)}, bf16[3,4,2,128,256]{4,3,2,1,0:T(8,128)(2,1)S(1)}, u32[]{:S(2)}, u32[]{:S(2)}) collective-permute-start(bf16[3,4,2,128,256]{4,3,2,1,0:T(8,128)(2,1)S(1)} %pack.1.refs_1_), channel_id=1, source_target_pairs={{0,8},{8,0},{1,9},{9,1},{2,10},{10,2},{3,11},{11,3},{4,12},{12,4},... | collective-permute-start | bytes 4718600 | tf_op jit(solution)/shard_map/ppermute | solution.py:192
  146.3 3.0 %collective-permute-done.11.refs_3_ = bf16[3,4,2,128,256]{4,3,2,1,0:T(8,128)(2,1)S(1)} collective-permute-done((bf16[3,4,2,128,256]{4,3,2,1,0:T(8,128)(2,1)S(1)}, bf16[3,4,2,128,256]{4,3,2,1,0:T(8,128)(2,1)S(1)}, u32[]{:S(2)}, u32[]{:S(2)}) %collective-permute-start.11) | collective-permute-done | bytes 1572896 | tf_op jit(solution)/shard_map/ppermute | solution.py:192
  150.7 19.3 %all_to_all.10.diffs = bf16[8,128,512]{2,1,0:T(8,128)(2,1)S(1)} all-to-all(bf16[8,128,512]{2,1,0:T(8,128)(2,1)S(1)} %get-tuple-element.35), channel_id=1, replica_groups=mesh['ylo'=2,'zh'=4,'zl'=4,'core'=2,'yhi'=2,'x'=4] {'yhi','x'}, dimensions={0} | all-to-all | bytes 2097152 | tf_op jit(solution)/shard_map/all_to_all | solution.py:196
  170.0 2.0 %last_step.1 = bf16[128,512]{1,0:T(8,128)(2,1)} custom-call(bf16[8,128,512]{2,1,0:T(8,128)(2,1)S(1)} %all_to_all.10.diffs, bf16[4,2,128,256]{3,2,1,0:T(8,128)(2,1)S(1)} %bitcast.12, bf16[3,4,2,128,256]{4,3,2,1,0:T(8,128)(2,1)S(1)} %pack.1.refs_1_, bf16[4,2,128,256]{3,2,1,0:T(8,128)(2,1)S(1)} %collective-permute-done.9.refs_2_, ...), custom_call_target="tpu_custom_call" | custom-call | flops 536870912 | bytes 3145728 | tf_op jit(solution)/shard_map/last_step/pallas_call | solution.py:127
  (27 shorter events, 7.2 us)
Async XLA Ops:
  6.5 80.2 %all-gather.5.cloned.1.call-start = ((), (), s32[]{:S(2)}) async-start(), calls=%async_computation.2 | async-start | bytes 1179648 | tf_op jit(solution)/shard_map/all_gather | solution.py:168
  6.5 0.9 copy-start
  7.4 0.7 copy-start.4
  41.1 19.7 %collective-permute-start = (bf16[256,1024]{1,0:T(8,128)(2,1)S(1)}, bf16[256,1024]{1,0:T(8,128)(2,1)S(1)}, u32[]{:S(2)}, u32[]{:S(2)}) collective-permute-start(bf16[256,1024]{1,0:T(8,128)(2,1)S(1)} %all_gather.21.s00), channel_id=1, source_target_pairs={{0,256},{256,0},{1,257},{257,1},{2,258},{258,2},{3,259},{259,3},{4... | collective-permute-start | bytes 1572872 | tf_op jit(solution)/shard_map/ppermute | solution.py:172
  44.3 16.5 %collective-permute-start.3 = (bf16[64,1024]{1,0:T(8,128)(2,1)}, bf16[64,1024]{1,0:T(8,128)(2,1)S(1)}, u32[]{:S(2)}, u32[]{:S(2)}) collective-permute-start(bf16[64,1024]{1,0:T(8,128)(2,1)} %bitcast.15), channel_id=1, source_target_pairs={{48,0},{0,16},{16,32},{32,48},{49,1},{1,17},{17,33},{33,49},{50,2}... | collective-permute-start | bytes 393224 | tf_op jit(solution)/shard_map/ppermute | solution.py:175
  46.8 14.0 %collective-permute-start.2 = (bf16[64,1024]{1,0:T(8,128)(2,1)}, bf16[64,1024]{1,0:T(8,128)(2,1)S(1)}, u32[]{:S(2)}, u32[]{:S(2)}) collective-permute-start(bf16[64,1024]{1,0:T(8,128)(2,1)} %bitcast.16), channel_id=1, source_target_pairs={{32,0},{48,16},{0,32},{16,48},{33,1},{49,17},{1,33},{17,49},{34,2}... | collective-permute-start | bytes 393224 | tf_op jit(solution)/shard_map/ppermute | solution.py:175
  49.4 11.4 %collective-permute-start.1 = (bf16[64,1024]{1,0:T(8,128)(2,1)}, bf16[64,1024]{1,0:T(8,128)(2,1)S(1)}, u32[]{:S(2)}, u32[]{:S(2)}) collective-permute-start(bf16[64,1024]{1,0:T(8,128)(2,1)} %bitcast.17), channel_id=1, source_target_pairs={{16,0},{32,16},{48,32},{0,48},{17,1},{33,17},{49,33},{1,49},{18,2}... | collective-permute-start | bytes 393224 | tf_op jit(solution)/shard_map/ppermute | solution.py:175
  53.6 11.1 %collective-permute-start.4 = (bf16[256,1024]{1,0:T(8,128)(2,1)S(1)}, bf16[256,1024]{1,0:T(8,128)(2,1)S(1)}, u32[]{:S(2)}, u32[]{:S(2)}) collective-permute-start(bf16[256,1024]{1,0:T(8,128)(2,1)S(1)} %all_gather.21.s00), channel_id=1, source_target_pairs={{0,8},{8,0},{1,9},{9,1},{2,10},{10,2},{3,11},{11,3},{4,12},{12,4},... | collective-permute-start | bytes 1572872 | tf_op jit(solution)/shard_map/ppermute | solution.py:173
  60.8 5.4 %collective-permute-start.5 = (bf16[256,1024]{1,0:T(8,128)(2,1)S(1)}, bf16[256,1024]{1,0:T(8,128)(2,1)S(1)}, u32[]{:S(2)}, u32[]{:S(2)}) collective-permute-start(bf16[256,1024]{1,0:T(8,128)(2,1)S(1)} %collective-permute-done.s10), channel_id=1, source_target_pairs={{0,8},{8,0},{1,9},{9,1},{2,10},{10,2},{3,11},{11,3},{4,12},{12,4},... | collective-permute-start | bytes 1572872 | tf_op jit(solution)/shard_map/ppermute | solution.py:177
  66.2 0.9 copy-start.3
  68.7 18.1 %all-to-all-start = ((bf16[8,128,256]{2,1,0:T(8,128)(2,1)}), bf16[8,128,256]{2,1,0:T(8,128)(2,1)S(1)}, u32[]{:S(2)}, u32[]{:S(2)}) async-start(bf16[8,128,256]{2,1,0:T(8,128)(2,1)} %partial_gram.1), calls=%async_computation | async-start | bytes 1048576 | tf_op jit(solution)/shard_map/all_to_all | solution.py:179
  111.8 37.6 %copy-start.1 = (bf16[128,512]{1,0:T(8,128)(2,1)S(1)}, bf16[128,512]{1,0:T(8,128)(2,1)}, u32[]{:S(2)}) copy-start(bf16[128,512]{1,0:T(8,128)(2,1)} %refs_5_.3) | copy-start | bytes 393220
  111.8 37.5 %copy-start.2 = (bf16[1024,512]{1,0:T(8,128)(2,1)S(1)}, bf16[1024,512]{1,0:T(8,128)(2,1)}, u32[]{:S(2)}) copy-start(bf16[1024,512]{1,0:T(8,128)(2,1)} %all-gather.5.cloned.1.call-done) | copy-start | bytes 3145732
  111.8 18.3 %collective-permute-start.8 = (bf16[4,128,256]{2,1,0:T(8,128)(2,1)S(1)}, bf16[4,128,256]{2,1,0:T(8,128)(2,1)S(1)}, u32[]{:S(2)}, u32[]{:S(2)}) collective-permute-start(bf16[4,128,256]{2,1,0:T(8,128)(2,1)S(1)} %dynamic-slice_bitcast_fusion), channel_id=1, source_target_pairs={{32,0},{232,8},{48,16},{248,24},{64,32},{8,40},{80,48},{24,56},{96... | collective-permute-start | bytes 786440 | tf_op jit(solution)/shard_map/ppermute | solution.py:186
  113.9 24.4 %collective-permute-start.9 = (bf16[4,2,128,256]{3,2,1,0:T(8,128)(2,1)S(1)}, bf16[4,2,128,256]{3,2,1,0:T(8,128)(2,1)S(1)}, u32[]{:S(2)}, u32[]{:S(2)}) collective-permute-start(bf16[4,2,128,256]{3,2,1,0:T(8,128)(2,1)S(1)} %bitcast.8), channel_id=1, source_target_pairs={{0,8},{8,0},{1,9},{9,1},{2,10},{10,2},{3,11},{11,3},{4,12},{12,4},... | collective-permute-start | bytes 1572872 | tf_op jit(solution)/shard_map/ppermute | solution.py:188
  123.6 16.6 %collective-permute-start.7 = (bf16[4,2,128,256]{3,2,1,0:T(8,128)(2,1)S(1)}, bf16[4,2,128,256]{3,2,1,0:T(8,128)(2,1)S(1)}, u32[]{:S(2)}, u32[]{:S(2)}) collective-permute-start(bf16[4,2,128,256]{3,2,1,0:T(8,128)(2,1)S(1)} %bitcast.9), channel_id=1, source_target_pairs={{240,0},{248,8},{0,16},{8,24},{16,32},{24,40},{32,48},{40,56},{48,... | collective-permute-start | bytes 1572872 | tf_op jit(solution)/shard_map/ppermute | solution.py:187
  128.1 15.1 %collective-permute-start.6 = (bf16[4,2,128,256]{3,2,1,0:T(8,128)(2,1)S(1)}, bf16[4,2,128,256]{3,2,1,0:T(8,128)(2,1)S(1)}, u32[]{:S(2)}, u32[]{:S(2)}) collective-permute-start(bf16[4,2,128,256]{3,2,1,0:T(8,128)(2,1)S(1)} %bitcast.10), channel_id=1, source_target_pairs={{16,0},{24,8},{32,16},{40,24},{48,32},{56,40},{64,48},{72,56},{80,... | collective-permute-start | bytes 1572872 | tf_op jit(solution)/shard_map/ppermute | solution.py:187
  130.1 8.1 %collective-permute-start.10 = (bf16[4,128,256]{2,1,0:T(8,128)(2,1)S(1)}, bf16[4,128,256]{2,1,0:T(8,128)(2,1)S(1)}, u32[]{:S(2)}, u32[]{:S(2)}) collective-permute-start(bf16[4,128,256]{2,1,0:T(8,128)(2,1)S(1)} %collective-permute-done.8.two), channel_id=1, source_target_pairs={{0,256},{256,0},{1,257},{257,1},{2,258},{258,2},{3,259},{259,3},{4... | collective-permute-start | bytes 786440 | tf_op jit(solution)/shard_map/ppermute | solution.py:189
  143.3 6.0 %collective-permute-start.11 = (bf16[3,4,2,128,256]{4,3,2,1,0:T(8,128)(2,1)S(1)}, bf16[3,4,2,128,256]{4,3,2,1,0:T(8,128)(2,1)S(1)}, u32[]{:S(2)}, u32[]{:S(2)}) collective-permute-start(bf16[3,4,2,128,256]{4,3,2,1,0:T(8,128)(2,1)S(1)} %pack.1.refs_1_), channel_id=1, source_target_pairs={{0,8},{8,0},{1,9},{9,1},{2,10},{10,2},{3,11},{11,3},{4,12},{12,4},... | collective-permute-start | bytes 4718600 | tf_op jit(solution)/shard_map/ppermute | solution.py:192
Sparse Core Ops, SparseCore 0:
  10.6 67.1 all-gather.4

commit v7 on v6

--- a/solution.py
+++ b/solution.py
@@ -65,25 +65,25 @@
     )(keep_blocks.T, base)
 
 
-def partial_gram_kernel(r0, r1, r2, r3, s00, s10, s01, s11, out, rows):
+def partial_gram_kernel(r0, r1, r2, r3, cols, mates, out, rows):
     ylo, zl, core = (lax.axis_index(a) for a in ("ylo", "zl", "core"))
     chunk = BLOCK // 2
     for d, part in enumerate((r0, r1, r2, r3)):
         place = lax.rem(zl + d, 4) * chunk
         rows[pl.ds(pl.multiple_of(place, chunk), chunk), :] = part[...]
-    for dy, dc, cols in ((0, 0, s00), (1, 0, s10), (0, 1, s01), (1, 1, s11)):
-        term = lax.dot_general(cols[...], rows[...], NT, preferred_element_type=jnp.float32)
+    for dy, dc, part in ((0, 0, cols), (1, 0, cols), (0, 1, mates), (1, 1, mates)):
+        term = lax.dot_general(part[dy], rows[...], NT, preferred_element_type=jnp.float32)
         term = term.astype(jnp.bfloat16).reshape(4, chunk, rows.shape[0])
         half = pl.ds(pl.multiple_of((core ^ dc) * chunk, chunk), chunk)
         out[pl.ds((ylo ^ dy) * 4, 4), half, :] = term
 
 
 def partial_gram(rows, *cols):
-    k, depth = cols[0].shape
+    k, depth = cols[0].shape[1:]
     return pl.pallas_call(
         partial_gram_kernel,
         out_shape=jax.ShapeDtypeStruct((8, BLOCK, k), jnp.bfloat16),
-        in_specs=[vmem()] * 8,
+        in_specs=[vmem()] * 6,
         out_specs=vmem(),
         scratch_shapes=[pltpu.VMEM((k, depth), jnp.bfloat16)],
         name="partial_gram",
@@ -95,18 +95,17 @@
 
 
 def step_kernel(last, diffs, *refs):
-    grams, (weight, base, keep), outs, total = refs[:4], refs[4:7], refs[7:-1], refs[-1]
+    grams, (weight, base, keep), outs, total = refs[:2], refs[2:5], refs[5:-1], refs[-1]
     zl, core = lax.axis_index("zl"), lax.axis_index("core")
-    half = grams[0].shape[3]
+    half = grams[0].shape[4]
     for j, shift in enumerate(CLASSES):
         part = jnp.zeros((weight.shape[0], BLOCK), jnp.float32)
         for c in range(2):
-            gram = grams[2 * c + 1].at[j - 1] if j else grams[2 * c]
             lanes = pl.ds(pl.multiple_of((core ^ c) * half, half), half)
             for h in range(4):
                 for y in range(2):
                     part += lax.dot_general(
-                        diffs[y * 4 + h, :, lanes], gram[h, y], NT,
+                        diffs[y * 4 + h, :, lanes], grams[c][j, h, y], NT,
                         preferred_element_type=jnp.float32,
                     )
         place = lax.rem(zl + shift, 4) * BLOCK
@@ -139,45 +138,53 @@
     )(diffs, *grams, weight, base, keep)
 
 
-def pack_kernel(up, down, two, two_far, out):
+def pair_kernel(own, other, out):
+    out[0] = own[...]
+    out[1] = other[...]
+
+
+def classes_kernel(mine, up, down, two, two_far, out):
     ylo = lax.axis_index("ylo")
-    out[0] = up[...]
-    out[1] = down[...]
-    out[2, :, ylo] = two[...]
-    out[2, :, 1 - ylo] = two_far[...]
-
-
-def pack(up, *others):
-    return pl.pallas_call(
-        pack_kernel,
-        out_shape=jax.ShapeDtypeStruct((3,) + up.shape, up.dtype),
-        in_specs=[vmem()] * 4,
+    out[0] = mine[...]
+    out[1] = up[...]
+    out[2] = down[...]
+    out[3, :, ylo] = two[...]
+    out[3, :, 1 - ylo] = two_far[...]
+
+
+def pack(kernel, name, *parts):
+    shape = ((2 if name == "pair" else 4),) + parts[0].shape
+    return pl.pallas_call(
+        kernel,
+        out_shape=jax.ShapeDtypeStruct(shape, parts[0].dtype),
+        in_specs=[vmem()] * len(parts),
         out_specs=vmem(),
-        name="pack",
+        name=name,
         compiler_params=pltpu.CompilerParams(vmem_limit_bytes=4 << 20),
         cost_estimate=pl.CostEstimate(
-            flops=0, bytes_accessed=12 * up.size, transcendentals=0
+            flops=0, bytes_accessed=4 * shape[0] * parts[0].size, transcendentals=0
         ),
-    )(up, *others)
+    )(*parts)
 
 
 def on_device(calib, base_weight, keep_blocks):
     tokens = calib.shape[0] * 8
-    weight, diff, keep = start(keep_blocks, base_weight)
-    diff, calib = lax.optimization_barrier((diff, calib))
-    diffs = lax.all_gather(diff, ROW, axis=0)
-
     feats = calib.T
     own = lax.all_gather(feats, "zh", axis=0, tiled=True)
     other = lax.ppermute(own, "ylo", SWAP)
-    own_mate = lax.ppermute(own, "core", SWAP)
     near = lax.optimization_barrier((feats, own))[0]
     rows = [feats] + [lax.ppermute(near, "zl", [((i + d) % 4, i) for i in range(4)]) for d in (1, 2, 3)]
     other, *rows[1:] = lax.optimization_barrier((other, *rows[1:]))
-    other_mate = lax.ppermute(other, "core", SWAP)
-    term = partial_gram(rows, own, other, own_mate, other_mate)
+    cols = pack(pair_kernel, "pair", own, other)
+    mates = lax.ppermute(cols, "core", SWAP)
+
+    base_weight = lax.optimization_barrier((base_weight, cols))[0]
+    weight, diff, keep = start(keep_blocks, base_weight)
+    diff, mates = lax.optimization_barrier((diff, mates))
+    diffs = lax.all_gather(diff, ROW, axis=0)
+
+    term = partial_gram(rows, cols, mates)
     terms = lax.all_to_all(term, ROW, 0, 0, tiled=True)
-    diffs, terms = lax.optimization_barrier((diffs, terms))
     gram = (jnp.sum(terms.astype(jnp.float32), axis=0) / tokens).astype(jnp.bfloat16)
 
     line = ("zh", "zl", "core")
@@ -185,12 +192,10 @@
     half = lax.dynamic_index_in_dim(mine, lax.axis_index("ylo"), 1, keepdims=False)
     two = lax.ppermute(half, line, from_z(2, -2))
     up, down = (lax.ppermute(mine, line, from_z(s, s)) for s in (1, -1))
-    mine_mate = lax.ppermute(mine, "core", SWAP)
     two_far = lax.ppermute(two, "ylo", SWAP)
-    mine_mate, two_far = lax.optimization_barrier((mine_mate, two_far))
-    packed = pack(up, down, two, two_far)
-    packed_mate = lax.ppermute(packed, "core", SWAP)
-    grams = (mine, packed, mine_mate, packed_mate)
+    diffs, two_far = lax.optimization_barrier((diffs, two_far))
+    packed = pack(classes_kernel, "classes", mine, up, down, two, two_far)
+    grams = (packed, lax.ppermute(packed, "core", SWAP))
 
     weight, sent = step(False, diffs, grams, weight, base_weight, keep)
     diffs = lax.all_to_all(sent, ROW, 0, 0, tiled=True)

time: 180 us -> 176 us (0.978)
  starting transfers between devices: 53.8 us -> 43.4 us
  waiting for transfers between devices: 26.7 us -> 32.3 us
  blocking collectives: 75.6 us -> 79.1 us
  local copies, waits for them, and re-layouts: 2.53 us -> 0.03 us
    ppermute x4 -> x2, starting transfers between devices: 23.7 us -> 11.2 us  [the longest x1 6.05 us: on_device(): mates = lax.ppermute(cols, 'core', SWAP)]
    ppermute x3, waiting for transfers between devices: 0.01 us -> 5 us  [on_device(): lax.ppermute(near, 'zl', [((i + d) % 4, i) for i in range(4)])]
    ppermute x2, starting transfers between devices: 6.49 us -> 9.5 us  [on_device(): up, down = (lax.ppermute(mine, line, from_z(s, s)) for s in (1, -1))]
    all_gather x2, blocking collectives: 24.9 us -> 27.8 us  [on_device(): mine = lax.all_gather(lax.all_gather(gram, 'ylo', axis=0), 'zh', axis=0)]
    unnamed x10 -> x8, local copies, waits for them, and re-layouts: 2.51 us -> 0.01 us
    ppermute x4 -> x2, waiting for transfers between devices: 4.52 us -> 4.5 us  [the longest x1 3.76 us: on_device(): grams = (packed, lax.ppermute(packed, 'core', SWAP))]
  transfers between devices with their start and end apart: 14 -> 12, of which waited for: 6 -> 8; matrix products, arithmetic and copies ran while one was open for 0% -> 0% of each run, Pallas kernels for 1% -> 2%
where the time goes in v7:
time: 176 us; the launch traced here: 175 us
  blocking collectives  79.1 us (45%)
  starting transfers between devices  43.4 us (25%)
  waiting for transfers between devices  32.3 us (18%)
  between operations  13.5 us (8%)
  Pallas kernels  6.72 us (4%)
    all_gather x1, blocking collectives, on_device(): own = lax.all_gather(feats, 'zh', axis=0, tiled=True)  31.5 us
    all_gather x2, blocking collectives, on_device(): mine = lax.all_gather(lax.all_gather(gram, 'ylo', axis=0), 'zh', axis=0)  27.8 us
    all_to_all x1, blocking collectives, on_device(): diffs = lax.all_to_all(sent, ROW, 0, 0, tiled=True)  19.8 us
    all_to_all x1, waiting for transfers between devices, on_device(): terms = lax.all_to_all(term, ROW, 0, 0, tiled=True)  11.7 us
    ppermute x2, starting transfers between devices, on_device(): up, down = (lax.ppermute(mine, line, from_z(s, s)) for s in (1, -1))  9.5 us
    ppermute x3, starting transfers between devices, on_device(): lax.ppermute(near, 'zl', [((i + d) % 4, i) for i in range(4)])  9.29 us
    all_to_all x1, starting transfers between devices, on_device(): terms = lax.all_to_all(term, ROW, 0, 0, tiled=True)  6.36 us
    ppermute x1, starting transfers between devices, on_device(): mates = lax.ppermute(cols, 'core', SWAP)  6.05 us
  transfers between devices with their start and end apart: 12, of which 8 were waited for; matrix products, arithmetic and copies ran while one was open for 0% of the time, Pallas kernels for 2%

profile of v7, /device:TPU:1, one launch (start us, length us, event | category | flops | bytes accessed | tf_op | source)
XLA Modules:
  0.0 175.2 jit_solution(7880838675270893212)
XLA Ops:
  6.5 31.5 %all_gather.19.own = bf16[256,1024]{1,0:T(8,128)(2,1)S(1)} all-gather(bf16[64,1024]{1,0:T(8,128)(2,1)} %bitcast.12), channel_id=1, replica_groups=mesh['ylo'=2,'zh'=4,'zl'=4,'core'=2,'yhi'=2,'x'=4] {'zh'}, dimensions={0}, use_global_device_ids=true | all-gather | bytes 655360 | tf_op jit(solution)/shard_map/all_gather | solution.py:173
  38.1 3.2 %collective-permute-start = (bf16[256,1024]{1,0:T(8,128)(2,1)S(1)}, bf16[256,1024]{1,0:T(8,128)(2,1)S(1)}, u32[]{:S(2)}, u32[]{:S(2)}) collective-permute-start(bf16[256,1024]{1,0:T(8,128)(2,1)S(1)} %all_gather.19.own), channel_id=1, source_target_pairs={{0,256},{256,0},{1,257},{257,1},{2,258},{258,2},{3,259},{259,3},{4... | collective-permute-start | bytes 1572872 | tf_op jit(solution)/shard_map/ppermute | solution.py:174
  41.3 2.5 %collective-permute-start.3 = (bf16[64,1024]{1,0:T(8,128)(2,1)}, bf16[64,1024]{1,0:T(8,128)(2,1)S(1)}, u32[]{:S(2)}, u32[]{:S(2)}) collective-permute-start(bf16[64,1024]{1,0:T(8,128)(2,1)} %bitcast.13), channel_id=1, source_target_pairs={{48,0},{0,16},{16,32},{32,48},{49,1},{1,17},{17,33},{33,49},{50,2}... | collective-permute-start | bytes 393224 | tf_op jit(solution)/shard_map/ppermute | solution.py:176
  43.8 2.6 %collective-permute-start.2 = (bf16[64,1024]{1,0:T(8,128)(2,1)}, bf16[64,1024]{1,0:T(8,128)(2,1)S(1)}, u32[]{:S(2)}, u32[]{:S(2)}) collective-permute-start(bf16[64,1024]{1,0:T(8,128)(2,1)} %bitcast.14), channel_id=1, source_target_pairs={{32,0},{48,16},{0,32},{16,48},{33,1},{49,17},{1,33},{17,49},{34,2}... | collective-permute-start | bytes 393224 | tf_op jit(solution)/shard_map/ppermute | solution.py:176
  46.4 4.2 %collective-permute-start.1 = (bf16[64,1024]{1,0:T(8,128)(2,1)}, bf16[64,1024]{1,0:T(8,128)(2,1)S(1)}, u32[]{:S(2)}, u32[]{:S(2)}) collective-permute-start(bf16[64,1024]{1,0:T(8,128)(2,1)} %bitcast.15), channel_id=1, source_target_pairs={{16,0},{32,16},{48,32},{0,48},{17,1},{33,17},{49,33},{1,49},{18,2}... | collective-permute-start | bytes 393224 | tf_op jit(solution)/shard_map/ppermute | solution.py:176
  50.6 3.1 %collective-permute-done.2.r2 = bf16[64,1024]{1,0:T(8,128)(2,1)S(1)} collective-permute-done((bf16[64,1024]{1,0:T(8,128)(2,1)}, bf16[64,1024]{1,0:T(8,128)(2,1)S(1)}, u32[]{:S(2)}, u32[]{:S(2)}) %collective-permute-start.2) | collective-permute-done | bytes 131104 | tf_op jit(solution)/shard_map/ppermute | solution.py:176
  53.7 1.9 %collective-permute-done.1.r1 = bf16[64,1024]{1,0:T(8,128)(2,1)S(1)} collective-permute-done((bf16[64,1024]{1,0:T(8,128)(2,1)}, bf16[64,1024]{1,0:T(8,128)(2,1)S(1)}, u32[]{:S(2)}, u32[]{:S(2)}) %collective-permute-start.1) | collective-permute-done | bytes 131104 | tf_op jit(solution)/shard_map/ppermute | solution.py:176
  55.7 6.0 %collective-permute-start.4 = (bf16[2,256,1024]{2,1,0:T(8,128)(2,1)S(1)}, bf16[2,256,1024]{2,1,0:T(8,128)(2,1)S(1)}, u32[]{:S(2)}, u32[]{:S(2)}) collective-permute-start(bf16[2,256,1024]{2,1,0:T(8,128)(2,1)S(1)} %pair.1.cols), channel_id=1, source_target_pairs={{0,8},{8,0},{1,9},{9,1},{2,10},{10,2},{3,11},{11,3},{4,12},{12,4},... | collective-permute-start | bytes 3145736 | tf_op jit(solution)/shard_map/ppermute | solution.py:179
  64.0 1.6 partial_gram.1
  65.7 6.4 %all-to-all-start = ((bf16[8,128,256]{2,1,0:T(8,128)(2,1)}), bf16[8,128,256]{2,1,0:T(8,128)(2,1)S(1)}, u32[]{:S(2)}, u32[]{:S(2)}) async-start(bf16[8,128,256]{2,1,0:T(8,128)(2,1)} %partial_gram.1), calls=%async_computation | async-start | bytes 1048576 | tf_op jit(solution)/shard_map/all_to_all | solution.py:187
  72.0 11.7 %all-to-all-done = bf16[8,128,256]{2,1,0:T(8,128)(2,1)S(1)} async-done(((bf16[8,128,256]{2,1,0:T(8,128)(2,1)}), bf16[8,128,256]{2,1,0:T(8,128)(2,1)S(1)}, u32[]{:S(2)}, u32[]{:S(2)}) %all-to-all-start) | async-done | bytes 524320 | tf_op jit(solution)/shard_map/all_to_all | solution.py:187
  83.9 4.2 %all-gather.1 = bf16[256,256]{1,0:T(8,128)(2,1)S(1)} all-gather(bf16[128,256]{1,0:T(8,128)(2,1)S(1)} %multiply_convert_fusion), channel_id=3, replica_groups=mesh['ylo'=2,'zh'=4,'zl'=4,'core'=2,'yhi'=2,'x'=4] {'ylo'}, dimensions={0}, use_global_device_ids=true | all-gather | bytes 196608 | tf_op jit(solution)/shard_map/all_gather | solution.py:191
  88.1 23.6 %all-gather.2 = bf16[8,128,256]{2,1,0:T(8,128)(2,1)S(1)} all-gather(bf16[2,128,256]{2,1,0:T(8,128)(2,1)S(1)} %bitcast.18), channel_id=4, replica_groups=mesh['ylo'=2,'zh'=4,'zl'=4,'core'=2,'yhi'=2,'x'=4] {'zh'}, dimensions={0}, use_global_device_ids=true | all-gather | bytes 655360 | tf_op jit(solution)/shard_map/all_gather | solution.py:191
  111.7 1.9 %collective-permute-start.5 = (bf16[4,128,256]{2,1,0:T(8,128)(2,1)S(1)}, bf16[4,128,256]{2,1,0:T(8,128)(2,1)S(1)}, u32[]{:S(2)}, u32[]{:S(2)}) collective-permute-start(bf16[4,128,256]{2,1,0:T(8,128)(2,1)S(1)} %dynamic-slice_bitcast_fusion), channel_id=1, source_target_pairs={{32,0},{232,8},{48,16},{248,24},{64,32},{8,40},{80,48},{24,56},{96... | collective-permute-start | bytes 786440 | tf_op jit(solution)/shard_map/ppermute | solution.py:193
  113.6 7.5 %collective-permute-start.8 = (bf16[4,2,128,256]{3,2,1,0:T(8,128)(2,1)S(1)}, bf16[4,2,128,256]{3,2,1,0:T(8,128)(2,1)S(1)}, u32[]{:S(2)}, u32[]{:S(2)}) collective-permute-start(bf16[4,2,128,256]{3,2,1,0:T(8,128)(2,1)S(1)} %bitcast.8), channel_id=1, source_target_pairs={{240,0},{248,8},{0,16},{8,24},{16,32},{24,40},{32,48},{40,56},{48,... | collective-permute-start | bytes 1572872 | tf_op jit(solution)/shard_map/ppermute | solution.py:194
  121.1 2.0 %collective-permute-start.7 = (bf16[4,2,128,256]{3,2,1,0:T(8,128)(2,1)S(1)}, bf16[4,2,128,256]{3,2,1,0:T(8,128)(2,1)S(1)}, u32[]{:S(2)}, u32[]{:S(2)}) collective-permute-start(bf16[4,2,128,256]{3,2,1,0:T(8,128)(2,1)S(1)} %bitcast.9), channel_id=1, source_target_pairs={{16,0},{24,8},{32,16},{40,24},{48,32},{56,40},{64,48},{72,56},{80,... | collective-permute-start | bytes 1572872 | tf_op jit(solution)/shard_map/ppermute | solution.py:194
  123.1 1.9 %collective-permute-start.6 = (bf16[4,128,256]{2,1,0:T(8,128)(2,1)S(1)}, bf16[4,128,256]{2,1,0:T(8,128)(2,1)S(1)}, u32[]{:S(2)}, u32[]{:S(2)}) collective-permute-start(bf16[4,128,256]{2,1,0:T(8,128)(2,1)S(1)} %collective-permute-done.5.two), channel_id=1, source_target_pairs={{0,256},{256,0},{1,257},{257,1},{2,258},{258,2},{3,259},{259,3},{4... | collective-permute-start | bytes 786440 | tf_op jit(solution)/shard_map/ppermute | solution.py:195
  125.1 5.5 %collective-permute-done.6.two_far = bf16[4,128,256]{2,1,0:T(8,128)(2,1)S(1)} collective-permute-done((bf16[4,128,256]{2,1,0:T(8,128)(2,1)S(1)}, bf16[4,128,256]{2,1,0:T(8,128)(2,1)S(1)}, u32[]{:S(2)}, u32[]{:S(2)}) %collective-permute-start.6) | collective-permute-done | bytes 262176 | tf_op jit(solution)/shard_map/ppermute | solution.py:195
  130.5 3.8 %collective-permute-done.8.down = bf16[4,2,128,256]{3,2,1,0:T(8,128)(2,1)S(1)} collective-permute-done((bf16[4,2,128,256]{3,2,1,0:T(8,128)(2,1)S(1)}, bf16[4,2,128,256]{3,2,1,0:T(8,128)(2,1)S(1)}, u32[]{:S(2)}, u32[]{:S(2)}) %collective-permute-start.8) | collective-permute-done | bytes 524320 | tf_op jit(solution)/shard_map/ppermute | solution.py:194
  134.4 1.8 %collective-permute-done.7.up = bf16[4,2,128,256]{3,2,1,0:T(8,128)(2,1)S(1)} collective-permute-done((bf16[4,2,128,256]{3,2,1,0:T(8,128)(2,1)S(1)}, bf16[4,2,128,256]{3,2,1,0:T(8,128)(2,1)S(1)}, u32[]{:S(2)}, u32[]{:S(2)}) %collective-permute-start.7) | collective-permute-done | bytes 524320 | tf_op jit(solution)/shard_map/ppermute | solution.py:194
  136.3 5.2 %collective-permute-start.9 = (bf16[4,4,2,128,256]{4,3,2,1,0:T(8,128)(2,1)S(1)}, bf16[4,4,2,128,256]{4,3,2,1,0:T(8,128)(2,1)S(1)}, u32[]{:S(2)}, u32[]{:S(2)}) collective-permute-start(bf16[4,4,2,128,256]{4,3,2,1,0:T(8,128)(2,1)S(1)} %classes.1.refs_0_), channel_id=1, source_target_pairs={{0,8},{8,0},{1,9},{9,1},{2,10},{10,2},{3,11},{11,3},{4,12},{12,4},... | collective-permute-start | bytes 6291464 | tf_op jit(solution)/shard_map/ppermute | solution.py:198
  141.4 3.8 %collective-permute-done.9.refs_1_ = bf16[4,4,2,128,256]{4,3,2,1,0:T(8,128)(2,1)S(1)} collective-permute-done((bf16[4,4,2,128,256]{4,3,2,1,0:T(8,128)(2,1)S(1)}, bf16[4,4,2,128,256]{4,3,2,1,0:T(8,128)(2,1)S(1)}, u32[]{:S(2)}, u32[]{:S(2)}) %collective-permute-start.9) | collective-permute-done | bytes 2097184 | tf_op jit(solution)/shard_map/ppermute | solution.py:198
  146.6 19.8 %all_to_all.10.diffs = bf16[8,128,512]{2,1,0:T(8,128)(2,1)S(1)} all-to-all(bf16[8,128,512]{2,1,0:T(8,128)(2,1)S(1)} %get-tuple-element.33), channel_id=1, replica_groups=mesh['ylo'=2,'zh'=4,'zl'=4,'core'=2,'yhi'=2,'x'=4] {'yhi','x'}, dimensions={0} | all-to-all | bytes 2097152 | tf_op jit(solution)/shard_map/all_to_all | solution.py:201
  166.4 2.0 %last_step.1 = bf16[128,512]{1,0:T(8,128)(2,1)} custom-call(bf16[8,128,512]{2,1,0:T(8,128)(2,1)S(1)} %all_to_all.10.diffs, bf16[4,4,2,128,256]{4,3,2,1,0:T(8,128)(2,1)S(1)} %classes.1.refs_0_, bf16[4,4,2,128,256]{4,3,2,1,0:T(8,128)(2,1)S(1)} %collective-permute-done.9.refs_1_, bf16[128,512]{1,0:T(8,128)(2,1)S(1)} %get-tuple-element.34.refs_2_, ...), custom_call_target="tpu_custom_call" | custom-call | flops 536870912 | bytes 3145728 | tf_op jit(solution)/shard_map/last_step/pallas_call | solution.py:126
  (22 shorter events, 4.0 us)
Async XLA Ops:
  6.5 57.5 %copy-start.2 = (bf16[1024,64]{0,1:T(8,128)(2,1)S(1)}, bf16[1024,64]{0,1:T(8,128)(2,1)}, u32[]{:S(2)}) copy-start(bf16[1024,64]{0,1:T(8,128)(2,1)} %param.3) | copy-start | bytes 393220
  6.5 55.2 %copy-start = (bf16[128,512]{1,0:T(8,128)(2,1)S(1)}, bf16[128,512]{1,0:T(8,128)(2,1)}, u32[]{:S(2)}) copy-start(bf16[128,512]{1,0:T(8,128)(2,1)} %refs_3_.1) | copy-start | bytes 393220
  6.5 55.2 %copy-start.3 = (s32[64,16]{0,1:T(8,128)S(1)}, s32[64,16]{0,1:T(8,128)}, u32[]{:S(2)}) copy-start(s32[64,16]{0,1:T(8,128)} %param.5) | copy-start | bytes 12292
  6.5 124.0 %all-gather.5.cloned.1.call-start = ((), (), s32[]{:S(2)}) async-start(), calls=%async_computation.2 | async-start | bytes 1179648 | tf_op jit(solution)/shard_map/all_gather | solution.py:184
  38.1 17.5 %collective-permute-start = (bf16[256,1024]{1,0:T(8,128)(2,1)S(1)}, bf16[256,1024]{1,0:T(8,128)(2,1)S(1)}, u32[]{:S(2)}, u32[]{:S(2)}) collective-permute-start(bf16[256,1024]{1,0:T(8,128)(2,1)S(1)} %all_gather.19.own), channel_id=1, source_target_pairs={{0,256},{256,0},{1,257},{257,1},{2,258},{258,2},{3,259},{259,3},{4... | collective-permute-start | bytes 1572872 | tf_op jit(solution)/shard_map/ppermute | solution.py:174
  41.3 9.3 %collective-permute-start.3 = (bf16[64,1024]{1,0:T(8,128)(2,1)}, bf16[64,1024]{1,0:T(8,128)(2,1)S(1)}, u32[]{:S(2)}, u32[]{:S(2)}) collective-permute-start(bf16[64,1024]{1,0:T(8,128)(2,1)} %bitcast.13), channel_id=1, source_target_pairs={{48,0},{0,16},{16,32},{32,48},{49,1},{1,17},{17,33},{33,49},{50,2}... | collective-permute-start | bytes 393224 | tf_op jit(solution)/shard_map/ppermute | solution.py:176
  43.8 9.9 %collective-permute-start.2 = (bf16[64,1024]{1,0:T(8,128)(2,1)}, bf16[64,1024]{1,0:T(8,128)(2,1)S(1)}, u32[]{:S(2)}, u32[]{:S(2)}) collective-permute-start(bf16[64,1024]{1,0:T(8,128)(2,1)} %bitcast.14), channel_id=1, source_target_pairs={{32,0},{48,16},{0,32},{16,48},{33,1},{49,17},{1,33},{17,49},{34,2}... | collective-permute-start | bytes 393224 | tf_op jit(solution)/shard_map/ppermute | solution.py:176
  46.4 9.2 %collective-permute-start.1 = (bf16[64,1024]{1,0:T(8,128)(2,1)}, bf16[64,1024]{1,0:T(8,128)(2,1)S(1)}, u32[]{:S(2)}, u32[]{:S(2)}) collective-permute-start(bf16[64,1024]{1,0:T(8,128)(2,1)} %bitcast.15), channel_id=1, source_target_pairs={{16,0},{32,16},{48,32},{0,48},{17,1},{33,17},{49,33},{1,49},{18,2}... | collective-permute-start | bytes 393224 | tf_op jit(solution)/shard_map/ppermute | solution.py:176
  55.7 8.3 %collective-permute-start.4 = (bf16[2,256,1024]{2,1,0:T(8,128)(2,1)S(1)}, bf16[2,256,1024]{2,1,0:T(8,128)(2,1)S(1)}, u32[]{:S(2)}, u32[]{:S(2)}) collective-permute-start(bf16[2,256,1024]{2,1,0:T(8,128)(2,1)S(1)} %pair.1.cols), channel_id=1, source_target_pairs={{0,8},{8,0},{1,9},{9,1},{2,10},{10,2},{3,11},{11,3},{4,12},{12,4},... | collective-permute-start | bytes 3145736 | tf_op jit(solution)/shard_map/ppermute | solution.py:179
  65.7 18.1 %all-to-all-start = ((bf16[8,128,256]{2,1,0:T(8,128)(2,1)}), bf16[8,128,256]{2,1,0:T(8,128)(2,1)S(1)}, u32[]{:S(2)}, u32[]{:S(2)}) async-start(bf16[8,128,256]{2,1,0:T(8,128)(2,1)} %partial_gram.1), calls=%async_computation | async-start | bytes 1048576 | tf_op jit(solution)/shard_map/all_to_all | solution.py:187
  111.7 11.4 %collective-permute-start.5 = (bf16[4,128,256]{2,1,0:T(8,128)(2,1)S(1)}, bf16[4,128,256]{2,1,0:T(8,128)(2,1)S(1)}, u32[]{:S(2)}, u32[]{:S(2)}) collective-permute-start(bf16[4,128,256]{2,1,0:T(8,128)(2,1)S(1)} %dynamic-slice_bitcast_fusion), channel_id=1, source_target_pairs={{32,0},{232,8},{48,16},{248,24},{64,32},{8,40},{80,48},{24,56},{96... | collective-permute-start | bytes 786440 | tf_op jit(solution)/shard_map/ppermute | solution.py:193
  113.6 20.8 %collective-permute-start.8 = (bf16[4,2,128,256]{3,2,1,0:T(8,128)(2,1)S(1)}, bf16[4,2,128,256]{3,2,1,0:T(8,128)(2,1)S(1)}, u32[]{:S(2)}, u32[]{:S(2)}) collective-permute-start(bf16[4,2,128,256]{3,2,1,0:T(8,128)(2,1)S(1)} %bitcast.8), channel_id=1, source_target_pairs={{240,0},{248,8},{0,16},{8,24},{16,32},{24,40},{32,48},{40,56},{48,... | collective-permute-start | bytes 1572872 | tf_op jit(solution)/shard_map/ppermute | solution.py:194
  121.1 15.1 %collective-permute-start.7 = (bf16[4,2,128,256]{3,2,1,0:T(8,128)(2,1)S(1)}, bf16[4,2,128,256]{3,2,1,0:T(8,128)(2,1)S(1)}, u32[]{:S(2)}, u32[]{:S(2)}) collective-permute-start(bf16[4,2,128,256]{3,2,1,0:T(8,128)(2,1)S(1)} %bitcast.9), channel_id=1, source_target_pairs={{16,0},{24,8},{32,16},{40,24},{48,32},{56,40},{64,48},{72,56},{80,... | collective-permute-start | bytes 1572872 | tf_op jit(solution)/shard_map/ppermute | solution.py:194
  123.1 7.4 %collective-permute-start.6 = (bf16[4,128,256]{2,1,0:T(8,128)(2,1)S(1)}, bf16[4,128,256]{2,1,0:T(8,128)(2,1)S(1)}, u32[]{:S(2)}, u32[]{:S(2)}) collective-permute-start(bf16[4,128,256]{2,1,0:T(8,128)(2,1)S(1)} %collective-permute-done.5.two), channel_id=1, source_target_pairs={{0,256},{256,0},{1,257},{257,1},{2,258},{258,2},{3,259},{259,3},{4... | collective-permute-start | bytes 786440 | tf_op jit(solution)/shard_map/ppermute | solution.py:195
  130.5 14.7 %copy-start.1 = (bf16[1024,512]{1,0:T(8,128)(2,1)S(1)}, bf16[1024,512]{1,0:T(8,128)(2,1)}, u32[]{:S(2)}) copy-start(bf16[1024,512]{1,0:T(8,128)(2,1)} %all-gather.5.cloned.1.call-done) | copy-start | bytes 3145732
  136.3 8.9 %collective-permute-start.9 = (bf16[4,4,2,128,256]{4,3,2,1,0:T(8,128)(2,1)S(1)}, bf16[4,4,2,128,256]{4,3,2,1,0:T(8,128)(2,1)S(1)}, u32[]{:S(2)}, u32[]{:S(2)}) collective-permute-start(bf16[4,4,2,128,256]{4,3,2,1,0:T(8,128)(2,1)S(1)} %classes.1.refs_0_), channel_id=1, source_target_pairs={{0,8},{8,0},{1,9},{9,1},{2,10},{10,2},{3,11},{11,3},{4,12},{12,4},... | collective-permute-start | bytes 6291464 | tf_op jit(solution)/shard_map/ppermute | solution.py:198
Sparse Core Ops, SparseCore 0:
  64.1 58.0 all-gather.4

commit v8 on v7

--- a/solution.py
+++ b/solution.py
@@ -65,21 +65,70 @@
     )(keep_blocks.T, base)
 
 
+def forward_kernel(below, above, both, onward):
+    both[0] = below[...]
+    both[1] = above[...]
+    onward[...] = jnp.where(lax.axis_index("core") == 0, below[...], above[...])
+
+
+def forward(below, above):
+    shape = below.shape
+    return pl.pallas_call(
+        forward_kernel,
+        out_shape=tuple(jax.ShapeDtypeStruct(d + shape, below.dtype) for d in ((2,), ())),
+        in_specs=[vmem()] * 2,
+        out_specs=(vmem(),) * 2,
+        name="forward",
+        compiler_params=pltpu.CompilerParams(vmem_limit_bytes=2 << 20),
+        cost_estimate=pl.CostEstimate(
+            flops=0, bytes_accessed=10 * below.size, transcendentals=0
+        ),
+    )(below, above)
+
+
+def columns_kernel(*refs):
+    ylo, zh, out = lax.axis_index("ylo"), lax.axis_index("zh"), refs[-1]
+    for y in range(2):
+        mine, both, across = refs[3 * y : 3 * y + 3]
+        for d, part in ((0, mine), (3, both.at[0]), (1, both.at[1]), (2, across)):
+            out[ylo ^ y, lax.rem(zh + d, 4)] = part[...]
+
+
+def columns(*parts):
+    shape = (2, 4) + parts[0].shape
+    return pl.pallas_call(
+        columns_kernel,
+        out_shape=jax.ShapeDtypeStruct(shape, parts[0].dtype),
+        in_specs=[vmem()] * len(parts),
+        out_specs=vmem(),
+        name="columns",
+        compiler_params=pltpu.CompilerParams(vmem_limit_bytes=4 << 20),
+        cost_estimate=pl.CostEstimate(
+            flops=0, bytes_accessed=32 * parts[0].size, transcendentals=0
+        ),
+    )(*parts)
+
+
 def partial_gram_kernel(r0, r1, r2, r3, cols, mates, out, rows):
-    ylo, zl, core = (lax.axis_index(a) for a in ("ylo", "zl", "core"))
-    chunk = BLOCK // 2
+    zl, core = lax.axis_index("zl"), lax.axis_index("core")
+    chunk, depth = r0.shape
     for d, part in enumerate((r0, r1, r2, r3)):
         place = lax.rem(zl + d, 4) * chunk
         rows[pl.ds(pl.multiple_of(place, chunk), chunk), :] = part[...]
-    for dy, dc, part in ((0, 0, cols), (1, 0, cols), (0, 1, mates), (1, 1, mates)):
-        term = lax.dot_general(part[dy], rows[...], NT, preferred_element_type=jnp.float32)
-        term = term.astype(jnp.bfloat16).reshape(4, chunk, rows.shape[0])
-        half = pl.ds(pl.multiple_of((core ^ dc) * chunk, chunk), chunk)
-        out[pl.ds((ylo ^ dy) * 4, 4), half, :] = term
+    for c, part in enumerate((cols, mates)):
+        half = pl.ds(pl.multiple_of((core ^ c) * chunk, chunk), chunk)
+        for y in range(2):
+            term = lax.dot_general(
+                part[y].reshape(4 * chunk, depth), rows[...], NT,
+                preferred_element_type=jnp.float32,
+            )
+            term = term.astype(jnp.bfloat16).reshape(4, chunk, rows.shape[0])
+            out[4 * y : 4 * y + 4, half, :] = term
 
 
 def partial_gram(rows, *cols):
-    k, depth = cols[0].shape[1:]
+    chunk, depth = rows[0].shape
+    k = 4 * chunk
     return pl.pallas_call(
         partial_gram_kernel,
         out_shape=jax.ShapeDtypeStruct((8, BLOCK, k), jnp.bfloat16),
@@ -138,11 +187,6 @@
     )(diffs, *grams, weight, base, keep)
 
 
-def pair_kernel(own, other, out):
-    out[0] = own[...]
-    out[1] = other[...]
-
-
 def classes_kernel(mine, up, down, two, two_far, out):
     ylo = lax.axis_index("ylo")
     out[0] = mine[...]
@@ -152,14 +196,14 @@
     out[3, :, 1 - ylo] = two_far[...]
 
 
-def pack(kernel, name, *parts):
-    shape = ((2 if name == "pair" else 4),) + parts[0].shape
-    return pl.pallas_call(
-        kernel,
+def pack(*parts):
+    shape = (4,) + parts[0].shape
+    return pl.pallas_call(
+        classes_kernel,
         out_shape=jax.ShapeDtypeStruct(shape, parts[0].dtype),
         in_specs=[vmem()] * len(parts),
         out_specs=vmem(),
-        name=name,
+        name="classes",
         compiler_params=pltpu.CompilerParams(vmem_limit_bytes=4 << 20),
         cost_estimate=pl.CostEstimate(
             flops=0, bytes_accessed=4 * shape[0] * parts[0].size, transcendentals=0
@@ -170,12 +214,18 @@
 def on_device(calib, base_weight, keep_blocks):
     tokens = calib.shape[0] * 8
     feats = calib.T
-    own = lax.all_gather(feats, "zh", axis=0, tiled=True)
-    other = lax.ppermute(own, "ylo", SWAP)
-    near = lax.optimization_barrier((feats, own))[0]
+    line = ("zh", "zl", "core")
+    below, above = (lax.ppermute(feats, line, from_z(d, d)) for d in (-4, 4))
+    other = lax.ppermute(feats, "ylo", SWAP)
+    near, other = lax.optimization_barrier((feats, other))
     rows = [feats] + [lax.ppermute(near, "zl", [((i + d) % 4, i) for i in range(4)]) for d in (1, 2, 3)]
-    other, *rows[1:] = lax.optimization_barrier((other, *rows[1:]))
-    cols = pack(pair_kernel, "pair", own, other)
+    both, onward = forward(below, above)
+    both, *rows[2:] = lax.optimization_barrier((both, *rows[2:]))
+    across = lax.ppermute(onward, line, from_z(-4, 4))
+    other_both = lax.ppermute(both, "ylo", SWAP)
+    other_across = lax.ppermute(across, "ylo", SWAP)
+    other_both, rows[1] = lax.optimization_barrier((other_both, rows[1]))
+    cols = columns(feats, both, across, other, other_both, other_across)
     mates = lax.ppermute(cols, "core", SWAP)
 
     base_weight = lax.optimization_barrier((base_weight, cols))[0]
@@ -187,14 +237,13 @@
     terms = lax.all_to_all(term, ROW, 0, 0, tiled=True)
     gram = (jnp.sum(terms.astype(jnp.float32), axis=0) / tokens).astype(jnp.bfloat16)
 
-    line = ("zh", "zl", "core")
     mine = lax.all_gather(lax.all_gather(gram, "ylo", axis=0), "zh", axis=0)
     half = lax.dynamic_index_in_dim(mine, lax.axis_index("ylo"), 1, keepdims=False)
     two = lax.ppermute(half, line, from_z(2, -2))
     up, down = (lax.ppermute(mine, line, from_z(s, s)) for s in (1, -1))
     two_far = lax.ppermute(two, "ylo", SWAP)
     diffs, two_far = lax.optimization_barrier((diffs, two_far))
-    packed = pack(classes_kernel, "classes", mine, up, down, two, two_far)
+    packed = pack(mine, up, down, two, two_far)
     grams = (packed, lax.ppermute(packed, "core", SWAP))
 
     weight, sent = step(False, diffs, grams, weight, base_weight, keep)

time: 176 us -> 187 us (1.062)
  blocking collectives: 79.1 us -> 44.7 us
  starting transfers between devices: 43.4 us -> 77.2 us
  waiting for transfers between devices: 32.3 us -> 42.6 us
    all_gather x1 -> x0, blocking collectives: 31.5 us -> none  [on_device(): own = lax.all_gather(feats, 'zh', axis=0, tiled=True)]
    ppermute x1 -> x6, starting transfers between devices: 3.19 us -> 32.2 us  [the longest x2 14.4 us: on_device(): below, above = (lax.ppermute(feats, line, from_z(d, d)) for d in (-4, 4))]
    ppermute x1, starting transfers between devices: 1.92 us -> 9.78 us  [on_device(): two = lax.ppermute(half, line, from_z(2, -2))]
    ppermute x1 -> x6, waiting for transfers between devices: 0.01 us -> 6.06 us  [the longest x1 3.64 us: on_device(): other_across = lax.ppermute(across, 'ylo', SWAP)]
    ppermute x3, waiting for transfers between devices: 5 us -> 9.17 us  [on_device(): lax.ppermute(near, 'zl', [((i + d) % 4, i) for i in range(4)])]
    ppermute x3, starting transfers between devices: 9.29 us -> 12.9 us  [on_device(): lax.ppermute(near, 'zl', [((i + d) % 4, i) for i in range(4)])]
    ppermute x1, starting transfers between devices: 6.05 us -> 2.48 us  [on_device(): mates = lax.ppermute(cols, 'core', SWAP)]
    all_gather x2, blocking collectives: 27.8 us -> 24.7 us  [on_device(): mine = lax.all_gather(lax.all_gather(gram, 'ylo', axis=0), 'zh', axis=0)]
  transfers between devices with their start and end apart: 12 -> 17, of which waited for: 8 -> 12; matrix products, arithmetic and copies ran while one was open for 0% -> 0% of each run, Pallas kernels for 2% -> 2%
where the time goes in v8:
time: 187 us; the launch traced here: 186 us
  starting transfers between devices  77.2 us (41%)
  blocking collectives  44.7 us (24%)
  waiting for transfers between devices  42.6 us (23%)
  between operations  13.6 us (7%)
  Pallas kernels  6.72 us (4%)
    all_gather x2, blocking collectives, on_device(): mine = lax.all_gather(lax.all_gather(gram, 'ylo', axis=0), 'zh', axis=0)  24.7 us
    all_to_all x1, blocking collectives, on_device(): diffs = lax.all_to_all(sent, ROW, 0, 0, tiled=True)  20.1 us
    ppermute x2, starting transfers between devices, on_device(): below, above = (lax.ppermute(feats, line, from_z(d, d)) for d in (-4, 4))  14.4 us
    ppermute x3, starting transfers between devices, on_device(): lax.ppermute(near, 'zl', [((i + d) % 4, i) for i in range(4)])  12.9 us
    all_to_all x1, waiting for transfers between devices, on_device(): terms = lax.all_to_all(term, ROW, 0, 0, tiled=True)  11.7 us
    ppermute x1, starting transfers between devices, on_device(): two = lax.ppermute(half, line, from_z(2, -2))  9.78 us
    ppermute x3, waiting for transfers between devices, on_device(): lax.ppermute(near, 'zl', [((i + d) % 4, i) for i in range(4)])  9.17 us
    ppermute x2, starting transfers between devices, on_device(): up, down = (lax.ppermute(mine, line, from_z(s, s)) for s in (1, -1))  8.05 us
  transfers between devices with their start and end apart: 17, of which 12 were waited for; matrix products, arithmetic and copies ran while one was open for 0% of the time, Pallas kernels for 2%

profile of v8, /device:TPU:1, one launch (start us, length us, event | category | flops | bytes accessed | tf_op | source)
XLA Modules:
  0.0 185.9 jit_solution(10585020268432062242)
XLA Ops:
  6.5 4.2 %collective-permute-start.2 = (bf16[64,1024]{1,0:T(8,128)(2,1)}, bf16[64,1024]{1,0:T(8,128)(2,1)S(1)}, u32[]{:S(2)}, u32[]{:S(2)}) collective-permute-start(bf16[64,1024]{1,0:T(8,128)(2,1)} %bitcast.12), channel_id=1, source_target_pairs={{0,256},{256,0},{1,257},{257,1},{2,258},{258,2},{3,259},{259,3},{4... | collective-permute-start | bytes 393224 | tf_op jit(solution)/shard_map/ppermute | solution.py:219
  10.7 12.5 %collective-permute-start.1 = (bf16[64,1024]{1,0:T(8,128)(2,1)}, bf16[64,1024]{1,0:T(8,128)(2,1)S(1)}, u32[]{:S(2)}, u32[]{:S(2)}) collective-permute-start(bf16[64,1024]{1,0:T(8,128)(2,1)} %bitcast.13), channel_id=1, source_target_pairs={{64,0},{72,8},{80,16},{88,24},{96,32},{104,40},{112,48},{120,56},{... | collective-permute-start | bytes 393224 | tf_op jit(solution)/shard_map/ppermute | solution.py:218
  25.1 2.6 %collective-permute-start.4 = (bf16[64,1024]{1,0:T(8,128)(2,1)}, bf16[64,1024]{1,0:T(8,128)(2,1)S(1)}, u32[]{:S(2)}, u32[]{:S(2)}) collective-permute-start(bf16[64,1024]{1,0:T(8,128)(2,1)} %bitcast.15), channel_id=1, source_target_pairs={{48,0},{0,16},{16,32},{32,48},{49,1},{1,17},{17,33},{33,49},{50,2}... | collective-permute-start | bytes 393224 | tf_op jit(solution)/shard_map/ppermute | solution.py:221
  27.8 3.1 %collective-permute-start.3 = (bf16[64,1024]{1,0:T(8,128)(2,1)}, bf16[64,1024]{1,0:T(8,128)(2,1)S(1)}, u32[]{:S(2)}, u32[]{:S(2)}) collective-permute-start(bf16[64,1024]{1,0:T(8,128)(2,1)} %bitcast.16), channel_id=1, source_target_pairs={{32,0},{48,16},{0,32},{16,48},{33,1},{49,17},{1,33},{17,49},{34,2}... | collective-permute-start | bytes 393224 | tf_op jit(solution)/shard_map/ppermute | solution.py:221
  35.2 6.9 %collective-permute-done.3.r2 = bf16[64,1024]{1,0:T(8,128)(2,1)S(1)} collective-permute-done((bf16[64,1024]{1,0:T(8,128)(2,1)}, bf16[64,1024]{1,0:T(8,128)(2,1)S(1)}, u32[]{:S(2)}, u32[]{:S(2)}) %collective-permute-start.3) | collective-permute-done | bytes 131104 | tf_op jit(solution)/shard_map/ppermute | solution.py:221
  42.1 2.5 %collective-permute-start.6 = (bf16[2,64,1024]{2,1,0:T(8,128)(2,1)S(1)}, bf16[2,64,1024]{2,1,0:T(8,128)(2,1)S(1)}, u32[]{:S(2)}, u32[]{:S(2)}) collective-permute-start(bf16[2,64,1024]{2,1,0:T(8,128)(2,1)S(1)} %get-tuple-element.26.refs_1_), channel_id=1, source_target_pairs={{0,256},{256,0},{1,257},{257,1},{2,258},{258,2},{3,259},{259,3},{4... | collective-permute-start | bytes 786440 | tf_op jit(solution)/shard_map/ppermute | solution.py:225
  44.7 8.0 %collective-permute-start.5 = (bf16[64,1024]{1,0:T(8,128)(2,1)S(1)}, bf16[64,1024]{1,0:T(8,128)(2,1)S(1)}, u32[]{:S(2)}, u32[]{:S(2)}) collective-permute-start(bf16[64,1024]{1,0:T(8,128)(2,1)S(1)} %get-tuple-element.27), channel_id=1, source_target_pairs={{192,0},{72,8},{208,16},{88,24},{224,32},{104,40},{240,48},{120,56... | collective-permute-start | bytes 393224 | tf_op jit(solution)/shard_map/ppermute | solution.py:224
  52.6 7.2 %collective-permute-start.7 = (bf16[64,1024]{1,0:T(8,128)(2,1)}, bf16[64,1024]{1,0:T(8,128)(2,1)S(1)}, u32[]{:S(2)}, u32[]{:S(2)}) collective-permute-start(bf16[64,1024]{1,0:T(8,128)(2,1)} %bitcast.17), channel_id=1, source_target_pairs={{16,0},{32,16},{48,32},{0,48},{17,1},{33,17},{49,33},{1,49},{18,2}... | collective-permute-start | bytes 393224 | tf_op jit(solution)/shard_map/ppermute | solution.py:221
  59.8 3.2 %collective-permute-start.8 = (bf16[64,1024]{1,0:T(8,128)(2,1)S(1)}, bf16[64,1024]{1,0:T(8,128)(2,1)S(1)}, u32[]{:S(2)}, u32[]{:S(2)}) collective-permute-start(bf16[64,1024]{1,0:T(8,128)(2,1)S(1)} %collective-permute-done.5.refs_2_), channel_id=1, source_target_pairs={{0,256},{256,0},{1,257},{257,1},{2,258},{258,2},{3,259},{259,3},{4... | collective-permute-start | bytes 393224 | tf_op jit(solution)/shard_map/ppermute | solution.py:226
  63.4 3.6 %collective-permute-done.8.refs_5_ = bf16[64,1024]{1,0:T(8,128)(2,1)S(1)} collective-permute-done((bf16[64,1024]{1,0:T(8,128)(2,1)S(1)}, bf16[64,1024]{1,0:T(8,128)(2,1)S(1)}, u32[]{:S(2)}, u32[]{:S(2)}) %collective-permute-start.8) | collective-permute-done | bytes 131104 | tf_op jit(solution)/shard_map/ppermute | solution.py:226
  68.0 2.5 %collective-permute-start.9 = (bf16[2,4,64,1024]{3,2,1,0:T(8,128)(2,1)S(1)}, bf16[2,4,64,1024]{3,2,1,0:T(8,128)(2,1)S(1)}, u32[]{:S(2)}, u32[]{:S(2)}) collective-permute-start(bf16[2,4,64,1024]{3,2,1,0:T(8,128)(2,1)S(1)} %columns.1.cols), channel_id=1, source_target_pairs={{0,8},{8,0},{1,9},{9,1},{2,10},{10,2},{3,11},{11,3},{4,12},{12,4},... | collective-permute-start | bytes 3145736 | tf_op jit(solution)/shard_map/ppermute | solution.py:229
  74.4 6.7 %all-to-all-start = ((bf16[8,128,256]{2,1,0:T(8,128)(2,1)}), bf16[8,128,256]{2,1,0:T(8,128)(2,1)S(1)}, u32[]{:S(2)}, u32[]{:S(2)}) async-start(bf16[8,128,256]{2,1,0:T(8,128)(2,1)} %partial_gram.1), calls=%async_computation | async-start | bytes 1048576 | tf_op jit(solution)/shard_map/all_to_all | solution.py:237
  81.1 11.7 %all-to-all-done = bf16[8,128,256]{2,1,0:T(8,128)(2,1)S(1)} async-done(((bf16[8,128,256]{2,1,0:T(8,128)(2,1)}), bf16[8,128,256]{2,1,0:T(8,128)(2,1)S(1)}, u32[]{:S(2)}, u32[]{:S(2)}) %all-to-all-start) | async-done | bytes 524320 | tf_op jit(solution)/shard_map/all_to_all | solution.py:237
  92.9 4.2 %all-gather.1 = bf16[256,256]{1,0:T(8,128)(2,1)S(1)} all-gather(bf16[128,256]{1,0:T(8,128)(2,1)S(1)} %multiply_convert_fusion), channel_id=3, replica_groups=mesh['ylo'=2,'zh'=4,'zl'=4,'core'=2,'yhi'=2,'x'=4] {'ylo'}, dimensions={0}, use_global_device_ids=true | all-gather | bytes 196608 | tf_op jit(solution)/shard_map/all_gather | solution.py:240
  97.1 20.5 %all-gather.2 = bf16[8,128,256]{2,1,0:T(8,128)(2,1)S(1)} all-gather(bf16[2,128,256]{2,1,0:T(8,128)(2,1)S(1)} %bitcast.21), channel_id=4, replica_groups=mesh['ylo'=2,'zh'=4,'zl'=4,'core'=2,'yhi'=2,'x'=4] {'zh'}, dimensions={0}, use_global_device_ids=true | all-gather | bytes 655360 | tf_op jit(solution)/shard_map/all_gather | solution.py:240
  117.6 9.8 %collective-permute-start.10 = (bf16[4,128,256]{2,1,0:T(8,128)(2,1)S(1)}, bf16[4,128,256]{2,1,0:T(8,128)(2,1)S(1)}, u32[]{:S(2)}, u32[]{:S(2)}) collective-permute-start(bf16[4,128,256]{2,1,0:T(8,128)(2,1)S(1)} %dynamic-slice_bitcast_fusion), channel_id=1, source_target_pairs={{32,0},{232,8},{48,16},{248,24},{64,32},{8,40},{80,48},{24,56},{96... | collective-permute-start | bytes 786440 | tf_op jit(solution)/shard_map/ppermute | solution.py:242
  127.4 6.1 %collective-permute-start.13 = (bf16[4,2,128,256]{3,2,1,0:T(8,128)(2,1)S(1)}, bf16[4,2,128,256]{3,2,1,0:T(8,128)(2,1)S(1)}, u32[]{:S(2)}, u32[]{:S(2)}) collective-permute-start(bf16[4,2,128,256]{3,2,1,0:T(8,128)(2,1)S(1)} %bitcast.8), channel_id=1, source_target_pairs={{240,0},{248,8},{0,16},{8,24},{16,32},{24,40},{32,48},{40,56},{48,... | collective-permute-start | bytes 1572872 | tf_op jit(solution)/shard_map/ppermute | solution.py:243
  135.5 2.0 %collective-permute-start.11 = (bf16[4,128,256]{2,1,0:T(8,128)(2,1)S(1)}, bf16[4,128,256]{2,1,0:T(8,128)(2,1)S(1)}, u32[]{:S(2)}, u32[]{:S(2)}) collective-permute-start(bf16[4,128,256]{2,1,0:T(8,128)(2,1)S(1)} %collective-permute-done.10.two), channel_id=1, source_target_pairs={{0,256},{256,0},{1,257},{257,1},{2,258},{258,2},{3,259},{259,3},{4... | collective-permute-start | bytes 786440 | tf_op jit(solution)/shard_map/ppermute | solution.py:244
  137.5 5.4 %collective-permute-done.11.two_far = bf16[4,128,256]{2,1,0:T(8,128)(2,1)S(1)} collective-permute-done((bf16[4,128,256]{2,1,0:T(8,128)(2,1)S(1)}, bf16[4,128,256]{2,1,0:T(8,128)(2,1)S(1)}, u32[]{:S(2)}, u32[]{:S(2)}) %collective-permute-start.11) | collective-permute-done | bytes 262176 | tf_op jit(solution)/shard_map/ppermute | solution.py:244
  142.9 3.3 %collective-permute-done.13.down = bf16[4,2,128,256]{3,2,1,0:T(8,128)(2,1)S(1)} collective-permute-done((bf16[4,2,128,256]{3,2,1,0:T(8,128)(2,1)S(1)}, bf16[4,2,128,256]{3,2,1,0:T(8,128)(2,1)S(1)}, u32[]{:S(2)}, u32[]{:S(2)}) %collective-permute-start.13) | collective-permute-done | bytes 524320 | tf_op jit(solution)/shard_map/ppermute | solution.py:243
  146.1 2.5 %collective-permute-done.12.up = bf16[4,2,128,256]{3,2,1,0:T(8,128)(2,1)S(1)} collective-permute-done((bf16[4,2,128,256]{3,2,1,0:T(8,128)(2,1)S(1)}, bf16[4,2,128,256]{3,2,1,0:T(8,128)(2,1)S(1)}, u32[]{:S(2)}, u32[]{:S(2)}) %collective-permute-start.12) | collective-permute-done | bytes 524320 | tf_op jit(solution)/shard_map/ppermute | solution.py:243
  148.8 3.0 %collective-permute-start.14 = (bf16[4,4,2,128,256]{4,3,2,1,0:T(8,128)(2,1)S(1)}, bf16[4,4,2,128,256]{4,3,2,1,0:T(8,128)(2,1)S(1)}, u32[]{:S(2)}, u32[]{:S(2)}) collective-permute-start(bf16[4,4,2,128,256]{4,3,2,1,0:T(8,128)(2,1)S(1)} %classes.1.refs_0_), channel_id=1, source_target_pairs={{0,8},{8,0},{1,9},{9,1},{2,10},{10,2},{3,11},{11,3},{4,12},{12,4},... | collective-permute-start | bytes 6291464 | tf_op jit(solution)/shard_map/ppermute | solution.py:247
  151.8 3.8 %collective-permute-done.14.refs_1_ = bf16[4,4,2,128,256]{4,3,2,1,0:T(8,128)(2,1)S(1)} collective-permute-done((bf16[4,4,2,128,256]{4,3,2,1,0:T(8,128)(2,1)S(1)}, bf16[4,4,2,128,256]{4,3,2,1,0:T(8,128)(2,1)S(1)}, u32[]{:S(2)}, u32[]{:S(2)}) %collective-permute-start.14) | collective-permute-done | bytes 2097184 | tf_op jit(solution)/shard_map/ppermute | solution.py:247
  157.0 20.1 %all_to_all.10.diffs = bf16[8,128,512]{2,1,0:T(8,128)(2,1)S(1)} all-to-all(bf16[8,128,512]{2,1,0:T(8,128)(2,1)S(1)} %get-tuple-element.41), channel_id=1, replica_groups=mesh['ylo'=2,'zh'=4,'zl'=4,'core'=2,'yhi'=2,'x'=4] {'yhi','x'}, dimensions={0} | all-to-all | bytes 2097152 | tf_op jit(solution)/shard_map/all_to_all | solution.py:250
  (34 shorter events, 17.0 us)
Async XLA Ops:
  6.5 66.3 %copy-start.3 = (bf16[1024,64]{0,1:T(8,128)(2,1)S(1)}, bf16[1024,64]{0,1:T(8,128)(2,1)}, u32[]{:S(2)}) copy-start(bf16[1024,64]{0,1:T(8,128)(2,1)} %param.3) | copy-start | bytes 393220
  6.5 64.0 %copy-start = (bf16[128,512]{1,0:T(8,128)(2,1)S(1)}, bf16[128,512]{1,0:T(8,128)(2,1)}, u32[]{:S(2)}) copy-start(bf16[128,512]{1,0:T(8,128)(2,1)} %refs_3_.1) | copy-start | bytes 393220
  6.5 136.3 %all-gather.5.cloned.1.call-start = ((), (), s32[]{:S(2)}) async-start(), calls=%async_computation.2 | async-start | bytes 1179648 | tf_op jit(solution)/shard_map/all_gather | solution.py:234
  6.5 18.6 %collective-permute-start.2 = (bf16[64,1024]{1,0:T(8,128)(2,1)}, bf16[64,1024]{1,0:T(8,128)(2,1)S(1)}, u32[]{:S(2)}, u32[]{:S(2)}) collective-permute-start(bf16[64,1024]{1,0:T(8,128)(2,1)} %bitcast.12), channel_id=1, source_target_pairs={{0,256},{256,0},{1,257},{257,1},{2,258},{258,2},{3,259},{259,3},{4... | collective-permute-start | bytes 393224 | tf_op jit(solution)/shard_map/ppermute | solution.py:219
  10.7 21.2 %collective-permute-start.1 = (bf16[64,1024]{1,0:T(8,128)(2,1)}, bf16[64,1024]{1,0:T(8,128)(2,1)S(1)}, u32[]{:S(2)}, u32[]{:S(2)}) collective-permute-start(bf16[64,1024]{1,0:T(8,128)(2,1)} %bitcast.13), channel_id=1, source_target_pairs={{64,0},{72,8},{80,16},{88,24},{96,32},{104,40},{112,48},{120,56},{... | collective-permute-start | bytes 393224 | tf_op jit(solution)/shard_map/ppermute | solution.py:218
  23.2 10.1 %collective-permute-start = (bf16[64,1024]{1,0:T(8,128)(2,1)}, bf16[64,1024]{1,0:T(8,128)(2,1)S(1)}, u32[]{:S(2)}, u32[]{:S(2)}) collective-permute-start(bf16[64,1024]{1,0:T(8,128)(2,1)} %bitcast.14), channel_id=1, source_target_pairs={{192,0},{200,8},{208,16},{216,24},{224,32},{232,40},{240,48},{248,... | collective-permute-start | bytes 393224 | tf_op jit(solution)/shard_map/ppermute | solution.py:218
  25.1 10.1 %collective-permute-start.4 = (bf16[64,1024]{1,0:T(8,128)(2,1)}, bf16[64,1024]{1,0:T(8,128)(2,1)S(1)}, u32[]{:S(2)}, u32[]{:S(2)}) collective-permute-start(bf16[64,1024]{1,0:T(8,128)(2,1)} %bitcast.15), channel_id=1, source_target_pairs={{48,0},{0,16},{16,32},{32,48},{49,1},{1,17},{17,33},{33,49},{50,2}... | collective-permute-start | bytes 393224 | tf_op jit(solution)/shard_map/ppermute | solution.py:221
  27.8 14.3 %collective-permute-start.3 = (bf16[64,1024]{1,0:T(8,128)(2,1)}, bf16[64,1024]{1,0:T(8,128)(2,1)S(1)}, u32[]{:S(2)}, u32[]{:S(2)}) collective-permute-start(bf16[64,1024]{1,0:T(8,128)(2,1)} %bitcast.16), channel_id=1, source_target_pairs={{32,0},{48,16},{0,32},{16,48},{33,1},{49,17},{1,33},{17,49},{34,2}... | collective-permute-start | bytes 393224 | tf_op jit(solution)/shard_map/ppermute | solution.py:221
  42.1 21.3 %collective-permute-start.6 = (bf16[2,64,1024]{2,1,0:T(8,128)(2,1)S(1)}, bf16[2,64,1024]{2,1,0:T(8,128)(2,1)S(1)}, u32[]{:S(2)}, u32[]{:S(2)}) collective-permute-start(bf16[2,64,1024]{2,1,0:T(8,128)(2,1)S(1)} %get-tuple-element.26.refs_1_), channel_id=1, source_target_pairs={{0,256},{256,0},{1,257},{257,1},{2,258},{258,2},{3,259},{259,3},{4... | collective-permute-start | bytes 786440 | tf_op jit(solution)/shard_map/ppermute | solution.py:225
  44.7 15.2 %collective-permute-start.5 = (bf16[64,1024]{1,0:T(8,128)(2,1)S(1)}, bf16[64,1024]{1,0:T(8,128)(2,1)S(1)}, u32[]{:S(2)}, u32[]{:S(2)}) collective-permute-start(bf16[64,1024]{1,0:T(8,128)(2,1)S(1)} %get-tuple-element.27), channel_id=1, source_target_pairs={{192,0},{72,8},{208,16},{88,24},{224,32},{104,40},{240,48},{120,56... | collective-permute-start | bytes 393224 | tf_op jit(solution)/shard_map/ppermute | solution.py:224
  52.6 10.8 %collective-permute-start.7 = (bf16[64,1024]{1,0:T(8,128)(2,1)}, bf16[64,1024]{1,0:T(8,128)(2,1)S(1)}, u32[]{:S(2)}, u32[]{:S(2)}) collective-permute-start(bf16[64,1024]{1,0:T(8,128)(2,1)} %bitcast.17), channel_id=1, source_target_pairs={{16,0},{32,16},{48,32},{0,48},{17,1},{33,17},{49,33},{1,49},{18,2}... | collective-permute-start | bytes 393224 | tf_op jit(solution)/shard_map/ppermute | solution.py:221
  59.8 7.2 %collective-permute-start.8 = (bf16[64,1024]{1,0:T(8,128)(2,1)S(1)}, bf16[64,1024]{1,0:T(8,128)(2,1)S(1)}, u32[]{:S(2)}, u32[]{:S(2)}) collective-permute-start(bf16[64,1024]{1,0:T(8,128)(2,1)S(1)} %collective-permute-done.5.refs_2_), channel_id=1, source_target_pairs={{0,256},{256,0},{1,257},{257,1},{2,258},{258,2},{3,259},{259,3},{4... | collective-permute-start | bytes 393224 | tf_op jit(solution)/shard_map/ppermute | solution.py:226
  67.1 0.9 copy-start.2
  68.0 2.6 %copy-start.4 = (s32[64,16]{0,1:T(8,128)S(1)}, s32[64,16]{0,1:T(8,128)}, u32[]{:S(2)}) copy-start(s32[64,16]{0,1:T(8,128)} %param.5) | copy-start | bytes 12292
  68.0 4.8 %collective-permute-start.9 = (bf16[2,4,64,1024]{3,2,1,0:T(8,128)(2,1)S(1)}, bf16[2,4,64,1024]{3,2,1,0:T(8,128)(2,1)S(1)}, u32[]{:S(2)}, u32[]{:S(2)}) collective-permute-start(bf16[2,4,64,1024]{3,2,1,0:T(8,128)(2,1)S(1)} %columns.1.cols), channel_id=1, source_target_pairs={{0,8},{8,0},{1,9},{9,1},{2,10},{10,2},{3,11},{11,3},{4,12},{12,4},... | collective-permute-start | bytes 3145736 | tf_op jit(solution)/shard_map/ppermute | solution.py:229
  74.4 18.4 %all-to-all-start = ((bf16[8,128,256]{2,1,0:T(8,128)(2,1)}), bf16[8,128,256]{2,1,0:T(8,128)(2,1)S(1)}, u32[]{:S(2)}, u32[]{:S(2)}) async-start(bf16[8,128,256]{2,1,0:T(8,128)(2,1)} %partial_gram.1), calls=%async_computation | async-start | bytes 1048576 | tf_op jit(solution)/shard_map/all_to_all | solution.py:237
  117.6 17.9 %collective-permute-start.10 = (bf16[4,128,256]{2,1,0:T(8,128)(2,1)S(1)}, bf16[4,128,256]{2,1,0:T(8,128)(2,1)S(1)}, u32[]{:S(2)}, u32[]{:S(2)}) collective-permute-start(bf16[4,128,256]{2,1,0:T(8,128)(2,1)S(1)} %dynamic-slice_bitcast_fusion), channel_id=1, source_target_pairs={{32,0},{232,8},{48,16},{248,24},{64,32},{8,40},{80,48},{24,56},{96... | collective-permute-start | bytes 786440 | tf_op jit(solution)/shard_map/ppermute | solution.py:242
  127.4 18.8 %collective-permute-start.13 = (bf16[4,2,128,256]{3,2,1,0:T(8,128)(2,1)S(1)}, bf16[4,2,128,256]{3,2,1,0:T(8,128)(2,1)S(1)}, u32[]{:S(2)}, u32[]{:S(2)}) collective-permute-start(bf16[4,2,128,256]{3,2,1,0:T(8,128)(2,1)S(1)} %bitcast.8), channel_id=1, source_target_pairs={{240,0},{248,8},{0,16},{8,24},{16,32},{24,40},{32,48},{40,56},{48,... | collective-permute-start | bytes 1572872 | tf_op jit(solution)/shard_map/ppermute | solution.py:243
  133.5 15.1 %collective-permute-start.12 = (bf16[4,2,128,256]{3,2,1,0:T(8,128)(2,1)S(1)}, bf16[4,2,128,256]{3,2,1,0:T(8,128)(2,1)S(1)}, u32[]{:S(2)}, u32[]{:S(2)}) collective-permute-start(bf16[4,2,128,256]{3,2,1,0:T(8,128)(2,1)S(1)} %bitcast.9), channel_id=1, source_target_pairs={{16,0},{24,8},{32,16},{40,24},{48,32},{56,40},{64,48},{72,56},{80,... | collective-permute-start | bytes 1572872 | tf_op jit(solution)/shard_map/ppermute | solution.py:243
  135.5 7.4 %collective-permute-start.11 = (bf16[4,128,256]{2,1,0:T(8,128)(2,1)S(1)}, bf16[4,128,256]{2,1,0:T(8,128)(2,1)S(1)}, u32[]{:S(2)}, u32[]{:S(2)}) collective-permute-start(bf16[4,128,256]{2,1,0:T(8,128)(2,1)S(1)} %collective-permute-done.10.two), channel_id=1, source_target_pairs={{0,256},{256,0},{1,257},{257,1},{2,258},{258,2},{3,259},{259,3},{4... | collective-permute-start | bytes 786440 | tf_op jit(solution)/shard_map/ppermute | solution.py:244
  142.9 12.7 %copy-start.1 = (bf16[1024,512]{1,0:T(8,128)(2,1)S(1)}, bf16[1024,512]{1,0:T(8,128)(2,1)}, u32[]{:S(2)}) copy-start(bf16[1024,512]{1,0:T(8,128)(2,1)} %all-gather.5.cloned.1.call-done) | copy-start | bytes 3145732
  148.8 6.8 %collective-permute-start.14 = (bf16[4,4,2,128,256]{4,3,2,1,0:T(8,128)(2,1)S(1)}, bf16[4,4,2,128,256]{4,3,2,1,0:T(8,128)(2,1)S(1)}, u32[]{:S(2)}, u32[]{:S(2)}) collective-permute-start(bf16[4,4,2,128,256]{4,3,2,1,0:T(8,128)(2,1)S(1)} %classes.1.refs_0_), channel_id=1, source_target_pairs={{0,8},{8,0},{1,9},{9,1},{2,10},{10,2},{3,11},{11,3},{4,12},{12,4},... | collective-permute-start | bytes 6291464 | tf_op jit(solution)/shard_map/ppermute | solution.py:247
Sparse Core Ops, SparseCore 0:
  72.9 60.9 all-gather.4

commit v9 on v7

--- a/solution.py
+++ b/solution.py
@@ -50,14 +50,20 @@
     new = (keep * base_float).astype(jnp.bfloat16)
     weight[...] = new
     keep_out[...] = keep
-    diff[...] = by_core((new.astype(jnp.float32) - base_float).astype(jnp.bfloat16))
+    sent = by_core((new.astype(jnp.float32) - base_float).astype(jnp.bfloat16))
+    for i in range(diff.shape[0]):
+        diff[i] = sent
 
 
 def start(keep_blocks, base):
     bf16 = jax.ShapeDtypeStruct(base.shape, base.dtype)
     return pl.pallas_call(
         start_kernel,
-        out_shape=(bf16, bf16, jax.ShapeDtypeStruct(base.shape, jnp.float32)),
+        out_shape=(
+            bf16,
+            jax.ShapeDtypeStruct((8,) + base.shape, base.dtype),
+            jax.ShapeDtypeStruct(base.shape, jnp.float32),
+        ),
         in_specs=[smem(), vmem()],
         out_specs=(vmem(),) * 3,
         name="start",
@@ -181,8 +187,6 @@
     base_weight = lax.optimization_barrier((base_weight, cols))[0]
     weight, diff, keep = start(keep_blocks, base_weight)
     diff, mates = lax.optimization_barrier((diff, mates))
-    diffs = lax.all_gather(diff, ROW, axis=0)
-
     term = partial_gram(rows, cols, mates)
     terms = lax.all_to_all(term, ROW, 0, 0, tiled=True)
     gram = (jnp.sum(terms.astype(jnp.float32), axis=0) / tokens).astype(jnp.bfloat16)
@@ -193,6 +197,8 @@
     two = lax.ppermute(half, line, from_z(2, -2))
     up, down = (lax.ppermute(mine, line, from_z(s, s)) for s in (1, -1))
     two_far = lax.ppermute(two, "ylo", SWAP)
+    diff = lax.optimization_barrier((diff, mine))[0]
+    diffs = lax.all_to_all(diff, ROW, 0, 0, tiled=True)
     diffs, two_far = lax.optimization_barrier((diffs, two_far))
     packed = pack(classes_kernel, "classes", mine, up, down, two, two_far)
     grams = (packed, lax.ppermute(packed, "core", SWAP))

time: 176 us -> 168 us (0.955)
  blocking collectives: 79.1 us -> 97.8 us
  between operations: 13.5 us -> 0.16 us
  waiting for transfers between devices: 32.3 us -> 21.4 us
  starting transfers between devices: 43.4 us -> 41.4 us
    all_to_all x0 -> x1, blocking collectives: none -> 17.9 us  [on_device(): terms = lax.all_to_all(term, ROW, 0, 0, tiled=True)]
    all_to_all x1, waiting for transfers between devices: 11.7 us -> 0.01 us  [on_device(): diffs = lax.all_to_all(diff, ROW, 0, 0, tiled=True)]
    all_to_all x1, blocking collectives: 19.8 us -> 23.2 us  [on_device(): diffs = lax.all_to_all(sent, ROW, 0, 0, tiled=True)]
    all_to_all x1, starting transfers between devices: 6.36 us -> 3.63 us  [on_device(): diffs = lax.all_to_all(diff, ROW, 0, 0, tiled=True)]
    all_gather x2, blocking collectives: 27.8 us -> 25.1 us  [on_device(): mine = lax.all_gather(lax.all_gather(gram, 'ylo', axis=0), 'zh', axis=0)]
    ppermute x2, waiting for transfers between devices: 5.57 us -> 7.61 us  [on_device(): up, down = (lax.ppermute(mine, line, from_z(s, s)) for s in (1, -1))]
  transfers between devices with their start and end apart: 12 -> 11, of which waited for: 8 -> 6; matrix products, arithmetic and copies ran while one was open for 0% -> 0% of each run, Pallas kernels for 2% -> 1%
where the time goes in v9:
time: 168 us
  blocking collectives  97.8 us (58%)
  starting transfers between devices  41.4 us (25%)
  waiting for transfers between devices  21.4 us (13%)
  Pallas kernels  6.25 us (4%)
    all_gather x1, blocking collectives, on_device(): own = lax.all_gather(feats, 'zh', axis=0, tiled=True)  31.5 us
    all_gather x2, blocking collectives, on_device(): mine = lax.all_gather(lax.all_gather(gram, 'ylo', axis=0), 'zh', axis=0)  25.1 us
    all_to_all x1, blocking collectives, on_device(): diffs = lax.all_to_all(sent, ROW, 0, 0, tiled=True)  23.2 us
    all_to_all x1, blocking collectives, on_device(): terms = lax.all_to_all(term, ROW, 0, 0, tiled=True)  17.9 us
    ppermute x2, starting transfers between devices, on_device(): up, down = (lax.ppermute(mine, line, from_z(s, s)) for s in (1, -1))  9.35 us
    ppermute x3, starting transfers between devices, on_device(): lax.ppermute(near, 'zl', [((i + d) % 4, i) for i in range(4)])  9.29 us
    ppermute x2, waiting for transfers between devices, on_device(): up, down = (lax.ppermute(mine, line, from_z(s, s)) for s in (1, -1))  7.61 us
    ppermute x1, starting transfers between devices, on_device(): mates = lax.ppermute(cols, 'core', SWAP)  6.05 us
  transfers between devices with their start and end apart: 11, of which 6 were waited for; matrix products, arithmetic and copies ran while one was open for 0% of the time, Pallas kernels for 1%

profile of v9, /device:TPU:1, one launch (start us, length us, event | category | flops | bytes accessed | tf_op | source)
XLA Modules:
  0.0 167.8 jit_solution(331984912546062823)
XLA Ops:
  0.0 31.5 %all_gather.13.own = bf16[256,1024]{1,0:T(8,128)(2,1)S(1)} all-gather(bf16[64,1024]{1,0:T(8,128)(2,1)} %bitcast.10), channel_id=1, replica_groups=mesh['ylo'=2,'zh'=4,'zl'=4,'core'=2,'yhi'=2,'x'=4] {'zh'}, dimensions={0}, use_global_device_ids=true | all-gather | bytes 655360 | tf_op jit(solution)/shard_map/all_gather | solution.py:179
  31.5 3.2 %collective-permute-start = (bf16[256,1024]{1,0:T(8,128)(2,1)S(1)}, bf16[256,1024]{1,0:T(8,128)(2,1)S(1)}, u32[]{:S(2)}, u32[]{:S(2)}) collective-permute-start(bf16[256,1024]{1,0:T(8,128)(2,1)S(1)} %all_gather.13.own), channel_id=1, source_target_pairs={{0,256},{256,0},{1,257},{257,1},{2,258},{258,2},{3,259},{259,3},{4... | collective-permute-start | bytes 1572872 | tf_op jit(solution)/shard_map/ppermute | solution.py:180
  34.7 2.5 %collective-permute-start.3 = (bf16[64,1024]{1,0:T(8,128)(2,1)}, bf16[64,1024]{1,0:T(8,128)(2,1)S(1)}, u32[]{:S(2)}, u32[]{:S(2)}) collective-permute-start(bf16[64,1024]{1,0:T(8,128)(2,1)} %bitcast.11), channel_id=1, source_target_pairs={{48,0},{0,16},{16,32},{32,48},{49,1},{1,17},{17,33},{33,49},{50,2}... | collective-permute-start | bytes 393224 | tf_op jit(solution)/shard_map/ppermute | solution.py:182
  37.2 2.6 %collective-permute-start.2 = (bf16[64,1024]{1,0:T(8,128)(2,1)}, bf16[64,1024]{1,0:T(8,128)(2,1)S(1)}, u32[]{:S(2)}, u32[]{:S(2)}) collective-permute-start(bf16[64,1024]{1,0:T(8,128)(2,1)} %bitcast.12), channel_id=1, source_target_pairs={{32,0},{48,16},{0,32},{16,48},{33,1},{49,17},{1,33},{17,49},{34,2}... | collective-permute-start | bytes 393224 | tf_op jit(solution)/shard_map/ppermute | solution.py:182
  39.8 4.2 %collective-permute-start.1 = (bf16[64,1024]{1,0:T(8,128)(2,1)}, bf16[64,1024]{1,0:T(8,128)(2,1)S(1)}, u32[]{:S(2)}, u32[]{:S(2)}) collective-permute-start(bf16[64,1024]{1,0:T(8,128)(2,1)} %bitcast.13), channel_id=1, source_target_pairs={{16,0},{32,16},{48,32},{0,48},{17,1},{33,17},{49,33},{1,49},{18,2}... | collective-permute-start | bytes 393224 | tf_op jit(solution)/shard_map/ppermute | solution.py:182
  44.1 3.1 %collective-permute-done.2.r2 = bf16[64,1024]{1,0:T(8,128)(2,1)S(1)} collective-permute-done((bf16[64,1024]{1,0:T(8,128)(2,1)}, bf16[64,1024]{1,0:T(8,128)(2,1)S(1)}, u32[]{:S(2)}, u32[]{:S(2)}) %collective-permute-start.2) | collective-permute-done | bytes 131104 | tf_op jit(solution)/shard_map/ppermute | solution.py:182
  47.2 1.9 %collective-permute-done.1.r1 = bf16[64,1024]{1,0:T(8,128)(2,1)S(1)} collective-permute-done((bf16[64,1024]{1,0:T(8,128)(2,1)}, bf16[64,1024]{1,0:T(8,128)(2,1)S(1)}, u32[]{:S(2)}, u32[]{:S(2)}) %collective-permute-start.1) | collective-permute-done | bytes 131104 | tf_op jit(solution)/shard_map/ppermute | solution.py:182
  49.1 6.0 %collective-permute-start.4 = (bf16[2,256,1024]{2,1,0:T(8,128)(2,1)S(1)}, bf16[2,256,1024]{2,1,0:T(8,128)(2,1)S(1)}, u32[]{:S(2)}, u32[]{:S(2)}) collective-permute-start(bf16[2,256,1024]{2,1,0:T(8,128)(2,1)S(1)} %pair.1.cols), channel_id=1, source_target_pairs={{0,8},{8,0},{1,9},{9,1},{2,10},{10,2},{3,11},{11,3},{4,12},{12,4},... | collective-permute-start | bytes 3145736 | tf_op jit(solution)/shard_map/ppermute | solution.py:185
  55.2 1.9 %start.1 = (bf16[128,512]{1,0:T(8,128)(2,1)S(1)}, bf16[8,128,512]{2,1,0:T(8,128)(2,1)}, f32[128,512]{1,0:T(8,128)S(1)}) custom-call(s32[16,64]{1,0:T(8,128)S(1)} %bitcast.15, bf16[128,512]{1,0:T(8,128)(2,1)S(1)} %copy-done), custom_call_target="tpu_custom_call" | custom-call | tf_op jit(solution)/shard_map/start/pallas_call | solution.py:60
  58.6 17.9 %all_to_all.15 = bf16[8,128,256]{2,1,0:T(8,128)(2,1)S(1)} all-to-all(bf16[8,128,256]{2,1,0:T(8,128)(2,1)S(1)} %partial_gram.1), channel_id=1, replica_groups=mesh['ylo'=2,'zh'=4,'zl'=4,'core'=2,'yhi'=2,'x'=4] {'yhi','x'}, dimensions={0} | all-to-all | bytes 1048576 | tf_op jit(solution)/shard_map/all_to_all | solution.py:191
  76.6 3.8 %all-gather = bf16[256,256]{1,0:T(8,128)(2,1)S(1)} all-gather(bf16[128,256]{1,0:T(8,128)(2,1)S(1)} %multiply_convert_fusion), channel_id=2, replica_groups=mesh['ylo'=2,'zh'=4,'zl'=4,'core'=2,'yhi'=2,'x'=4] {'ylo'}, dimensions={0}, use_global_device_ids=true | all-gather | bytes 196608 | tf_op jit(solution)/shard_map/all_gather | solution.py:195
  80.4 21.3 %all-gather.1 = bf16[8,128,256]{2,1,0:T(8,128)(2,1)S(1)} all-gather(bf16[2,128,256]{2,1,0:T(8,128)(2,1)S(1)} %bitcast.16), channel_id=3, replica_groups=mesh['ylo'=2,'zh'=4,'zl'=4,'core'=2,'yhi'=2,'x'=4] {'zh'}, dimensions={0}, use_global_device_ids=true | all-gather | bytes 655360 | tf_op jit(solution)/shard_map/all_gather | solution.py:195
  101.7 3.6 %all-to-all-start.1 = ((bf16[8,128,512]{2,1,0:T(8,128)(2,1)}), bf16[8,128,512]{2,1,0:T(8,128)(2,1)S(1)}, u32[]{:S(2)}, u32[]{:S(2)}) async-start(bf16[8,128,512]{2,1,0:T(8,128)(2,1)} %get-tuple-element.30), calls=%async_computation.1 | async-start | bytes 2097152 | tf_op jit(solution)/shard_map/all_to_all | solution.py:201
  105.3 2.5 %collective-permute-start.5 = (bf16[4,128,256]{2,1,0:T(8,128)(2,1)S(1)}, bf16[4,128,256]{2,1,0:T(8,128)(2,1)S(1)}, u32[]{:S(2)}, u32[]{:S(2)}) collective-permute-start(bf16[4,128,256]{2,1,0:T(8,128)(2,1)S(1)} %dynamic-slice_bitcast_fusion), channel_id=1, source_target_pairs={{32,0},{232,8},{48,16},{248,24},{64,32},{8,40},{80,48},{24,56},{96... | collective-permute-start | bytes 786440 | tf_op jit(solution)/shard_map/ppermute | solution.py:197
  107.8 7.4 %collective-permute-start.8 = (bf16[4,2,128,256]{3,2,1,0:T(8,128)(2,1)S(1)}, bf16[4,2,128,256]{3,2,1,0:T(8,128)(2,1)S(1)}, u32[]{:S(2)}, u32[]{:S(2)}) collective-permute-start(bf16[4,2,128,256]{3,2,1,0:T(8,128)(2,1)S(1)} %bitcast.7), channel_id=1, source_target_pairs={{240,0},{248,8},{0,16},{8,24},{16,32},{24,40},{32,48},{40,56},{48,... | collective-permute-start | bytes 1572872 | tf_op jit(solution)/shard_map/ppermute | solution.py:198
  115.3 1.9 %collective-permute-start.7 = (bf16[4,2,128,256]{3,2,1,0:T(8,128)(2,1)S(1)}, bf16[4,2,128,256]{3,2,1,0:T(8,128)(2,1)S(1)}, u32[]{:S(2)}, u32[]{:S(2)}) collective-permute-start(bf16[4,2,128,256]{3,2,1,0:T(8,128)(2,1)S(1)} %bitcast.8), channel_id=1, source_target_pairs={{16,0},{24,8},{32,16},{40,24},{48,32},{56,40},{64,48},{72,56},{80,... | collective-permute-start | bytes 1572872 | tf_op jit(solution)/shard_map/ppermute | solution.py:198
  117.2 2.6 %collective-permute-start.6 = (bf16[4,128,256]{2,1,0:T(8,128)(2,1)S(1)}, bf16[4,128,256]{2,1,0:T(8,128)(2,1)S(1)}, u32[]{:S(2)}, u32[]{:S(2)}) collective-permute-start(bf16[4,128,256]{2,1,0:T(8,128)(2,1)S(1)} %collective-permute-done.5.two), channel_id=1, source_target_pairs={{0,256},{256,0},{1,257},{257,1},{2,258},{258,2},{3,259},{259,3},{4... | collective-permute-start | bytes 786440 | tf_op jit(solution)/shard_map/ppermute | solution.py:199
  119.8 5.0 %collective-permute-done.6.two_far = bf16[4,128,256]{2,1,0:T(8,128)(2,1)S(1)} collective-permute-done((bf16[4,128,256]{2,1,0:T(8,128)(2,1)S(1)}, bf16[4,128,256]{2,1,0:T(8,128)(2,1)S(1)}, u32[]{:S(2)}, u32[]{:S(2)}) %collective-permute-start.6) | collective-permute-done | bytes 262176 | tf_op jit(solution)/shard_map/ppermute | solution.py:199
  126.1 6.3 %collective-permute-done.7.up = bf16[4,2,128,256]{3,2,1,0:T(8,128)(2,1)S(1)} collective-permute-done((bf16[4,2,128,256]{3,2,1,0:T(8,128)(2,1)S(1)}, bf16[4,2,128,256]{3,2,1,0:T(8,128)(2,1)S(1)}, u32[]{:S(2)}, u32[]{:S(2)}) %collective-permute-start.7) | collective-permute-done | bytes 524320 | tf_op jit(solution)/shard_map/ppermute | solution.py:198
  132.6 4.9 %collective-permute-start.9 = (bf16[4,4,2,128,256]{4,3,2,1,0:T(8,128)(2,1)S(1)}, bf16[4,4,2,128,256]{4,3,2,1,0:T(8,128)(2,1)S(1)}, u32[]{:S(2)}, u32[]{:S(2)}) collective-permute-start(bf16[4,4,2,128,256]{4,3,2,1,0:T(8,128)(2,1)S(1)} %classes.1.refs_0_), channel_id=1, source_target_pairs={{0,8},{8,0},{1,9},{9,1},{2,10},{10,2},{3,11},{11,3},{4,12},{12,4},... | collective-permute-start | bytes 6291464 | tf_op jit(solution)/shard_map/ppermute | solution.py:204
  137.5 3.8 %collective-permute-done.9.refs_1_ = bf16[4,4,2,128,256]{4,3,2,1,0:T(8,128)(2,1)S(1)} collective-permute-done((bf16[4,4,2,128,256]{4,3,2,1,0:T(8,128)(2,1)S(1)}, bf16[4,4,2,128,256]{4,3,2,1,0:T(8,128)(2,1)S(1)}, u32[]{:S(2)}, u32[]{:S(2)}) %collective-permute-start.9) | collective-permute-done | bytes 2097184 | tf_op jit(solution)/shard_map/ppermute | solution.py:204
  141.2 1.4 first_step.1
  142.6 23.2 %all_to_all.16.diffs = bf16[8,128,512]{2,1,0:T(8,128)(2,1)S(1)} all-to-all(bf16[8,128,512]{2,1,0:T(8,128)(2,1)S(1)} %get-tuple-element.35), channel_id=1, replica_groups=mesh['ylo'=2,'zh'=4,'zl'=4,'core'=2,'yhi'=2,'x'=4] {'yhi','x'}, dimensions={0} | all-to-all | bytes 2097152 | tf_op jit(solution)/shard_map/all_to_all | solution.py:207
  165.9 2.0 %last_step.1 = bf16[128,512]{1,0:T(8,128)(2,1)} custom-call(bf16[8,128,512]{2,1,0:T(8,128)(2,1)S(1)} %all_to_all.16.diffs, bf16[4,4,2,128,256]{4,3,2,1,0:T(8,128)(2,1)S(1)} %classes.1.refs_0_, bf16[4,4,2,128,256]{4,3,2,1,0:T(8,128)(2,1)S(1)} %collective-permute-done.9.refs_1_, bf16[128,512]{1,0:T(8,128)(2,1)S(1)} %get-tuple-element.36.refs_2_, ...), custom_call_target="tpu_custom_call" | custom-call | flops 536870912 | bytes 3145728 | tf_op jit(solution)/shard_map/last_step/pallas_call | solution.py:132
  (22 shorter events, 3.1 us)
Async XLA Ops:
  0.0 57.8 %copy-start.1 = (bf16[1024,64]{0,1:T(8,128)(2,1)S(1)}, bf16[1024,64]{0,1:T(8,128)(2,1)}, u32[]{:S(2)}) copy-start(bf16[1024,64]{0,1:T(8,128)(2,1)} %param.3) | copy-start | bytes 393220
  0.0 55.2 %copy-start = (bf16[128,512]{1,0:T(8,128)(2,1)S(1)}, bf16[128,512]{1,0:T(8,128)(2,1)}, u32[]{:S(2)}) copy-start(bf16[128,512]{1,0:T(8,128)(2,1)} %refs_3_.1) | copy-start | bytes 393220
  0.0 55.2 %copy-start.4 = (s32[64,16]{0,1:T(8,128)S(1)}, s32[64,16]{0,1:T(8,128)}, u32[]{:S(2)}) copy-start(s32[64,16]{0,1:T(8,128)} %param.5) | copy-start | bytes 12292
  31.5 17.5 %collective-permute-start = (bf16[256,1024]{1,0:T(8,128)(2,1)S(1)}, bf16[256,1024]{1,0:T(8,128)(2,1)S(1)}, u32[]{:S(2)}, u32[]{:S(2)}) collective-permute-start(bf16[256,1024]{1,0:T(8,128)(2,1)S(1)} %all_gather.13.own), channel_id=1, source_target_pairs={{0,256},{256,0},{1,257},{257,1},{2,258},{258,2},{3,259},{259,3},{4... | collective-permute-start | bytes 1572872 | tf_op jit(solution)/shard_map/ppermute | solution.py:180
  34.7 9.3 %collective-permute-start.3 = (bf16[64,1024]{1,0:T(8,128)(2,1)}, bf16[64,1024]{1,0:T(8,128)(2,1)S(1)}, u32[]{:S(2)}, u32[]{:S(2)}) collective-permute-start(bf16[64,1024]{1,0:T(8,128)(2,1)} %bitcast.11), channel_id=1, source_target_pairs={{48,0},{0,16},{16,32},{32,48},{49,1},{1,17},{17,33},{33,49},{50,2}... | collective-permute-start | bytes 393224 | tf_op jit(solution)/shard_map/ppermute | solution.py:182
  37.2 9.9 %collective-permute-start.2 = (bf16[64,1024]{1,0:T(8,128)(2,1)}, bf16[64,1024]{1,0:T(8,128)(2,1)S(1)}, u32[]{:S(2)}, u32[]{:S(2)}) collective-permute-start(bf16[64,1024]{1,0:T(8,128)(2,1)} %bitcast.12), channel_id=1, source_target_pairs={{32,0},{48,16},{0,32},{16,48},{33,1},{49,17},{1,33},{17,49},{34,2}... | collective-permute-start | bytes 393224 | tf_op jit(solution)/shard_map/ppermute | solution.py:182
  39.8 9.2 %collective-permute-start.1 = (bf16[64,1024]{1,0:T(8,128)(2,1)}, bf16[64,1024]{1,0:T(8,128)(2,1)S(1)}, u32[]{:S(2)}, u32[]{:S(2)}) collective-permute-start(bf16[64,1024]{1,0:T(8,128)(2,1)} %bitcast.13), channel_id=1, source_target_pairs={{16,0},{32,16},{48,32},{0,48},{17,1},{33,17},{49,33},{1,49},{18,2}... | collective-permute-start | bytes 393224 | tf_op jit(solution)/shard_map/ppermute | solution.py:182
  49.1 8.6 %collective-permute-start.4 = (bf16[2,256,1024]{2,1,0:T(8,128)(2,1)S(1)}, bf16[2,256,1024]{2,1,0:T(8,128)(2,1)S(1)}, u32[]{:S(2)}, u32[]{:S(2)}) collective-permute-start(bf16[2,256,1024]{2,1,0:T(8,128)(2,1)S(1)} %pair.1.cols), channel_id=1, source_target_pairs={{0,8},{8,0},{1,9},{9,1},{2,10},{10,2},{3,11},{11,3},{4,12},{12,4},... | collective-permute-start | bytes 3145736 | tf_op jit(solution)/shard_map/ppermute | solution.py:185
  57.1 0.7 copy-start.2
  101.7 23.1 %all-to-all-start.1 = ((bf16[8,128,512]{2,1,0:T(8,128)(2,1)}), bf16[8,128,512]{2,1,0:T(8,128)(2,1)S(1)}, u32[]{:S(2)}, u32[]{:S(2)}) async-start(bf16[8,128,512]{2,1,0:T(8,128)(2,1)} %get-tuple-element.30), calls=%async_computation.1 | async-start | bytes 2097152 | tf_op jit(solution)/shard_map/all_to_all | solution.py:201
  105.3 11.9 %collective-permute-start.5 = (bf16[4,128,256]{2,1,0:T(8,128)(2,1)S(1)}, bf16[4,128,256]{2,1,0:T(8,128)(2,1)S(1)}, u32[]{:S(2)}, u32[]{:S(2)}) collective-permute-start(bf16[4,128,256]{2,1,0:T(8,128)(2,1)S(1)} %dynamic-slice_bitcast_fusion), channel_id=1, source_target_pairs={{32,0},{232,8},{48,16},{248,24},{64,32},{8,40},{80,48},{24,56},{96... | collective-permute-start | bytes 786440 | tf_op jit(solution)/shard_map/ppermute | solution.py:197
  107.8 18.3 %collective-permute-start.8 = (bf16[4,2,128,256]{3,2,1,0:T(8,128)(2,1)S(1)}, bf16[4,2,128,256]{3,2,1,0:T(8,128)(2,1)S(1)}, u32[]{:S(2)}, u32[]{:S(2)}) collective-permute-start(bf16[4,2,128,256]{3,2,1,0:T(8,128)(2,1)S(1)} %bitcast.7), channel_id=1, source_target_pairs={{240,0},{248,8},{0,16},{8,24},{16,32},{24,40},{32,48},{40,56},{48,... | collective-permute-start | bytes 1572872 | tf_op jit(solution)/shard_map/ppermute | solution.py:198
  115.3 17.1 %collective-permute-start.7 = (bf16[4,2,128,256]{3,2,1,0:T(8,128)(2,1)S(1)}, bf16[4,2,128,256]{3,2,1,0:T(8,128)(2,1)S(1)}, u32[]{:S(2)}, u32[]{:S(2)}) collective-permute-start(bf16[4,2,128,256]{3,2,1,0:T(8,128)(2,1)S(1)} %bitcast.8), channel_id=1, source_target_pairs={{16,0},{24,8},{32,16},{40,24},{48,32},{56,40},{64,48},{72,56},{80,... | collective-permute-start | bytes 1572872 | tf_op jit(solution)/shard_map/ppermute | solution.py:198
  117.2 7.6 %collective-permute-start.6 = (bf16[4,128,256]{2,1,0:T(8,128)(2,1)S(1)}, bf16[4,128,256]{2,1,0:T(8,128)(2,1)S(1)}, u32[]{:S(2)}, u32[]{:S(2)}) collective-permute-start(bf16[4,128,256]{2,1,0:T(8,128)(2,1)S(1)} %collective-permute-done.5.two), channel_id=1, source_target_pairs={{0,256},{256,0},{1,257},{257,1},{2,258},{258,2},{3,259},{259,3},{4... | collective-permute-start | bytes 786440 | tf_op jit(solution)/shard_map/ppermute | solution.py:199
  124.8 16.4 %copy-start.3 = (bf16[128,512]{1,0:T(8,128)(2,1)S(1)}, bf16[128,512]{1,0:T(8,128)(2,1)}, u32[]{:S(2)}) copy-start(bf16[128,512]{1,0:T(8,128)(2,1)} %copy-done.2) | copy-start | bytes 393220
  132.6 8.6 %collective-permute-start.9 = (bf16[4,4,2,128,256]{4,3,2,1,0:T(8,128)(2,1)S(1)}, bf16[4,4,2,128,256]{4,3,2,1,0:T(8,128)(2,1)S(1)}, u32[]{:S(2)}, u32[]{:S(2)}) collective-permute-start(bf16[4,4,2,128,256]{4,3,2,1,0:T(8,128)(2,1)S(1)} %classes.1.refs_0_), channel_id=1, source_target_pairs={{0,8},{8,0},{1,9},{9,1},{2,10},{10,2},{3,11},{11,3},{4,12},{12,4},... | collective-permute-start | bytes 6291464 | tf_op jit(solution)/shard_map/ppermute | solution.py:204

commit v10 on v9

--- a/solution.py
+++ b/solution.py
@@ -71,10 +71,11 @@
     )(keep_blocks.T, base)
 
 
-def partial_gram_kernel(r0, r1, r2, r3, cols, mates, out, rows):
-    ylo, zl, core = (lax.axis_index(a) for a in ("ylo", "zl", "core"))
+def partial_gram_kernel(r1, r2, r3, cols, mates, out, rows):
+    ylo, zh, zl, core = (lax.axis_index(a) for a in TOK)
     chunk = BLOCK // 2
-    for d, part in enumerate((r0, r1, r2, r3)):
+    mine = cols[0, pl.ds(pl.multiple_of(zh * chunk, chunk), chunk), :]
+    for d, part in enumerate((mine, r1, r2, r3)):
         place = lax.rem(zl + d, 4) * chunk
         rows[pl.ds(pl.multiple_of(place, chunk), chunk), :] = part[...]
     for dy, dc, part in ((0, 0, cols), (1, 0, cols), (0, 1, mates), (1, 1, mates)):
@@ -89,7 +90,7 @@
     return pl.pallas_call(
         partial_gram_kernel,
         out_shape=jax.ShapeDtypeStruct((8, BLOCK, k), jnp.bfloat16),
-        in_specs=[vmem()] * 6,
+        in_specs=[vmem()] * 5,
         out_specs=vmem(),
         scratch_shapes=[pltpu.VMEM((k, depth), jnp.bfloat16)],
         name="partial_gram",
@@ -179,8 +180,8 @@
     own = lax.all_gather(feats, "zh", axis=0, tiled=True)
     other = lax.ppermute(own, "ylo", SWAP)
     near = lax.optimization_barrier((feats, own))[0]
-    rows = [feats] + [lax.ppermute(near, "zl", [((i + d) % 4, i) for i in range(4)]) for d in (1, 2, 3)]
-    other, *rows[1:] = lax.optimization_barrier((other, *rows[1:]))
+    rows = [lax.ppermute(near, "zl", [((i + d) % 4, i) for i in range(4)]) for d in (1, 2, 3)]
+    other, *rows = lax.optimization_barrier((other, *rows))
     cols = pack(pair_kernel, "pair", own, other)
     mates = lax.ppermute(cols, "core", SWAP)
 
@@ -188,7 +189,9 @@
     weight, diff, keep = start(keep_blocks, base_weight)
     diff, mates = lax.optimization_barrier((diff, mates))
     term = partial_gram(rows, cols, mates)
+    diff, term = lax.optimization_barrier((diff, term))
     terms = lax.all_to_all(term, ROW, 0, 0, tiled=True)
+    diffs = lax.all_to_all(diff, ROW, 0, 0, tiled=True)
     gram = (jnp.sum(terms.astype(jnp.float32), axis=0) / tokens).astype(jnp.bfloat16)
 
     line = ("zh", "zl", "core")
@@ -197,8 +200,6 @@
     two = lax.ppermute(half, line, from_z(2, -2))
     up, down = (lax.ppermute(mine, line, from_z(s, s)) for s in (1, -1))
     two_far = lax.ppermute(two, "ylo", SWAP)
-    diff = lax.optimization_barrier((diff, mine))[0]
-    diffs = lax.all_to_all(diff, ROW, 0, 0, tiled=True)
     diffs, two_far = lax.optimization_barrier((diffs, two_far))
     packed = pack(classes_kernel, "classes", mine, up, down, two, two_far)
     grams = (packed, lax.ppermute(packed, "core", SWAP))

time: 168 us -> 178 us (1.060)
  waiting for transfers between devices: 21.4 us -> 30.8 us
  blocking collectives: 97.8 us -> 93.4 us
  starting transfers between devices: 41.4 us -> 45.5 us
    all_to_all x1 -> x0, blocking collectives: 17.9 us -> none  [on_device(): terms = lax.all_to_all(term, ROW, 0, 0, tiled=True)]
    all_to_all x0 -> x1, waiting for transfers between devices: none -> 11.8 us  [on_device(): terms = lax.all_to_all(term, ROW, 0, 0, tiled=True)]
    all_gather x2, blocking collectives: 25.1 us -> 33.7 us  [on_device(): mine = lax.all_gather(lax.all_gather(gram, 'ylo', axis=0), 'zh', axis=0)]
    all_to_all x0 -> x1, starting transfers between devices: none -> 6.38 us  [on_device(): terms = lax.all_to_all(term, ROW, 0, 0, tiled=True)]
    all_to_all x1, blocking collectives: 23.2 us -> 28.2 us  [on_device(): diffs = lax.all_to_all(sent, ROW, 0, 0, tiled=True)]
    ppermute x2, waiting for transfers between devices: 7.61 us -> 4.75 us  [on_device(): up, down = (lax.ppermute(mine, line, from_z(s, s)) for s in (1, -1))]
  transfers between devices with their start and end apart: 11 -> 12, of which waited for: 6 -> 6; matrix products, arithmetic and copies ran while one was open for 0% -> 0% of each run, Pallas kernels for 1% -> 1%
where the time goes in v10:
time: 178 us
  blocking collectives  93.4 us (52%)
  starting transfers between devices  45.5 us (26%)
  waiting for transfers between devices  30.8 us (17%)
  Pallas kernels  7.07 us (4%)
    all_gather x2, blocking collectives, on_device(): mine = lax.all_gather(lax.all_gather(gram, 'ylo', axis=0), 'zh', axis=0)  33.7 us
    all_gather x1, blocking collectives, on_device(): own = lax.all_gather(feats, 'zh', axis=0, tiled=True)  31.5 us
    all_to_all x1, blocking collectives, on_device(): diffs = lax.all_to_all(sent, ROW, 0, 0, tiled=True)  28.2 us
    all_to_all x1, waiting for transfers between devices, on_device(): terms = lax.all_to_all(term, ROW, 0, 0, tiled=True)  11.8 us
    ppermute x3, starting transfers between devices, on_device(): lax.ppermute(near, 'zl', [((i + d) % 4, i) for i in range(4)])  9.29 us
    ppermute x2, starting transfers between devices, on_device(): up, down = (lax.ppermute(mine, line, from_z(s, s)) for s in (1, -1))  9.16 us
    all_to_all x1, starting transfers between devices, on_device(): terms = lax.all_to_all(term, ROW, 0, 0, tiled=True)  6.38 us
    ppermute x1, starting transfers between devices, on_device(): mates = lax.ppermute(cols, 'core', SWAP)  6.05 us
  transfers between devices with their start and end apart: 12, of which 6 were waited for; matrix products, arithmetic and copies ran while one was open for 0% of the time, Pallas kernels for 1%

profile of v10, /device:TPU:1, one launch (start us, length us, event | category | flops | bytes accessed | tf_op | source)
XLA Modules:
  0.0 177.8 jit_solution(10027833307486436034)
XLA Ops:
  0.0 31.5 %all_gather.13.own = bf16[256,1024]{1,0:T(8,128)(2,1)S(1)} all-gather(bf16[64,1024]{1,0:T(8,128)(2,1)} %bitcast.12), channel_id=1, replica_groups=mesh['ylo'=2,'zh'=4,'zl'=4,'core'=2,'yhi'=2,'x'=4] {'zh'}, dimensions={0}, use_global_device_ids=true | all-gather | bytes 655360 | tf_op jit(solution)/shard_map/all_gather | solution.py:180
  31.5 3.2 %collective-permute-start = (bf16[256,1024]{1,0:T(8,128)(2,1)S(1)}, bf16[256,1024]{1,0:T(8,128)(2,1)S(1)}, u32[]{:S(2)}, u32[]{:S(2)}) collective-permute-start(bf16[256,1024]{1,0:T(8,128)(2,1)S(1)} %all_gather.13.own), channel_id=1, source_target_pairs={{0,256},{256,0},{1,257},{257,1},{2,258},{258,2},{3,259},{259,3},{4... | collective-permute-start | bytes 1572872 | tf_op jit(solution)/shard_map/ppermute | solution.py:181
  34.7 2.5 %collective-permute-start.3 = (bf16[64,1024]{1,0:T(8,128)(2,1)}, bf16[64,1024]{1,0:T(8,128)(2,1)S(1)}, u32[]{:S(2)}, u32[]{:S(2)}) collective-permute-start(bf16[64,1024]{1,0:T(8,128)(2,1)} %bitcast.13), channel_id=1, source_target_pairs={{48,0},{0,16},{16,32},{32,48},{49,1},{1,17},{17,33},{33,49},{50,2}... | collective-permute-start | bytes 393224 | tf_op jit(solution)/shard_map/ppermute | solution.py:183
  37.2 2.6 %collective-permute-start.2 = (bf16[64,1024]{1,0:T(8,128)(2,1)}, bf16[64,1024]{1,0:T(8,128)(2,1)S(1)}, u32[]{:S(2)}, u32[]{:S(2)}) collective-permute-start(bf16[64,1024]{1,0:T(8,128)(2,1)} %bitcast.14), channel_id=1, source_target_pairs={{32,0},{48,16},{0,32},{16,48},{33,1},{49,17},{1,33},{17,49},{34,2}... | collective-permute-start | bytes 393224 | tf_op jit(solution)/shard_map/ppermute | solution.py:183
  39.8 4.2 %collective-permute-start.1 = (bf16[64,1024]{1,0:T(8,128)(2,1)}, bf16[64,1024]{1,0:T(8,128)(2,1)S(1)}, u32[]{:S(2)}, u32[]{:S(2)}) collective-permute-start(bf16[64,1024]{1,0:T(8,128)(2,1)} %bitcast.15), channel_id=1, source_target_pairs={{16,0},{32,16},{48,32},{0,48},{17,1},{33,17},{49,33},{1,49},{18,2}... | collective-permute-start | bytes 393224 | tf_op jit(solution)/shard_map/ppermute | solution.py:183
  44.0 3.1 %collective-permute-done.2.r2 = bf16[64,1024]{1,0:T(8,128)(2,1)S(1)} collective-permute-done((bf16[64,1024]{1,0:T(8,128)(2,1)}, bf16[64,1024]{1,0:T(8,128)(2,1)S(1)}, u32[]{:S(2)}, u32[]{:S(2)}) %collective-permute-start.2) | collective-permute-done | bytes 131104 | tf_op jit(solution)/shard_map/ppermute | solution.py:183
  47.1 1.9 %collective-permute-done.1.r1 = bf16[64,1024]{1,0:T(8,128)(2,1)S(1)} collective-permute-done((bf16[64,1024]{1,0:T(8,128)(2,1)}, bf16[64,1024]{1,0:T(8,128)(2,1)S(1)}, u32[]{:S(2)}, u32[]{:S(2)}) %collective-permute-start.1) | collective-permute-done | bytes 131104 | tf_op jit(solution)/shard_map/ppermute | solution.py:183
  49.1 6.0 %collective-permute-start.4 = (bf16[2,256,1024]{2,1,0:T(8,128)(2,1)S(1)}, bf16[2,256,1024]{2,1,0:T(8,128)(2,1)S(1)}, u32[]{:S(2)}, u32[]{:S(2)}) collective-permute-start(bf16[2,256,1024]{2,1,0:T(8,128)(2,1)S(1)} %pair.1.cols), channel_id=1, source_target_pairs={{0,8},{8,0},{1,9},{9,1},{2,10},{10,2},{3,11},{11,3},{4,12},{12,4},... | collective-permute-start | bytes 3145736 | tf_op jit(solution)/shard_map/ppermute | solution.py:186
  55.2 1.9 %start.1 = (bf16[128,512]{1,0:T(8,128)(2,1)S(1)}, bf16[8,128,512]{2,1,0:T(8,128)(2,1)}, f32[128,512]{1,0:T(8,128)S(1)}) custom-call(s32[16,64]{1,0:T(8,128)S(1)} %bitcast.10, bf16[128,512]{1,0:T(8,128)(2,1)S(1)} %copy-done), custom_call_target="tpu_custom_call" | custom-call | tf_op jit(solution)/shard_map/start/pallas_call | solution.py:60
  59.4 6.4 %all-to-all-start.1 = ((bf16[8,128,256]{2,1,0:T(8,128)(2,1)}), bf16[8,128,256]{2,1,0:T(8,128)(2,1)S(1)}, u32[]{:S(2)}, u32[]{:S(2)}) async-start(bf16[8,128,256]{2,1,0:T(8,128)(2,1)} %partial_gram.1), calls=%async_computation.1 | async-start | bytes 1048576 | tf_op jit(solution)/shard_map/all_to_all | solution.py:193
  65.7 11.8 %all-to-all-done.1 = bf16[8,128,256]{2,1,0:T(8,128)(2,1)S(1)} async-done(((bf16[8,128,256]{2,1,0:T(8,128)(2,1)}), bf16[8,128,256]{2,1,0:T(8,128)(2,1)S(1)}, u32[]{:S(2)}, u32[]{:S(2)}) %all-to-all-start.1) | async-done | bytes 524320 | tf_op jit(solution)/shard_map/all_to_all | solution.py:193
  77.5 3.6 %all-to-all-start = ((bf16[8,128,512]{2,1,0:T(8,128)(2,1)}), bf16[8,128,512]{2,1,0:T(8,128)(2,1)S(1)}, u32[]{:S(2)}, u32[]{:S(2)}) async-start(bf16[8,128,512]{2,1,0:T(8,128)(2,1)} %get-tuple-element.31), calls=%async_computation | async-start | bytes 2097152 | tf_op jit(solution)/shard_map/all_to_all | solution.py:194
  81.2 10.2 %all-gather = bf16[256,256]{1,0:T(8,128)(2,1)S(1)} all-gather(bf16[128,256]{1,0:T(8,128)(2,1)S(1)} %multiply_convert_fusion), channel_id=2, replica_groups=mesh['ylo'=2,'zh'=4,'zl'=4,'core'=2,'yhi'=2,'x'=4] {'ylo'}, dimensions={0}, use_global_device_ids=true | all-gather | bytes 196608 | tf_op jit(solution)/shard_map/all_gather | solution.py:198
  91.4 23.5 %all-gather.1 = bf16[8,128,256]{2,1,0:T(8,128)(2,1)S(1)} all-gather(bf16[2,128,256]{2,1,0:T(8,128)(2,1)S(1)} %bitcast.11), channel_id=3, replica_groups=mesh['ylo'=2,'zh'=4,'zl'=4,'core'=2,'yhi'=2,'x'=4] {'zh'}, dimensions={0}, use_global_device_ids=true | all-gather | bytes 655360 | tf_op jit(solution)/shard_map/all_gather | solution.py:198
  114.9 1.9 %collective-permute-start.5 = (bf16[4,128,256]{2,1,0:T(8,128)(2,1)S(1)}, bf16[4,128,256]{2,1,0:T(8,128)(2,1)S(1)}, u32[]{:S(2)}, u32[]{:S(2)}) collective-permute-start(bf16[4,128,256]{2,1,0:T(8,128)(2,1)S(1)} %dynamic-slice_bitcast_fusion), channel_id=1, source_target_pairs={{32,0},{232,8},{48,16},{248,24},{64,32},{8,40},{80,48},{24,56},{96... | collective-permute-start | bytes 786440 | tf_op jit(solution)/shard_map/ppermute | solution.py:200
  116.9 7.2 %collective-permute-start.8 = (bf16[4,2,128,256]{3,2,1,0:T(8,128)(2,1)S(1)}, bf16[4,2,128,256]{3,2,1,0:T(8,128)(2,1)S(1)}, u32[]{:S(2)}, u32[]{:S(2)}) collective-permute-start(bf16[4,2,128,256]{3,2,1,0:T(8,128)(2,1)S(1)} %bitcast.7), channel_id=1, source_target_pairs={{240,0},{248,8},{0,16},{8,24},{16,32},{24,40},{32,48},{40,56},{48,... | collective-permute-start | bytes 1572872 | tf_op jit(solution)/shard_map/ppermute | solution.py:201
  124.1 1.9 %collective-permute-start.7 = (bf16[4,2,128,256]{3,2,1,0:T(8,128)(2,1)S(1)}, bf16[4,2,128,256]{3,2,1,0:T(8,128)(2,1)S(1)}, u32[]{:S(2)}, u32[]{:S(2)}) collective-permute-start(bf16[4,2,128,256]{3,2,1,0:T(8,128)(2,1)S(1)} %bitcast.8), channel_id=1, source_target_pairs={{16,0},{24,8},{32,16},{40,24},{48,32},{56,40},{64,48},{72,56},{80,... | collective-permute-start | bytes 1572872 | tf_op jit(solution)/shard_map/ppermute | solution.py:201
  126.0 1.9 %collective-permute-start.6 = (bf16[4,128,256]{2,1,0:T(8,128)(2,1)S(1)}, bf16[4,128,256]{2,1,0:T(8,128)(2,1)S(1)}, u32[]{:S(2)}, u32[]{:S(2)}) collective-permute-start(bf16[4,128,256]{2,1,0:T(8,128)(2,1)S(1)} %collective-permute-done.5.two), channel_id=1, source_target_pairs={{0,256},{256,0},{1,257},{257,1},{2,258},{258,2},{3,259},{259,3},{4... | collective-permute-start | bytes 786440 | tf_op jit(solution)/shard_map/ppermute | solution.py:202
  128.0 5.5 %collective-permute-done.6.two_far = bf16[4,128,256]{2,1,0:T(8,128)(2,1)S(1)} collective-permute-done((bf16[4,128,256]{2,1,0:T(8,128)(2,1)S(1)}, bf16[4,128,256]{2,1,0:T(8,128)(2,1)S(1)}, u32[]{:S(2)}, u32[]{:S(2)}) %collective-permute-start.6) | collective-permute-done | bytes 262176 | tf_op jit(solution)/shard_map/ppermute | solution.py:202
  133.5 4.7 %collective-permute-done.8.down = bf16[4,2,128,256]{3,2,1,0:T(8,128)(2,1)S(1)} collective-permute-done((bf16[4,2,128,256]{3,2,1,0:T(8,128)(2,1)S(1)}, bf16[4,2,128,256]{3,2,1,0:T(8,128)(2,1)S(1)}, u32[]{:S(2)}, u32[]{:S(2)}) %collective-permute-start.8) | collective-permute-done | bytes 524320 | tf_op jit(solution)/shard_map/ppermute | solution.py:201
  138.3 4.1 %collective-permute-start.9 = (bf16[4,4,2,128,256]{4,3,2,1,0:T(8,128)(2,1)S(1)}, bf16[4,4,2,128,256]{4,3,2,1,0:T(8,128)(2,1)S(1)}, u32[]{:S(2)}, u32[]{:S(2)}) collective-permute-start(bf16[4,4,2,128,256]{4,3,2,1,0:T(8,128)(2,1)S(1)} %classes.1.refs_0_), channel_id=1, source_target_pairs={{0,8},{8,0},{1,9},{9,1},{2,10},{10,2},{3,11},{11,3},{4,12},{12,4},... | collective-permute-start | bytes 6291464 | tf_op jit(solution)/shard_map/ppermute | solution.py:205
  142.4 3.8 %collective-permute-done.9.refs_1_ = bf16[4,4,2,128,256]{4,3,2,1,0:T(8,128)(2,1)S(1)} collective-permute-done((bf16[4,4,2,128,256]{4,3,2,1,0:T(8,128)(2,1)S(1)}, bf16[4,4,2,128,256]{4,3,2,1,0:T(8,128)(2,1)S(1)}, u32[]{:S(2)}, u32[]{:S(2)}) %collective-permute-start.9) | collective-permute-done | bytes 2097184 | tf_op jit(solution)/shard_map/ppermute | solution.py:205
  147.6 28.2 %all_to_all.15.diffs = bf16[8,128,512]{2,1,0:T(8,128)(2,1)S(1)} all-to-all(bf16[8,128,512]{2,1,0:T(8,128)(2,1)S(1)} %get-tuple-element.37), channel_id=1, replica_groups=mesh['ylo'=2,'zh'=4,'zl'=4,'core'=2,'yhi'=2,'x'=4] {'yhi','x'}, dimensions={0} | all-to-all | bytes 2097152 | tf_op jit(solution)/shard_map/all_to_all | solution.py:208
  175.8 2.0 %last_step.1 = bf16[128,512]{1,0:T(8,128)(2,1)} custom-call(bf16[8,128,512]{2,1,0:T(8,128)(2,1)S(1)} %all_to_all.15.diffs, bf16[4,4,2,128,256]{4,3,2,1,0:T(8,128)(2,1)S(1)} %classes.1.refs_0_, bf16[4,4,2,128,256]{4,3,2,1,0:T(8,128)(2,1)S(1)} %collective-permute-done.9.refs_1_, bf16[128,512]{1,0:T(8,128)(2,1)S(1)} %get-tuple-element.38.refs_2_, ...), custom_call_target="tpu_custom_call" | custom-call | flops 536870912 | bytes 3145728 | tf_op jit(solution)/shard_map/last_step/pallas_call | solution.py:133
  (21 shorter events, 4.0 us)
Async XLA Ops:
  0.0 55.2 %copy-start = (bf16[128,512]{1,0:T(8,128)(2,1)S(1)}, bf16[128,512]{1,0:T(8,128)(2,1)}, u32[]{:S(2)}) copy-start(bf16[128,512]{1,0:T(8,128)(2,1)} %refs_3_.1) | copy-start | bytes 393220
  0.0 55.2 %copy-start.3 = (s32[64,16]{0,1:T(8,128)S(1)}, s32[64,16]{0,1:T(8,128)}, u32[]{:S(2)}) copy-start(s32[64,16]{0,1:T(8,128)} %param.5) | copy-start | bytes 12292
  31.5 17.5 %collective-permute-start = (bf16[256,1024]{1,0:T(8,128)(2,1)S(1)}, bf16[256,1024]{1,0:T(8,128)(2,1)S(1)}, u32[]{:S(2)}, u32[]{:S(2)}) collective-permute-start(bf16[256,1024]{1,0:T(8,128)(2,1)S(1)} %all_gather.13.own), channel_id=1, source_target_pairs={{0,256},{256,0},{1,257},{257,1},{2,258},{258,2},{3,259},{259,3},{4... | collective-permute-start | bytes 1572872 | tf_op jit(solution)/shard_map/ppermute | solution.py:181
  34.7 9.3 %collective-permute-start.3 = (bf16[64,1024]{1,0:T(8,128)(2,1)}, bf16[64,1024]{1,0:T(8,128)(2,1)S(1)}, u32[]{:S(2)}, u32[]{:S(2)}) collective-permute-start(bf16[64,1024]{1,0:T(8,128)(2,1)} %bitcast.13), channel_id=1, source_target_pairs={{48,0},{0,16},{16,32},{32,48},{49,1},{1,17},{17,33},{33,49},{50,2}... | collective-permute-start | bytes 393224 | tf_op jit(solution)/shard_map/ppermute | solution.py:183
  37.2 9.9 %collective-permute-start.2 = (bf16[64,1024]{1,0:T(8,128)(2,1)}, bf16[64,1024]{1,0:T(8,128)(2,1)S(1)}, u32[]{:S(2)}, u32[]{:S(2)}) collective-permute-start(bf16[64,1024]{1,0:T(8,128)(2,1)} %bitcast.14), channel_id=1, source_target_pairs={{32,0},{48,16},{0,32},{16,48},{33,1},{49,17},{1,33},{17,49},{34,2}... | collective-permute-start | bytes 393224 | tf_op jit(solution)/shard_map/ppermute | solution.py:183
  39.8 9.2 %collective-permute-start.1 = (bf16[64,1024]{1,0:T(8,128)(2,1)}, bf16[64,1024]{1,0:T(8,128)(2,1)S(1)}, u32[]{:S(2)}, u32[]{:S(2)}) collective-permute-start(bf16[64,1024]{1,0:T(8,128)(2,1)} %bitcast.15), channel_id=1, source_target_pairs={{16,0},{32,16},{48,32},{0,48},{17,1},{33,17},{49,33},{1,49},{18,2}... | collective-permute-start | bytes 393224 | tf_op jit(solution)/shard_map/ppermute | solution.py:183
  49.1 8.6 %collective-permute-start.4 = (bf16[2,256,1024]{2,1,0:T(8,128)(2,1)S(1)}, bf16[2,256,1024]{2,1,0:T(8,128)(2,1)S(1)}, u32[]{:S(2)}, u32[]{:S(2)}) collective-permute-start(bf16[2,256,1024]{2,1,0:T(8,128)(2,1)S(1)} %pair.1.cols), channel_id=1, source_target_pairs={{0,8},{8,0},{1,9},{9,1},{2,10},{10,2},{3,11},{11,3},{4,12},{12,4},... | collective-permute-start | bytes 3145736 | tf_op jit(solution)/shard_map/ppermute | solution.py:186
  57.1 0.7 copy-start.1
  59.4 18.2 %all-to-all-start.1 = ((bf16[8,128,256]{2,1,0:T(8,128)(2,1)}), bf16[8,128,256]{2,1,0:T(8,128)(2,1)S(1)}, u32[]{:S(2)}, u32[]{:S(2)}) async-start(bf16[8,128,256]{2,1,0:T(8,128)(2,1)} %partial_gram.1), calls=%async_computation.1 | async-start | bytes 1048576 | tf_op jit(solution)/shard_map/all_to_all | solution.py:193
  77.5 50.4 %all-to-all-start = ((bf16[8,128,512]{2,1,0:T(8,128)(2,1)}), bf16[8,128,512]{2,1,0:T(8,128)(2,1)S(1)}, u32[]{:S(2)}, u32[]{:S(2)}) async-start(bf16[8,128,512]{2,1,0:T(8,128)(2,1)} %get-tuple-element.31), calls=%async_computation | async-start | bytes 2097152 | tf_op jit(solution)/shard_map/all_to_all | solution.py:194
  114.9 11.1 %collective-permute-start.5 = (bf16[4,128,256]{2,1,0:T(8,128)(2,1)S(1)}, bf16[4,128,256]{2,1,0:T(8,128)(2,1)S(1)}, u32[]{:S(2)}, u32[]{:S(2)}) collective-permute-start(bf16[4,128,256]{2,1,0:T(8,128)(2,1)S(1)} %dynamic-slice_bitcast_fusion), channel_id=1, source_target_pairs={{32,0},{232,8},{48,16},{248,24},{64,32},{8,40},{80,48},{24,56},{96... | collective-permute-start | bytes 786440 | tf_op jit(solution)/shard_map/ppermute | solution.py:200
  116.9 21.3 %collective-permute-start.8 = (bf16[4,2,128,256]{3,2,1,0:T(8,128)(2,1)S(1)}, bf16[4,2,128,256]{3,2,1,0:T(8,128)(2,1)S(1)}, u32[]{:S(2)}, u32[]{:S(2)}) collective-permute-start(bf16[4,2,128,256]{3,2,1,0:T(8,128)(2,1)S(1)} %bitcast.7), channel_id=1, source_target_pairs={{240,0},{248,8},{0,16},{8,24},{16,32},{24,40},{32,48},{40,56},{48,... | collective-permute-start | bytes 1572872 | tf_op jit(solution)/shard_map/ppermute | solution.py:201
  124.1 14.1 %collective-permute-start.7 = (bf16[4,2,128,256]{3,2,1,0:T(8,128)(2,1)S(1)}, bf16[4,2,128,256]{3,2,1,0:T(8,128)(2,1)S(1)}, u32[]{:S(2)}, u32[]{:S(2)}) collective-permute-start(bf16[4,2,128,256]{3,2,1,0:T(8,128)(2,1)S(1)} %bitcast.8), channel_id=1, source_target_pairs={{16,0},{24,8},{32,16},{40,24},{48,32},{56,40},{64,48},{72,56},{80,... | collective-permute-start | bytes 1572872 | tf_op jit(solution)/shard_map/ppermute | solution.py:201
  126.0 7.4 %collective-permute-start.6 = (bf16[4,128,256]{2,1,0:T(8,128)(2,1)S(1)}, bf16[4,128,256]{2,1,0:T(8,128)(2,1)S(1)}, u32[]{:S(2)}, u32[]{:S(2)}) collective-permute-start(bf16[4,128,256]{2,1,0:T(8,128)(2,1)S(1)} %collective-permute-done.5.two), channel_id=1, source_target_pairs={{0,256},{256,0},{1,257},{257,1},{2,258},{258,2},{3,259},{259,3},{4... | collective-permute-start | bytes 786440 | tf_op jit(solution)/shard_map/ppermute | solution.py:202
  128.0 18.2 %copy-start.2 = (bf16[128,512]{1,0:T(8,128)(2,1)S(1)}, bf16[128,512]{1,0:T(8,128)(2,1)}, u32[]{:S(2)}) copy-start(bf16[128,512]{1,0:T(8,128)(2,1)} %copy-done.1) | copy-start | bytes 393220
  138.3 7.8 %collective-permute-start.9 = (bf16[4,4,2,128,256]{4,3,2,1,0:T(8,128)(2,1)S(1)}, bf16[4,4,2,128,256]{4,3,2,1,0:T(8,128)(2,1)S(1)}, u32[]{:S(2)}, u32[]{:S(2)}) collective-permute-start(bf16[4,4,2,128,256]{4,3,2,1,0:T(8,128)(2,1)S(1)} %classes.1.refs_0_), channel_id=1, source_target_pairs={{0,8},{8,0},{1,9},{9,1},{2,10},{10,2},{3,11},{11,3},{4,12},{12,4},... | collective-permute-start | bytes 6291464 | tf_op jit(solution)/shard_map/ppermute | solution.py:205

commit v11 on v9

--- a/solution.py
+++ b/solution.py
@@ -192,14 +192,15 @@
     gram = (jnp.sum(terms.astype(jnp.float32), axis=0) / tokens).astype(jnp.bfloat16)
 
     line = ("zh", "zl", "core")
-    mine = lax.all_gather(lax.all_gather(gram, "ylo", axis=0), "zh", axis=0)
+    gram = lax.all_gather(gram, "ylo", axis=0)
+    diff = lax.optimization_barrier((diff, gram))[0]
+    diffs = lax.all_to_all(diff, ROW, 0, 0, tiled=True)
+    mine = lax.all_gather(gram, "zh", axis=0)
+    diffs, mine = lax.optimization_barrier((diffs, mine))
     half = lax.dynamic_index_in_dim(mine, lax.axis_index("ylo"), 1, keepdims=False)
     two = lax.ppermute(half, line, from_z(2, -2))
     up, down = (lax.ppermute(mine, line, from_z(s, s)) for s in (1, -1))
     two_far = lax.ppermute(two, "ylo", SWAP)
-    diff = lax.optimization_barrier((diff, mine))[0]
-    diffs = lax.all_to_all(diff, ROW, 0, 0, tiled=True)
-    diffs, two_far = lax.optimization_barrier((diffs, two_far))
     packed = pack(classes_kernel, "classes", mine, up, down, two, two_far)
     grams = (packed, lax.ppermute(packed, "core", SWAP))
 

time: 168 us -> 167 us (level)
  blocking collectives: 97.8 us -> 94.9 us
    ppermute x1, starting transfers between devices: 2.49 us -> 4.98 us  [on_device(): two = lax.ppermute(half, line, from_z(2, -2))]
  transfers between devices with their start and end apart: 11 -> 11, of which waited for: 6 -> 7; matrix products, arithmetic and copies ran while one was open for 0% -> 0% of each run, Pallas kernels for 1% -> 1%
where the time goes in v11:
time: 167 us; the launch traced here: 166 us
  blocking collectives  94.9 us (57%)
  starting transfers between devices  42.9 us (26%)
  waiting for transfers between devices  21.6 us (13%)
  Pallas kernels  6.25 us (4%)
    all_gather x1, blocking collectives, on_device(): own = lax.all_gather(feats, 'zh', axis=0, tiled=True)  31.5 us
    all_to_all x1, blocking collectives, on_device(): diffs = lax.all_to_all(sent, ROW, 0, 0, tiled=True)  22.3 us
    all_gather x1, blocking collectives, on_device(): mine = lax.all_gather(gram, 'zh', axis=0)  20.2 us
    all_to_all x1, blocking collectives, on_device(): terms = lax.all_to_all(term, ROW, 0, 0, tiled=True)  17.1 us
    ppermute x3, starting transfers between devices, on_device(): lax.ppermute(near, 'zl', [((i + d) % 4, i) for i in range(4)])  9.29 us
    ppermute x2, starting transfers between devices, on_device(): up, down = (lax.ppermute(mine, line, from_z(s, s)) for s in (1, -1))  8.09 us
    ppermute x2, waiting for transfers between devices, on_device(): up, down = (lax.ppermute(mine, line, from_z(s, s)) for s in (1, -1))  7.57 us
    ppermute x1, starting transfers between devices, on_device(): mates = lax.ppermute(cols, 'core', SWAP)  6.05 us
  transfers between devices with their start and end apart: 11, of which 7 were waited for; matrix products, arithmetic and copies ran while one was open for 0% of the time, Pallas kernels for 1%

profile of v11, /device:TPU:1, one launch (start us, length us, event | category | flops | bytes accessed | tf_op | source)
XLA Modules:
  0.0 166.0 jit_solution(4305625329788771527)
XLA Ops:
  0.0 31.5 %all_gather.13.own = bf16[256,1024]{1,0:T(8,128)(2,1)S(1)} all-gather(bf16[64,1024]{1,0:T(8,128)(2,1)} %bitcast.10), channel_id=1, replica_groups=mesh['ylo'=2,'zh'=4,'zl'=4,'core'=2,'yhi'=2,'x'=4] {'zh'}, dimensions={0}, use_global_device_ids=true | all-gather | bytes 655360 | tf_op jit(solution)/shard_map/all_gather | solution.py:179
  31.5 3.2 %collective-permute-start = (bf16[256,1024]{1,0:T(8,128)(2,1)S(1)}, bf16[256,1024]{1,0:T(8,128)(2,1)S(1)}, u32[]{:S(2)}, u32[]{:S(2)}) collective-permute-start(bf16[256,1024]{1,0:T(8,128)(2,1)S(1)} %all_gather.13.own), channel_id=1, source_target_pairs={{0,256},{256,0},{1,257},{257,1},{2,258},{258,2},{3,259},{259,3},{4... | collective-permute-start | bytes 1572872 | tf_op jit(solution)/shard_map/ppermute | solution.py:180
  34.7 2.5 %collective-permute-start.3 = (bf16[64,1024]{1,0:T(8,128)(2,1)}, bf16[64,1024]{1,0:T(8,128)(2,1)S(1)}, u32[]{:S(2)}, u32[]{:S(2)}) collective-permute-start(bf16[64,1024]{1,0:T(8,128)(2,1)} %bitcast.11), channel_id=1, source_target_pairs={{48,0},{0,16},{16,32},{32,48},{49,1},{1,17},{17,33},{33,49},{50,2}... | collective-permute-start | bytes 393224 | tf_op jit(solution)/shard_map/ppermute | solution.py:182
  37.2 2.6 %collective-permute-start.2 = (bf16[64,1024]{1,0:T(8,128)(2,1)}, bf16[64,1024]{1,0:T(8,128)(2,1)S(1)}, u32[]{:S(2)}, u32[]{:S(2)}) collective-permute-start(bf16[64,1024]{1,0:T(8,128)(2,1)} %bitcast.12), channel_id=1, source_target_pairs={{32,0},{48,16},{0,32},{16,48},{33,1},{49,17},{1,33},{17,49},{34,2}... | collective-permute-start | bytes 393224 | tf_op jit(solution)/shard_map/ppermute | solution.py:182
  39.8 4.2 %collective-permute-start.1 = (bf16[64,1024]{1,0:T(8,128)(2,1)}, bf16[64,1024]{1,0:T(8,128)(2,1)S(1)}, u32[]{:S(2)}, u32[]{:S(2)}) collective-permute-start(bf16[64,1024]{1,0:T(8,128)(2,1)} %bitcast.13), channel_id=1, source_target_pairs={{16,0},{32,16},{48,32},{0,48},{17,1},{33,17},{49,33},{1,49},{18,2}... | collective-permute-start | bytes 393224 | tf_op jit(solution)/shard_map/ppermute | solution.py:182
  44.1 3.1 %collective-permute-done.2.r2 = bf16[64,1024]{1,0:T(8,128)(2,1)S(1)} collective-permute-done((bf16[64,1024]{1,0:T(8,128)(2,1)}, bf16[64,1024]{1,0:T(8,128)(2,1)S(1)}, u32[]{:S(2)}, u32[]{:S(2)}) %collective-permute-start.2) | collective-permute-done | bytes 131104 | tf_op jit(solution)/shard_map/ppermute | solution.py:182
  47.2 1.9 %collective-permute-done.1.r1 = bf16[64,1024]{1,0:T(8,128)(2,1)S(1)} collective-permute-done((bf16[64,1024]{1,0:T(8,128)(2,1)}, bf16[64,1024]{1,0:T(8,128)(2,1)S(1)}, u32[]{:S(2)}, u32[]{:S(2)}) %collective-permute-start.1) | collective-permute-done | bytes 131104 | tf_op jit(solution)/shard_map/ppermute | solution.py:182
  49.1 6.0 %collective-permute-start.4 = (bf16[2,256,1024]{2,1,0:T(8,128)(2,1)S(1)}, bf16[2,256,1024]{2,1,0:T(8,128)(2,1)S(1)}, u32[]{:S(2)}, u32[]{:S(2)}) collective-permute-start(bf16[2,256,1024]{2,1,0:T(8,128)(2,1)S(1)} %pair.1.cols), channel_id=1, source_target_pairs={{0,8},{8,0},{1,9},{9,1},{2,10},{10,2},{3,11},{11,3},{4,12},{12,4},... | collective-permute-start | bytes 3145736 | tf_op jit(solution)/shard_map/ppermute | solution.py:185
  55.2 1.9 %start.1 = (bf16[128,512]{1,0:T(8,128)(2,1)S(1)}, bf16[8,128,512]{2,1,0:T(8,128)(2,1)}, f32[128,512]{1,0:T(8,128)S(1)}) custom-call(s32[16,64]{1,0:T(8,128)S(1)} %bitcast.15, bf16[128,512]{1,0:T(8,128)(2,1)S(1)} %copy-done), custom_call_target="tpu_custom_call" | custom-call | tf_op jit(solution)/shard_map/start/pallas_call | solution.py:60
  58.3 17.1 %all_to_all.15 = bf16[8,128,256]{2,1,0:T(8,128)(2,1)S(1)} all-to-all(bf16[8,128,256]{2,1,0:T(8,128)(2,1)S(1)} %partial_gram.1), channel_id=1, replica_groups=mesh['ylo'=2,'zh'=4,'zl'=4,'core'=2,'yhi'=2,'x'=4] {'yhi','x'}, dimensions={0} | all-to-all | bytes 1048576 | tf_op jit(solution)/shard_map/all_to_all | solution.py:191
  75.5 3.8 %all-gather = bf16[256,256]{1,0:T(8,128)(2,1)S(1)} all-gather(bf16[128,256]{1,0:T(8,128)(2,1)S(1)} %multiply_convert_fusion), channel_id=2, replica_groups=mesh['ylo'=2,'zh'=4,'zl'=4,'core'=2,'yhi'=2,'x'=4] {'ylo'}, dimensions={0}, use_global_device_ids=true | all-gather | bytes 196608 | tf_op jit(solution)/shard_map/all_gather | solution.py:195
  79.3 3.6 %all-to-all-start.1 = ((bf16[8,128,512]{2,1,0:T(8,128)(2,1)}), bf16[8,128,512]{2,1,0:T(8,128)(2,1)S(1)}, u32[]{:S(2)}, u32[]{:S(2)}) async-start(bf16[8,128,512]{2,1,0:T(8,128)(2,1)} %get-tuple-element.30), calls=%async_computation.1 | async-start | bytes 2097152 | tf_op jit(solution)/shard_map/all_to_all | solution.py:197
  82.8 20.2 %all-gather.1 = bf16[8,128,256]{2,1,0:T(8,128)(2,1)S(1)} all-gather(bf16[2,128,256]{2,1,0:T(8,128)(2,1)S(1)} %bitcast.16), channel_id=3, replica_groups=mesh['ylo'=2,'zh'=4,'zl'=4,'core'=2,'yhi'=2,'x'=4] {'zh'}, dimensions={0}, use_global_device_ids=true | all-gather | bytes 655360 | tf_op jit(solution)/shard_map/all_gather | solution.py:198
  103.1 5.0 %collective-permute-start.7 = (bf16[4,128,256]{2,1,0:T(8,128)(2,1)S(1)}, bf16[4,128,256]{2,1,0:T(8,128)(2,1)S(1)}, u32[]{:S(2)}, u32[]{:S(2)}) collective-permute-start(bf16[4,128,256]{2,1,0:T(8,128)(2,1)S(1)} %dynamic-slice_bitcast_fusion), channel_id=1, source_target_pairs={{32,0},{232,8},{48,16},{248,24},{64,32},{8,40},{80,48},{24,56},{96... | collective-permute-start | bytes 786440 | tf_op jit(solution)/shard_map/ppermute | solution.py:201
  108.1 4.7 %collective-permute-start.6 = (bf16[4,2,128,256]{3,2,1,0:T(8,128)(2,1)S(1)}, bf16[4,2,128,256]{3,2,1,0:T(8,128)(2,1)S(1)}, u32[]{:S(2)}, u32[]{:S(2)}) collective-permute-start(bf16[4,2,128,256]{3,2,1,0:T(8,128)(2,1)S(1)} %bitcast.7), channel_id=1, source_target_pairs={{240,0},{248,8},{0,16},{8,24},{16,32},{24,40},{32,48},{40,56},{48,... | collective-permute-start | bytes 1572872 | tf_op jit(solution)/shard_map/ppermute | solution.py:202
  112.8 3.4 %collective-permute-start.5 = (bf16[4,2,128,256]{3,2,1,0:T(8,128)(2,1)S(1)}, bf16[4,2,128,256]{3,2,1,0:T(8,128)(2,1)S(1)}, u32[]{:S(2)}, u32[]{:S(2)}) collective-permute-start(bf16[4,2,128,256]{3,2,1,0:T(8,128)(2,1)S(1)} %bitcast.8), channel_id=1, source_target_pairs={{16,0},{24,8},{32,16},{40,24},{48,32},{56,40},{64,48},{72,56},{80,... | collective-permute-start | bytes 1572872 | tf_op jit(solution)/shard_map/ppermute | solution.py:202
  116.2 2.5 %collective-permute-start.8 = (bf16[4,128,256]{2,1,0:T(8,128)(2,1)S(1)}, bf16[4,128,256]{2,1,0:T(8,128)(2,1)S(1)}, u32[]{:S(2)}, u32[]{:S(2)}) collective-permute-start(bf16[4,128,256]{2,1,0:T(8,128)(2,1)S(1)} %collective-permute-done.7.two), channel_id=1, source_target_pairs={{0,256},{256,0},{1,257},{257,1},{2,258},{258,2},{3,259},{259,3},{4... | collective-permute-start | bytes 786440 | tf_op jit(solution)/shard_map/ppermute | solution.py:203
  118.7 4.9 %collective-permute-done.8.two_far = bf16[4,128,256]{2,1,0:T(8,128)(2,1)S(1)} collective-permute-done((bf16[4,128,256]{2,1,0:T(8,128)(2,1)S(1)}, bf16[4,128,256]{2,1,0:T(8,128)(2,1)S(1)}, u32[]{:S(2)}, u32[]{:S(2)}) %collective-permute-start.8) | collective-permute-done | bytes 262176 | tf_op jit(solution)/shard_map/ppermute | solution.py:203
  124.1 7.1 %collective-permute-done.5.up = bf16[4,2,128,256]{3,2,1,0:T(8,128)(2,1)S(1)} collective-permute-done((bf16[4,2,128,256]{3,2,1,0:T(8,128)(2,1)S(1)}, bf16[4,2,128,256]{3,2,1,0:T(8,128)(2,1)S(1)}, u32[]{:S(2)}, u32[]{:S(2)}) %collective-permute-start.5) | collective-permute-done | bytes 524320 | tf_op jit(solution)/shard_map/ppermute | solution.py:202
  131.3 5.3 %collective-permute-start.9 = (bf16[4,4,2,128,256]{4,3,2,1,0:T(8,128)(2,1)S(1)}, bf16[4,4,2,128,256]{4,3,2,1,0:T(8,128)(2,1)S(1)}, u32[]{:S(2)}, u32[]{:S(2)}) collective-permute-start(bf16[4,4,2,128,256]{4,3,2,1,0:T(8,128)(2,1)S(1)} %classes.1.refs_0_), channel_id=1, source_target_pairs={{0,8},{8,0},{1,9},{9,1},{2,10},{10,2},{3,11},{11,3},{4,12},{12,4},... | collective-permute-start | bytes 6291464 | tf_op jit(solution)/shard_map/ppermute | solution.py:205
  136.6 3.8 %collective-permute-done.9.refs_1_ = bf16[4,4,2,128,256]{4,3,2,1,0:T(8,128)(2,1)S(1)} collective-permute-done((bf16[4,4,2,128,256]{4,3,2,1,0:T(8,128)(2,1)S(1)}, bf16[4,4,2,128,256]{4,3,2,1,0:T(8,128)(2,1)S(1)}, u32[]{:S(2)}, u32[]{:S(2)}) %collective-permute-start.9) | collective-permute-done | bytes 2097184 | tf_op jit(solution)/shard_map/ppermute | solution.py:205
  140.3 1.4 first_step.1
  141.7 22.3 %all_to_all.16.diffs = bf16[8,128,512]{2,1,0:T(8,128)(2,1)S(1)} all-to-all(bf16[8,128,512]{2,1,0:T(8,128)(2,1)S(1)} %get-tuple-element.35), channel_id=1, replica_groups=mesh['ylo'=2,'zh'=4,'zl'=4,'core'=2,'yhi'=2,'x'=4] {'yhi','x'}, dimensions={0} | all-to-all | bytes 2097152 | tf_op jit(solution)/shard_map/all_to_all | solution.py:208
  164.0 2.0 %last_step.1 = bf16[128,512]{1,0:T(8,128)(2,1)} custom-call(bf16[8,128,512]{2,1,0:T(8,128)(2,1)S(1)} %all_to_all.16.diffs, bf16[4,4,2,128,256]{4,3,2,1,0:T(8,128)(2,1)S(1)} %classes.1.refs_0_, bf16[4,4,2,128,256]{4,3,2,1,0:T(8,128)(2,1)S(1)} %collective-permute-done.9.refs_1_, bf16[128,512]{1,0:T(8,128)(2,1)S(1)} %get-tuple-element.36.refs_2_, ...), custom_call_target="tpu_custom_call" | custom-call | flops 536870912 | bytes 3145728 | tf_op jit(solution)/shard_map/last_step/pallas_call | solution.py:132
  (18 shorter events, 2.0 us)
Async XLA Ops:
  0.0 57.5 %copy-start.1 = (bf16[1024,64]{0,1:T(8,128)(2,1)S(1)}, bf16[1024,64]{0,1:T(8,128)(2,1)}, u32[]{:S(2)}) copy-start(bf16[1024,64]{0,1:T(8,128)(2,1)} %param.3) | copy-start | bytes 393220
  0.0 55.2 %copy-start = (bf16[128,512]{1,0:T(8,128)(2,1)S(1)}, bf16[128,512]{1,0:T(8,128)(2,1)}, u32[]{:S(2)}) copy-start(bf16[128,512]{1,0:T(8,128)(2,1)} %refs_3_.1) | copy-start | bytes 393220
  0.0 55.2 %copy-start.2 = (s32[64,16]{0,1:T(8,128)S(1)}, s32[64,16]{0,1:T(8,128)}, u32[]{:S(2)}) copy-start(s32[64,16]{0,1:T(8,128)} %param.5) | copy-start | bytes 12292
  31.5 17.5 %collective-permute-start = (bf16[256,1024]{1,0:T(8,128)(2,1)S(1)}, bf16[256,1024]{1,0:T(8,128)(2,1)S(1)}, u32[]{:S(2)}, u32[]{:S(2)}) collective-permute-start(bf16[256,1024]{1,0:T(8,128)(2,1)S(1)} %all_gather.13.own), channel_id=1, source_target_pairs={{0,256},{256,0},{1,257},{257,1},{2,258},{258,2},{3,259},{259,3},{4... | collective-permute-start | bytes 1572872 | tf_op jit(solution)/shard_map/ppermute | solution.py:180
  34.7 9.3 %collective-permute-start.3 = (bf16[64,1024]{1,0:T(8,128)(2,1)}, bf16[64,1024]{1,0:T(8,128)(2,1)S(1)}, u32[]{:S(2)}, u32[]{:S(2)}) collective-permute-start(bf16[64,1024]{1,0:T(8,128)(2,1)} %bitcast.11), channel_id=1, source_target_pairs={{48,0},{0,16},{16,32},{32,48},{49,1},{1,17},{17,33},{33,49},{50,2}... | collective-permute-start | bytes 393224 | tf_op jit(solution)/shard_map/ppermute | solution.py:182
  37.2 9.9 %collective-permute-start.2 = (bf16[64,1024]{1,0:T(8,128)(2,1)}, bf16[64,1024]{1,0:T(8,128)(2,1)S(1)}, u32[]{:S(2)}, u32[]{:S(2)}) collective-permute-start(bf16[64,1024]{1,0:T(8,128)(2,1)} %bitcast.12), channel_id=1, source_target_pairs={{32,0},{48,16},{0,32},{16,48},{33,1},{49,17},{1,33},{17,49},{34,2}... | collective-permute-start | bytes 393224 | tf_op jit(solution)/shard_map/ppermute | solution.py:182
  39.8 9.2 %collective-permute-start.1 = (bf16[64,1024]{1,0:T(8,128)(2,1)}, bf16[64,1024]{1,0:T(8,128)(2,1)S(1)}, u32[]{:S(2)}, u32[]{:S(2)}) collective-permute-start(bf16[64,1024]{1,0:T(8,128)(2,1)} %bitcast.13), channel_id=1, source_target_pairs={{16,0},{32,16},{48,32},{0,48},{17,1},{33,17},{49,33},{1,49},{18,2}... | collective-permute-start | bytes 393224 | tf_op jit(solution)/shard_map/ppermute | solution.py:182
  49.1 8.3 %collective-permute-start.4 = (bf16[2,256,1024]{2,1,0:T(8,128)(2,1)S(1)}, bf16[2,256,1024]{2,1,0:T(8,128)(2,1)S(1)}, u32[]{:S(2)}, u32[]{:S(2)}) collective-permute-start(bf16[2,256,1024]{2,1,0:T(8,128)(2,1)S(1)} %pair.1.cols), channel_id=1, source_target_pairs={{0,8},{8,0},{1,9},{9,1},{2,10},{10,2},{3,11},{11,3},{4,12},{12,4},... | collective-permute-start | bytes 3145736 | tf_op jit(solution)/shard_map/ppermute | solution.py:185
  79.3 23.8 %all-to-all-start.1 = ((bf16[8,128,512]{2,1,0:T(8,128)(2,1)}), bf16[8,128,512]{2,1,0:T(8,128)(2,1)S(1)}, u32[]{:S(2)}, u32[]{:S(2)}) async-start(bf16[8,128,512]{2,1,0:T(8,128)(2,1)} %get-tuple-element.30), calls=%async_computation.1 | async-start | bytes 2097152 | tf_op jit(solution)/shard_map/all_to_all | solution.py:197
  103.1 13.1 %collective-permute-start.7 = (bf16[4,128,256]{2,1,0:T(8,128)(2,1)S(1)}, bf16[4,128,256]{2,1,0:T(8,128)(2,1)S(1)}, u32[]{:S(2)}, u32[]{:S(2)}) collective-permute-start(bf16[4,128,256]{2,1,0:T(8,128)(2,1)S(1)} %dynamic-slice_bitcast_fusion), channel_id=1, source_target_pairs={{32,0},{232,8},{48,16},{248,24},{64,32},{8,40},{80,48},{24,56},{96... | collective-permute-start | bytes 786440 | tf_op jit(solution)/shard_map/ppermute | solution.py:201
  108.1 16.0 %collective-permute-start.6 = (bf16[4,2,128,256]{3,2,1,0:T(8,128)(2,1)S(1)}, bf16[4,2,128,256]{3,2,1,0:T(8,128)(2,1)S(1)}, u32[]{:S(2)}, u32[]{:S(2)}) collective-permute-start(bf16[4,2,128,256]{3,2,1,0:T(8,128)(2,1)S(1)} %bitcast.7), channel_id=1, source_target_pairs={{240,0},{248,8},{0,16},{8,24},{16,32},{24,40},{32,48},{40,56},{48,... | collective-permute-start | bytes 1572872 | tf_op jit(solution)/shard_map/ppermute | solution.py:202
  112.8 18.4 %collective-permute-start.5 = (bf16[4,2,128,256]{3,2,1,0:T(8,128)(2,1)S(1)}, bf16[4,2,128,256]{3,2,1,0:T(8,128)(2,1)S(1)}, u32[]{:S(2)}, u32[]{:S(2)}) collective-permute-start(bf16[4,2,128,256]{3,2,1,0:T(8,128)(2,1)S(1)} %bitcast.8), channel_id=1, source_target_pairs={{16,0},{24,8},{32,16},{40,24},{48,32},{56,40},{64,48},{72,56},{80,... | collective-permute-start | bytes 1572872 | tf_op jit(solution)/shard_map/ppermute | solution.py:202
  116.2 7.4 %collective-permute-start.8 = (bf16[4,128,256]{2,1,0:T(8,128)(2,1)S(1)}, bf16[4,128,256]{2,1,0:T(8,128)(2,1)S(1)}, u32[]{:S(2)}, u32[]{:S(2)}) collective-permute-start(bf16[4,128,256]{2,1,0:T(8,128)(2,1)S(1)} %collective-permute-done.7.two), channel_id=1, source_target_pairs={{0,256},{256,0},{1,257},{257,1},{2,258},{258,2},{3,259},{259,3},{4... | collective-permute-start | bytes 786440 | tf_op jit(solution)/shard_map/ppermute | solution.py:203
  131.3 9.0 %collective-permute-start.9 = (bf16[4,4,2,128,256]{4,3,2,1,0:T(8,128)(2,1)S(1)}, bf16[4,4,2,128,256]{4,3,2,1,0:T(8,128)(2,1)S(1)}, u32[]{:S(2)}, u32[]{:S(2)}) collective-permute-start(bf16[4,4,2,128,256]{4,3,2,1,0:T(8,128)(2,1)S(1)} %classes.1.refs_0_), channel_id=1, source_target_pairs={{0,8},{8,0},{1,9},{9,1},{2,10},{10,2},{3,11},{11,3},{4,12},{12,4},... | collective-permute-start | bytes 6291464 | tf_op jit(solution)/shard_map/ppermute | solution.py:205

commit v12 on v11

--- a/solution.py
+++ b/solution.py
@@ -102,7 +102,7 @@
 
 def step_kernel(last, diffs, *refs):
     grams, (weight, base, keep), outs, total = refs[:2], refs[2:5], refs[5:-1], refs[-1]
-    zl, core = lax.axis_index("zl"), lax.axis_index("core")
+    ylo, zl, core = (lax.axis_index(a) for a in ("ylo", "zl", "core"))
     half = grams[0].shape[4]
     for j, shift in enumerate(CLASSES):
         part = jnp.zeros((weight.shape[0], BLOCK), jnp.float32)
@@ -111,7 +111,7 @@
             for h in range(4):
                 for y in range(2):
                     part += lax.dot_general(
-                        diffs[y * 4 + h, :, lanes], grams[c][j, h, y], NT,
+                        diffs[(ylo ^ y) * 4 + h, :, lanes], grams[c][j, h, y], NT,
                         preferred_element_type=jnp.float32,
                     )
         place = lax.rem(zl + shift, 4) * BLOCK
@@ -150,12 +150,11 @@
 
 
 def classes_kernel(mine, up, down, two, two_far, out):
-    ylo = lax.axis_index("ylo")
     out[0] = mine[...]
     out[1] = up[...]
     out[2] = down[...]
-    out[3, :, ylo] = two[...]
-    out[3, :, 1 - ylo] = two_far[...]
+    out[3, :, 0] = two[...]
+    out[3, :, 1] = two_far[...]
 
 
 def pack(kernel, name, *parts):
@@ -192,12 +191,12 @@
     gram = (jnp.sum(terms.astype(jnp.float32), axis=0) / tokens).astype(jnp.bfloat16)
 
     line = ("zh", "zl", "core")
-    gram = lax.all_gather(gram, "ylo", axis=0)
-    diff = lax.optimization_barrier((diff, gram))[0]
+    far_gram = lax.ppermute(gram, "ylo", SWAP)
+    diff = lax.optimization_barrier((diff, far_gram))[0]
     diffs = lax.all_to_all(diff, ROW, 0, 0, tiled=True)
-    mine = lax.all_gather(gram, "zh", axis=0)
+    mine = lax.all_gather(pack(pair_kernel, "pair", gram, far_gram), "zh", axis=0)
     diffs, mine = lax.optimization_barrier((diffs, mine))
-    half = lax.dynamic_index_in_dim(mine, lax.axis_index("ylo"), 1, keepdims=False)
+    half = mine[:, 0]
     two = lax.ppermute(half, line, from_z(2, -2))
     up, down = (lax.ppermute(mine, line, from_z(s, s)) for s in (1, -1))
     two_far = lax.ppermute(two, "ylo", SWAP)

time: 167 us -> 168 us (level)
  blocking collectives: 94.9 us -> 91.2 us
  waiting for transfers between devices: 21.6 us -> 25.3 us
    all_gather x2 -> x1, blocking collectives: 24 us -> 20.2 us  [on_device(): lax.all_gather(pack(pair_kernel, 'pair', gram, far_gram), 'zh', axis=0)]
    ppermute x0 -> x1, waiting for transfers between devices: none -> 3.08 us  [on_device(): far_gram = lax.ppermute(gram, 'ylo', SWAP)]
    ppermute x0 -> x1, starting transfers between devices: none -> 1.92 us  [on_device(): far_gram = lax.ppermute(gram, 'ylo', SWAP)]
  transfers between devices with their start and end apart: 11 -> 12, of which waited for: 7 -> 8; matrix products, arithmetic and copies ran while one was open for 0% -> 0% of each run, Pallas kernels for 1% -> 1%
where the time goes in v12:
time: 168 us; the launch traced here: 167 us
  blocking collectives  91.2 us (54%)
  starting transfers between devices  44.3 us (26%)
  waiting for transfers between devices  25.3 us (15%)
  Pallas kernels  6.26 us (4%)
    all_gather x1, blocking collectives, on_device(): own = lax.all_gather(feats, 'zh', axis=0, tiled=True)  31.5 us
    all_to_all x1, blocking collectives, on_device(): diffs = lax.all_to_all(sent, ROW, 0, 0, tiled=True)  22.3 us
    all_gather x1, blocking collectives, on_device(): lax.all_gather(pack(pair_kernel, 'pair', gram, far_gram), 'zh', axis=0)  20.2 us
    all_to_all x1, blocking collectives, on_device(): terms = lax.all_to_all(term, ROW, 0, 0, tiled=True)  17.1 us
    ppermute x3, starting transfers between devices, on_device(): lax.ppermute(near, 'zl', [((i + d) % 4, i) for i in range(4)])  9.29 us
    ppermute x2, starting transfers between devices, on_device(): up, down = (lax.ppermute(mine, line, from_z(s, s)) for s in (1, -1))  8.09 us
    ppermute x2, waiting for transfers between devices, on_device(): up, down = (lax.ppermute(mine, line, from_z(s, s)) for s in (1, -1))  7.57 us
    ppermute x1, starting transfers between devices, on_device(): mates = lax.ppermute(cols, 'core', SWAP)  6.05 us
  transfers between devices with their start and end apart: 12, of which 8 were waited for; matrix products, arithmetic and copies ran while one was open for 0% of the time, Pallas kernels for 1%

profile of v12, /device:TPU:1, one launch (start us, length us, event | category | flops | bytes accessed | tf_op | source)
XLA Modules:
  0.0 167.3 jit_solution(17043437470523736981)
XLA Ops:
  0.0 31.5 %all_gather.9.own = bf16[256,1024]{1,0:T(8,128)(2,1)S(1)} all-gather(bf16[64,1024]{1,0:T(8,128)(2,1)} %bitcast.9), channel_id=1, replica_groups=mesh['ylo'=2,'zh'=4,'zl'=4,'core'=2,'yhi'=2,'x'=4] {'zh'}, dimensions={0}, use_global_device_ids=true | all-gather | bytes 655360 | tf_op jit(solution)/shard_map/all_gather | solution.py:178
  31.5 3.2 %collective-permute-start = (bf16[256,1024]{1,0:T(8,128)(2,1)S(1)}, bf16[256,1024]{1,0:T(8,128)(2,1)S(1)}, u32[]{:S(2)}, u32[]{:S(2)}) collective-permute-start(bf16[256,1024]{1,0:T(8,128)(2,1)S(1)} %all_gather.9.own), channel_id=1, source_target_pairs={{0,256},{256,0},{1,257},{257,1},{2,258},{258,2},{3,259},{259,3},{4... | collective-permute-start | bytes 1572872 | tf_op jit(solution)/shard_map/ppermute | solution.py:179
  34.7 2.5 %collective-permute-start.3 = (bf16[64,1024]{1,0:T(8,128)(2,1)}, bf16[64,1024]{1,0:T(8,128)(2,1)S(1)}, u32[]{:S(2)}, u32[]{:S(2)}) collective-permute-start(bf16[64,1024]{1,0:T(8,128)(2,1)} %bitcast.10), channel_id=1, source_target_pairs={{48,0},{0,16},{16,32},{32,48},{49,1},{1,17},{17,33},{33,49},{50,2}... | collective-permute-start | bytes 393224 | tf_op jit(solution)/shard_map/ppermute | solution.py:181
  37.2 2.6 %collective-permute-start.2 = (bf16[64,1024]{1,0:T(8,128)(2,1)}, bf16[64,1024]{1,0:T(8,128)(2,1)S(1)}, u32[]{:S(2)}, u32[]{:S(2)}) collective-permute-start(bf16[64,1024]{1,0:T(8,128)(2,1)} %bitcast.11), channel_id=1, source_target_pairs={{32,0},{48,16},{0,32},{16,48},{33,1},{49,17},{1,33},{17,49},{34,2}... | collective-permute-start | bytes 393224 | tf_op jit(solution)/shard_map/ppermute | solution.py:181
  39.8 4.2 %collective-permute-start.1 = (bf16[64,1024]{1,0:T(8,128)(2,1)}, bf16[64,1024]{1,0:T(8,128)(2,1)S(1)}, u32[]{:S(2)}, u32[]{:S(2)}) collective-permute-start(bf16[64,1024]{1,0:T(8,128)(2,1)} %bitcast.12), channel_id=1, source_target_pairs={{16,0},{32,16},{48,32},{0,48},{17,1},{33,17},{49,33},{1,49},{18,2}... | collective-permute-start | bytes 393224 | tf_op jit(solution)/shard_map/ppermute | solution.py:181
  44.1 3.1 %collective-permute-done.2.r2 = bf16[64,1024]{1,0:T(8,128)(2,1)S(1)} collective-permute-done((bf16[64,1024]{1,0:T(8,128)(2,1)}, bf16[64,1024]{1,0:T(8,128)(2,1)S(1)}, u32[]{:S(2)}, u32[]{:S(2)}) %collective-permute-start.2) | collective-permute-done | bytes 131104 | tf_op jit(solution)/shard_map/ppermute | solution.py:181
  47.2 1.9 %collective-permute-done.1.r1 = bf16[64,1024]{1,0:T(8,128)(2,1)S(1)} collective-permute-done((bf16[64,1024]{1,0:T(8,128)(2,1)}, bf16[64,1024]{1,0:T(8,128)(2,1)S(1)}, u32[]{:S(2)}, u32[]{:S(2)}) %collective-permute-start.1) | collective-permute-done | bytes 131104 | tf_op jit(solution)/shard_map/ppermute | solution.py:181
  49.1 6.0 %collective-permute-start.4 = (bf16[2,256,1024]{2,1,0:T(8,128)(2,1)S(1)}, bf16[2,256,1024]{2,1,0:T(8,128)(2,1)S(1)}, u32[]{:S(2)}, u32[]{:S(2)}) collective-permute-start(bf16[2,256,1024]{2,1,0:T(8,128)(2,1)S(1)} %pair.2.cols), channel_id=1, source_target_pairs={{0,8},{8,0},{1,9},{9,1},{2,10},{10,2},{3,11},{11,3},{4,12},{12,4},... | collective-permute-start | bytes 3145736 | tf_op jit(solution)/shard_map/ppermute | solution.py:184
  55.2 1.9 %start.1 = (bf16[128,512]{1,0:T(8,128)(2,1)S(1)}, bf16[8,128,512]{2,1,0:T(8,128)(2,1)}, f32[128,512]{1,0:T(8,128)S(1)}) custom-call(s32[16,64]{1,0:T(8,128)S(1)} %bitcast.14, bf16[128,512]{1,0:T(8,128)(2,1)S(1)} %copy-done), custom_call_target="tpu_custom_call" | custom-call | tf_op jit(solution)/shard_map/start/pallas_call | solution.py:60
  58.3 17.1 %all_to_all.15 = bf16[8,128,256]{2,1,0:T(8,128)(2,1)S(1)} all-to-all(bf16[8,128,256]{2,1,0:T(8,128)(2,1)S(1)} %partial_gram.1), channel_id=1, replica_groups=mesh['ylo'=2,'zh'=4,'zl'=4,'core'=2,'yhi'=2,'x'=4] {'yhi','x'}, dimensions={0} | all-to-all | bytes 1048576 | tf_op jit(solution)/shard_map/all_to_all | solution.py:190
  75.5 1.9 %collective-permute-start.5 = (bf16[128,256]{1,0:T(8,128)(2,1)S(1)}, bf16[128,256]{1,0:T(8,128)(2,1)S(1)}, u32[]{:S(2)}, u32[]{:S(2)}) collective-permute-start(bf16[128,256]{1,0:T(8,128)(2,1)S(1)} %multiply_convert_fusion.own), channel_id=1, source_target_pairs={{0,256},{256,0},{1,257},{257,1},{2,258},{258,2},{3,259},{259,3},{4... | collective-permute-start | bytes 196616 | tf_op jit(solution)/shard_map/ppermute | solution.py:194
  77.4 3.1 %collective-permute-done.5.other = bf16[128,256]{1,0:T(8,128)(2,1)S(1)} collective-permute-done((bf16[128,256]{1,0:T(8,128)(2,1)S(1)}, bf16[128,256]{1,0:T(8,128)(2,1)S(1)}, u32[]{:S(2)}, u32[]{:S(2)}) %collective-permute-start.5) | collective-permute-done | bytes 65568 | tf_op jit(solution)/shard_map/ppermute | solution.py:194
  80.5 3.6 %all-to-all-start.1 = ((bf16[8,128,512]{2,1,0:T(8,128)(2,1)}), bf16[8,128,512]{2,1,0:T(8,128)(2,1)S(1)}, u32[]{:S(2)}, u32[]{:S(2)}) async-start(bf16[8,128,512]{2,1,0:T(8,128)(2,1)} %get-tuple-element.30), calls=%async_computation.1 | async-start | bytes 2097152 | tf_op jit(solution)/shard_map/all_to_all | solution.py:196
  84.1 20.2 %all-gather = bf16[8,128,256]{2,1,0:T(8,128)(2,1)S(1)} all-gather(bf16[2,128,256]{2,1,0:T(8,128)(2,1)S(1)} %pair.3), channel_id=2, replica_groups=mesh['ylo'=2,'zh'=4,'zl'=4,'core'=2,'yhi'=2,'x'=4] {'zh'}, dimensions={0}, use_global_device_ids=true | all-gather | bytes 655360 | tf_op jit(solution)/shard_map/all_gather | solution.py:197
  104.3 5.0 %collective-permute-start.8 = (bf16[4,128,256]{2,1,0:T(8,128)(2,1)S(1)}, bf16[4,128,256]{2,1,0:T(8,128)(2,1)S(1)}, u32[]{:S(2)}, u32[]{:S(2)}) collective-permute-start(bf16[4,128,256]{2,1,0:T(8,128)(2,1)S(1)} %slice_bitcast_fusion), channel_id=1, source_target_pairs={{32,0},{232,8},{48,16},{248,24},{64,32},{8,40},{80,48},{24,56},{96... | collective-permute-start | bytes 786440 | tf_op jit(solution)/shard_map/ppermute | solution.py:200
  109.3 4.7 %collective-permute-start.7 = (bf16[4,2,128,256]{3,2,1,0:T(8,128)(2,1)S(1)}, bf16[4,2,128,256]{3,2,1,0:T(8,128)(2,1)S(1)}, u32[]{:S(2)}, u32[]{:S(2)}) collective-permute-start(bf16[4,2,128,256]{3,2,1,0:T(8,128)(2,1)S(1)} %bitcast.6), channel_id=1, source_target_pairs={{240,0},{248,8},{0,16},{8,24},{16,32},{24,40},{32,48},{40,56},{48,... | collective-permute-start | bytes 1572872 | tf_op jit(solution)/shard_map/ppermute | solution.py:201
  114.0 3.4 %collective-permute-start.6 = (bf16[4,2,128,256]{3,2,1,0:T(8,128)(2,1)S(1)}, bf16[4,2,128,256]{3,2,1,0:T(8,128)(2,1)S(1)}, u32[]{:S(2)}, u32[]{:S(2)}) collective-permute-start(bf16[4,2,128,256]{3,2,1,0:T(8,128)(2,1)S(1)} %bitcast.7), channel_id=1, source_target_pairs={{16,0},{24,8},{32,16},{40,24},{48,32},{56,40},{64,48},{72,56},{80,... | collective-permute-start | bytes 1572872 | tf_op jit(solution)/shard_map/ppermute | solution.py:201
  117.4 1.9 %collective-permute-start.9 = (bf16[4,128,256]{2,1,0:T(8,128)(2,1)S(1)}, bf16[4,128,256]{2,1,0:T(8,128)(2,1)S(1)}, u32[]{:S(2)}, u32[]{:S(2)}) collective-permute-start(bf16[4,128,256]{2,1,0:T(8,128)(2,1)S(1)} %collective-permute-done.8.two), channel_id=1, source_target_pairs={{0,256},{256,0},{1,257},{257,1},{2,258},{258,2},{3,259},{259,3},{4... | collective-permute-start | bytes 786440 | tf_op jit(solution)/shard_map/ppermute | solution.py:202
  119.3 5.5 %collective-permute-done.9.two_far = bf16[4,128,256]{2,1,0:T(8,128)(2,1)S(1)} collective-permute-done((bf16[4,128,256]{2,1,0:T(8,128)(2,1)S(1)}, bf16[4,128,256]{2,1,0:T(8,128)(2,1)S(1)}, u32[]{:S(2)}, u32[]{:S(2)}) %collective-permute-start.9) | collective-permute-done | bytes 262176 | tf_op jit(solution)/shard_map/ppermute | solution.py:202
  125.3 7.1 %collective-permute-done.6.up = bf16[4,2,128,256]{3,2,1,0:T(8,128)(2,1)S(1)} collective-permute-done((bf16[4,2,128,256]{3,2,1,0:T(8,128)(2,1)S(1)}, bf16[4,2,128,256]{3,2,1,0:T(8,128)(2,1)S(1)}, u32[]{:S(2)}, u32[]{:S(2)}) %collective-permute-start.6) | collective-permute-done | bytes 524320 | tf_op jit(solution)/shard_map/ppermute | solution.py:201
  132.5 5.3 %collective-permute-start.10 = (bf16[4,4,2,128,256]{4,3,2,1,0:T(8,128)(2,1)S(1)}, bf16[4,4,2,128,256]{4,3,2,1,0:T(8,128)(2,1)S(1)}, u32[]{:S(2)}, u32[]{:S(2)}) collective-permute-start(bf16[4,4,2,128,256]{4,3,2,1,0:T(8,128)(2,1)S(1)} %classes.1.refs_0_), channel_id=1, source_target_pairs={{0,8},{8,0},{1,9},{9,1},{2,10},{10,2},{3,11},{11,3},{4,12},{12,4},... | collective-permute-start | bytes 6291464 | tf_op jit(solution)/shard_map/ppermute | solution.py:204
  137.8 3.8 %collective-permute-done.10.refs_1_ = bf16[4,4,2,128,256]{4,3,2,1,0:T(8,128)(2,1)S(1)} collective-permute-done((bf16[4,4,2,128,256]{4,3,2,1,0:T(8,128)(2,1)S(1)}, bf16[4,4,2,128,256]{4,3,2,1,0:T(8,128)(2,1)S(1)}, u32[]{:S(2)}, u32[]{:S(2)}) %collective-permute-start.10) | collective-permute-done | bytes 2097184 | tf_op jit(solution)/shard_map/ppermute | solution.py:204
  143.0 22.3 %all_to_all.16.diffs = bf16[8,128,512]{2,1,0:T(8,128)(2,1)S(1)} all-to-all(bf16[8,128,512]{2,1,0:T(8,128)(2,1)S(1)} %get-tuple-element.35), channel_id=1, replica_groups=mesh['ylo'=2,'zh'=4,'zl'=4,'core'=2,'yhi'=2,'x'=4] {'yhi','x'}, dimensions={0} | all-to-all | bytes 2097152 | tf_op jit(solution)/shard_map/all_to_all | solution.py:207
  165.3 2.0 %last_step.1 = bf16[128,512]{1,0:T(8,128)(2,1)} custom-call(bf16[8,128,512]{2,1,0:T(8,128)(2,1)S(1)} %all_to_all.16.diffs, bf16[4,4,2,128,256]{4,3,2,1,0:T(8,128)(2,1)S(1)} %classes.1.refs_0_, bf16[4,4,2,128,256]{4,3,2,1,0:T(8,128)(2,1)S(1)} %collective-permute-done.10.refs_1_, bf16[128,512]{1,0:T(8,128)(2,1)S(1)} %get-tuple-element.36.refs_2_, ...), custom_call_target="tpu_custom_call" | custom-call | flops 536870912 | bytes 3145728 | tf_op jit(solution)/shard_map/last_step/pallas_call | solution.py:132
  (20 shorter events, 3.4 us)
Async XLA Ops:
  0.0 57.5 %copy-start.1 = (bf16[1024,64]{0,1:T(8,128)(2,1)S(1)}, bf16[1024,64]{0,1:T(8,128)(2,1)}, u32[]{:S(2)}) copy-start(bf16[1024,64]{0,1:T(8,128)(2,1)} %param.3) | copy-start | bytes 393220
  0.0 55.2 %copy-start = (bf16[128,512]{1,0:T(8,128)(2,1)S(1)}, bf16[128,512]{1,0:T(8,128)(2,1)}, u32[]{:S(2)}) copy-start(bf16[128,512]{1,0:T(8,128)(2,1)} %refs_3_.1) | copy-start | bytes 393220
  0.0 55.2 %copy-start.2 = (s32[64,16]{0,1:T(8,128)S(1)}, s32[64,16]{0,1:T(8,128)}, u32[]{:S(2)}) copy-start(s32[64,16]{0,1:T(8,128)} %param.5) | copy-start | bytes 12292
  31.5 17.5 %collective-permute-start = (bf16[256,1024]{1,0:T(8,128)(2,1)S(1)}, bf16[256,1024]{1,0:T(8,128)(2,1)S(1)}, u32[]{:S(2)}, u32[]{:S(2)}) collective-permute-start(bf16[256,1024]{1,0:T(8,128)(2,1)S(1)} %all_gather.9.own), channel_id=1, source_target_pairs={{0,256},{256,0},{1,257},{257,1},{2,258},{258,2},{3,259},{259,3},{4... | collective-permute-start | bytes 1572872 | tf_op jit(solution)/shard_map/ppermute | solution.py:179
  34.7 9.3 %collective-permute-start.3 = (bf16[64,1024]{1,0:T(8,128)(2,1)}, bf16[64,1024]{1,0:T(8,128)(2,1)S(1)}, u32[]{:S(2)}, u32[]{:S(2)}) collective-permute-start(bf16[64,1024]{1,0:T(8,128)(2,1)} %bitcast.10), channel_id=1, source_target_pairs={{48,0},{0,16},{16,32},{32,48},{49,1},{1,17},{17,33},{33,49},{50,2}... | collective-permute-start | bytes 393224 | tf_op jit(solution)/shard_map/ppermute | solution.py:181
  37.2 9.9 %collective-permute-start.2 = (bf16[64,1024]{1,0:T(8,128)(2,1)}, bf16[64,1024]{1,0:T(8,128)(2,1)S(1)}, u32[]{:S(2)}, u32[]{:S(2)}) collective-permute-start(bf16[64,1024]{1,0:T(8,128)(2,1)} %bitcast.11), channel_id=1, source_target_pairs={{32,0},{48,16},{0,32},{16,48},{33,1},{49,17},{1,33},{17,49},{34,2}... | collective-permute-start | bytes 393224 | tf_op jit(solution)/shard_map/ppermute | solution.py:181
  39.8 9.2 %collective-permute-start.1 = (bf16[64,1024]{1,0:T(8,128)(2,1)}, bf16[64,1024]{1,0:T(8,128)(2,1)S(1)}, u32[]{:S(2)}, u32[]{:S(2)}) collective-permute-start(bf16[64,1024]{1,0:T(8,128)(2,1)} %bitcast.12), channel_id=1, source_target_pairs={{16,0},{32,16},{48,32},{0,48},{17,1},{33,17},{49,33},{1,49},{18,2}... | collective-permute-start | bytes 393224 | tf_op jit(solution)/shard_map/ppermute | solution.py:181
  49.1 8.3 %collective-permute-start.4 = (bf16[2,256,1024]{2,1,0:T(8,128)(2,1)S(1)}, bf16[2,256,1024]{2,1,0:T(8,128)(2,1)S(1)}, u32[]{:S(2)}, u32[]{:S(2)}) collective-permute-start(bf16[2,256,1024]{2,1,0:T(8,128)(2,1)S(1)} %pair.2.cols), channel_id=1, source_target_pairs={{0,8},{8,0},{1,9},{9,1},{2,10},{10,2},{3,11},{11,3},{4,12},{12,4},... | collective-permute-start | bytes 3145736 | tf_op jit(solution)/shard_map/ppermute | solution.py:184
  75.5 5.0 %collective-permute-start.5 = (bf16[128,256]{1,0:T(8,128)(2,1)S(1)}, bf16[128,256]{1,0:T(8,128)(2,1)S(1)}, u32[]{:S(2)}, u32[]{:S(2)}) collective-permute-start(bf16[128,256]{1,0:T(8,128)(2,1)S(1)} %multiply_convert_fusion.own), channel_id=1, source_target_pairs={{0,256},{256,0},{1,257},{257,1},{2,258},{258,2},{3,259},{259,3},{4... | collective-permute-start | bytes 196616 | tf_op jit(solution)/shard_map/ppermute | solution.py:194
  80.5 23.8 %all-to-all-start.1 = ((bf16[8,128,512]{2,1,0:T(8,128)(2,1)}), bf16[8,128,512]{2,1,0:T(8,128)(2,1)S(1)}, u32[]{:S(2)}, u32[]{:S(2)}) async-start(bf16[8,128,512]{2,1,0:T(8,128)(2,1)} %get-tuple-element.30), calls=%async_computation.1 | async-start | bytes 2097152 | tf_op jit(solution)/shard_map/all_to_all | solution.py:196
  104.3 13.1 %collective-permute-start.8 = (bf16[4,128,256]{2,1,0:T(8,128)(2,1)S(1)}, bf16[4,128,256]{2,1,0:T(8,128)(2,1)S(1)}, u32[]{:S(2)}, u32[]{:S(2)}) collective-permute-start(bf16[4,128,256]{2,1,0:T(8,128)(2,1)S(1)} %slice_bitcast_fusion), channel_id=1, source_target_pairs={{32,0},{232,8},{48,16},{248,24},{64,32},{8,40},{80,48},{24,56},{96... | collective-permute-start | bytes 786440 | tf_op jit(solution)/shard_map/ppermute | solution.py:200
  109.3 16.0 %collective-permute-start.7 = (bf16[4,2,128,256]{3,2,1,0:T(8,128)(2,1)S(1)}, bf16[4,2,128,256]{3,2,1,0:T(8,128)(2,1)S(1)}, u32[]{:S(2)}, u32[]{:S(2)}) collective-permute-start(bf16[4,2,128,256]{3,2,1,0:T(8,128)(2,1)S(1)} %bitcast.6), channel_id=1, source_target_pairs={{240,0},{248,8},{0,16},{8,24},{16,32},{24,40},{32,48},{40,56},{48,... | collective-permute-start | bytes 1572872 | tf_op jit(solution)/shard_map/ppermute | solution.py:201
  114.0 18.4 %collective-permute-start.6 = (bf16[4,2,128,256]{3,2,1,0:T(8,128)(2,1)S(1)}, bf16[4,2,128,256]{3,2,1,0:T(8,128)(2,1)S(1)}, u32[]{:S(2)}, u32[]{:S(2)}) collective-permute-start(bf16[4,2,128,256]{3,2,1,0:T(8,128)(2,1)S(1)} %bitcast.7), channel_id=1, source_target_pairs={{16,0},{24,8},{32,16},{40,24},{48,32},{56,40},{64,48},{72,56},{80,... | collective-permute-start | bytes 1572872 | tf_op jit(solution)/shard_map/ppermute | solution.py:201
  117.4 7.4 %collective-permute-start.9 = (bf16[4,128,256]{2,1,0:T(8,128)(2,1)S(1)}, bf16[4,128,256]{2,1,0:T(8,128)(2,1)S(1)}, u32[]{:S(2)}, u32[]{:S(2)}) collective-permute-start(bf16[4,128,256]{2,1,0:T(8,128)(2,1)S(1)} %collective-permute-done.8.two), channel_id=1, source_target_pairs={{0,256},{256,0},{1,257},{257,1},{2,258},{258,2},{3,259},{259,3},{4... | collective-permute-start | bytes 786440 | tf_op jit(solution)/shard_map/ppermute | solution.py:202
  132.5 9.0 %collective-permute-start.10 = (bf16[4,4,2,128,256]{4,3,2,1,0:T(8,128)(2,1)S(1)}, bf16[4,4,2,128,256]{4,3,2,1,0:T(8,128)(2,1)S(1)}, u32[]{:S(2)}, u32[]{:S(2)}) collective-permute-start(bf16[4,4,2,128,256]{4,3,2,1,0:T(8,128)(2,1)S(1)} %classes.1.refs_0_), channel_id=1, source_target_pairs={{0,8},{8,0},{1,9},{9,1},{2,10},{10,2},{3,11},{11,3},{4,12},{12,4},... | collective-permute-start | bytes 6291464 | tf_op jit(solution)/shard_map/ppermute | solution.py:204

commit v13 on v11

--- a/solution.py
+++ b/solution.py
@@ -179,8 +179,9 @@
     own = lax.all_gather(feats, "zh", axis=0, tiled=True)
     other = lax.ppermute(own, "ylo", SWAP)
     near = lax.optimization_barrier((feats, own))[0]
-    rows = [feats] + [lax.ppermute(near, "zl", [((i + d) % 4, i) for i in range(4)]) for d in (1, 2, 3)]
-    other, *rows[1:] = lax.optimization_barrier((other, *rows[1:]))
+    parts = {d: lax.ppermute(near, "zl", [((i + d) % 4, i) for i in range(4)]) for d in (1, 3, 2)}
+    rows = [feats, parts[1], parts[2], parts[3]]
+    other, rows[1], rows[3], rows[2] = lax.optimization_barrier((other, rows[1], rows[3], rows[2]))
     cols = pack(pair_kernel, "pair", own, other)
     mates = lax.ppermute(cols, "core", SWAP)
 

time: 167 us -> 166 us (level)
    ppermute x1, waiting for transfers between devices: 0.01 us -> 2.88 us  [on_device(): two = lax.ppermute(half, line, from_z(2, -2))]
    all_gather x1, blocking collectives: 20.2 us -> 22.6 us  [on_device(): mine = lax.all_gather(gram, 'zh', axis=0)]
    ppermute x3, waiting for transfers between devices: 5 us -> 2.66 us  [on_device(): lax.ppermute(near, 'zl', [((i + d) % 4, i) for i in range(4)])]
    ppermute x1, starting transfers between devices: 4.98 us -> 2.82 us  [on_device(): two = lax.ppermute(half, line, from_z(2, -2))]
    ppermute x2, waiting for transfers between devices: 7.57 us -> 5.87 us  [on_device(): up, down = (lax.ppermute(mine, line, from_z(s, s)) for s in (1, -1))]
where the time goes in v13:
time: 166 us
  blocking collectives  96.5 us (58%)
  starting transfers between devices  41.4 us (25%)
  waiting for transfers between devices  21 us (13%)
  Pallas kernels  6.25 us (4%)
    all_gather x1, blocking collectives, on_device(): own = lax.all_gather(feats, 'zh', axis=0, tiled=True)  31.5 us
    all_gather x1, blocking collectives, on_device(): mine = lax.all_gather(gram, 'zh', axis=0)  22.6 us
    all_to_all x1, blocking collectives, on_device(): diffs = lax.all_to_all(sent, ROW, 0, 0, tiled=True)  21.5 us
    all_to_all x1, blocking collectives, on_device(): terms = lax.all_to_all(term, ROW, 0, 0, tiled=True)  17.1 us
    ppermute x3, starting transfers between devices, on_device(): lax.ppermute(near, 'zl', [((i + d) % 4, i) for i in range(4)])  10.2 us
    ppermute x1, starting transfers between devices, on_device(): mates = lax.ppermute(cols, 'core', SWAP)  7.45 us
    ppermute x2, starting transfers between devices, on_device(): up, down = (lax.ppermute(mine, line, from_z(s, s)) for s in (1, -1))  6.77 us
    ppermute x2, waiting for transfers between devices, on_device(): up, down = (lax.ppermute(mine, line, from_z(s, s)) for s in (1, -1))  5.87 us
  transfers between devices with their start and end apart: 11, of which 7 were waited for; matrix products, arithmetic and copies ran while one was open for 0% of the time, Pallas kernels for 1%

profile of v13, /device:TPU:1, one launch (start us, length us, event | category | flops | bytes accessed | tf_op | source)
XLA Modules:
  0.0 165.5 jit_solution(4110592101951807344)
XLA Ops:
  0.0 31.5 %all_gather.13.own = bf16[256,1024]{1,0:T(8,128)(2,1)S(1)} all-gather(bf16[64,1024]{1,0:T(8,128)(2,1)} %bitcast.10), channel_id=1, replica_groups=mesh['ylo'=2,'zh'=4,'zl'=4,'core'=2,'yhi'=2,'x'=4] {'zh'}, dimensions={0}, use_global_device_ids=true | all-gather | bytes 655360 | tf_op jit(solution)/shard_map/all_gather | solution.py:179
  31.5 3.2 %collective-permute-start = (bf16[256,1024]{1,0:T(8,128)(2,1)S(1)}, bf16[256,1024]{1,0:T(8,128)(2,1)S(1)}, u32[]{:S(2)}, u32[]{:S(2)}) collective-permute-start(bf16[256,1024]{1,0:T(8,128)(2,1)S(1)} %all_gather.13.own), channel_id=1, source_target_pairs={{0,256},{256,0},{1,257},{257,1},{2,258},{258,2},{3,259},{259,3},{4... | collective-permute-start | bytes 1572872 | tf_op jit(solution)/shard_map/ppermute | solution.py:180
  34.7 3.1 %collective-permute-start.3 = (bf16[64,1024]{1,0:T(8,128)(2,1)}, bf16[64,1024]{1,0:T(8,128)(2,1)S(1)}, u32[]{:S(2)}, u32[]{:S(2)}) collective-permute-start(bf16[64,1024]{1,0:T(8,128)(2,1)} %bitcast.11), channel_id=1, source_target_pairs={{32,0},{48,16},{0,32},{16,48},{33,1},{49,17},{1,33},{17,49},{34,2}... | collective-permute-start | bytes 393224 | tf_op jit(solution)/shard_map/ppermute | solution.py:182
  37.9 2.0 %collective-permute-start.2 = (bf16[64,1024]{1,0:T(8,128)(2,1)}, bf16[64,1024]{1,0:T(8,128)(2,1)S(1)}, u32[]{:S(2)}, u32[]{:S(2)}) collective-permute-start(bf16[64,1024]{1,0:T(8,128)(2,1)} %bitcast.12), channel_id=1, source_target_pairs={{48,0},{0,16},{16,32},{32,48},{49,1},{1,17},{17,33},{33,49},{50,2}... | collective-permute-start | bytes 393224 | tf_op jit(solution)/shard_map/ppermute | solution.py:182
  39.8 5.1 %collective-permute-start.1 = (bf16[64,1024]{1,0:T(8,128)(2,1)}, bf16[64,1024]{1,0:T(8,128)(2,1)S(1)}, u32[]{:S(2)}, u32[]{:S(2)}) collective-permute-start(bf16[64,1024]{1,0:T(8,128)(2,1)} %bitcast.13), channel_id=1, source_target_pairs={{16,0},{32,16},{48,32},{0,48},{17,1},{33,17},{49,33},{1,49},{18,2}... | collective-permute-start | bytes 393224 | tf_op jit(solution)/shard_map/ppermute | solution.py:182
  46.3 1.4 collective-permute-done.1.r1
  47.7 7.5 %collective-permute-start.4 = (bf16[2,256,1024]{2,1,0:T(8,128)(2,1)S(1)}, bf16[2,256,1024]{2,1,0:T(8,128)(2,1)S(1)}, u32[]{:S(2)}, u32[]{:S(2)}) collective-permute-start(bf16[2,256,1024]{2,1,0:T(8,128)(2,1)S(1)} %pair.1.cols), channel_id=1, source_target_pairs={{0,8},{8,0},{1,9},{9,1},{2,10},{10,2},{3,11},{11,3},{4,12},{12,4},... | collective-permute-start | bytes 3145736 | tf_op jit(solution)/shard_map/ppermute | solution.py:186
  55.2 1.9 %start.1 = (bf16[128,512]{1,0:T(8,128)(2,1)S(1)}, bf16[8,128,512]{2,1,0:T(8,128)(2,1)}, f32[128,512]{1,0:T(8,128)S(1)}) custom-call(s32[16,64]{1,0:T(8,128)S(1)} %bitcast.15, bf16[128,512]{1,0:T(8,128)(2,1)S(1)} %copy-done), custom_call_target="tpu_custom_call" | custom-call | tf_op jit(solution)/shard_map/start/pallas_call | solution.py:60
  58.2 17.1 %all_to_all.15 = bf16[8,128,256]{2,1,0:T(8,128)(2,1)S(1)} all-to-all(bf16[8,128,256]{2,1,0:T(8,128)(2,1)S(1)} %partial_gram.1), channel_id=1, replica_groups=mesh['ylo'=2,'zh'=4,'zl'=4,'core'=2,'yhi'=2,'x'=4] {'yhi','x'}, dimensions={0} | all-to-all | bytes 1048576 | tf_op jit(solution)/shard_map/all_to_all | solution.py:192
  75.5 3.8 %all-gather = bf16[256,256]{1,0:T(8,128)(2,1)S(1)} all-gather(bf16[128,256]{1,0:T(8,128)(2,1)S(1)} %multiply_convert_fusion), channel_id=2, replica_groups=mesh['ylo'=2,'zh'=4,'zl'=4,'core'=2,'yhi'=2,'x'=4] {'ylo'}, dimensions={0}, use_global_device_ids=true | all-gather | bytes 196608 | tf_op jit(solution)/shard_map/all_gather | solution.py:196
  79.3 3.6 %all-to-all-start.1 = ((bf16[8,128,512]{2,1,0:T(8,128)(2,1)}), bf16[8,128,512]{2,1,0:T(8,128)(2,1)S(1)}, u32[]{:S(2)}, u32[]{:S(2)}) async-start(bf16[8,128,512]{2,1,0:T(8,128)(2,1)} %get-tuple-element.30), calls=%async_computation.1 | async-start | bytes 2097152 | tf_op jit(solution)/shard_map/all_to_all | solution.py:198
  82.8 22.6 %all-gather.1 = bf16[8,128,256]{2,1,0:T(8,128)(2,1)S(1)} all-gather(bf16[2,128,256]{2,1,0:T(8,128)(2,1)S(1)} %bitcast.16), channel_id=3, replica_groups=mesh['ylo'=2,'zh'=4,'zl'=4,'core'=2,'yhi'=2,'x'=4] {'zh'}, dimensions={0}, use_global_device_ids=true | all-gather | bytes 655360 | tf_op jit(solution)/shard_map/all_gather | solution.py:199
  105.4 2.8 %collective-permute-start.7 = (bf16[4,128,256]{2,1,0:T(8,128)(2,1)S(1)}, bf16[4,128,256]{2,1,0:T(8,128)(2,1)S(1)}, u32[]{:S(2)}, u32[]{:S(2)}) collective-permute-start(bf16[4,128,256]{2,1,0:T(8,128)(2,1)S(1)} %dynamic-slice_bitcast_fusion), channel_id=1, source_target_pairs={{32,0},{232,8},{48,16},{248,24},{64,32},{8,40},{80,48},{24,56},{96... | collective-permute-start | bytes 786440 | tf_op jit(solution)/shard_map/ppermute | solution.py:202
  108.3 4.9 %collective-permute-start.6 = (bf16[4,2,128,256]{3,2,1,0:T(8,128)(2,1)S(1)}, bf16[4,2,128,256]{3,2,1,0:T(8,128)(2,1)S(1)}, u32[]{:S(2)}, u32[]{:S(2)}) collective-permute-start(bf16[4,2,128,256]{3,2,1,0:T(8,128)(2,1)S(1)} %bitcast.7), channel_id=1, source_target_pairs={{240,0},{248,8},{0,16},{8,24},{16,32},{24,40},{32,48},{40,56},{48,... | collective-permute-start | bytes 1572872 | tf_op jit(solution)/shard_map/ppermute | solution.py:203
  113.1 1.9 %collective-permute-start.5 = (bf16[4,2,128,256]{3,2,1,0:T(8,128)(2,1)S(1)}, bf16[4,2,128,256]{3,2,1,0:T(8,128)(2,1)S(1)}, u32[]{:S(2)}, u32[]{:S(2)}) collective-permute-start(bf16[4,2,128,256]{3,2,1,0:T(8,128)(2,1)S(1)} %bitcast.8), channel_id=1, source_target_pairs={{16,0},{24,8},{32,16},{40,24},{48,32},{56,40},{64,48},{72,56},{80,... | collective-permute-start | bytes 1572872 | tf_op jit(solution)/shard_map/ppermute | solution.py:203
  115.1 2.9 %collective-permute-done.7.two = bf16[4,128,256]{2,1,0:T(8,128)(2,1)S(1)} collective-permute-done((bf16[4,128,256]{2,1,0:T(8,128)(2,1)S(1)}, bf16[4,128,256]{2,1,0:T(8,128)(2,1)S(1)}, u32[]{:S(2)}, u32[]{:S(2)}) %collective-permute-start.7) | collective-permute-done | bytes 262176 | tf_op jit(solution)/shard_map/ppermute | solution.py:202
  117.9 1.9 %collective-permute-start.8 = (bf16[4,128,256]{2,1,0:T(8,128)(2,1)S(1)}, bf16[4,128,256]{2,1,0:T(8,128)(2,1)S(1)}, u32[]{:S(2)}, u32[]{:S(2)}) collective-permute-start(bf16[4,128,256]{2,1,0:T(8,128)(2,1)S(1)} %collective-permute-done.7.two), channel_id=1, source_target_pairs={{0,256},{256,0},{1,257},{257,1},{2,258},{258,2},{3,259},{259,3},{4... | collective-permute-start | bytes 786440 | tf_op jit(solution)/shard_map/ppermute | solution.py:204
  119.8 5.5 %collective-permute-done.8.two_far = bf16[4,128,256]{2,1,0:T(8,128)(2,1)S(1)} collective-permute-done((bf16[4,128,256]{2,1,0:T(8,128)(2,1)S(1)}, bf16[4,128,256]{2,1,0:T(8,128)(2,1)S(1)}, u32[]{:S(2)}, u32[]{:S(2)}) %collective-permute-start.8) | collective-permute-done | bytes 262176 | tf_op jit(solution)/shard_map/ppermute | solution.py:204
  125.3 5.9 %collective-permute-done.5.up = bf16[4,2,128,256]{3,2,1,0:T(8,128)(2,1)S(1)} collective-permute-done((bf16[4,2,128,256]{3,2,1,0:T(8,128)(2,1)S(1)}, bf16[4,2,128,256]{3,2,1,0:T(8,128)(2,1)S(1)}, u32[]{:S(2)}, u32[]{:S(2)}) %collective-permute-start.5) | collective-permute-done | bytes 524320 | tf_op jit(solution)/shard_map/ppermute | solution.py:203
  131.4 5.5 %collective-permute-start.9 = (bf16[4,4,2,128,256]{4,3,2,1,0:T(8,128)(2,1)S(1)}, bf16[4,4,2,128,256]{4,3,2,1,0:T(8,128)(2,1)S(1)}, u32[]{:S(2)}, u32[]{:S(2)}) collective-permute-start(bf16[4,4,2,128,256]{4,3,2,1,0:T(8,128)(2,1)S(1)} %classes.1.refs_0_), channel_id=1, source_target_pairs={{0,8},{8,0},{1,9},{9,1},{2,10},{10,2},{3,11},{11,3},{4,12},{12,4},... | collective-permute-start | bytes 6291464 | tf_op jit(solution)/shard_map/ppermute | solution.py:206
  136.9 3.8 %collective-permute-done.9.refs_1_ = bf16[4,4,2,128,256]{4,3,2,1,0:T(8,128)(2,1)S(1)} collective-permute-done((bf16[4,4,2,128,256]{4,3,2,1,0:T(8,128)(2,1)S(1)}, bf16[4,4,2,128,256]{4,3,2,1,0:T(8,128)(2,1)S(1)}, u32[]{:S(2)}, u32[]{:S(2)}) %collective-permute-start.9) | collective-permute-done | bytes 2097184 | tf_op jit(solution)/shard_map/ppermute | solution.py:206
  140.6 1.4 first_step.1
  142.1 21.5 %all_to_all.16.diffs = bf16[8,128,512]{2,1,0:T(8,128)(2,1)S(1)} all-to-all(bf16[8,128,512]{2,1,0:T(8,128)(2,1)S(1)} %get-tuple-element.35), channel_id=1, replica_groups=mesh['ylo'=2,'zh'=4,'zl'=4,'core'=2,'yhi'=2,'x'=4] {'yhi','x'}, dimensions={0} | all-to-all | bytes 2097152 | tf_op jit(solution)/shard_map/all_to_all | solution.py:209
  163.6 2.0 %last_step.1 = bf16[128,512]{1,0:T(8,128)(2,1)} custom-call(bf16[8,128,512]{2,1,0:T(8,128)(2,1)S(1)} %all_to_all.16.diffs, bf16[4,4,2,128,256]{4,3,2,1,0:T(8,128)(2,1)S(1)} %classes.1.refs_0_, bf16[4,4,2,128,256]{4,3,2,1,0:T(8,128)(2,1)S(1)} %collective-permute-done.9.refs_1_, bf16[128,512]{1,0:T(8,128)(2,1)S(1)} %get-tuple-element.36.refs_2_, ...), custom_call_target="tpu_custom_call" | custom-call | flops 536870912 | bytes 3145728 | tf_op jit(solution)/shard_map/last_step/pallas_call | solution.py:132
  (18 shorter events, 2.8 us)
Async XLA Ops:
  0.0 57.4 %copy-start.1 = (bf16[1024,64]{0,1:T(8,128)(2,1)S(1)}, bf16[1024,64]{0,1:T(8,128)(2,1)}, u32[]{:S(2)}) copy-start(bf16[1024,64]{0,1:T(8,128)(2,1)} %param.3) | copy-start | bytes 393220
  0.0 55.2 %copy-start = (bf16[128,512]{1,0:T(8,128)(2,1)S(1)}, bf16[128,512]{1,0:T(8,128)(2,1)}, u32[]{:S(2)}) copy-start(bf16[128,512]{1,0:T(8,128)(2,1)} %refs_3_.1) | copy-start | bytes 393220
  0.0 55.2 %copy-start.2 = (s32[64,16]{0,1:T(8,128)S(1)}, s32[64,16]{0,1:T(8,128)}, u32[]{:S(2)}) copy-start(s32[64,16]{0,1:T(8,128)} %param.5) | copy-start | bytes 12292
  31.5 16.1 %collective-permute-start = (bf16[256,1024]{1,0:T(8,128)(2,1)S(1)}, bf16[256,1024]{1,0:T(8,128)(2,1)S(1)}, u32[]{:S(2)}, u32[]{:S(2)}) collective-permute-start(bf16[256,1024]{1,0:T(8,128)(2,1)S(1)} %all_gather.13.own), channel_id=1, source_target_pairs={{0,256},{256,0},{1,257},{257,1},{2,258},{258,2},{3,259},{259,3},{4... | collective-permute-start | bytes 1572872 | tf_op jit(solution)/shard_map/ppermute | solution.py:180
  34.7 10.2 %collective-permute-start.3 = (bf16[64,1024]{1,0:T(8,128)(2,1)}, bf16[64,1024]{1,0:T(8,128)(2,1)S(1)}, u32[]{:S(2)}, u32[]{:S(2)}) collective-permute-start(bf16[64,1024]{1,0:T(8,128)(2,1)} %bitcast.11), channel_id=1, source_target_pairs={{32,0},{48,16},{0,32},{16,48},{33,1},{49,17},{1,33},{17,49},{34,2}... | collective-permute-start | bytes 393224 | tf_op jit(solution)/shard_map/ppermute | solution.py:182
  37.9 8.4 %collective-permute-start.2 = (bf16[64,1024]{1,0:T(8,128)(2,1)}, bf16[64,1024]{1,0:T(8,128)(2,1)S(1)}, u32[]{:S(2)}, u32[]{:S(2)}) collective-permute-start(bf16[64,1024]{1,0:T(8,128)(2,1)} %bitcast.12), channel_id=1, source_target_pairs={{48,0},{0,16},{16,32},{32,48},{49,1},{1,17},{17,33},{33,49},{50,2}... | collective-permute-start | bytes 393224 | tf_op jit(solution)/shard_map/ppermute | solution.py:182
  39.8 7.8 %collective-permute-start.1 = (bf16[64,1024]{1,0:T(8,128)(2,1)}, bf16[64,1024]{1,0:T(8,128)(2,1)S(1)}, u32[]{:S(2)}, u32[]{:S(2)}) collective-permute-start(bf16[64,1024]{1,0:T(8,128)(2,1)} %bitcast.13), channel_id=1, source_target_pairs={{16,0},{32,16},{48,32},{0,48},{17,1},{33,17},{49,33},{1,49},{18,2}... | collective-permute-start | bytes 393224 | tf_op jit(solution)/shard_map/ppermute | solution.py:182
  47.7 9.7 %collective-permute-start.4 = (bf16[2,256,1024]{2,1,0:T(8,128)(2,1)S(1)}, bf16[2,256,1024]{2,1,0:T(8,128)(2,1)S(1)}, u32[]{:S(2)}, u32[]{:S(2)}) collective-permute-start(bf16[2,256,1024]{2,1,0:T(8,128)(2,1)S(1)} %pair.1.cols), channel_id=1, source_target_pairs={{0,8},{8,0},{1,9},{9,1},{2,10},{10,2},{3,11},{11,3},{4,12},{12,4},... | collective-permute-start | bytes 3145736 | tf_op jit(solution)/shard_map/ppermute | solution.py:186
  79.3 26.1 %all-to-all-start.1 = ((bf16[8,128,512]{2,1,0:T(8,128)(2,1)}), bf16[8,128,512]{2,1,0:T(8,128)(2,1)S(1)}, u32[]{:S(2)}, u32[]{:S(2)}) async-start(bf16[8,128,512]{2,1,0:T(8,128)(2,1)} %get-tuple-element.30), calls=%async_computation.1 | async-start | bytes 2097152 | tf_op jit(solution)/shard_map/all_to_all | solution.py:198
  105.4 12.5 %collective-permute-start.7 = (bf16[4,128,256]{2,1,0:T(8,128)(2,1)S(1)}, bf16[4,128,256]{2,1,0:T(8,128)(2,1)S(1)}, u32[]{:S(2)}, u32[]{:S(2)}) collective-permute-start(bf16[4,128,256]{2,1,0:T(8,128)(2,1)S(1)} %dynamic-slice_bitcast_fusion), channel_id=1, source_target_pairs={{32,0},{232,8},{48,16},{248,24},{64,32},{8,40},{80,48},{24,56},{96... | collective-permute-start | bytes 786440 | tf_op jit(solution)/shard_map/ppermute | solution.py:202
  108.3 17.1 %collective-permute-start.6 = (bf16[4,2,128,256]{3,2,1,0:T(8,128)(2,1)S(1)}, bf16[4,2,128,256]{3,2,1,0:T(8,128)(2,1)S(1)}, u32[]{:S(2)}, u32[]{:S(2)}) collective-permute-start(bf16[4,2,128,256]{3,2,1,0:T(8,128)(2,1)S(1)} %bitcast.7), channel_id=1, source_target_pairs={{240,0},{248,8},{0,16},{8,24},{16,32},{24,40},{32,48},{40,56},{48,... | collective-permute-start | bytes 1572872 | tf_op jit(solution)/shard_map/ppermute | solution.py:203
  113.1 18.1 %collective-permute-start.5 = (bf16[4,2,128,256]{3,2,1,0:T(8,128)(2,1)S(1)}, bf16[4,2,128,256]{3,2,1,0:T(8,128)(2,1)S(1)}, u32[]{:S(2)}, u32[]{:S(2)}) collective-permute-start(bf16[4,2,128,256]{3,2,1,0:T(8,128)(2,1)S(1)} %bitcast.8), channel_id=1, source_target_pairs={{16,0},{24,8},{32,16},{40,24},{48,32},{56,40},{64,48},{72,56},{80,... | collective-permute-start | bytes 1572872 | tf_op jit(solution)/shard_map/ppermute | solution.py:203
  117.9 7.4 %collective-permute-start.8 = (bf16[4,128,256]{2,1,0:T(8,128)(2,1)S(1)}, bf16[4,128,256]{2,1,0:T(8,128)(2,1)S(1)}, u32[]{:S(2)}, u32[]{:S(2)}) collective-permute-start(bf16[4,128,256]{2,1,0:T(8,128)(2,1)S(1)} %collective-permute-done.7.two), channel_id=1, source_target_pairs={{0,256},{256,0},{1,257},{257,1},{2,258},{258,2},{3,259},{259,3},{4... | collective-permute-start | bytes 786440 | tf_op jit(solution)/shard_map/ppermute | solution.py:204
  131.4 9.3 %collective-permute-start.9 = (bf16[4,4,2,128,256]{4,3,2,1,0:T(8,128)(2,1)S(1)}, bf16[4,4,2,128,256]{4,3,2,1,0:T(8,128)(2,1)S(1)}, u32[]{:S(2)}, u32[]{:S(2)}) collective-permute-start(bf16[4,4,2,128,256]{4,3,2,1,0:T(8,128)(2,1)S(1)} %classes.1.refs_0_), channel_id=1, source_target_pairs={{0,8},{8,0},{1,9},{9,1},{2,10},{10,2},{3,11},{11,3},{4,12},{12,4},... | collective-permute-start | bytes 6291464 | tf_op jit(solution)/shard_map/ppermute | solution.py:206

commit v14 on v13

--- a/solution.py
+++ b/solution.py
@@ -149,13 +149,9 @@
     out[1] = other[...]
 
 
-def classes_kernel(mine, up, down, two, two_far, out):
-    ylo = lax.axis_index("ylo")
-    out[0] = mine[...]
-    out[1] = up[...]
-    out[2] = down[...]
-    out[3, :, ylo] = two[...]
-    out[3, :, 1 - ylo] = two_far[...]
+def classes_kernel(*refs):
+    for i, ref in enumerate(refs[:-1]):
+        refs[-1][i] = ref[...]
 
 
 def pack(kernel, name, *parts):
@@ -198,11 +194,8 @@
     diffs = lax.all_to_all(diff, ROW, 0, 0, tiled=True)
     mine = lax.all_gather(gram, "zh", axis=0)
     diffs, mine = lax.optimization_barrier((diffs, mine))
-    half = lax.dynamic_index_in_dim(mine, lax.axis_index("ylo"), 1, keepdims=False)
-    two = lax.ppermute(half, line, from_z(2, -2))
-    up, down = (lax.ppermute(mine, line, from_z(s, s)) for s in (1, -1))
-    two_far = lax.ppermute(two, "ylo", SWAP)
-    packed = pack(classes_kernel, "classes", mine, up, down, two, two_far)
+    two, up, down = (lax.ppermute(mine, line, from_z(*d)) for d in ((2, -2), (1, 1), (-1, -1)))
+    packed = pack(classes_kernel, "classes", mine, up, down, two)
     grams = (packed, lax.ppermute(packed, "core", SWAP))
 
     weight, sent = step(False, diffs, grams, weight, base_weight, keep)

time: 166 us -> 172 us (1.036)
  waiting for transfers between devices: 21 us -> 25.5 us
    ppermute x4 -> x3, waiting for transfers between devices: 14.2 us -> 18.7 us  [on_device(): lax.ppermute(mine, line, from_z(*d))]
    ppermute x1, starting transfers between devices: 5.52 us -> 8.62 us  [on_device(): grams = (packed, lax.ppermute(packed, 'core', SWAP))]
    ppermute x4 -> x3, starting transfers between devices: 11.5 us -> 9.58 us  [on_device(): lax.ppermute(mine, line, from_z(*d))]
  transfers between devices with their start and end apart: 11 -> 10, of which waited for: 7 -> 7; matrix products, arithmetic and copies ran while one was open for 0% -> 0% of each run, Pallas kernels for 1% -> 1%
where the time goes in v14:
time: 172 us; the launch traced here: 171 us
  blocking collectives  96.6 us (56%)
  starting transfers between devices  42.6 us (25%)
  waiting for transfers between devices  25.5 us (15%)
  Pallas kernels  6.23 us (4%)
    all_gather x1, blocking collectives, on_device(): own = lax.all_gather(feats, 'zh', axis=0, tiled=True)  31.5 us
    all_gather x1, blocking collectives, on_device(): mine = lax.all_gather(gram, 'zh', axis=0)  22.6 us
    all_to_all x1, blocking collectives, on_device(): diffs = lax.all_to_all(sent, ROW, 0, 0, tiled=True)  21.5 us
    ppermute x3, waiting for transfers between devices, on_device(): lax.ppermute(mine, line, from_z(*d))  18.7 us
    all_to_all x1, blocking collectives, on_device(): terms = lax.all_to_all(term, ROW, 0, 0, tiled=True)  17.1 us
    ppermute x3, starting transfers between devices, on_device(): lax.ppermute(near, 'zl', [((i + d) % 4, i) for i in range(4)])  10.2 us
    ppermute x3, starting transfers between devices, on_device(): lax.ppermute(mine, line, from_z(*d))  9.58 us
    ppermute x1, starting transfers between devices, on_device(): grams = (packed, lax.ppermute(packed, 'core', SWAP))  8.62 us
  transfers between devices with their start and end apart: 10, of which 7 were waited for; matrix products, arithmetic and copies ran while one was open for 0% of the time, Pallas kernels for 1%

profile of v14, /device:TPU:1, one launch (start us, length us, event | category | flops | bytes accessed | tf_op | source)
XLA Modules:
  0.0 171.1 jit_solution(7623347229014002528)
XLA Ops:
  0.0 31.5 %all_gather.13.own = bf16[256,1024]{1,0:T(8,128)(2,1)S(1)} all-gather(bf16[64,1024]{1,0:T(8,128)(2,1)} %bitcast.8), channel_id=1, replica_groups=mesh['ylo'=2,'zh'=4,'zl'=4,'core'=2,'yhi'=2,'x'=4] {'zh'}, dimensions={0}, use_global_device_ids=true | all-gather | bytes 655360 | tf_op jit(solution)/shard_map/all_gather | solution.py:175
  31.5 3.2 %collective-permute-start = (bf16[256,1024]{1,0:T(8,128)(2,1)S(1)}, bf16[256,1024]{1,0:T(8,128)(2,1)S(1)}, u32[]{:S(2)}, u32[]{:S(2)}) collective-permute-start(bf16[256,1024]{1,0:T(8,128)(2,1)S(1)} %all_gather.13.own), channel_id=1, source_target_pairs={{0,256},{256,0},{1,257},{257,1},{2,258},{258,2},{3,259},{259,3},{4... | collective-permute-start | bytes 1572872 | tf_op jit(solution)/shard_map/ppermute | solution.py:176
  34.7 3.1 %collective-permute-start.3 = (bf16[64,1024]{1,0:T(8,128)(2,1)}, bf16[64,1024]{1,0:T(8,128)(2,1)S(1)}, u32[]{:S(2)}, u32[]{:S(2)}) collective-permute-start(bf16[64,1024]{1,0:T(8,128)(2,1)} %bitcast.9), channel_id=1, source_target_pairs={{32,0},{48,16},{0,32},{16,48},{33,1},{49,17},{1,33},{17,49},{34,2}... | collective-permute-start | bytes 393224 | tf_op jit(solution)/shard_map/ppermute | solution.py:178
  37.9 2.0 %collective-permute-start.2 = (bf16[64,1024]{1,0:T(8,128)(2,1)}, bf16[64,1024]{1,0:T(8,128)(2,1)S(1)}, u32[]{:S(2)}, u32[]{:S(2)}) collective-permute-start(bf16[64,1024]{1,0:T(8,128)(2,1)} %bitcast.10), channel_id=1, source_target_pairs={{48,0},{0,16},{16,32},{32,48},{49,1},{1,17},{17,33},{33,49},{50,2}... | collective-permute-start | bytes 393224 | tf_op jit(solution)/shard_map/ppermute | solution.py:178
  39.8 5.1 %collective-permute-start.1 = (bf16[64,1024]{1,0:T(8,128)(2,1)}, bf16[64,1024]{1,0:T(8,128)(2,1)S(1)}, u32[]{:S(2)}, u32[]{:S(2)}) collective-permute-start(bf16[64,1024]{1,0:T(8,128)(2,1)} %bitcast.11), channel_id=1, source_target_pairs={{16,0},{32,16},{48,32},{0,48},{17,1},{33,17},{49,33},{1,49},{18,2}... | collective-permute-start | bytes 393224 | tf_op jit(solution)/shard_map/ppermute | solution.py:178
  45.0 1.3 collective-permute-done.2.r3
  46.3 1.4 collective-permute-done.1.r1
  47.7 7.5 %collective-permute-start.4 = (bf16[2,256,1024]{2,1,0:T(8,128)(2,1)S(1)}, bf16[2,256,1024]{2,1,0:T(8,128)(2,1)S(1)}, u32[]{:S(2)}, u32[]{:S(2)}) collective-permute-start(bf16[2,256,1024]{2,1,0:T(8,128)(2,1)S(1)} %pair.1.cols), channel_id=1, source_target_pairs={{0,8},{8,0},{1,9},{9,1},{2,10},{10,2},{3,11},{11,3},{4,12},{12,4},... | collective-permute-start | bytes 3145736 | tf_op jit(solution)/shard_map/ppermute | solution.py:182
  55.2 1.9 %start.1 = (bf16[128,512]{1,0:T(8,128)(2,1)S(1)}, bf16[8,128,512]{2,1,0:T(8,128)(2,1)}, f32[128,512]{1,0:T(8,128)S(1)}) custom-call(s32[16,64]{1,0:T(8,128)S(1)} %bitcast.13, bf16[128,512]{1,0:T(8,128)(2,1)S(1)} %copy-done), custom_call_target="tpu_custom_call" | custom-call | tf_op jit(solution)/shard_map/start/pallas_call | solution.py:60
  57.4 0.8 partial_gram.1
  58.2 17.1 %all_to_all.15 = bf16[8,128,256]{2,1,0:T(8,128)(2,1)S(1)} all-to-all(bf16[8,128,256]{2,1,0:T(8,128)(2,1)S(1)} %partial_gram.1), channel_id=1, replica_groups=mesh['ylo'=2,'zh'=4,'zl'=4,'core'=2,'yhi'=2,'x'=4] {'yhi','x'}, dimensions={0} | all-to-all | bytes 1048576 | tf_op jit(solution)/shard_map/all_to_all | solution.py:188
  75.5 3.8 %all-gather = bf16[256,256]{1,0:T(8,128)(2,1)S(1)} all-gather(bf16[128,256]{1,0:T(8,128)(2,1)S(1)} %multiply_convert_fusion), channel_id=2, replica_groups=mesh['ylo'=2,'zh'=4,'zl'=4,'core'=2,'yhi'=2,'x'=4] {'ylo'}, dimensions={0}, use_global_device_ids=true | all-gather | bytes 196608 | tf_op jit(solution)/shard_map/all_gather | solution.py:192
  79.3 3.6 %all-to-all-start.1 = ((bf16[8,128,512]{2,1,0:T(8,128)(2,1)}), bf16[8,128,512]{2,1,0:T(8,128)(2,1)S(1)}, u32[]{:S(2)}, u32[]{:S(2)}) async-start(bf16[8,128,512]{2,1,0:T(8,128)(2,1)} %get-tuple-element.30), calls=%async_computation.1 | async-start | bytes 2097152 | tf_op jit(solution)/shard_map/all_to_all | solution.py:194
  82.8 22.6 %all-gather.1 = bf16[8,128,256]{2,1,0:T(8,128)(2,1)S(1)} all-gather(bf16[2,128,256]{2,1,0:T(8,128)(2,1)S(1)} %bitcast.14), channel_id=3, replica_groups=mesh['ylo'=2,'zh'=4,'zl'=4,'core'=2,'yhi'=2,'x'=4] {'zh'}, dimensions={0}, use_global_device_ids=true | all-gather | bytes 655360 | tf_op jit(solution)/shard_map/all_gather | solution.py:195
  105.4 2.8 %collective-permute-start.7 = (bf16[4,2,128,256]{3,2,1,0:T(8,128)(2,1)S(1)}, bf16[4,2,128,256]{3,2,1,0:T(8,128)(2,1)S(1)}, u32[]{:S(2)}, u32[]{:S(2)}) collective-permute-start(bf16[4,2,128,256]{3,2,1,0:T(8,128)(2,1)S(1)} %bitcast.4), channel_id=1, source_target_pairs={{32,0},{232,8},{48,16},{248,24},{64,32},{8,40},{80,48},{24,56},{96... | collective-permute-start | bytes 1572872 | tf_op jit(solution)/shard_map/ppermute | solution.py:197
  108.2 4.9 %collective-permute-start.6 = (bf16[4,2,128,256]{3,2,1,0:T(8,128)(2,1)S(1)}, bf16[4,2,128,256]{3,2,1,0:T(8,128)(2,1)S(1)}, u32[]{:S(2)}, u32[]{:S(2)}) collective-permute-start(bf16[4,2,128,256]{3,2,1,0:T(8,128)(2,1)S(1)} %bitcast.5), channel_id=1, source_target_pairs={{240,0},{248,8},{0,16},{8,24},{16,32},{24,40},{32,48},{40,56},{48,... | collective-permute-start | bytes 1572872 | tf_op jit(solution)/shard_map/ppermute | solution.py:197
  113.1 1.9 %collective-permute-start.5 = (bf16[4,2,128,256]{3,2,1,0:T(8,128)(2,1)S(1)}, bf16[4,2,128,256]{3,2,1,0:T(8,128)(2,1)S(1)}, u32[]{:S(2)}, u32[]{:S(2)}) collective-permute-start(bf16[4,2,128,256]{3,2,1,0:T(8,128)(2,1)S(1)} %bitcast.6), channel_id=1, source_target_pairs={{16,0},{24,8},{32,16},{40,24},{48,32},{56,40},{64,48},{72,56},{80,... | collective-permute-start | bytes 1572872 | tf_op jit(solution)/shard_map/ppermute | solution.py:197
  115.0 8.1 %collective-permute-done.7.refs_3_ = bf16[4,2,128,256]{3,2,1,0:T(8,128)(2,1)S(1)} collective-permute-done((bf16[4,2,128,256]{3,2,1,0:T(8,128)(2,1)S(1)}, bf16[4,2,128,256]{3,2,1,0:T(8,128)(2,1)S(1)}, u32[]{:S(2)}, u32[]{:S(2)}) %collective-permute-start.7) | collective-permute-done | bytes 524320 | tf_op jit(solution)/shard_map/ppermute | solution.py:197
  123.2 10.1 %collective-permute-done.6.refs_2_ = bf16[4,2,128,256]{3,2,1,0:T(8,128)(2,1)S(1)} collective-permute-done((bf16[4,2,128,256]{3,2,1,0:T(8,128)(2,1)S(1)}, bf16[4,2,128,256]{3,2,1,0:T(8,128)(2,1)S(1)}, u32[]{:S(2)}, u32[]{:S(2)}) %collective-permute-start.6) | collective-permute-done | bytes 524320 | tf_op jit(solution)/shard_map/ppermute | solution.py:197
  133.8 8.6 %collective-permute-start.8 = (bf16[4,4,2,128,256]{4,3,2,1,0:T(8,128)(2,1)S(1)}, bf16[4,4,2,128,256]{4,3,2,1,0:T(8,128)(2,1)S(1)}, u32[]{:S(2)}, u32[]{:S(2)}) collective-permute-start(bf16[4,4,2,128,256]{4,3,2,1,0:T(8,128)(2,1)S(1)} %classes.1.refs_0_), channel_id=1, source_target_pairs={{0,8},{8,0},{1,9},{9,1},{2,10},{10,2},{3,11},{11,3},{4,12},{12,4},... | collective-permute-start | bytes 6291464 | tf_op jit(solution)/shard_map/ppermute | solution.py:199
  142.5 3.8 %collective-permute-done.8.refs_1_ = bf16[4,4,2,128,256]{4,3,2,1,0:T(8,128)(2,1)S(1)} collective-permute-done((bf16[4,4,2,128,256]{4,3,2,1,0:T(8,128)(2,1)S(1)}, bf16[4,4,2,128,256]{4,3,2,1,0:T(8,128)(2,1)S(1)}, u32[]{:S(2)}, u32[]{:S(2)}) %collective-permute-start.8) | collective-permute-done | bytes 2097184 | tf_op jit(solution)/shard_map/ppermute | solution.py:199
  146.2 1.4 first_step.1
  147.6 21.5 %all_to_all.16.diffs = bf16[8,128,512]{2,1,0:T(8,128)(2,1)S(1)} all-to-all(bf16[8,128,512]{2,1,0:T(8,128)(2,1)S(1)} %get-tuple-element.35), channel_id=1, replica_groups=mesh['ylo'=2,'zh'=4,'zl'=4,'core'=2,'yhi'=2,'x'=4] {'yhi','x'}, dimensions={0} | all-to-all | bytes 2097152 | tf_op jit(solution)/shard_map/all_to_all | solution.py:202
  169.1 2.0 %last_step.1 = bf16[128,512]{1,0:T(8,128)(2,1)} custom-call(bf16[8,128,512]{2,1,0:T(8,128)(2,1)S(1)} %all_to_all.16.diffs, bf16[4,4,2,128,256]{4,3,2,1,0:T(8,128)(2,1)S(1)} %classes.1.refs_0_, bf16[4,4,2,128,256]{4,3,2,1,0:T(8,128)(2,1)S(1)} %collective-permute-done.8.refs_1_, bf16[128,512]{1,0:T(8,128)(2,1)S(1)} %get-tuple-element.36.refs_2_, ...), custom_call_target="tpu_custom_call" | custom-call | flops 536870912 | bytes 3145728 | tf_op jit(solution)/shard_map/last_step/pallas_call | solution.py:132
  (15 shorter events, 1.1 us)
Async XLA Ops:
  0.0 57.4 %copy-start.1 = (bf16[1024,64]{0,1:T(8,128)(2,1)S(1)}, bf16[1024,64]{0,1:T(8,128)(2,1)}, u32[]{:S(2)}) copy-start(bf16[1024,64]{0,1:T(8,128)(2,1)} %param.3) | copy-start | bytes 393220
  0.0 55.2 %copy-start = (bf16[128,512]{1,0:T(8,128)(2,1)S(1)}, bf16[128,512]{1,0:T(8,128)(2,1)}, u32[]{:S(2)}) copy-start(bf16[128,512]{1,0:T(8,128)(2,1)} %refs_3_.1) | copy-start | bytes 393220
  0.0 55.2 %copy-start.2 = (s32[64,16]{0,1:T(8,128)S(1)}, s32[64,16]{0,1:T(8,128)}, u32[]{:S(2)}) copy-start(s32[64,16]{0,1:T(8,128)} %param.5) | copy-start | bytes 12292
  31.5 16.1 %collective-permute-start = (bf16[256,1024]{1,0:T(8,128)(2,1)S(1)}, bf16[256,1024]{1,0:T(8,128)(2,1)S(1)}, u32[]{:S(2)}, u32[]{:S(2)}) collective-permute-start(bf16[256,1024]{1,0:T(8,128)(2,1)S(1)} %all_gather.13.own), channel_id=1, source_target_pairs={{0,256},{256,0},{1,257},{257,1},{2,258},{258,2},{3,259},{259,3},{4... | collective-permute-start | bytes 1572872 | tf_op jit(solution)/shard_map/ppermute | solution.py:176
  34.7 10.2 %collective-permute-start.3 = (bf16[64,1024]{1,0:T(8,128)(2,1)}, bf16[64,1024]{1,0:T(8,128)(2,1)S(1)}, u32[]{:S(2)}, u32[]{:S(2)}) collective-permute-start(bf16[64,1024]{1,0:T(8,128)(2,1)} %bitcast.9), channel_id=1, source_target_pairs={{32,0},{48,16},{0,32},{16,48},{33,1},{49,17},{1,33},{17,49},{34,2}... | collective-permute-start | bytes 393224 | tf_op jit(solution)/shard_map/ppermute | solution.py:178
  37.9 8.4 %collective-permute-start.2 = (bf16[64,1024]{1,0:T(8,128)(2,1)}, bf16[64,1024]{1,0:T(8,128)(2,1)S(1)}, u32[]{:S(2)}, u32[]{:S(2)}) collective-permute-start(bf16[64,1024]{1,0:T(8,128)(2,1)} %bitcast.10), channel_id=1, source_target_pairs={{48,0},{0,16},{16,32},{32,48},{49,1},{1,17},{17,33},{33,49},{50,2}... | collective-permute-start | bytes 393224 | tf_op jit(solution)/shard_map/ppermute | solution.py:178
  39.8 7.8 %collective-permute-start.1 = (bf16[64,1024]{1,0:T(8,128)(2,1)}, bf16[64,1024]{1,0:T(8,128)(2,1)S(1)}, u32[]{:S(2)}, u32[]{:S(2)}) collective-permute-start(bf16[64,1024]{1,0:T(8,128)(2,1)} %bitcast.11), channel_id=1, source_target_pairs={{16,0},{32,16},{48,32},{0,48},{17,1},{33,17},{49,33},{1,49},{18,2}... | collective-permute-start | bytes 393224 | tf_op jit(solution)/shard_map/ppermute | solution.py:178
  47.7 9.7 %collective-permute-start.4 = (bf16[2,256,1024]{2,1,0:T(8,128)(2,1)S(1)}, bf16[2,256,1024]{2,1,0:T(8,128)(2,1)S(1)}, u32[]{:S(2)}, u32[]{:S(2)}) collective-permute-start(bf16[2,256,1024]{2,1,0:T(8,128)(2,1)S(1)} %pair.1.cols), channel_id=1, source_target_pairs={{0,8},{8,0},{1,9},{9,1},{2,10},{10,2},{3,11},{11,3},{4,12},{12,4},... | collective-permute-start | bytes 3145736 | tf_op jit(solution)/shard_map/ppermute | solution.py:182
  79.3 26.1 %all-to-all-start.1 = ((bf16[8,128,512]{2,1,0:T(8,128)(2,1)}), bf16[8,128,512]{2,1,0:T(8,128)(2,1)S(1)}, u32[]{:S(2)}, u32[]{:S(2)}) async-start(bf16[8,128,512]{2,1,0:T(8,128)(2,1)} %get-tuple-element.30), calls=%async_computation.1 | async-start | bytes 2097152 | tf_op jit(solution)/shard_map/all_to_all | solution.py:194
  105.4 17.7 %collective-permute-start.7 = (bf16[4,2,128,256]{3,2,1,0:T(8,128)(2,1)S(1)}, bf16[4,2,128,256]{3,2,1,0:T(8,128)(2,1)S(1)}, u32[]{:S(2)}, u32[]{:S(2)}) collective-permute-start(bf16[4,2,128,256]{3,2,1,0:T(8,128)(2,1)S(1)} %bitcast.4), channel_id=1, source_target_pairs={{32,0},{232,8},{48,16},{248,24},{64,32},{8,40},{80,48},{24,56},{96... | collective-permute-start | bytes 1572872 | tf_op jit(solution)/shard_map/ppermute | solution.py:197
  108.2 25.0 %collective-permute-start.6 = (bf16[4,2,128,256]{3,2,1,0:T(8,128)(2,1)S(1)}, bf16[4,2,128,256]{3,2,1,0:T(8,128)(2,1)S(1)}, u32[]{:S(2)}, u32[]{:S(2)}) collective-permute-start(bf16[4,2,128,256]{3,2,1,0:T(8,128)(2,1)S(1)} %bitcast.5), channel_id=1, source_target_pairs={{240,0},{248,8},{0,16},{8,24},{16,32},{24,40},{32,48},{40,56},{48,... | collective-permute-start | bytes 1572872 | tf_op jit(solution)/shard_map/ppermute | solution.py:197
  113.1 20.6 %collective-permute-start.5 = (bf16[4,2,128,256]{3,2,1,0:T(8,128)(2,1)S(1)}, bf16[4,2,128,256]{3,2,1,0:T(8,128)(2,1)S(1)}, u32[]{:S(2)}, u32[]{:S(2)}) collective-permute-start(bf16[4,2,128,256]{3,2,1,0:T(8,128)(2,1)S(1)} %bitcast.6), channel_id=1, source_target_pairs={{16,0},{24,8},{32,16},{40,24},{48,32},{56,40},{64,48},{72,56},{80,... | collective-permute-start | bytes 1572872 | tf_op jit(solution)/shard_map/ppermute | solution.py:197
  133.8 12.4 %collective-permute-start.8 = (bf16[4,4,2,128,256]{4,3,2,1,0:T(8,128)(2,1)S(1)}, bf16[4,4,2,128,256]{4,3,2,1,0:T(8,128)(2,1)S(1)}, u32[]{:S(2)}, u32[]{:S(2)}) collective-permute-start(bf16[4,4,2,128,256]{4,3,2,1,0:T(8,128)(2,1)S(1)} %classes.1.refs_0_), channel_id=1, source_target_pairs={{0,8},{8,0},{1,9},{9,1},{2,10},{10,2},{3,11},{11,3},{4,12},{12,4},... | collective-permute-start | bytes 6291464 | tf_op jit(solution)/shard_map/ppermute | solution.py:199

commit v15 on v13

--- a/solution.py
+++ b/solution.py
@@ -149,13 +149,12 @@
     out[1] = other[...]
 
 
-def classes_kernel(mine, up, down, two, two_far, out):
-    ylo = lax.axis_index("ylo")
+def classes_kernel(mine, up, down, two, out):
     out[0] = mine[...]
     out[1] = up[...]
     out[2] = down[...]
-    out[3, :, ylo] = two[...]
-    out[3, :, 1 - ylo] = two_far[...]
+    for y in range(2):
+        out[3, :, y] = two[y]
 
 
 def pack(kernel, name, *parts):
@@ -201,8 +200,7 @@
     half = lax.dynamic_index_in_dim(mine, lax.axis_index("ylo"), 1, keepdims=False)
     two = lax.ppermute(half, line, from_z(2, -2))
     up, down = (lax.ppermute(mine, line, from_z(s, s)) for s in (1, -1))
-    two_far = lax.ppermute(two, "ylo", SWAP)
-    packed = pack(classes_kernel, "classes", mine, up, down, two, two_far)
+    packed = pack(classes_kernel, "classes", mine, up, down, lax.all_gather(two, "ylo", axis=0))
     grams = (packed, lax.ppermute(packed, "core", SWAP))
 
     weight, sent = step(False, diffs, grams, weight, base_weight, keep)

time: 166 us -> 171 us (1.030)
  blocking collectives: 96.5 us -> 104 us
  waiting for transfers between devices: 21 us -> 18.5 us
    ppermute x1, waiting for transfers between devices: 2.88 us -> 11.7 us  [on_device(): two = lax.ppermute(half, line, from_z(2, -2))]
    all_gather x0 -> x1, blocking collectives: none -> 5.89 us  [on_device(): lax.all_gather(two, 'ylo', axis=0)]
    ppermute x2, waiting for transfers between devices: 5.87 us -> 0.01 us  [on_device(): up, down = (lax.ppermute(mine, line, from_z(s, s)) for s in (1, -1))]
    ppermute x1 -> x0, waiting for transfers between devices: 5.48 us -> none  [on_device(): two_far = lax.ppermute(two, 'ylo', SWAP)]
    ppermute x1, starting transfers between devices: 5.52 us -> 7.92 us  [on_device(): grams = (packed, lax.ppermute(packed, 'core', SWAP))]
    ppermute x1 -> x0, starting transfers between devices: 1.91 us -> none  [on_device(): two_far = lax.ppermute(two, 'ylo', SWAP)]
  transfers between devices with their start and end apart: 11 -> 10, of which waited for: 7 -> 5; matrix products, arithmetic and copies ran while one was open for 0% -> 0% of each run, Pallas kernels for 1% -> 1%
where the time goes in v15:
time: 171 us
  blocking collectives  104 us (61%)
  starting transfers between devices  41.9 us (25%)
  waiting for transfers between devices  18.5 us (11%)
  Pallas kernels  6.23 us (4%)
    all_gather x1, blocking collectives, on_device(): own = lax.all_gather(feats, 'zh', axis=0, tiled=True)  31.5 us
    all_to_all x1, blocking collectives, on_device(): diffs = lax.all_to_all(sent, ROW, 0, 0, tiled=True)  23.1 us
    all_gather x1, blocking collectives, on_device(): mine = lax.all_gather(gram, 'zh', axis=0)  22.6 us
    all_to_all x1, blocking collectives, on_device(): terms = lax.all_to_all(term, ROW, 0, 0, tiled=True)  17.1 us
    ppermute x1, waiting for transfers between devices, on_device(): two = lax.ppermute(half, line, from_z(2, -2))  11.7 us
    ppermute x3, starting transfers between devices, on_device(): lax.ppermute(near, 'zl', [((i + d) % 4, i) for i in range(4)])  10.2 us
    ppermute x1, starting transfers between devices, on_device(): grams = (packed, lax.ppermute(packed, 'core', SWAP))  7.92 us
    ppermute x1, starting transfers between devices, on_device(): mates = lax.ppermute(cols, 'core', SWAP)  7.45 us
  transfers between devices with their start and end apart: 10, of which 5 were waited for; matrix products, arithmetic and copies ran while one was open for 0% of the time, Pallas kernels for 1%

profile of v15, /device:TPU:1, one launch (start us, length us, event | category | flops | bytes accessed | tf_op | source)
XLA Modules:
  0.0 171.0 jit_solution(15198068642748943092)
XLA Ops:
  0.0 31.5 %all_gather.19.own = bf16[256,1024]{1,0:T(8,128)(2,1)S(1)} all-gather(bf16[64,1024]{1,0:T(8,128)(2,1)} %bitcast.12), channel_id=1, replica_groups=mesh['ylo'=2,'zh'=4,'zl'=4,'core'=2,'yhi'=2,'x'=4] {'zh'}, dimensions={0}, use_global_device_ids=true | all-gather | bytes 655360 | tf_op jit(solution)/shard_map/all_gather | solution.py:178
  31.5 3.2 %collective-permute-start = (bf16[256,1024]{1,0:T(8,128)(2,1)S(1)}, bf16[256,1024]{1,0:T(8,128)(2,1)S(1)}, u32[]{:S(2)}, u32[]{:S(2)}) collective-permute-start(bf16[256,1024]{1,0:T(8,128)(2,1)S(1)} %all_gather.19.own), channel_id=1, source_target_pairs={{0,256},{256,0},{1,257},{257,1},{2,258},{258,2},{3,259},{259,3},{4... | collective-permute-start | bytes 1572872 | tf_op jit(solution)/shard_map/ppermute | solution.py:179
  34.7 3.1 %collective-permute-start.3 = (bf16[64,1024]{1,0:T(8,128)(2,1)}, bf16[64,1024]{1,0:T(8,128)(2,1)S(1)}, u32[]{:S(2)}, u32[]{:S(2)}) collective-permute-start(bf16[64,1024]{1,0:T(8,128)(2,1)} %bitcast.13), channel_id=1, source_target_pairs={{32,0},{48,16},{0,32},{16,48},{33,1},{49,17},{1,33},{17,49},{34,2}... | collective-permute-start | bytes 393224 | tf_op jit(solution)/shard_map/ppermute | solution.py:181
  37.9 2.0 %collective-permute-start.2 = (bf16[64,1024]{1,0:T(8,128)(2,1)}, bf16[64,1024]{1,0:T(8,128)(2,1)S(1)}, u32[]{:S(2)}, u32[]{:S(2)}) collective-permute-start(bf16[64,1024]{1,0:T(8,128)(2,1)} %bitcast.14), channel_id=1, source_target_pairs={{48,0},{0,16},{16,32},{32,48},{49,1},{1,17},{17,33},{33,49},{50,2}... | collective-permute-start | bytes 393224 | tf_op jit(solution)/shard_map/ppermute | solution.py:181
  39.8 5.1 %collective-permute-start.1 = (bf16[64,1024]{1,0:T(8,128)(2,1)}, bf16[64,1024]{1,0:T(8,128)(2,1)S(1)}, u32[]{:S(2)}, u32[]{:S(2)}) collective-permute-start(bf16[64,1024]{1,0:T(8,128)(2,1)} %bitcast.15), channel_id=1, source_target_pairs={{16,0},{32,16},{48,32},{0,48},{17,1},{33,17},{49,33},{1,49},{18,2}... | collective-permute-start | bytes 393224 | tf_op jit(solution)/shard_map/ppermute | solution.py:181
  45.0 1.3 collective-permute-done.2.r3
  46.3 1.4 collective-permute-done.1.r1
  47.7 7.5 %collective-permute-start.4 = (bf16[2,256,1024]{2,1,0:T(8,128)(2,1)S(1)}, bf16[2,256,1024]{2,1,0:T(8,128)(2,1)S(1)}, u32[]{:S(2)}, u32[]{:S(2)}) collective-permute-start(bf16[2,256,1024]{2,1,0:T(8,128)(2,1)S(1)} %pair.1.cols), channel_id=1, source_target_pairs={{0,8},{8,0},{1,9},{9,1},{2,10},{10,2},{3,11},{11,3},{4,12},{12,4},... | collective-permute-start | bytes 3145736 | tf_op jit(solution)/shard_map/ppermute | solution.py:185
  55.2 1.9 %start.1 = (bf16[128,512]{1,0:T(8,128)(2,1)S(1)}, bf16[8,128,512]{2,1,0:T(8,128)(2,1)}, f32[128,512]{1,0:T(8,128)S(1)}) custom-call(s32[16,64]{1,0:T(8,128)S(1)} %bitcast.17, bf16[128,512]{1,0:T(8,128)(2,1)S(1)} %copy-done), custom_call_target="tpu_custom_call" | custom-call | tf_op jit(solution)/shard_map/start/pallas_call | solution.py:60
  57.4 0.8 partial_gram.1
  58.2 17.1 %all_to_all.15 = bf16[8,128,256]{2,1,0:T(8,128)(2,1)S(1)} all-to-all(bf16[8,128,256]{2,1,0:T(8,128)(2,1)S(1)} %partial_gram.1), channel_id=1, replica_groups=mesh['ylo'=2,'zh'=4,'zl'=4,'core'=2,'yhi'=2,'x'=4] {'yhi','x'}, dimensions={0} | all-to-all | bytes 1048576 | tf_op jit(solution)/shard_map/all_to_all | solution.py:191
  75.5 3.8 %all-gather = bf16[256,256]{1,0:T(8,128)(2,1)S(1)} all-gather(bf16[128,256]{1,0:T(8,128)(2,1)S(1)} %multiply_convert_fusion), channel_id=2, replica_groups=mesh['ylo'=2,'zh'=4,'zl'=4,'core'=2,'yhi'=2,'x'=4] {'ylo'}, dimensions={0}, use_global_device_ids=true | all-gather | bytes 196608 | tf_op jit(solution)/shard_map/all_gather | solution.py:195
  79.3 3.6 %all-to-all-start.1 = ((bf16[8,128,512]{2,1,0:T(8,128)(2,1)}), bf16[8,128,512]{2,1,0:T(8,128)(2,1)S(1)}, u32[]{:S(2)}, u32[]{:S(2)}) async-start(bf16[8,128,512]{2,1,0:T(8,128)(2,1)} %get-tuple-element.30), calls=%async_computation.1 | async-start | bytes 2097152 | tf_op jit(solution)/shard_map/all_to_all | solution.py:197
  82.8 22.6 %all-gather.1 = bf16[8,128,256]{2,1,0:T(8,128)(2,1)S(1)} all-gather(bf16[2,128,256]{2,1,0:T(8,128)(2,1)S(1)} %bitcast.18), channel_id=3, replica_groups=mesh['ylo'=2,'zh'=4,'zl'=4,'core'=2,'yhi'=2,'x'=4] {'zh'}, dimensions={0}, use_global_device_ids=true | all-gather | bytes 655360 | tf_op jit(solution)/shard_map/all_gather | solution.py:198
  105.4 1.9 %collective-permute-start.6 = (bf16[4,2,128,256]{3,2,1,0:T(8,128)(2,1)S(1)}, bf16[4,2,128,256]{3,2,1,0:T(8,128)(2,1)S(1)}, u32[]{:S(2)}, u32[]{:S(2)}) collective-permute-start(bf16[4,2,128,256]{3,2,1,0:T(8,128)(2,1)S(1)} %bitcast.7), channel_id=1, source_target_pairs={{240,0},{248,8},{0,16},{8,24},{16,32},{24,40},{32,48},{40,56},{48,... | collective-permute-start | bytes 1572872 | tf_op jit(solution)/shard_map/ppermute | solution.py:202
  107.3 4.6 %collective-permute-start.5 = (bf16[4,2,128,256]{3,2,1,0:T(8,128)(2,1)S(1)}, bf16[4,2,128,256]{3,2,1,0:T(8,128)(2,1)S(1)}, u32[]{:S(2)}, u32[]{:S(2)}) collective-permute-start(bf16[4,2,128,256]{3,2,1,0:T(8,128)(2,1)S(1)} %bitcast.8), channel_id=1, source_target_pairs={{16,0},{24,8},{32,16},{40,24},{48,32},{56,40},{64,48},{72,56},{80,... | collective-permute-start | bytes 1572872 | tf_op jit(solution)/shard_map/ppermute | solution.py:202
  111.9 3.1 %collective-permute-start.7 = (bf16[4,128,256]{2,1,0:T(8,128)(2,1)S(1)}, bf16[4,128,256]{2,1,0:T(8,128)(2,1)S(1)}, u32[]{:S(2)}, u32[]{:S(2)}) collective-permute-start(bf16[4,128,256]{2,1,0:T(8,128)(2,1)S(1)} %dynamic-slice_bitcast_fusion), channel_id=1, source_target_pairs={{32,0},{232,8},{48,16},{248,24},{64,32},{8,40},{80,48},{24,56},{96... | collective-permute-start | bytes 786440 | tf_op jit(solution)/shard_map/ppermute | solution.py:201
  115.1 11.7 %collective-permute-done.7 = bf16[4,128,256]{2,1,0:T(8,128)(2,1)S(1)} collective-permute-done((bf16[4,128,256]{2,1,0:T(8,128)(2,1)S(1)}, bf16[4,128,256]{2,1,0:T(8,128)(2,1)S(1)}, u32[]{:S(2)}, u32[]{:S(2)}) %collective-permute-start.7) | collective-permute-done | bytes 262176 | tf_op jit(solution)/shard_map/ppermute | solution.py:201
  126.8 5.9 %all-gather.2 = bf16[8,128,256]{2,1,0:T(8,128)(2,1)S(1)} all-gather(bf16[4,128,256]{2,1,0:T(8,128)(2,1)S(1)} %collective-permute-done.7), channel_id=4, replica_groups=mesh['ylo'=2,'zh'=4,'zl'=4,'core'=2,'yhi'=2,'x'=4] {'ylo'}, dimensions={0}, use_global_device_ids=true | all-gather | bytes 786432 | tf_op jit(solution)/shard_map/all_gather | solution.py:203
  132.8 7.9 %collective-permute-start.8 = (bf16[4,4,2,128,256]{4,3,2,1,0:T(8,128)(2,1)S(1)}, bf16[4,4,2,128,256]{4,3,2,1,0:T(8,128)(2,1)S(1)}, u32[]{:S(2)}, u32[]{:S(2)}) collective-permute-start(bf16[4,4,2,128,256]{4,3,2,1,0:T(8,128)(2,1)S(1)} %classes.1.refs_0_), channel_id=1, source_target_pairs={{0,8},{8,0},{1,9},{9,1},{2,10},{10,2},{3,11},{11,3},{4,12},{12,4},... | collective-permute-start | bytes 6291464 | tf_op jit(solution)/shard_map/ppermute | solution.py:204
  140.7 3.8 %collective-permute-done.8.refs_1_ = bf16[4,4,2,128,256]{4,3,2,1,0:T(8,128)(2,1)S(1)} collective-permute-done((bf16[4,4,2,128,256]{4,3,2,1,0:T(8,128)(2,1)S(1)}, bf16[4,4,2,128,256]{4,3,2,1,0:T(8,128)(2,1)S(1)}, u32[]{:S(2)}, u32[]{:S(2)}) %collective-permute-start.8) | collective-permute-done | bytes 2097184 | tf_op jit(solution)/shard_map/ppermute | solution.py:204
  144.5 1.4 first_step.1
  145.9 23.1 %all_to_all.16.diffs = bf16[8,128,512]{2,1,0:T(8,128)(2,1)S(1)} all-to-all(bf16[8,128,512]{2,1,0:T(8,128)(2,1)S(1)} %get-tuple-element.35), channel_id=1, replica_groups=mesh['ylo'=2,'zh'=4,'zl'=4,'core'=2,'yhi'=2,'x'=4] {'yhi','x'}, dimensions={0} | all-to-all | bytes 2097152 | tf_op jit(solution)/shard_map/all_to_all | solution.py:207
  169.0 2.0 %last_step.1 = bf16[128,512]{1,0:T(8,128)(2,1)} custom-call(bf16[8,128,512]{2,1,0:T(8,128)(2,1)S(1)} %all_to_all.16.diffs, bf16[4,4,2,128,256]{4,3,2,1,0:T(8,128)(2,1)S(1)} %classes.1.refs_0_, bf16[4,4,2,128,256]{4,3,2,1,0:T(8,128)(2,1)S(1)} %collective-permute-done.8.refs_1_, bf16[128,512]{1,0:T(8,128)(2,1)S(1)} %get-tuple-element.36.refs_2_, ...), custom_call_target="tpu_custom_call" | custom-call | flops 536870912 | bytes 3145728 | tf_op jit(solution)/shard_map/last_step/pallas_call | solution.py:132
  (17 shorter events, 0.7 us)
Async XLA Ops:
  0.0 57.4 %copy-start.1 = (bf16[1024,64]{0,1:T(8,128)(2,1)S(1)}, bf16[1024,64]{0,1:T(8,128)(2,1)}, u32[]{:S(2)}) copy-start(bf16[1024,64]{0,1:T(8,128)(2,1)} %param.3) | copy-start | bytes 393220
  0.0 55.2 %copy-start = (bf16[128,512]{1,0:T(8,128)(2,1)S(1)}, bf16[128,512]{1,0:T(8,128)(2,1)}, u32[]{:S(2)}) copy-start(bf16[128,512]{1,0:T(8,128)(2,1)} %refs_3_.1) | copy-start | bytes 393220
  0.0 55.2 %copy-start.2 = (s32[64,16]{0,1:T(8,128)S(1)}, s32[64,16]{0,1:T(8,128)}, u32[]{:S(2)}) copy-start(s32[64,16]{0,1:T(8,128)} %param.5) | copy-start | bytes 12292
  31.5 16.1 %collective-permute-start = (bf16[256,1024]{1,0:T(8,128)(2,1)S(1)}, bf16[256,1024]{1,0:T(8,128)(2,1)S(1)}, u32[]{:S(2)}, u32[]{:S(2)}) collective-permute-start(bf16[256,1024]{1,0:T(8,128)(2,1)S(1)} %all_gather.19.own), channel_id=1, source_target_pairs={{0,256},{256,0},{1,257},{257,1},{2,258},{258,2},{3,259},{259,3},{4... | collective-permute-start | bytes 1572872 | tf_op jit(solution)/shard_map/ppermute | solution.py:179
  34.7 10.2 %collective-permute-start.3 = (bf16[64,1024]{1,0:T(8,128)(2,1)}, bf16[64,1024]{1,0:T(8,128)(2,1)S(1)}, u32[]{:S(2)}, u32[]{:S(2)}) collective-permute-start(bf16[64,1024]{1,0:T(8,128)(2,1)} %bitcast.13), channel_id=1, source_target_pairs={{32,0},{48,16},{0,32},{16,48},{33,1},{49,17},{1,33},{17,49},{34,2}... | collective-permute-start | bytes 393224 | tf_op jit(solution)/shard_map/ppermute | solution.py:181
  37.9 8.4 %collective-permute-start.2 = (bf16[64,1024]{1,0:T(8,128)(2,1)}, bf16[64,1024]{1,0:T(8,128)(2,1)S(1)}, u32[]{:S(2)}, u32[]{:S(2)}) collective-permute-start(bf16[64,1024]{1,0:T(8,128)(2,1)} %bitcast.14), channel_id=1, source_target_pairs={{48,0},{0,16},{16,32},{32,48},{49,1},{1,17},{17,33},{33,49},{50,2}... | collective-permute-start | bytes 393224 | tf_op jit(solution)/shard_map/ppermute | solution.py:181
  39.8 7.8 %collective-permute-start.1 = (bf16[64,1024]{1,0:T(8,128)(2,1)}, bf16[64,1024]{1,0:T(8,128)(2,1)S(1)}, u32[]{:S(2)}, u32[]{:S(2)}) collective-permute-start(bf16[64,1024]{1,0:T(8,128)(2,1)} %bitcast.15), channel_id=1, source_target_pairs={{16,0},{32,16},{48,32},{0,48},{17,1},{33,17},{49,33},{1,49},{18,2}... | collective-permute-start | bytes 393224 | tf_op jit(solution)/shard_map/ppermute | solution.py:181
  47.7 9.7 %collective-permute-start.4 = (bf16[2,256,1024]{2,1,0:T(8,128)(2,1)S(1)}, bf16[2,256,1024]{2,1,0:T(8,128)(2,1)S(1)}, u32[]{:S(2)}, u32[]{:S(2)}) collective-permute-start(bf16[2,256,1024]{2,1,0:T(8,128)(2,1)S(1)} %pair.1.cols), channel_id=1, source_target_pairs={{0,8},{8,0},{1,9},{9,1},{2,10},{10,2},{3,11},{11,3},{4,12},{12,4},... | collective-permute-start | bytes 3145736 | tf_op jit(solution)/shard_map/ppermute | solution.py:185
  79.3 26.1 %all-to-all-start.1 = ((bf16[8,128,512]{2,1,0:T(8,128)(2,1)}), bf16[8,128,512]{2,1,0:T(8,128)(2,1)S(1)}, u32[]{:S(2)}, u32[]{:S(2)}) async-start(bf16[8,128,512]{2,1,0:T(8,128)(2,1)} %get-tuple-element.30), calls=%async_computation.1 | async-start | bytes 2097152 | tf_op jit(solution)/shard_map/all_to_all | solution.py:197
  105.4 27.2 %collective-permute-start.6 = (bf16[4,2,128,256]{3,2,1,0:T(8,128)(2,1)S(1)}, bf16[4,2,128,256]{3,2,1,0:T(8,128)(2,1)S(1)}, u32[]{:S(2)}, u32[]{:S(2)}) collective-permute-start(bf16[4,2,128,256]{3,2,1,0:T(8,128)(2,1)S(1)} %bitcast.7), channel_id=1, source_target_pairs={{240,0},{248,8},{0,16},{8,24},{16,32},{24,40},{32,48},{40,56},{48,... | collective-permute-start | bytes 1572872 | tf_op jit(solution)/shard_map/ppermute | solution.py:202
  107.3 25.3 %collective-permute-start.5 = (bf16[4,2,128,256]{3,2,1,0:T(8,128)(2,1)S(1)}, bf16[4,2,128,256]{3,2,1,0:T(8,128)(2,1)S(1)}, u32[]{:S(2)}, u32[]{:S(2)}) collective-permute-start(bf16[4,2,128,256]{3,2,1,0:T(8,128)(2,1)S(1)} %bitcast.8), channel_id=1, source_target_pairs={{16,0},{24,8},{32,16},{40,24},{48,32},{56,40},{64,48},{72,56},{80,... | collective-permute-start | bytes 1572872 | tf_op jit(solution)/shard_map/ppermute | solution.py:202
  111.9 14.8 %collective-permute-start.7 = (bf16[4,128,256]{2,1,0:T(8,128)(2,1)S(1)}, bf16[4,128,256]{2,1,0:T(8,128)(2,1)S(1)}, u32[]{:S(2)}, u32[]{:S(2)}) collective-permute-start(bf16[4,128,256]{2,1,0:T(8,128)(2,1)S(1)} %dynamic-slice_bitcast_fusion), channel_id=1, source_target_pairs={{32,0},{232,8},{48,16},{248,24},{64,32},{8,40},{80,48},{24,56},{96... | collective-permute-start | bytes 786440 | tf_op jit(solution)/shard_map/ppermute | solution.py:201
  132.8 11.7 %collective-permute-start.8 = (bf16[4,4,2,128,256]{4,3,2,1,0:T(8,128)(2,1)S(1)}, bf16[4,4,2,128,256]{4,3,2,1,0:T(8,128)(2,1)S(1)}, u32[]{:S(2)}, u32[]{:S(2)}) collective-permute-start(bf16[4,4,2,128,256]{4,3,2,1,0:T(8,128)(2,1)S(1)} %classes.1.refs_0_), channel_id=1, source_target_pairs={{0,8},{8,0},{1,9},{9,1},{2,10},{10,2},{3,11},{11,3},{4,12},{12,4},... | collective-permute-start | bytes 6291464 | tf_op jit(solution)/shard_map/ppermute | solution.py:204
